TPU v7x, 32 devices: a whole 2x2x4 slice. The times are simulated.
32 devices in a mesh: seq: 4 (over y, x), ctx: 8 (over z, core).
Axes of the slice: x: 2, y: 2, z: 4, core: 2. Of those that a mesh axis runs over, the one named last changes fastest.
Arguments:
- block_input: bfloat16 [4096, 1024], P(('ctx', 'seq')), may hold values from -6 to 6
- teacher: bfloat16 [4096, 1024], P(('ctx', 'seq')), may hold values from -6 to 6
- valid_mask: int32 [4096], P(('ctx', 'seq')), may hold values from 0 to 1
- segments: int32 [4096], replicated, may hold values from 0 to 7, never falling along the last dimension, each value on 1 to 2048 neighbouring positions
- mix_proj: bfloat16 [1024, 5120], P(('seq', 'ctx')), may hold values from -0.1875 to 0.1875
- scalar_proj: bfloat16 [1024, 24], P(('seq', 'ctx')), may hold values from -0.1875 to 0.1875
- gate_proj: bfloat16 [1024, 1024], P(('seq', 'ctx')), may hold values from -0.1875 to 0.1875
- out_proj: bfloat16 [1024, 1024], P(('seq', 'ctx')), may hold values from -0.375 to 0.375
- conv_weight: bfloat16 [5120, 4], P(('seq', 'ctx')), may hold values from -2 to 2
- norm_attn: bfloat16 [1024], P(('seq', 'ctx')), may hold values from 0.5 to 1.5
- norm_mlp: bfloat16 [1024], P(('seq', 'ctx')), may hold values from 0.5 to 1.5
- head_gain: bfloat16 [128], replicated, may hold values from 0.5 to 1.5
- a_log: bfloat16 [8], replicated, may hold values from -8 to 1
- dt_bias: bfloat16 [8], replicated, may hold values from -4 to 0.5
- w_gate: bfloat16 [1024, 2816], P(('seq', 'ctx')), may hold values from -0.1875 to 0.1875
- w_up: bfloat16 [1024, 2816], P(('seq', 'ctx')), may hold values from -0.1875 to 0.1875
- w_down: bfloat16 [2816, 1024], P(('seq', 'ctx')), may hold values from -0.109375 to 0.109375
Outputs:
- output: bfloat16 [4096, 1024], P(('ctx', 'seq'))
- mean_loss: float32 [], replicated
- input_grad: float32 [4096, 1024], P(('ctx', 'seq'))
- grad_mix_proj: float32 [1024, 5120], P(('seq', 'ctx'))
- grad_scalar_proj: float32 [1024, 24], P(('seq', 'ctx'))
- grad_gate_proj: float32 [1024, 1024], P(('seq', 'ctx'))
- grad_out_proj: float32 [1024, 1024], P(('seq', 'ctx'))
- grad_conv_weight: float32 [5120, 4], P(('seq', 'ctx'))
- grad_norm_attn: float32 [1024], P(('seq', 'ctx'))
- grad_norm_mlp: float32 [1024], P(('seq', 'ctx'))
- grad_head_gain: float32 [128], replicated
- grad_a_log: float32 [8], replicated
- grad_dt_bias: float32 [8], replicated
- grad_w_gate: float32 [1024, 2816], P(('seq', 'ctx'))
- grad_w_up: float32 [1024, 2816], P(('seq', 'ctx'))
- grad_w_down: float32 [2816, 1024], P(('seq', 'ctx'))
Inputs may be any that keep to these rules, and one draw needn't show every extreme that they name: `segments`: segment numbers never fall along the tokens; each document has 1 to 2048 tokens and one has exactly 2048.
All inputs are finite; a program needn't handle non-finite values.
Results may differ from a plain program's by a relative error of at most 0.013.
The roundings to bfloat16 on the way count: a program that leaves them out, or rounds other values in their place, can miss the bound.
Values may be sent and summed in bfloat16 or wider, within the bound.
A program may use at most 320 MiB of HBM per device.

v0:
```python
import functools
import math

import jax
import jax.numpy as jnp
from jax import lax
from jax.sharding import PartitionSpec as P

D = 1024
HEADS = 8
HEAD = 128
NH = 2
FF = 2816
BLOCK_LEN = 64
CONV = 4
SEQ_LEN = 32768


NORM_EPS = 1e-06


def passed_along(x, axis, by):
    devices = lax.axis_size(axis)
    pairs = [(i, i + by) for i in range(devices) if 0 <= i + by < devices]
    return lax.ppermute(x, axis, pairs)


def entering(x, axis, combine, identity, reverse):
    devices, index = (lax.axis_size(axis), lax.axis_index(axis))
    everything = jax.tree.map(
        lambda part, kind: lax.all_gather(part.astype(kind), axis), x, (jnp.bfloat16, jnp.bfloat16)
    )
    start = jax.tree.map(
        lambda part, zero: jnp.broadcast_to(jnp.asarray(zero, part.dtype), part.shape), x, identity
    )

    def hop(k, before):
        at = devices - 1 - k if reverse else k
        reached = at > index if reverse else at < index
        new = combine(
            before, jax.tree.map(lambda part, own: part[at].astype(own.dtype), everything, x)
        )
        return jax.tree.map(lambda a, b: jnp.where(reached, a, b), new, before)

    return lax.fori_loop(0, devices, hop, start)


def dense_product(left_mat, right_mat):
    return jnp.dot(
        left_mat, right_mat, precision=lax.Precision.HIGHEST, preferred_element_type=jnp.float32
    )


def rms_scale(values, gain_vec):
    return (
        values * lax.rsqrt(jnp.mean(values * values, axis=-1, keepdims=True) + NORM_EPS) * gain_vec
    )


def unit_rows(values):
    return values * lax.rsqrt(jnp.sum(values * values, axis=-1, keepdims=True) + NORM_EPS)


def gated_norm(head_values, gate_values, gain_vec):
    token_count = head_values.shape[0]
    scaled = rms_scale(head_values, gain_vec)
    gated = scaled * jax.nn.silu(gate_values.reshape(head_values.shape))
    return gated.reshape(token_count, -1)


def swiglu_mix(gate_values, up_values):
    return jax.nn.silu(gate_values) * up_values


def causal_mix(extended, ext_doc, weight):
    span_rows = extended.shape[0] - (CONV - 1)
    own_doc = ext_doc[CONV - 1 :]
    summed = jnp.zeros((span_rows,) + extended.shape[1:], jnp.float32)
    for tap_lag in range(CONV):
        tap_start = CONV - 1 - tap_lag
        linked = (ext_doc[tap_start : tap_start + span_rows] == own_doc).astype(jnp.float32)
        summed = (
            summed
            + linked[:, None, None]
            * extended[tap_start : tap_start + span_rows]
            * weight[:, :, CONV - 1 - tap_lag]
        )
    return summed


def head_inputs(conv_out, scal_rows, a_log, dt_bias):
    row_count = conv_out.shape[0]
    head_count = conv_out.shape[1]
    activated = jax.nn.silu(conv_out).reshape(row_count, head_count, 1 + 2 * NH, HEAD)
    query_vec = unit_rows(activated[:, :, 0]) / math.sqrt(HEAD)
    key_vecs = unit_rows(activated[:, :, 1 : 1 + NH])
    value_vecs = activated[:, :, 1 + NH :]
    beta_gates = jax.nn.sigmoid(scal_rows[:, :, :NH])
    log_gates = -jnp.exp(a_log)[None, :] * jax.nn.softplus(scal_rows[:, :, NH] + dt_bias[None, :])
    return (query_vec, key_vecs, value_vecs, beta_gates, log_gates)


def block_update(state_matrix, pieces):
    query_vec, key_vecs, value_vecs, beta_gates, log_gates, starts = pieces
    step_count = key_vecs.shape[1]
    row_count = key_vecs.shape[0] * step_count
    flat_keys = key_vecs.reshape(row_count, key_vecs.shape[2])
    flat_values = value_vecs.reshape(row_count, value_vecs.shape[2])
    flat_beta = beta_gates.reshape(row_count)
    first_step = (jnp.arange(step_count) == 0).astype(jnp.float32)
    row_log = ((log_gates * (1.0 - starts))[:, None] * first_step[None, :]).reshape(row_count)
    row_start = (starts[:, None] * first_step[None, :]).reshape(row_count)
    cum_log = jnp.cumsum(row_log)
    cum_start = jnp.cumsum(row_start)
    row_index = jnp.arange(row_count)
    linked = (row_index[:, None] >= row_index[None, :]) & (cum_start[:, None] == cum_start[None, :])
    log_decay_spread = jnp.where(linked, cum_log[:, None] - cum_log[None, :], 0.0)
    decay_mat = jnp.where(linked, jnp.exp(log_decay_spread), 0.0)
    carry_in = jnp.where(cum_start == 0.0, jnp.exp(cum_log), 0.0)
    strict_mask = (row_index[:, None] > row_index[None, :]).astype(jnp.float32)
    system = jnp.eye(row_count, dtype=jnp.float32) + flat_beta[
        :, None
    ] * strict_mask * decay_mat * dense_product(flat_keys, flat_keys.T)
    right_side = flat_beta[:, None] * jnp.concatenate(
        [flat_values, carry_in[:, None] * flat_keys], axis=1
    )
    solved = jax.scipy.linalg.solve_triangular(system, right_side, lower=True, unit_diagonal=True)
    value_width = flat_values.shape[1]
    updates = solved[:, :value_width] - dense_product(solved[:, value_width:], state_matrix)
    query_decay = decay_mat[step_count - 1 :: step_count]
    query_carry = carry_in[step_count - 1 :: step_count]
    outputs = query_carry[:, None] * dense_product(query_vec, state_matrix) + dense_product(
        query_decay * dense_product(query_vec, flat_keys.T), updates
    )
    new_state = carry_in[row_count - 1] * state_matrix + dense_product(
        (decay_mat[row_count - 1][:, None] * flat_keys).T, updates
    )
    return (new_state, outputs)


def run_head(query_vec, key_vecs, value_vecs, beta_gates, log_gates, initial, starts):
    row_count = query_vec.shape[0]
    block_count = row_count // BLOCK_LEN
    pieces = (
        query_vec.reshape(block_count, BLOCK_LEN, -1),
        key_vecs.reshape(block_count, BLOCK_LEN, NH, -1),
        value_vecs.reshape(block_count, BLOCK_LEN, NH, -1),
        beta_gates.reshape(block_count, BLOCK_LEN, NH),
        log_gates.reshape(block_count, BLOCK_LEN),
        starts.reshape(block_count, BLOCK_LEN),
    )
    final_state, outputs = lax.scan(jax.checkpoint(block_update), initial, pieces)
    return (outputs.reshape(row_count, -1), final_state)


def piece_forward(
    proj_rows, tail_rows, scal_rows, conv_heads, alog_heads, dt_heads, ext_doc, starts
):
    extended = jnp.concatenate([tail_rows, proj_rows], axis=0)
    conv_out = causal_mix(extended, ext_doc, conv_heads)
    query_vec, key_vecs, value_vecs, beta_gates, log_gates = head_inputs(
        conv_out, scal_rows, alog_heads, dt_heads
    )
    row_count = value_vecs.shape[0]
    head_count = value_vecs.shape[1]
    padded_values = jnp.concatenate(
        [jnp.zeros((row_count, head_count, NH, HEAD), jnp.float32), value_vecs], axis=3
    )
    initial = jnp.concatenate(
        [jnp.eye(HEAD, dtype=jnp.float32), jnp.zeros((HEAD, HEAD), jnp.float32)], axis=1
    )
    outputs, finals = jax.vmap(run_head, in_axes=(1, 1, 1, 1, 1, None, None), out_axes=(1, 0))(
        query_vec, key_vecs, padded_values, beta_gates, log_gates, initial, starts
    )
    return (outputs, finals)


def compose_maps(preceding_transform, later_map):
    return (
        jnp.einsum(
            "hij,hjk->hik", later_map[0], preceding_transform[0], precision=lax.Precision.HIGHEST
        ),
        jnp.einsum(
            "hij,hjk->hik", later_map[0], preceding_transform[1], precision=lax.Precision.HIGHEST
        )
        + later_map[1],
    )


def gather_all(
    mix_proj,
    scalar_proj,
    gate_proj,
    out_proj,
    conv_weight,
    norm_attn,
    norm_mlp,
    w_gate,
    w_up,
    w_down,
):
    return (
        lax.all_gather(mix_proj, ("seq", "ctx"), axis=0, tiled=True),
        lax.all_gather(scalar_proj, ("seq", "ctx"), axis=0, tiled=True),
        lax.all_gather(gate_proj, ("seq", "ctx"), axis=0, tiled=True),
        lax.all_gather(out_proj, ("seq", "ctx"), axis=0, tiled=True),
        lax.all_gather(conv_weight, ("seq", "ctx"), axis=0, tiled=True),
        lax.all_gather(norm_attn, ("seq", "ctx"), axis=0, tiled=True),
        lax.all_gather(norm_mlp, ("seq", "ctx"), axis=0, tiled=True),
        lax.all_gather(w_gate, ("seq", "ctx"), axis=0, tiled=True),
        lax.all_gather(w_up, ("seq", "ctx"), axis=0, tiled=True),
        lax.all_gather(w_down, ("seq", "ctx"), axis=0, tiled=True),
    )


def local(
    block_input,
    teacher,
    valid_mask,
    segments,
    mix_proj,
    scalar_proj,
    gate_proj,
    out_proj,
    conv_weight,
    norm_attn,
    norm_mlp,
    head_gain,
    a_log,
    dt_bias,
    w_gate,
    w_up,
    w_down,
):
    tok_rows = block_input.shape[0]
    seq_size = lax.axis_size("seq")
    heads_here = HEADS // seq_size
    piece_rows = tok_rows * seq_size
    wide_cols = (1 + 2 * NH) * HEAD
    token_total = segments.shape[0]
    seq_length = min(SEQ_LEN, token_total)
    head_start = lax.axis_index("seq") * heads_here
    (
        full_mix,
        full_scal,
        full_gate,
        full_out,
        full_conv,
        full_norm_attn,
        full_norm_mlp,
        full_w_gate,
        full_w_up,
        full_w_down,
    ) = gather_all(
        mix_proj,
        scalar_proj,
        gate_proj,
        out_proj,
        conv_weight,
        norm_attn,
        norm_mlp,
        w_gate,
        w_up,
        w_down,
    )
    inputs_f = block_input.astype(jnp.float32)
    normed_f, norm_in_back = jax.vjp(rms_scale, inputs_f, full_norm_attn.astype(jnp.float32))
    normed = normed_f.astype(jnp.bfloat16)
    proj_tok = jnp.dot(normed, full_mix, preferred_element_type=jnp.float32).astype(jnp.bfloat16)
    scal_tok = jnp.dot(normed, full_scal, preferred_element_type=jnp.float32).astype(jnp.bfloat16)
    gate_out = jnp.dot(normed, full_gate, preferred_element_type=jnp.float32)
    proj_heads, scal_heads = (
        lax.all_to_all(
            proj_tok.reshape(tok_rows, HEADS, wide_cols),
            "seq",
            split_axis=1,
            concat_axis=0,
            tiled=True,
        ),
        lax.all_to_all(
            scal_tok.reshape(tok_rows, HEADS, NH + 1),
            "seq",
            split_axis=1,
            concat_axis=0,
            tiled=True,
        ),
    )
    tail_rows = passed_along(proj_heads[piece_rows - (CONV - 1) :], "ctx", 1)
    piece_start = lax.axis_index("ctx") * piece_rows
    padded_seg = jnp.pad(segments, (CONV, 0))
    window = lax.dynamic_slice_in_dim(padded_seg, piece_start, piece_rows + CONV)
    positions = piece_start - (CONV - 1) + jnp.arange(piece_rows + CONV - 1, dtype=jnp.int32)
    ext_reset = ((positions % seq_length == 0) | (window[1:] != window[:-1])).astype(jnp.int32)
    ext_doc = jnp.cumsum(ext_reset)
    starts = ext_reset[CONV - 1 :].astype(jnp.float32)
    conv_heads = lax.dynamic_slice_in_dim(
        full_conv.reshape(HEADS, wide_cols, CONV), head_start, heads_here, 0
    ).astype(jnp.float32)
    alog_heads = lax.dynamic_slice_in_dim(a_log.astype(jnp.float32), head_start, heads_here, 0)
    dt_heads = lax.dynamic_slice_in_dim(dt_bias.astype(jnp.float32), head_start, heads_here, 0)
    piece_fn = functools.partial(piece_forward, ext_doc=ext_doc, starts=starts)
    (aug_out, summary), piece_back = jax.vjp(
        piece_fn,
        proj_heads.astype(jnp.float32),
        tail_rows.astype(jnp.float32),
        scal_heads.astype(jnp.float32),
        conv_heads,
        alog_heads,
        dt_heads,
    )
    transfer = summary[:, :, :HEAD]
    local_state = summary[:, :, HEAD:]
    eye_stack = jnp.broadcast_to(jnp.eye(HEAD, dtype=jnp.float32), transfer.shape)
    prior_maps = entering(
        (transfer, local_state),
        "ctx",
        compose_maps,
        (eye_stack, jnp.zeros_like(local_state)),
        False,
    )
    incoming_state = prior_maps[1]
    carried_state = aug_out[:, :, :HEAD]
    head_out = aug_out[:, :, HEAD:] + jnp.einsum(
        "zrx,rxm->zrm", carried_state, incoming_state, precision=lax.Precision.HIGHEST
    )
    back_tok = lax.all_to_all(
        head_out.astype(jnp.bfloat16), "seq", split_axis=0, concat_axis=1, tiled=True
    )
    mixed_f, gate_norm_back = jax.vjp(
        gated_norm, back_tok.astype(jnp.float32), gate_out, head_gain.astype(jnp.float32)
    )
    mixed_bf = mixed_f.astype(jnp.bfloat16)
    middle = inputs_f + jnp.dot(mixed_bf, full_out, preferred_element_type=jnp.float32)
    second_f, norm_mlp_back = jax.vjp(rms_scale, middle, full_norm_mlp.astype(jnp.float32))
    second = second_f.astype(jnp.bfloat16)
    gate_values = jnp.dot(second, full_w_gate, preferred_element_type=jnp.float32)
    up_values = jnp.dot(second, full_w_up, preferred_element_type=jnp.float32)
    hidden_f, swiglu_back = jax.vjp(swiglu_mix, gate_values, up_values)
    hidden = hidden_f.astype(jnp.bfloat16)
    final_out = middle + jnp.dot(hidden, full_w_down, preferred_element_type=jnp.float32)
    mask_values = valid_mask.astype(jnp.float32)
    error_rows = final_out - teacher.astype(jnp.float32)
    totals = lax.psum(
        (jnp.sum(mask_values[:, None] * error_rows * error_rows), jnp.sum(mask_values)),
        ("seq", "ctx"),
    )
    valid_count = jnp.maximum(totals[1], 1.0)
    mean_loss = totals[0] / (D * valid_count)
    grad_final = token_total / valid_count * mask_values[:, None] * error_rows
    (
        full_mix,
        full_scal,
        full_gate,
        full_out,
        full_conv,
        full_norm_attn,
        full_norm_mlp,
        full_w_gate,
        full_w_up,
        full_w_down,
    ) = gather_all(
        mix_proj,
        scalar_proj,
        gate_proj,
        out_proj,
        conv_weight,
        norm_attn,
        norm_mlp,
        w_gate,
        w_up,
        w_down,
    )
    grad_branch = grad_final.astype(jnp.bfloat16)
    down_sums = lax.psum_scatter(
        jnp.einsum("tf,td->fd", hidden, grad_branch, preferred_element_type=jnp.float32),
        ("seq", "ctx"),
        scatter_dimension=0,
        tiled=True,
    )
    grad_hidden = jnp.einsum(
        "td,fd->tf", grad_branch, full_w_down, preferred_element_type=jnp.float32
    )
    grad_gate_f, grad_up_f = swiglu_back(grad_hidden)
    grad_gate_bf = grad_gate_f.astype(jnp.bfloat16)
    grad_up_bf = grad_up_f.astype(jnp.bfloat16)
    grad_second = jnp.einsum(
        "tf,df->td", grad_gate_bf, full_w_gate, preferred_element_type=jnp.float32
    ) + jnp.einsum("tf,df->td", grad_up_bf, full_w_up, preferred_element_type=jnp.float32)
    grad_mid_norm, grad_norm_mlp_term = norm_mlp_back(grad_second)
    grad_middle = grad_final + grad_mid_norm
    grad_mixed_bf = grad_middle.astype(jnp.bfloat16)
    grad_out_term = jnp.einsum(
        "tk,td->kd", mixed_bf, grad_mixed_bf, preferred_element_type=jnp.float32
    )
    grad_mixed = jnp.einsum(
        "td,kd->tk", grad_mixed_bf, full_out, preferred_element_type=jnp.float32
    )
    grad_heads_tok, grad_gate_out, grad_gain_term = gate_norm_back(grad_mixed)
    head_gradient = lax.all_to_all(
        grad_heads_tok.astype(jnp.bfloat16), "seq", split_axis=1, concat_axis=0, tiled=True
    ).astype(jnp.float32)
    local_cotangent = jnp.einsum(
        "sde,sdy->dey", carried_state, head_gradient, precision=lax.Precision.HIGHEST
    )
    later_maps = entering(
        (jnp.swapaxes(transfer, 1, 2), local_cotangent),
        "ctx",
        compose_maps,
        (eye_stack, jnp.zeros_like(local_cotangent)),
        True,
    )
    gradient_following = later_maps[1]
    grad_aug = jnp.concatenate(
        [
            jnp.einsum(
                "cxo,xfo->cxf", head_gradient, incoming_state, precision=lax.Precision.HIGHEST
            ),
            head_gradient,
        ],
        axis=2,
    )
    grad_summary = jnp.concatenate(
        [
            jnp.einsum(
                "ods,ozs->odz", gradient_following, incoming_state, precision=lax.Precision.HIGHEST
            ),
            gradient_following,
        ],
        axis=2,
    )
    grad_proj, grad_tail, grad_scal, grad_conv, grad_alog, grad_dt = piece_back(
        (grad_aug, grad_summary)
    )
    rim_back = passed_along(grad_tail, "ctx", -1)
    grad_proj = jnp.concatenate(
        [grad_proj[: piece_rows - (CONV - 1)], grad_proj[piece_rows - (CONV - 1) :] + rim_back],
        axis=0,
    )
    grad_proj_tok, grad_scal_tok = (
        lax.all_to_all(
            grad_proj.astype(jnp.bfloat16), "seq", split_axis=0, concat_axis=1, tiled=True
        ),
        lax.all_to_all(
            grad_scal.astype(jnp.bfloat16), "seq", split_axis=0, concat_axis=1, tiled=True
        ),
    )
    grad_proj_tok = grad_proj_tok.reshape(tok_rows, HEADS * wide_cols)
    grad_scal_tok = grad_scal_tok.reshape(tok_rows, HEADS * (NH + 1))
    grad_gate_out_bf = grad_gate_out.astype(jnp.bfloat16)
    grad_normed = (
        jnp.einsum("tc,dc->td", grad_proj_tok, full_mix, preferred_element_type=jnp.float32)
        + jnp.einsum("tc,dc->td", grad_scal_tok, full_scal, preferred_element_type=jnp.float32)
        + jnp.einsum("tc,dc->td", grad_gate_out_bf, full_gate, preferred_element_type=jnp.float32)
    )
    grad_in_norm, grad_norm_attn_term = norm_in_back(grad_normed)
    input_grad = grad_middle + grad_in_norm
    normed_side = jnp.concatenate([grad_proj_tok, grad_scal_tok, grad_gate_out_bf], axis=1)
    second_side = jnp.concatenate([grad_gate_bf, grad_up_bf], axis=1)
    row_sums = lax.psum_scatter(
        jnp.concatenate(
            [
                jnp.einsum("tr,tc->rc", normed, normed_side, preferred_element_type=jnp.float32),
                jnp.einsum("tr,tc->rc", second, second_side, preferred_element_type=jnp.float32),
            ],
            axis=1,
        ),
        ("seq", "ctx"),
        scatter_dimension=0,
        tiled=True,
    )
    mix_cols = HEADS * wide_cols
    scal_cols = HEADS * (NH + 1)
    gate_cols = HEADS * HEAD
    grad_mix_out = row_sums[:, :mix_cols]
    grad_scal_out = row_sums[:, mix_cols : mix_cols + scal_cols]
    grad_gateproj_out = row_sums[:, mix_cols + scal_cols : mix_cols + scal_cols + gate_cols]
    ff_start = mix_cols + scal_cols + gate_cols
    grad_wgate_out = row_sums[:, ff_start : ff_start + FF]
    grad_wup_out = row_sums[:, ff_start + FF : ff_start + 2 * FF]
    conv_term = lax.dynamic_update_slice_in_dim(
        jnp.zeros((HEADS, wide_cols, CONV), jnp.float32), grad_conv, head_start, 0
    ).reshape(HEADS * wide_cols, CONV)
    mix_sums = (
        lax.psum_scatter(grad_out_term, ("seq", "ctx"), scatter_dimension=0, tiled=True),
        lax.psum_scatter(conv_term, ("seq", "ctx"), scatter_dimension=0, tiled=True),
        lax.psum_scatter(grad_norm_attn_term, ("seq", "ctx"), scatter_dimension=0, tiled=True),
        lax.psum_scatter(grad_norm_mlp_term, ("seq", "ctx"), scatter_dimension=0, tiled=True),
    )
    head_pick = (jnp.arange(HEADS)[None, :] == head_start + jnp.arange(heads_here)[:, None]).astype(
        jnp.float32
    )
    small_sums = lax.psum(
        (
            grad_gain_term,
            jnp.dot(grad_alog, head_pick, precision=lax.Precision.HIGHEST),
            jnp.dot(grad_dt, head_pick, precision=lax.Precision.HIGHEST),
        ),
        ("seq", "ctx"),
    )
    return (
        final_out.astype(jnp.bfloat16),
        mean_loss,
        input_grad,
        grad_mix_out,
        grad_scal_out,
        grad_gateproj_out,
        mix_sums[0],
        mix_sums[1],
        mix_sums[2],
        mix_sums[3],
        small_sums[0],
        small_sums[1],
        small_sums[2],
        grad_wgate_out,
        grad_wup_out,
        down_sums,
    )


def solution(mesh):
    in_specs = (
        P(("ctx", "seq"), None),
        P(("ctx", "seq"), None),
        P(("ctx", "seq")),
        P(),
        P(("seq", "ctx"), None),
        P(("seq", "ctx"), None),
        P(("seq", "ctx"), None),
        P(("seq", "ctx"), None),
        P(("seq", "ctx"), None),
        P(("seq", "ctx")),
        P(("seq", "ctx")),
        P(),
        P(),
        P(),
        P(("seq", "ctx"), None),
        P(("seq", "ctx"), None),
        P(("seq", "ctx"), None),
    )
    out_specs = (
        P(("ctx", "seq"), None),
        P(),
        P(("ctx", "seq"), None),
        P(("seq", "ctx"), None),
        P(("seq", "ctx"), None),
        P(("seq", "ctx"), None),
        P(("seq", "ctx"), None),
        P(("seq", "ctx"), None),
        P(("seq", "ctx")),
        P(("seq", "ctx")),
        P(),
        P(),
        P(),
        P(("seq", "ctx"), None),
        P(("seq", "ctx"), None),
        P(("seq", "ctx"), None),
    )
    return jax.shard_map(local, mesh=mesh, in_specs=in_specs, out_specs=out_specs, check_vma=False)
```

profile of v0, /device:TPU:0, one launch (start us, length us, event | category | flops | bytes accessed | tf_op | source)
XLA Modules:
  0.0 2022.1 jit_solution(6830292870144924450)
XLA Ops:
  12.3 42.9 %all-reduce.28 = (bf16[1024]{0:T(1024)(128)(2,1)S(1)}, bf16[1024]{0:T(1024)(128)(2,1)S(1)}) all-reduce(bf16[1024]{0:T(1024)(128)(2,1)S(1)} %dynamic-update-slice, bf16[1024]{0:T(1024)(128)(2,1)S(1)} %dynamic-update-slice.1), channel_id=1, replica_groups=mesh['seq'=4,'ctx'=8] {'seq','ctx'}, use_global_device_ids=true, to_apply=%add.23 | all-reduce | flops 2048 | bytes 8192
  55.2 42.6 %all-gather.4 = bf16[32,32,24]{1,2,0:T(8,128)(2,1)S(1)} all-gather(bf16[1,32,24]{1,2,0:T(8,128)(2,1)} %bitcast.606), channel_id=1, replica_groups=mesh['seq'=4,'ctx'=8] {'seq','ctx'}, dimensions={0}, use_global_device_ids=true | all-gather | bytes 50688 | tf_op jit(solution)/shard_map/all_gather | solution.py:204
  107.1 38.7 %psum.36 = f32[]{:T(128)} all-reduce(f32[]{:T(128)} %convert_reduce_fusion), channel_id=1, replica_groups=mesh['seq'=4,'ctx'=8] {'seq','ctx'}, use_global_device_ids=true, to_apply=%region_16.18 | all-reduce | flops 1 | bytes 8 | tf_op jit(solution)/shard_map/psum | solution.py:343
  147.1 40.7 %all-gather.5 = bf16[32,160,4]{1,2,0:T(4,128)(2,1)S(1)} all-gather(bf16[1,160,4]{1,2,0:T(4,128)(2,1)S(1)} %bitcast.607), channel_id=1, replica_groups=mesh['seq'=4,'ctx'=8] {'seq','ctx'}, dimensions={0}, use_global_device_ids=true | all-gather | bytes 42240 | tf_op jit(solution)/shard_map/all_gather | solution.py:207
  188.8 5.6 convolution_convert_fusion
  202.0 18.1 all-to-all-done.1
  247.6 4.6 copy.394
  252.1 255.5 %while.72 = (s32[]{:T(128)}, f32[2,128,256]{2,1,0:T(8,128)S(1)}, f32[8,2,64,256]{3,2,1,0:T(8,128)}, f32[8,2,128,256]{3,2,1,0:T(8,128)}, f32[8,64]{1,0:T(8,128)},...) while((s32[]{:T(128)}, f32[2,128,256]{2,1,0:T(8,128)S(1)}, ...), condition=%wide.region_8.10_spmd.clone, body=%wide.region_5.9_spmd.clone.sunk | while | flops 529629888 | bytes 7259373 | solution.py:152
  260.1 19.7 custom-call.26
  292.0 19.7 custom-call.26
  324.0 19.7 custom-call.26
  355.9 19.7 custom-call.26
  387.8 19.7 custom-call.26
  419.7 19.7 custom-call.26
  451.7 19.7 custom-call.26
  483.6 19.7 custom-call.26
  509.0 15.1 all-gather.1
  524.1 15.8 all-gather
  539.9 8.9 while.73
  554.8 5.3 all-to-all-done.2
  569.3 4.7 fusion.219
  574.0 5.4 multiply_convert_fusion.1
  583.3 6.4 multiply_convert_fusion
  607.4 14.9 all-gather.2
  626.4 14.8 all-gather.3
  652.4 436.8 %while.71 = (s32[]{:T(128)}, f32[2,128,256]{2,1,0:T(8,128)S(1)}, f32[8,2,64,128]{3,2,0,1:T(8,128)}, f32[8,2,64,2,128]{4,2,0,3,1:T(8,128)}, f32[8,2,64,2,256]{4,2...) while((s32[]{:T(128)}, f32[2,128,256]{2,1,0:T(8,128)S(1)}, ...), condition=%wide.region_34.36_spmd, body=%wide.region_21.35_spmd.sunk | while | flops 1488291200 | bytes 20473336 | solution.py:152
  665.7 19.7 custom-call.25
  720.3 19.7 custom-call.25
  774.8 19.7 custom-call.25
  829.3 19.7 custom-call.25
  883.9 19.7 custom-call.25
  938.4 19.7 custom-call.25
  993.0 19.7 custom-call.25
  1047.6 19.7 custom-call.25
  1106.5 5.2 multiply_reduce_fusion.9
  1120.8 4.3 all-to-all-start.5
  1134.9 9.5 fusion.135
  1147.5 4.6 all-to-all-done.4
  1153.3 10.3 fusion.126
  1163.6 33.0 %pad_maximum_fusion.2 = f32[1024,11800]{0,1:T(8,128)} fusion(f32[1024,5632]{0,1:T(8,128)} %fusion.135, f32[1024,6168]{0,1:T(8,128)} %fusion.126), kind=kLoop, calls=%fused_computation.194 | loop fusion | flops 12083200 | bytes 96665600 | tf_op jit(solution)/shard_map/concatenate | solution.py:460
  1196.7 48.1 %copy.462 = f32[1024,11800]{1,0:T(8,128)} copy(f32[1024,11800]{0,1:T(8,128)} %pad_maximum_fusion.2) | data formatting | bytes 96665600
  1249.8 6.0 fusion.224
  1259.6 26.4 %reduce-scatter.15.cloned.1.call-done = f32[160,4]{1,0:T(8,128)} async-done(((f32[5120,4]{1,0:T(8,128)}), f32[160,4]{1,0:T(8,128)}) %reduce-scatter.15.cloned.1.call-update) | async-done | bytes 2576
  1287.6 7.6 fusion.222
  1295.6 37.4 %all-reduce.27 = (f32[]{:T(128)}, f32[1024]{0:T(1024)S(1)}, f32[1024]{0:T(1024)S(1)}, f32[128]{0:T(128)}, f32[8]{0:T(128)}, /*index=5*/f32[8]{0:T(128)}) all-reduce(f32[]{:T(128)} %get-tuple-element.1160, f32[1024]{0:T(1024)S(1)} %get-tuple-element.1042, f32[1024]{0:T(1024)S(1)} %copy-done.77, ...), channel_id=1, replica_groups=mesh['seq'=4,'ctx'=8] {'seq','ctx'}, use_global_device_ids=true, to_apply=%region_14.16 | all-reduce | flops 2193 | bytes 17544 | tf_op jit(solution)/shard_map/psum | solution.py:343
  1335.8 373.0 %reduce-scatter.13.cloned.1.call-done = f32[32,11800]{1,0:T(8,128)} async-done(((f32[1024,11800]{1,0:T(8,128)}), f32[32,11800]{1,0:T(8,128)}) %reduce-scatter.13.cloned.1.call-update) | async-done | bytes 1510416
  1716.1 137.2 %reduce-scatter.9.cloned.1.call-done = f32[32,1024]{1,0:T(8,128)} async-done(((f32[1024,1024]{1,0:T(8,128)}), f32[32,1024]{1,0:T(8,128)}) %reduce-scatter.9.cloned.1.call-update) | async-done | bytes 131088 | tf_op jit(solution)/shard_map/reduce_scatter | solution.py:484
  1853.3 160.6 %reduce-scatter.11.cloned.1.call-done = f32[88,1024]{1,0:T(8,128)} async-done(((f32[2816,1024]{1,0:T(8,128)}), f32[88,1024]{1,0:T(8,128)}) %reduce-scatter.11.cloned.1.call-update) | async-done | bytes 360464 | tf_op jit(solution)/shard_map/reduce_scatter | solution.py:374
  (1465 shorter events, 546.8 us)
Async XLA Ops:
  7.2 181.6 %copy-start.8 = (bf16[128,1024]{1,0:T(8,128)(2,1)S(1)}, bf16[128,1024]{1,0:T(8,128)(2,1)}, u32[]{:S(2)}) copy-start(bf16[128,1024]{1,0:T(8,128)(2,1)} %param.27) | copy-start | bytes 786436
  7.2 97.8 %copy-start.95 = (s32[128]{0:T(128)S(1)}, s32[128]{0:T(128)}, u32[]{:S(2)}) copy-start(s32[128]{0:T(128)} %param.29) | copy-start | bytes 1540
  7.2 98.9 %copy-start.78 = (s32[4096]{0:T(1024)S(1)}, s32[4096]{0:T(1024)}, u32[]{:S(2)}) copy-start(s32[4096]{0:T(1024)} %param.30) | copy-start | bytes 49156
  7.2 138.6 %copy-start.92 = (bf16[128]{0:T(256)(128)(2,1)S(1)}, bf16[128]{0:T(256)(128)(2,1)}, u32[]{:S(2)}) copy-start(bf16[128]{0:T(256)(128)(2,1)} %param.38) | copy-start | bytes 772
  7.2 138.6 %copy-start.93 = (bf16[8]{0:T(256)(128)(2,1)S(1)}, bf16[8]{0:T(256)(128)(2,1)}, u32[]{:S(2)}) copy-start(bf16[8]{0:T(256)(128)(2,1)} %param.39) | copy-start | bytes 52
  7.2 139.8 %copy-start.84 = (bf16[160,4]{0,1:T(4,128)(2,1)S(1)}, bf16[160,4]{0,1:T(4,128)(2,1)}, u32[]{:S(2)}) copy-start(bf16[160,4]{0,1:T(4,128)(2,1)} %param.35) | copy-start | bytes 3844
  7.2 180.7 %copy-start.94 = (bf16[8]{0:T(256)(128)(2,1)S(1)}, bf16[8]{0:T(256)(128)(2,1)}, u32[]{:S(2)}) copy-start(bf16[8]{0:T(256)(128)(2,1)} %param.40) | copy-start | bytes 52
  7.3 181.5 %all-gather.13.cloned.1.call-start = ((), (), s32[]{:S(2)}) async-start(), calls=%async_computation.10 | async-start | bytes 10813440 | tf_op jit(solution)/shard_map/all_gather | solution.py:203
  8.0 555.0 %all-gather.15.cloned.1.call-start = ((), (), s32[]{:S(2)}) async-start(), calls=%async_computation.11 | async-start | bytes 2162688 | tf_op jit(solution)/shard_map/all_gather | solution.py:205
  8.7 558.2 %all-gather.17.cloned.1.call-start = ((), (), s32[]{:S(2)}) async-start(), calls=%async_computation.12 | async-start | bytes 2162688 | tf_op jit(solution)/shard_map/all_gather | solution.py:206
  9.5 559.8 %all-gather.19.cloned.1.call-start = ((), (), s32[]{:S(2)}) async-start(), calls=%async_computation.13 | async-start | bytes 5947392 | tf_op jit(solution)/shard_map/all_gather | solution.py:210
  10.1 563.9 %all-gather.21.cloned.1.call-start = ((), (), s32[]{:S(2)}) async-start(), calls=%async_computation.14 | async-start | bytes 5947392 | tf_op jit(solution)/shard_map/all_gather | solution.py:211
  55.2 508.0 %copy-start.40 = (f32[1024]{0:T(1024)}, f32[1024]{0:T(1024)S(1)}, u32[]{:S(2)}) copy-start(f32[1024]{0:T(1024)S(1)} %convert_element_type.283) | copy-start | bytes 12292
  98.1 96.3 %copy-start.46 = (bf16[1024,24]{0,1:T(8,128)(2,1)}, bf16[1024,24]{0,1:T(8,128)(2,1)S(1)}, u32[]{:S(2)}) copy-start(bf16[1024,24]{0,1:T(8,128)(2,1)S(1)} %reshape.801) | copy-start | bytes 147460
  99.3 463.9 %copy-start.57 = (f32[128]{0:T(128)}, f32[128]{0:T(128)S(1)}, u32[]{:S(2)}) copy-start(f32[128]{0:T(128)S(1)} %fusion.197) | copy-start | bytes 1540
  101.2 94.5 %all-to-all-start = ((bf16[128,8,3]{0,2,1:T(4,128)(2,1)}), bf16[128,8,3]{0,2,1:T(4,128)(2,1)S(1)}, u32[]{:S(2)}, u32[]{:S(2)}) async-start(bf16[128,8,3]{0,2,1:T(4,128)(2,1)} %reshape.755), calls=%async_computation | async-start | bytes 16384 | tf_op jit(solution)/shard_map/all_to_all | solution.py:280
  104.4 475.0 %all-gather.23.cloned.1.call-start = ((), (), s32[]{:S(2)}) async-start(), calls=%async_computation.15 | async-start | bytes 5947392 | tf_op jit(solution)/shard_map/all_gather | solution.py:212
  145.8 53.4 %copy-start.97 = (f32[8]{0:T(128)}, f32[8]{0:T(128)S(1)}, u32[]{:S(2)}) copy-start(f32[8]{0:T(128)S(1)} %convert_element_type.282) | copy-start | bytes 100
  195.6 24.4 %all-to-all-start.1 = ((bf16[128,8,640]{2,0,1:T(8,128)(2,1)}), bf16[128,8,640]{2,0,1:T(8,128)(2,1)S(1)}, u32[]{:S(2)}, u32[]{:S(2)}) async-start(bf16[128,8,640]{2,0,1:T(8,128)(2,1)} %bitcast.396), calls=%async_computation.1 | async-start | bytes 2621440 | tf_op jit(solution)/shard_map/all_to_all | solution.py:273
  199.4 23.2 %copy-start.71 = (f32[512]{0:T(512)}, f32[512]{0:T(512)S(1)}, u32[]{:S(2)}) copy-start(f32[512]{0:T(512)S(1)} %get-tuple-element.1175) | copy-start | bytes 6148
  199.4 23.2 %copy-start.73 = (f32[512]{0:T(512)}, f32[512]{0:T(512)S(1)}, u32[]{:S(2)}) copy-start(f32[512]{0:T(512)S(1)} %get-tuple-element.1176) | copy-start | bytes 6148
  199.4 23.2 %copy-start.75 = (f32[512]{0:T(512)}, f32[512]{0:T(512)S(1)}, u32[]{:S(2)}) copy-start(f32[512]{0:T(512)S(1)} %get-tuple-element.1177) | copy-start | bytes 6148
  199.4 23.2 %copy-start.61 = (f32[2,640]{1,0:T(2,128)}, f32[2,640]{1,0:T(2,128)S(1)}, u32[]{:S(2)}) copy-start(f32[2,640]{1,0:T(2,128)S(1)} %get-tuple-element.1166) | copy-start | bytes 15364
  199.4 23.2 %copy-start.63 = (f32[2,640]{1,0:T(2,128)}, f32[2,640]{1,0:T(2,128)S(1)}, u32[]{:S(2)}) copy-start(f32[2,640]{1,0:T(2,128)S(1)} %get-tuple-element.1167) | copy-start | bytes 15364
  199.4 23.2 %copy-start.65 = (f32[2,640]{1,0:T(2,128)}, f32[2,640]{1,0:T(2,128)S(1)}, u32[]{:S(2)}) copy-start(f32[2,640]{1,0:T(2,128)S(1)} %get-tuple-element.1168) | copy-start | bytes 15364
  199.4 23.2 %copy-start.67 = (f32[2,640]{1,0:T(2,128)}, f32[2,640]{1,0:T(2,128)S(1)}, u32[]{:S(2)}) copy-start(f32[2,640]{1,0:T(2,128)S(1)} %get-tuple-element.1169) | copy-start | bytes 15364
  220.3 2.3 collective-permute-start
  508.9 40.4 %copy-start.13 = (f32[2,8,64,256]{3,2,1,0:T(8,128)}, f32[2,8,64,256]{3,2,1,0:T(8,128)S(1)}, u32[]{:S(2)}) copy-start(f32[2,8,64,256]{3,2,1,0:T(8,128)S(1)} %copy.396) | copy-start | bytes 3145732
  550.4 9.8 all-to-all-start.2
  599.1 26.6 %copy-start.14 = (f32[2,8,64,256]{3,2,1,0:T(8,128)S(1)}, f32[2,8,64,256]{3,2,1,0:T(8,128)}, u32[]{:S(2)}) copy-start(f32[2,8,64,256]{3,2,1,0:T(8,128)} %copy-done.13) | copy-start | bytes 3145732
  603.8 20.3 %all-to-all-start.3 = ((bf16[128,8,128]{2,0,1:T(8,128)(2,1)}), bf16[128,8,128]{2,0,1:T(8,128)(2,1)S(1)}, u32[]{:S(2)}, u32[]{:S(2)}) async-start(bf16[128,8,128]{2,0,1:T(8,128)(2,1)} %fusion.150), calls=%async_computation.3 | async-start | bytes 524288 | tf_op jit(solution)/shard_map/all_to_all | solution.py:399
  663.2 22.8 %copy-start.20 = (f32[2,128]{1,0:T(2,128)}, f32[2,128]{1,0:T(2,128)S(1)}, u32[]{:S(2)}) copy-start(f32[2,128]{1,0:T(2,128)S(1)} %reduce_window_sum.79) | copy-start | bytes 3076 | tf_op jit(solution)/shard_map/transpose(jvp(vmap()))/while
  663.2 22.8 %copy-start.45 = (f32[2,128]{1,0:T(2,128)}, f32[2,128]{1,0:T(2,128)S(1)}, u32[]{:S(2)}) copy-start(f32[2,128]{1,0:T(2,128)S(1)} %broadcast_select_fusion.2) | copy-start | bytes 3076 | tf_op jit(solution)/shard_map/transpose(jvp(vmap()))/while
  717.8 22.8 %copy-start.20 = (f32[2,128]{1,0:T(2,128)}, f32[2,128]{1,0:T(2,128)S(1)}, u32[]{:S(2)}) copy-start(f32[2,128]{1,0:T(2,128)S(1)} %reduce_window_sum.79) | copy-start | bytes 3076 | tf_op jit(solution)/shard_map/transpose(jvp(vmap()))/while
  717.8 22.8 %copy-start.45 = (f32[2,128]{1,0:T(2,128)}, f32[2,128]{1,0:T(2,128)S(1)}, u32[]{:S(2)}) copy-start(f32[2,128]{1,0:T(2,128)S(1)} %broadcast_select_fusion.2) | copy-start | bytes 3076 | tf_op jit(solution)/shard_map/transpose(jvp(vmap()))/while
  772.3 22.8 %copy-start.45 = (f32[2,128]{1,0:T(2,128)}, f32[2,128]{1,0:T(2,128)S(1)}, u32[]{:S(2)}) copy-start(f32[2,128]{1,0:T(2,128)S(1)} %broadcast_select_fusion.2) | copy-start | bytes 3076 | tf_op jit(solution)/shard_map/transpose(jvp(vmap()))/while
  826.8 22.8 %copy-start.45 = (f32[2,128]{1,0:T(2,128)}, f32[2,128]{1,0:T(2,128)S(1)}, u32[]{:S(2)}) copy-start(f32[2,128]{1,0:T(2,128)S(1)} %broadcast_select_fusion.2) | copy-start | bytes 3076 | tf_op jit(solution)/shard_map/transpose(jvp(vmap()))/while
  881.3 22.8 %copy-start.45 = (f32[2,128]{1,0:T(2,128)}, f32[2,128]{1,0:T(2,128)S(1)}, u32[]{:S(2)}) copy-start(f32[2,128]{1,0:T(2,128)S(1)} %broadcast_select_fusion.2) | copy-start | bytes 3076 | tf_op jit(solution)/shard_map/transpose(jvp(vmap()))/while
  935.9 22.8 %copy-start.45 = (f32[2,128]{1,0:T(2,128)}, f32[2,128]{1,0:T(2,128)S(1)}, u32[]{:S(2)}) copy-start(f32[2,128]{1,0:T(2,128)S(1)} %broadcast_select_fusion.2) | copy-start | bytes 3076 | tf_op jit(solution)/shard_map/transpose(jvp(vmap()))/while
  1045.1 22.8 %copy-start.45 = (f32[2,128]{1,0:T(2,128)}, f32[2,128]{1,0:T(2,128)S(1)}, u32[]{:S(2)}) copy-start(f32[2,128]{1,0:T(2,128)S(1)} %broadcast_select_fusion.2) | copy-start | bytes 3076 | tf_op jit(solution)/shard_map/transpose(jvp(vmap()))/while
  1118.1 8.9 collective-permute-start.1
  1120.8 9.9 all-to-all-start.5
  1130.7 21.4 %all-to-all-start.4 = ((bf16[512,2,640]{2,1,0:T(2,128)(2,1)}), bf16[512,2,640]{2,1,0:T(2,128)(2,1)S(1)}, u32[]{:S(2)}, u32[]{:S(2)}) async-start(bf16[512,2,640]{2,1,0:T(2,128)(2,1)} %copy.433), calls=%async_computation.4 | async-start | bytes 2621440 | tf_op jit(solution)/shard_map/all_to_all | solution.py:440
  1134.9 151.1 %reduce-scatter.15.cloned.1.call-start = ((), (), s32[]{:S(2)}) async-start(), calls=%async_computation.19 | async-start | bytes 2703360
  1146.8 562.1 %reduce-scatter.13.cloned.1.call-start = ((), (), s32[]{:S(2)}) async-start(), calls=%async_computation.18 | async-start | bytes 50282496
  1244.8 608.5 %reduce-scatter.9.cloned.1.call-start = ((), (), s32[]{:S(2)}) async-start(), calls=%async_computation.16 | async-start | bytes 4325376 | tf_op jit(solution)/shard_map/reduce_scatter | solution.py:484
  1248.7 765.2 %reduce-scatter.11.cloned.1.call-start = ((), (), s32[]{:S(2)}) async-start(), calls=%async_computation.17 | async-start | bytes 11894784 | tf_op jit(solution)/shard_map/reduce_scatter | solution.py:374
  1287.6 47.3 %copy-start.90 = (f32[128]{0:T(128)S(1)}, f32[128]{0:T(128)}, u32[]{:S(2)}) copy-start(f32[128]{0:T(128)} %copy-done.89) | copy-start | bytes 1540
  (136 other events, 859.2 us)
Sparse Core Ops, SparseCore 0:
  10.9 89.8 all-gather.12
  103.8 56.0 all-gather.14
  162.9 61.7 all-gather.16
  227.4 65.1 all-gather.18
  295.3 67.3 all-gather.20
  365.4 66.7 all-gather.22
  1146.9 139.0 reduce-scatter.14
  1292.4 416.3 reduce-scatter.12
  1711.8 141.3 reduce-scatter.8
  1856.1 157.7 reduce-scatter.10
where the time goes:
time: 2040 us; the launch traced here: 2020 us
  waiting for transfers between devices  729 us (36%)
  other arithmetic  450 us (22%)
  local copies, waits for them, and re-layouts  276 us (14%)
  blocking collectives  263 us (13%)
  matrix products  254 us (12%)
  starting transfers between devices  26 us (1%)
    unnamed x12, waiting for transfers between devices  403 us
    another operation x72, other arithmetic, block_update(): jax.scipy.linalg.solve_triangular(system, right_side, lower=True, unit_di...  318 us
    reduce_scatter x1, waiting for transfers between devices, local(): lax.psum_scatter(jnp.einsum('tf,td->fd', hidden, grad_branch, preferred_e...  161 us
    reduce_scatter x1, waiting for transfers between devices, local(): lax.psum_scatter(grad_out_term, ('seq', 'ctx'), scatter_dimension=0, tile...  137 us
    dot_general x176, matrix products, dense_product(): jnp.dot(left_mat, right_mat, precision=lax.Precision.HIGHEST, preferred_e...  125 us
    unnamed x207, local copies, waits for them, and re-layouts  77.4 us
    psum x2, blocking collectives, local(): lax.psum((jnp.sum(mask_values[:, None] * error_rows * error_rows), jnp.su...  76.1 us
    all_gather x4, blocking collectives, entering(): lax.all_gather(part.astype(kind), axis)  60.6 us
  transfers between devices with their start and end apart: 18, of which 8 were waited for; matrix products, arithmetic and copies ran while one was open for 24% of the time, Pallas kernels for 0%

commit v1 on v0

v1 whole, which is shorter than its diff:
```python
import functools
import math

import jax
import jax.numpy as jnp
from jax import lax
from jax.experimental import pallas as pl
from jax.experimental.pallas import tpu as pltpu
from jax.sharding import PartitionSpec as P

D = 1024
HEADS = 8
HEAD = 128
NH = 2
FF = 2816
BLOCK_LEN = 64
ROWS = BLOCK_LEN * NH
CONV = 4
SEQ_LEN = 32768
WIDE = (1 + 2 * NH) * HEAD
HALO = 16
NORM_EPS = 1e-06
F32 = jnp.float32
BF16 = jnp.bfloat16
BOTH = ("seq", "ctx")


def split_bf16(x):
    if x.dtype == BF16:
        return x, None
    high = x.astype(BF16)
    return high, (x - high.astype(F32)).astype(BF16)


def mm(a, b, ca=1, cb=0, passes=3):
    def one(x, y):
        return lax.dot_general(x, y, (((ca,), (cb,)), ((), ())), preferred_element_type=F32)

    if passes == 1:
        return one(a.astype(BF16), b.astype(BF16))
    ah, al = split_bf16(a)
    bh, bl = split_bf16(b)
    total = one(ah, bh)
    if bl is not None:
        total = total + one(ah, bl)
    if al is not None:
        total = total + one(al, bh)
    return total


def iota(shape, axis):
    return lax.broadcasted_iota(jnp.int32, shape, axis)


def unit_lower_inverse(a):
    n = a.shape[0]
    ri, ci = iota((n, n), 0), iota((n, n), 1)
    own = jnp.where(ri // 8 == ci // 8, a, 0.0)
    pick = (iota((n, 8), 0) % 8 == iota((n, 8), 1)).astype(BF16)
    small = mm(own, pick).reshape(n // 8, 8, 8)
    inv = (ri == ci).astype(F32).reshape(n // 8, 8, n)
    for j in range(7):
        inv = inv - small[:, :, j : j + 1] * inv[:, j : j + 1, :]
    inv = inv.reshape(n, n)
    size = 8
    while size < n:
        off = (ri // (2 * size) == ci // (2 * size)) & (ri // size != ci // size)
        inv = inv - mm(inv, mm(jnp.where(off, a, 0.0), inv))
        size *= 2
    return inv


def decays(rowp, colp, tokp, h):
    cs_row, g_row = rowp[0:1, :], rowp[2 + 2 * h : 3 + 2 * h, :]
    cs_col, g_col = colp[:, 0:1], colp[:, 2 + 2 * h : 3 + 2 * h]
    cs_tok, g_tok = tokp[:, 3:4], tokp[:, 4 + h : 5 + h]
    beta = colp[:, 3 + 2 * h : 4 + 2 * h]
    ri, ci = iota((ROWS, ROWS), 0), iota((ROWS, ROWS), 1)
    strict = (ri > ci) & (cs_col == cs_row)
    decay = jnp.where(strict, jnp.exp(jnp.where(strict, g_col - g_row, 0.0)), 0.0)
    rt, ct = iota((BLOCK_LEN, ROWS), 0), iota((BLOCK_LEN, ROWS), 1)
    seen = (rt * NH + NH - 1 >= ct) & (cs_tok == cs_row)
    qdecay = jnp.where(seen, jnp.exp(jnp.where(seen, g_tok - g_row, 0.0)), 0.0)
    carry = jnp.where(cs_col == 0.0, jnp.exp(g_col), 0.0)
    qcarry = jnp.where(cs_tok == 0.0, jnp.exp(g_tok), 0.0)
    cs_last, g_last = cs_row[:, ROWS - 1 :], g_row[:, ROWS - 1 :]
    same = cs_col == cs_last
    dlast = jnp.where(same, jnp.exp(jnp.where(same, g_last - g_col, 0.0)), 0.0)
    clast = jnp.where(cs_last == 0.0, jnp.exp(g_last), 0.0)
    return beta, decay, qdecay, carry, qcarry, dlast, clast


def lag_rows(ext, lag):
    moved = pltpu.roll(ext, lag, 0) if lag else ext
    return moved[HALO:]


def fwd_kernel(
    heads, proj_ref, w_ref, rowp_ref, colp_ref, tokp_ref,
    oloc_ref, carr_ref, fin_ref, conv_ref, q_ref, k_ref, v_ref, t_ref, kk_ref, at_ref, uw_ref, pl_ref,
    state, weave,
):
    step = pl.program_id(0)
    eye = (iota((HEAD, HEAD), 0) == iota((HEAD, HEAD), 1)).astype(F32)

    @pl.when(step == 0)
    def _():
        for h in range(heads):
            state[h, :, :HEAD] = eye
            state[h, :, HEAD:] = jnp.zeros((HEAD, HEAD), F32)

    base = pl.multiple_of(step * BLOCK_LEN, BLOCK_LEN)
    rowp, colp, tokp = rowp_ref[0], colp_ref[0], tokp_ref[0]
    for h in range(heads):
        cols = slice(h * WIDE, (h + 1) * WIDE)
        ext = proj_ref[pl.ds(base, BLOCK_LEN + HALO), cols].astype(F32)
        conv = ext[HALO:] * w_ref[0:1, cols]
        for lag in range(1, CONV):
            conv = conv + tokp[:, lag - 1 : lag] * lag_rows(ext, lag) * w_ref[lag : lag + 1, cols]
        conv_ref[:, cols] = conv
        act = conv * jax.nn.sigmoid(conv)
        unit = []
        for part in range(1 + NH):
            piece = act[:, part * HEAD : (part + 1) * HEAD]
            unit.append(piece * lax.rsqrt(jnp.sum(piece * piece, axis=1, keepdims=True) + NORM_EPS))
        query = unit[0] * (1.0 / math.sqrt(HEAD))
        for j in range(NH):
            weave[2 * h, pl.ds(j, BLOCK_LEN, NH), :] = unit[1 + j]
            weave[2 * h + 1, pl.ds(j, BLOCK_LEN, NH), :] = act[:, (1 + NH + j) * HEAD : (2 + NH + j) * HEAD]
        keys, values = weave[2 * h], weave[2 * h + 1]
        beta, decay, qdecay, carry, qcarry, dlast, clast = decays(rowp, colp, tokp, h)
        kk = decay * mm(keys, keys, 1, 1)
        inv = unit_lower_inverse(beta * kk)
        uw = mm(inv, jnp.concatenate([beta * values, (beta * carry) * keys], axis=1))
        attn = qdecay * mm(query, keys, 1, 1)
        auw = mm(attn, uw)
        nm = mm(dlast * keys, uw, 0, 0)
        before = state[h]
        out = mm(qcarry * query - auw[:, HEAD:], before)
        hc = slice(h * HEAD, (h + 1) * HEAD)
        carr_ref[:, hc] = out[:, :HEAD]
        oloc_ref[:, hc] = out[:, HEAD:] + auw[:, :HEAD]
        after = mm(clast * eye - nm[:, HEAD:], before)
        state[h, :, :HEAD] = after[:, :HEAD]
        state[h, :, HEAD:] = after[:, HEAD:] + nm[:, :HEAD]
        q_ref[0, h] = query
        k_ref[0, h] = keys
        v_ref[0, h] = values
        t_ref[0, h] = inv
        kk_ref[0, h] = kk
        at_ref[0, h] = attn
        uw_ref[0, h] = uw
        pl_ref[0, h] = before
    fin_ref[...] = state[...]


def recurrence_forward(proj_ext, conv_w, rowp, colp, tokp, heads):
    blocks = rowp.shape[0]
    rows = blocks * BLOCK_LEN
    whole = lambda *dims: pl.BlockSpec(dims, lambda i: (0,) * len(dims))
    by_block = lambda *dims: pl.BlockSpec((1,) + dims, lambda i: (i,) + (0,) * len(dims))
    token = lambda cols: pl.BlockSpec((BLOCK_LEN, cols), lambda i: (i, 0))
    shape = lambda *dims: jax.ShapeDtypeStruct(dims, F32)
    square = (heads, ROWS, HEAD)
    return pl.pallas_call(
        functools.partial(fwd_kernel, heads),
        grid=(blocks,),
        in_specs=[
            whole(*proj_ext.shape), whole(*conv_w.shape),
            by_block(*rowp.shape[1:]), by_block(*colp.shape[1:]), by_block(*tokp.shape[1:]),
        ],
        out_specs=[
            token(heads * HEAD), token(heads * HEAD), whole(heads, HEAD, 2 * HEAD), token(heads * WIDE),
            by_block(heads, BLOCK_LEN, HEAD), by_block(*square), by_block(*square), by_block(*square),
            by_block(*square), by_block(heads, BLOCK_LEN, ROWS), by_block(heads, ROWS, 2 * HEAD),
            by_block(heads, HEAD, 2 * HEAD),
        ],
        out_shape=[
            shape(rows, heads * HEAD), shape(rows, heads * HEAD), shape(heads, HEAD, 2 * HEAD), shape(rows, heads * WIDE),
            shape(blocks, heads, BLOCK_LEN, HEAD), shape(blocks, *square), shape(blocks, *square), shape(blocks, *square),
            shape(blocks, *square), shape(blocks, heads, BLOCK_LEN, ROWS), shape(blocks, heads, ROWS, 2 * HEAD),
            shape(blocks, heads, HEAD, 2 * HEAD),
        ],
        scratch_shapes=[pltpu.VMEM((heads, HEAD, 2 * HEAD), F32), pltpu.VMEM((2 * heads, ROWS, HEAD), F32)],
        compiler_params=pltpu.CompilerParams(vmem_limit_bytes=40 << 20),
        name="recurrence_forward",
    )(proj_ext, conv_w, rowp, colp, tokp)


def state_kernel(heads, index_ref, maps_ref, oloc_ref, carr_ref, gate_ref, gain_ref, heads_ref, mixed_ref, state_ref):
    def hop(k, states):
        return tuple(
            mm(maps_ref[k, h, :, :HEAD], states[h]) + maps_ref[k, h, :, HEAD:].astype(F32) for h in range(heads)
        )

    states = lax.fori_loop(0, index_ref[0], hop, tuple(jnp.zeros((HEAD, HEAD), F32) for _ in range(heads)))
    for h in range(heads):
        hc = slice(h * HEAD, (h + 1) * HEAD)
        state_ref[h] = states[h]
        out = (oloc_ref[:, hc] + mm(carr_ref[:, hc], states[h])).astype(BF16)
        heads_ref[:, hc] = out
        wide = out.astype(F32)
        gate = gate_ref[:, hc]
        scaled = wide * lax.rsqrt(jnp.mean(wide * wide, axis=1, keepdims=True) + NORM_EPS) * gain_ref[...]
        mixed_ref[:, hc] = (scaled * (gate * jax.nn.sigmoid(gate))).astype(BF16)


def state_and_gate(index, maps, oloc, carr, gate_out, gain, heads):
    rows = oloc.shape[0]
    vmem = pl.BlockSpec(memory_space=pltpu.VMEM)
    return pl.pallas_call(
        functools.partial(state_kernel, heads),
        in_specs=[pl.BlockSpec(memory_space=pltpu.SMEM)] + [vmem] * 5,
        out_specs=[vmem] * 3,
        out_shape=[
            jax.ShapeDtypeStruct((rows, heads * HEAD), BF16),
            jax.ShapeDtypeStruct((rows, heads * HEAD), BF16),
            jax.ShapeDtypeStruct((heads, HEAD, HEAD), F32),
        ],
        compiler_params=pltpu.CompilerParams(vmem_limit_bytes=40 << 20),
        name="state_and_gate",
    )(index, maps, oloc, carr, gate_out, gain)


def gate_back_kernel(heads, grad_ref, heads_ref, gate_ref, gain_ref, carr_ref, ghead_ref, ggate_ref, ggain_ref, cot_ref):
    total = jnp.zeros((1, HEAD), F32)
    for h in range(heads):
        hc = slice(h * HEAD, (h + 1) * HEAD)
        x = heads_ref[:, hc].astype(F32)
        gate = gate_ref[:, hc]
        grad = grad_ref[:, hc]
        gain = gain_ref[...]
        inv = lax.rsqrt(jnp.mean(x * x, axis=1, keepdims=True) + NORM_EPS)
        sig = jax.nn.sigmoid(gate)
        silu = gate * sig
        unit = x * inv
        ggate_ref[:, hc] = (grad * unit * gain * (sig * (1.0 + gate * (1.0 - sig)))).astype(BF16)
        weighted = grad * silu
        total = total + jnp.sum(weighted * unit, axis=0, keepdims=True)
        down = weighted * gain
        ghead = (inv * (down - unit * jnp.mean(down * unit, axis=1, keepdims=True))).astype(BF16)
        ghead_ref[:, hc] = ghead
        cot_ref[h] = mm(carr_ref[:, hc], ghead, 0, 0)
    ggain_ref[...] = total


def gate_back(grad_mixed, heads_out, gate_out, gain, carr, heads):
    rows = carr.shape[0]
    vmem = pl.BlockSpec(memory_space=pltpu.VMEM)
    return pl.pallas_call(
        functools.partial(gate_back_kernel, heads),
        in_specs=[vmem] * 5,
        out_specs=[vmem] * 4,
        out_shape=[
            jax.ShapeDtypeStruct((rows, heads * HEAD), BF16),
            jax.ShapeDtypeStruct((rows, heads * HEAD), BF16),
            jax.ShapeDtypeStruct((1, HEAD), F32),
            jax.ShapeDtypeStruct((heads, HEAD, HEAD), F32),
        ],
        compiler_params=pltpu.CompilerParams(vmem_limit_bytes=40 << 20),
        name="gate_back",
    )(grad_mixed, heads_out, gate_out, gain, carr)


def bwd_kernel(
    heads, index_ref, maps_ref, cots_ref, sin_ref, proj_ref, w_ref, rowp_ref, colp_ref, tokp_ref,
    go_ref, conv_ref, q_ref, k_ref, v_ref, t_ref, kk_ref, at_ref, uw_ref, pl_ref,
    gproj_ref, last_ref, spill_ref, gw_ref, gcol_ref, gtok_ref, grow_ref,
    dstate, weave, rim,
):
    step = pl.program_id(0)
    block = pl.num_programs(0) - 1 - step

    @pl.when(step == 0)
    def _():
        pieces = maps_ref.shape[0]

        def hop(i, states):
            k = pieces - 1 - i
            return tuple(
                mm(maps_ref[k, h, :, :HEAD], states[h], 0, 0) + cots_ref[k, h].astype(F32) for h in range(heads)
            )

        found = lax.fori_loop(
            0, pieces - 1 - index_ref[0], hop, tuple(jnp.zeros((HEAD, HEAD), F32) for _ in range(heads))
        )
        for h in range(heads):
            dstate[h] = found[h]
        rim[...] = jnp.zeros_like(rim)
        gw_ref[...] = jnp.zeros_like(gw_ref)

    base = pl.multiple_of(block * BLOCK_LEN, BLOCK_LEN)
    rowp, colp, tokp = rowp_ref[0], colp_ref[0], tokp_ref[0]
    last_row = iota((ROWS, 1), 0) == ROWS - 1
    for h in range(heads):
        cols = slice(h * WIDE, (h + 1) * WIDE)
        hc = slice(h * HEAD, (h + 1) * HEAD)
        beta, decay, qdecay, carry, qcarry, dlast, clast = decays(rowp, colp, tokp, h)
        go = go_ref[:, hc]
        query, keys, values = q_ref[0, h], k_ref[0, h], v_ref[0, h]
        inv, kk, attn, uw = t_ref[0, h], kk_ref[0, h], at_ref[0, h], uw_ref[0, h]
        dnext = dstate[h]
        state = mm(pl_ref[0, h, :, :HEAD], sin_ref[h]) + pl_ref[0, h, :, HEAD:]
        both = mm(jnp.concatenate([keys, uw[:, HEAD:]], axis=0), state)
        ks = both[:ROWS]
        upd = uw[:, :HEAD] - both[ROWS:]
        dupd = mm(attn, go, 0, 0) + dlast * mm(keys, dnext)
        dx = mm(inv, dupd, 0, 0)
        dv = beta * dx
        dy = -(carry * dv)
        go32 = go.astype(F32)
        outer = mm(jnp.concatenate([go32, dx], axis=0), upd, 1, 1)
        dattn, da = outer[:BLOCK_LEN], -outer[BLOCK_LEN:]
        dkd = mm(upd, dnext, 1, 1)
        right = mm(jnp.concatenate([go32, dy], axis=0), state, 1, 1)
        gos = right[:BLOCK_LEN]
        e = beta * da * decay
        f = dattn * qdecay
        ef = jnp.concatenate([f, e], axis=0)
        efk = mm(ef, keys)
        dq = qcarry * gos + efk[:BLOCK_LEN]
        dk = (
            right[BLOCK_LEN:]
            + dlast * dkd
            + efk[BLOCK_LEN:]
            + mm(ef, jnp.concatenate([query, keys], axis=0), 0, 0)
        )
        dstate[h] = clast * dnext + mm(
            jnp.concatenate([qcarry * query, keys], axis=0), jnp.concatenate([go32, dy], axis=0), 0, 0
        )
        dakk = da * kk
        z1 = beta * dakk
        z2 = dattn * attn
        dbeta = jnp.sum(dx * (values - carry * ks), axis=1, keepdims=True) + jnp.sum(dakk, axis=1, keepdims=True)
        dlk = dlast * jnp.sum(dkd * keys, axis=1, keepdims=True)
        tail = jnp.sum(dlk, axis=0, keepdims=True) + clast * jnp.sum(
            jnp.sum(state * dnext, axis=1, keepdims=True), axis=0, keepdims=True
        )
        dgrow = jnp.sum(z1, axis=1, keepdims=True) + jnp.sum(dy * ks, axis=1, keepdims=True) - dlk
        dgrow = dgrow + jnp.where(last_row, tail, 0.0)
        gcol_ref[0, :, 2 * h : 2 * h + 1] = dbeta
        gcol_ref[0, :, 2 * h + 1 : 2 * h + 2] = dgrow
        gtok_ref[0, :, h : h + 1] = jnp.sum(z2, axis=1, keepdims=True) + qcarry * jnp.sum(
            query * gos, axis=1, keepdims=True
        )
        grow_ref[0, h : h + 1, :] = jnp.sum(z1, axis=0, keepdims=True) + jnp.sum(z2, axis=0, keepdims=True)
        weave[2 * h] = dk
        weave[2 * h + 1] = dv
        conv = conv_ref[:, cols]
        sig = jax.nn.sigmoid(conv)
        act = conv * sig
        pieces = []
        for part in range(1 + NH):
            piece = act[:, part * HEAD : (part + 1) * HEAD]
            scale = lax.rsqrt(jnp.sum(piece * piece, axis=1, keepdims=True) + NORM_EPS)
            if part:
                grad = weave[2 * h, pl.ds(part - 1, BLOCK_LEN, NH), :]
            else:
                grad = dq * (1.0 / math.sqrt(HEAD))
            unit = piece * scale
            pieces.append(scale * (grad - unit * jnp.sum(grad * unit, axis=1, keepdims=True)))
        for j in range(NH):
            pieces.append(weave[2 * h + 1, pl.ds(j, BLOCK_LEN, NH), :])
        dconv = jnp.concatenate(pieces, axis=1) * (sig * (1.0 + conv * (1.0 - sig)))
        ext = proj_ref[pl.ds(base, BLOCK_LEN + HALO), cols].astype(F32)
        gw_ref[0:1, cols] += jnp.sum(dconv * ext[HALO:], axis=0, keepdims=True)
        zeros = jnp.zeros((8, WIDE), F32)
        length = BLOCK_LEN + 8
        total = jnp.concatenate([zeros, dconv * w_ref[0:1, cols]], axis=0)
        for lag in range(1, CONV):
            masked = tokp[:, lag - 1 : lag] * dconv
            gw_ref[lag : lag + 1, cols] += jnp.sum(masked * lag_rows(ext, lag), axis=0, keepdims=True)
            total = total + pltpu.roll(
                jnp.concatenate([zeros, masked * w_ref[lag : lag + 1, cols]], axis=0), length - lag, 0
            )
        fixed = total[length - 8 :] + rim[:, cols]
        gproj_ref[:, cols] = jnp.concatenate([total[8 : length - 8], fixed], axis=0).astype(BF16)
        rim[:, cols] = total[:8]
        spill_ref[:, cols] = total[:8]

        @pl.when(step == 0)
        def _():
            last_ref[:, cols] = fixed


def recurrence_backward(index, maps, cots, state_in, proj_ext, conv_w, rowp, colp, tokp, grad_heads, saved, heads):
    blocks = rowp.shape[0]
    rows = blocks * BLOCK_LEN
    whole = lambda *dims: pl.BlockSpec(dims, lambda i: (0,) * len(dims))
    by_block = lambda *dims: pl.BlockSpec((1,) + dims, lambda i: (blocks - 1 - i,) + (0,) * len(dims))
    token = lambda cols: pl.BlockSpec((BLOCK_LEN, cols), lambda i: (blocks - 1 - i, 0))
    shape = lambda *dims: jax.ShapeDtypeStruct(dims, F32)
    square = (heads, ROWS, HEAD)
    return pl.pallas_call(
        functools.partial(bwd_kernel, heads),
        grid=(blocks,),
        in_specs=[
            pl.BlockSpec(memory_space=pltpu.SMEM), whole(*maps.shape), whole(*cots.shape), whole(*state_in.shape),
            whole(*proj_ext.shape), whole(*conv_w.shape),
            by_block(*rowp.shape[1:]), by_block(*colp.shape[1:]), by_block(*tokp.shape[1:]),
            token(heads * HEAD), token(heads * WIDE),
            by_block(heads, BLOCK_LEN, HEAD), by_block(*square), by_block(*square), by_block(*square),
            by_block(*square), by_block(heads, BLOCK_LEN, ROWS), by_block(heads, ROWS, 2 * HEAD),
            by_block(heads, HEAD, 2 * HEAD),
        ],
        out_specs=[
            token(heads * WIDE), whole(8, heads * WIDE), whole(8, heads * WIDE), whole(8, heads * WIDE),
            by_block(ROWS, 2 * heads), by_block(BLOCK_LEN, heads), by_block(heads, ROWS),
        ],
        out_shape=[
            jax.ShapeDtypeStruct((rows, heads * WIDE), BF16), shape(8, heads * WIDE), shape(8, heads * WIDE),
            shape(8, heads * WIDE), shape(blocks, ROWS, 2 * heads), shape(blocks, BLOCK_LEN, heads),
            shape(blocks, heads, ROWS),
        ],
        scratch_shapes=[
            pltpu.VMEM((heads, HEAD, HEAD), F32), pltpu.VMEM((2 * heads, ROWS, HEAD), F32),
            pltpu.VMEM((8, heads * WIDE), F32),
        ],
        compiler_params=pltpu.CompilerParams(vmem_limit_bytes=48 << 20),
        name="recurrence_backward",
    )(index, maps, cots, state_in, proj_ext, conv_w, rowp, colp, tokp, grad_heads, *saved)


def passed_along(x, axis, by):
    devices = lax.axis_size(axis)
    pairs = [(i, i + by) for i in range(devices) if 0 <= i + by < devices]
    return lax.ppermute(x, axis, pairs)


def rms_scale(values, gain_vec):
    return values * lax.rsqrt(jnp.mean(values * values, axis=-1, keepdims=True) + NORM_EPS) * gain_vec


def swiglu_mix(gate_values, up_values):
    return jax.nn.silu(gate_values) * up_values


def scalar_gates(scal, a_log, dt_bias):
    beta = jax.nn.sigmoid(scal[:, :, :NH])
    logs = -jnp.exp(a_log)[None, :] * jax.nn.softplus(scal[:, :, NH] + dt_bias[None, :])
    return beta, logs


def columns_to_rank(w):
    ranks = lax.axis_size("seq")
    rows, cols = w.shape[0], w.shape[1] // ranks
    swapped = lax.all_to_all(w, "seq", split_axis=1, concat_axis=0, tiled=True)
    full = lax.all_gather(swapped.reshape(ranks, rows, cols), "ctx", axis=1, tiled=True)
    return full.reshape(-1, cols)


def rows_of_rank(w):
    return lax.all_gather(w, "ctx", axis=0, tiled=True)


def sum_columns_back(grad):
    ranks, pieces = lax.axis_size("seq"), lax.axis_size("ctx")
    cols = grad.shape[1]
    mine = lax.psum_scatter(
        grad.astype(BF16).reshape(ranks, pieces, -1, cols), "ctx", scatter_dimension=1, tiled=True
    )
    return lax.all_to_all(mine.reshape(-1, cols), "seq", split_axis=0, concat_axis=1, tiled=True).astype(F32)


def sum_rows_back(grad):
    return lax.psum_scatter(grad.astype(BF16), "ctx", scatter_dimension=0, tiled=True).astype(F32)


def gather_tokens(x):
    return lax.all_gather(x, "seq", axis=0, tiled=True)


def sum_tokens(partial):
    ranks = lax.axis_size("seq")
    parts = lax.all_to_all(partial.astype(BF16).reshape(ranks, -1, partial.shape[1]), "seq", 0, 0, tiled=True)
    return jnp.sum(parts.astype(F32), axis=0)


def dot(a, b):
    return jnp.dot(a, b, preferred_element_type=F32)


def dot_t(a, b):
    return jnp.einsum("tc,dc->td", a, b, preferred_element_type=F32)


def t_dot(a, b):
    return jnp.einsum("tr,tc->rc", a, b, preferred_element_type=F32)


def local(
    block_input, teacher, valid_mask, segments, mix_proj, scalar_proj, gate_proj, out_proj, conv_weight,
    norm_attn, norm_mlp, head_gain, a_log, dt_bias, w_gate, w_up, w_down,
):
    seq_size = lax.axis_size("seq")
    heads = HEADS // seq_size
    tok_rows = block_input.shape[0]
    rows = tok_rows * seq_size
    blocks = rows // BLOCK_LEN
    token_total = segments.shape[0]
    seq_length = min(SEQ_LEN, token_total)
    index = lax.axis_index("ctx")
    rank = lax.axis_index("seq")
    head_start = rank * heads

    mix_s = columns_to_rank(mix_proj)
    scal_s = columns_to_rank(scalar_proj)
    gate_s = columns_to_rank(gate_proj)
    wg_s = columns_to_rank(w_gate)
    wu_s = columns_to_rank(w_up)
    out_s = rows_of_rank(out_proj)
    down_s = rows_of_rank(w_down)
    conv_s = rows_of_rank(conv_weight)
    norm_a = lax.all_gather(norm_attn, BOTH, axis=0, tiled=True).astype(F32)
    norm_m = lax.all_gather(norm_mlp, BOTH, axis=0, tiled=True).astype(F32)
    valid_count = jnp.maximum(lax.psum(jnp.sum(valid_mask.astype(F32)), BOTH), 1.0)

    inputs_f = block_input.astype(F32)
    normed_f, norm_in_back = jax.vjp(rms_scale, inputs_f, norm_a)
    normed = gather_tokens(normed_f.astype(BF16))
    proj = dot(normed, mix_s).astype(BF16)
    scal = dot(normed, scal_s).astype(BF16)
    gate_out = dot(normed, gate_s)

    piece_start = index * rows
    window = lax.dynamic_slice_in_dim(jnp.pad(segments, (CONV, 0)), piece_start, rows + CONV)
    place_in = (piece_start + jnp.arange(rows, dtype=jnp.int32)) % seq_length
    own_seg = window[CONV:]
    linked = [
        ((window[CONV - lag : CONV - lag + rows] == own_seg) & (place_in >= lag)).astype(F32) for lag in range(1, CONV)
    ]
    starts = 1.0 - linked[0]
    alog_heads = lax.dynamic_slice_in_dim(a_log.astype(F32), head_start, heads, 0)
    dt_heads = lax.dynamic_slice_in_dim(dt_bias.astype(F32), head_start, heads, 0)
    (beta, logs), gates_back = jax.vjp(
        scalar_gates, scal.astype(F32).reshape(rows, heads, NH + 1), alog_heads, dt_heads
    )
    lower = jnp.tril(jnp.ones((BLOCK_LEN, BLOCK_LEN), F32))
    sums = jnp.einsum(
        "ts,bsh->bth",
        lower,
        jnp.concatenate([starts[:, None], logs * (1.0 - starts)[:, None]], axis=1).reshape(blocks, BLOCK_LEN, heads + 1),
        precision=lax.Precision.HIGHEST,
    )
    tokp = jnp.concatenate([jnp.stack(linked, axis=1).reshape(blocks, BLOCK_LEN, CONV - 1), sums], axis=2)
    sums_rows = jnp.repeat(sums, NH, axis=1)
    beta_rows = jnp.swapaxes(beta, 1, 2).reshape(blocks, ROWS, heads)
    colp = jnp.concatenate(
        [sums_rows[:, :, :1], jnp.zeros_like(sums_rows[:, :, :1])]
        + [x[:, :, h : h + 1] for h in range(heads) for x in (sums_rows[:, :, 1:], beta_rows)],
        axis=2,
    )
    rowp = jnp.swapaxes(colp, 1, 2)
    conv_w = jnp.pad(jnp.flip(conv_s.astype(F32).T, 0), ((0, 8 - CONV), (0, 0)))
    tail = passed_along(proj[rows - HALO :], "ctx", 1)
    proj_ext = jnp.concatenate([tail, proj], axis=0)

    oloc, carr, final, *saved = recurrence_forward(proj_ext, conv_w, rowp, colp, tokp, heads)
    maps = lax.all_gather(final.astype(BF16), "ctx")
    gain = head_gain.astype(F32)[None, :]
    index_arr = index.reshape(1).astype(jnp.int32)
    heads_out, mixed, state_in = state_and_gate(index_arr, maps, oloc, carr, gate_out, gain, heads)

    middle = inputs_f + sum_tokens(dot(mixed, out_s))
    second_f, norm_mlp_back = jax.vjp(rms_scale, middle, norm_m)
    second = gather_tokens(second_f.astype(BF16))
    gate_values = dot(second, wg_s)
    up_values = dot(second, wu_s)
    hidden_f, swiglu_back = jax.vjp(swiglu_mix, gate_values, up_values)
    hidden = hidden_f.astype(BF16)
    final_out = middle + sum_tokens(dot(hidden, down_s))
    mask_values = valid_mask.astype(F32)
    error_rows = final_out - teacher.astype(F32)
    error_sum = jnp.sum(mask_values[:, None] * error_rows * error_rows)
    grad_final = token_total / valid_count * mask_values[:, None] * error_rows

    grad_branch = gather_tokens(grad_final.astype(BF16))
    down_grad = sum_rows_back(t_dot(hidden, grad_branch))
    grad_gate_f, grad_up_f = swiglu_back(dot_t(grad_branch, down_s))
    grad_gate = grad_gate_f.astype(BF16)
    grad_up = grad_up_f.astype(BF16)
    grad_second = sum_tokens(dot_t(grad_gate, wg_s) + dot_t(grad_up, wu_s))
    wg_grad = sum_columns_back(t_dot(second, grad_gate))
    wu_grad = sum_columns_back(t_dot(second, grad_up))
    grad_mid_norm, norm_mlp_term = norm_mlp_back(grad_second)
    grad_middle = grad_final + grad_mid_norm
    grad_mixed_low = gather_tokens(grad_middle.astype(BF16))
    out_grad = sum_rows_back(t_dot(mixed, grad_mixed_low))
    grad_mixed = dot_t(grad_mixed_low, out_s)

    grad_heads, grad_gate_out, gain_term, cot = gate_back(grad_mixed, heads_out, gate_out, gain, carr, heads)
    cots = lax.all_gather(cot.astype(BF16), "ctx")
    grad_proj, last_rows, spill, gw, gcol, gtok, grow = recurrence_backward(
        index_arr, maps, cots, state_in, proj_ext, conv_w, rowp, colp, tokp, grad_heads, saved, heads
    )
    rim_back = passed_along(spill, "ctx", -1)
    grad_proj = lax.dynamic_update_slice_in_dim(grad_proj, (last_rows + rim_back).astype(BF16), rows - 8, 0)
    grad_beta = jnp.swapaxes(gcol[:, :, 0::2].reshape(rows, NH, heads), 1, 2)
    grad_cum = jnp.sum(
        (gcol[:, :, 1::2] - jnp.swapaxes(grow, 1, 2)).reshape(blocks, BLOCK_LEN, NH, heads), axis=2
    ) + gtok
    grad_logs = jnp.einsum("ts,bth->bsh", lower, grad_cum, precision=lax.Precision.HIGHEST).reshape(rows, heads)
    grad_scal_f, grad_alog, grad_dt = gates_back((grad_beta, grad_logs * (1.0 - starts)[:, None]))
    grad_scal = grad_scal_f.reshape(rows, heads * (NH + 1)).astype(BF16)

    grad_normed = sum_tokens(
        dot_t(grad_proj, mix_s) + dot_t(grad_scal, scal_s) + dot_t(grad_gate_out, gate_s)
    )
    grad_in_norm, norm_attn_term = norm_in_back(grad_normed)
    input_grad = grad_middle + grad_in_norm
    mix_grad = sum_columns_back(t_dot(normed, grad_proj))
    scal_grad = sum_columns_back(t_dot(normed, grad_scal))
    gate_grad = sum_columns_back(t_dot(normed, grad_gate_out))
    conv_grad = lax.psum_scatter(jnp.flip(gw[:CONV], 0).T, "ctx", scatter_dimension=0, tiled=True)
    pick = (jnp.arange(HEADS)[None, :] == head_start + jnp.arange(heads)[:, None]).astype(F32)
    small = jnp.concatenate(
        [
            gain_term[0], jnp.sum(grad_alog[:, None] * pick, axis=0), jnp.sum(grad_dt[:, None] * pick, axis=0),
            error_sum[None], norm_attn_term, norm_mlp_term,
        ]
    )
    small = lax.psum(small, BOTH)
    mean_loss = small[HEAD + 2 * HEADS] / (D * valid_count)
    norm_start = HEAD + 2 * HEADS + 1
    own = norm_attn.shape[0]
    place = (rank * lax.axis_size("ctx") + index) * own
    return (
        final_out.astype(BF16),
        mean_loss,
        input_grad,
        mix_grad,
        scal_grad,
        gate_grad,
        out_grad,
        conv_grad,
        lax.dynamic_slice_in_dim(small, norm_start + place, own),
        lax.dynamic_slice_in_dim(small, norm_start + D + place, own),
        small[:HEAD],
        small[HEAD : HEAD + HEADS],
        small[HEAD + HEADS : HEAD + 2 * HEADS],
        wg_grad,
        wu_grad,
        down_grad,
    )


def solution(mesh):
    tokens, vector, matrix = P(("ctx", "seq"), None), P(BOTH), P(BOTH, None)
    in_specs = (
        tokens, tokens, P(("ctx", "seq")), P(), matrix, matrix, matrix, matrix, matrix, vector, vector,
        P(), P(), P(), matrix, matrix, matrix,
    )
    out_specs = (
        tokens, P(), tokens, matrix, matrix, matrix, matrix, matrix, vector, vector, P(), P(), P(),
        matrix, matrix, matrix,
    )
    return jax.shard_map(local, mesh=mesh, in_specs=in_specs, out_specs=out_specs, check_vma=False)
```

time: 2040 us -> 800 us (0.39)
  waiting for transfers between devices: 729 us -> 248 us
  other arithmetic: 450 us -> 24.8 us
  matrix products: 254 us -> 44.5 us
  local copies, waits for them, and re-layouts: 276 us -> 82 us
  Pallas kernels: 0 us -> 69.8 us
  starting transfers between devices: 26 us -> 49.4 us
    another operation x133 -> x0, other arithmetic: 338 us -> none  [the longest x72 318 us: block_update(): jax.scipy.linalg.solve_triangular(system, right_side, lower=True, unit_di...]
    unnamed x12 -> x15, waiting for transfers between devices: 403 us -> 102 us
    reduce_scatter x2, waiting for transfers between devices: 298 us -> 0.01 us  [sum_rows_back(): lax.psum_scatter(grad.astype(BF16), 'ctx', scatter_dimension=0, tiled=True)]
    dot_general x224 -> x23, matrix products: 220 us -> 44.5 us  [the longest x7 16 us: dot(): return jnp.dot(a, b, preferred_element_type=F32)]
    all_gather x6 -> x9, waiting for transfers between devices: 0.05 us -> 97.4 us  [the longest x4 64.3 us: gather_tokens(): return lax.all_gather(x, 'seq', axis=0, tiled=True)]
    all_gather x6 -> x5, blocking collectives: 144 us -> 73.6 us  [the longest x2 30.4 us: columns_to_rank(): lax.all_gather(swapped.reshape(ranks, rows, cols), 'ctx', axis=1, tiled=T...]
    pallas_call x0 -> x4, Pallas kernels: none -> 69.8 us  [the longest x1 42.5 us: recurrence_forward(): pl.pallas_call(functools.partial(fwd_kernel, heads), grid=(blocks,), in_s...]
    squeeze x64 -> x1, local copies, waits for them, and re-layouts: 54.6 us -> 0.08 us  [scalar_gates(): scal[:, :, NH] + dt_bias[None, :]]
  transfers between devices with their start and end apart: 18 -> 27, of which waited for: 8 -> 14; matrix products, arithmetic and copies ran while one was open for 24% -> 12% of each run, Pallas kernels for 0% -> 0%
where the time goes in v1:
time: 800 us; the launch traced here: 789 us
  blocking collectives  252 us (32%)
  waiting for transfers between devices  248 us (31%)
  local copies, waits for them, and re-layouts  82 us (10%)
  Pallas kernels  69.8 us (9%)
  starting transfers between devices  49.4 us (6%)
  matrix products  44.5 us (6%)
  other arithmetic  24.8 us (3%)
  between operations  17.9 us (2%)
    unnamed x15, waiting for transfers between devices  102 us
    unnamed x2, blocking collectives  72 us
    all_gather x4, waiting for transfers between devices, gather_tokens(): return lax.all_gather(x, 'seq', axis=0, tiled=True)  64.3 us
    psum x1, blocking collectives, local(): lax.psum(jnp.sum(valid_mask.astype(F32)), BOTH)  46.1 us
    pallas_call x1, Pallas kernels, recurrence_forward(): pl.pallas_call(functools.partial(fwd_kernel, heads), grid=(blocks,), in_s...  42.5 us
    psum x1, blocking collectives, local(): small = lax.psum(small, BOTH)  40.7 us
    all_to_all x4, waiting for transfers between devices, sum_tokens(): lax.all_to_all(partial.astype(BF16).reshape(ranks, -1, partial.shape[1]),...  34.2 us
    unnamed x147, local copies, waits for them, and re-layouts  31 us
  transfers between devices with their start and end apart: 27, of which 14 were waited for; matrix products, arithmetic and copies ran while one was open for 12% of the time, Pallas kernels for 0%

profile of v1, /device:TPU:0, one launch (start us, length us, event | category | flops | bytes accessed | tf_op | source)
XLA Modules:
  0.0 788.8 jit_solution(4161137688954445569)
XLA Ops:
  8.9 42.0 %all-reduce.11 = (bf16[1024]{0:T(1024)(128)(2,1)S(1)}, bf16[1024]{0:T(1024)(128)(2,1)S(1)}) all-reduce(bf16[1024]{0:T(1024)(128)(2,1)S(1)} %dynamic-update-slice, bf16[1024]{0:T(1024)(128)(2,1)S(1)} %dynamic-update-slice.1), channel_id=1, replica_groups=mesh['seq'=4,'ctx'=8] {'seq','ctx'}, use_global_device_ids=true, to_apply=%add.4 | all-reduce | flops 2048 | bytes 8192
  56.0 9.6 %all_to_all.165 = bf16[32,4,1280]{2,0,1:T(8,128)(2,1)S(1)} all-to-all(bf16[32,4,1280]{2,0,1:T(8,128)(2,1)S(1)} %bitcast.197), channel_id=1, replica_groups=mesh['seq'=4,'ctx'=8] {'seq'}, dimensions={1} | all-to-all | bytes 655360 | tf_op jit(solution)/shard_map/all_to_all | solution.py:447
  67.3 3.2 all-to-all-start.1
  71.8 12.7 %all-gather.2 = bf16[8,160,4]{1,2,0:T(4,128)(2,1)S(1)} all-gather(bf16[1,160,4]{1,2,0:T(4,128)(2,1)S(1)} %bitcast.216), channel_id=1, replica_groups=mesh['seq'=4,'ctx'=8] {'ctx'}, dimensions={0}, use_global_device_ids=true | all-gather | bytes 11520 | tf_op jit(solution)/shard_map/all_gather | solution.py:453
  85.3 14.9 %all_gather.58 = bf16[4,256,6]{2,0,1:T(4,128)(2,1)S(1)} all-gather(bf16[4,32,6]{2,0,1:T(4,128)(2,1)S(1)} %copy.213), channel_id=1, replica_groups=mesh['seq'=4,'ctx'=8] {'ctx'}, dimensions={1}, use_global_device_ids=true | all-gather | bytes 13824 | tf_op jit(solution)/shard_map/all_gather | solution.py:448
  104.1 13.4 %all-gather.15.cloned.1.call-done = bf16[4,256,1280]{2,0,1:T(4,128)(2,1)} async-done(((bf16[4,32,1280]{2,0,1:T(4,128)(2,1)}), bf16[4,256,1280]{2,0,1:T(4,128)(2,1)}) %all-gather.15.cloned.1.call-update) | async-done | bytes 2621456 | tf_op jit(solution)/shard_map/all_gather | solution.py:448
  129.6 42.5 %recurrence_forward.1 = (f32[512,256]{1,0:T(8,128)S(1)}, f32[512,256]{1,0:T(8,128)S(1)}, f32[2,128,256]{2,1,0:T(8,128)S(1)}, f32[512,1280]{1,0:T(8,128)}, f32[8,...) custom-call(bf16[528,1280]{1,0:T(8,128)(2,1)S(1)} %pad_maximum_fusio, ...), custom_call_target="tpu_custom_call" | custom-call | tf_op jit(solution)/shard_map/recurrence_forward/pallas_call | solution.py:165
  182.5 10.1 %all_to_all.166 = bf16[32,4,704]{2,0,1:T(8,128)(2,1)S(1)} all-to-all(bf16[32,4,704]{2,0,1:T(8,128)(2,1)S(1)} %copy.227), channel_id=1, replica_groups=mesh['seq'=4,'ctx'=8] {'seq'}, dimensions={1} | all-to-all | bytes 360448 | tf_op jit(solution)/shard_map/all_to_all | solution.py:447
  195.3 3.4 all-to-all-start.5
  199.3 15.8 %all_gather.62 = bf16[256,1024]{1,0:T(8,128)(2,1)} all-gather(bf16[32,1024]{1,0:T(8,128)(2,1)S(1)} %copy-done.37), channel_id=1, replica_groups=mesh['seq'=4,'ctx'=8] {'ctx'}, dimensions={0}, use_global_device_ids=true | all-gather | bytes 589824 | tf_op jit(solution)/shard_map/all_gather | solution.py:453
  215.1 4.1 all-to-all-start.2
  220.1 4.0 all-to-all-done.2
  224.1 15.5 %all_gather.61 = bf16[4,256,256]{2,0,1:T(4,128)(2,1)S(1)} all-gather(bf16[4,32,256]{2,0,1:T(4,128)(2,1)S(1)} %copy.225), channel_id=1, replica_groups=mesh['seq'=4,'ctx'=8] {'ctx'}, dimensions={1}, use_global_device_ids=true | all-gather | bytes 589824 | tf_op jit(solution)/shard_map/all_gather | solution.py:448
  247.1 4.2 all-to-all-start.3
  251.4 14.6 %all-to-all-done.3 = bf16[4,128,1024]{2,1,0:T(8,128)(2,1)} async-done(((bf16[4,128,1024]{2,1,0:T(8,128)(2,1)}), bf16[4,128,1024]{2,1,0:T(8,128)(2,1)}, u32[]{:S(2)}, u32[]{:S(2)}) %all-to-all-start.3) | async-done | bytes 1048608 | tf_op jit(solution)/shard_map/all_to_all | solution.py:475
  270.2 4.3 copy.229
  274.5 2.9 copy.269
  277.4 4.3 copy.232
  281.7 2.8 copy.270
  284.5 10.9 %all-gather.17.cloned.1.call-done = bf16[512,1024]{1,0:T(8,128)(2,1)} async-done(((bf16[128,1024]{1,0:T(8,128)(2,1)}), bf16[512,1024]{1,0:T(8,128)(2,1)}) %all-gather.17.cloned.1.call-update) | async-done | bytes 1048592 | tf_op jit(solution)/shard_map/all_gather | solution.py:470
  295.3 2.8 fusion.57
  301.7 19.6 %all-gather.23.cloned.1.call-done = bf16[704,1024]{1,0:T(8,128)(2,1)} async-done(((bf16[88,1024]{1,0:T(8,128)(2,1)}), bf16[704,1024]{1,0:T(8,128)(2,1)}) %all-gather.23.cloned.1.call-update) | async-done | bytes 1441808 | tf_op jit(solution)/shard_map/all_gather | solution.py:453
  321.4 3.5 convolution_convert_fusion.5
  324.9 4.4 all-to-all-start.6
  329.9 46.1 %psum.14 = f32[]{:T(128)} all-reduce(f32[]{:T(128)} %convert_reduce_fusion.4), channel_id=1, replica_groups=mesh['seq'=4,'ctx'=8] {'seq','ctx'}, use_global_device_ids=true, to_apply=%region_5.6 | all-reduce | flops 1 | bytes 8 | tf_op jit(solution)/shard_map/psum | solution.py:516
  379.9 26.7 %all-gather.25.cloned.1.call-done = bf16[512,1024]{1,0:T(8,128)(2,1)} async-done(((bf16[128,1024]{1,0:T(8,128)(2,1)}), bf16[512,1024]{1,0:T(8,128)(2,1)}) %all-gather.25.cloned.1.call-update) | async-done | bytes 1048592 | tf_op jit(solution)/shard_map/all_gather | solution.py:470
  406.5 4.0 multiply_convert_fusion
  414.5 4.3 all-to-all-start.7
  418.8 13.9 %all-to-all-done.7 = bf16[4,128,1024]{2,1,0:T(8,128)(2,1)} async-done(((bf16[4,128,1024]{2,1,0:T(8,128)(2,1)}), bf16[4,128,1024]{2,1,0:T(8,128)(2,1)}, u32[]{:S(2)}, u32[]{:S(2)}) %all-to-all-start.7) | async-done | bytes 1048608 | tf_op jit(solution)/shard_map/all_to_all | solution.py:475
  436.4 26.7 %all-gather.27.cloned.1.call-done = bf16[512,1024]{1,0:T(8,128)(2,1)} async-done(((bf16[128,1024]{1,0:T(8,128)(2,1)}), bf16[512,1024]{1,0:T(8,128)(2,1)}) %all-gather.27.cloned.1.call-update) | async-done | bytes 1048592 | tf_op jit(solution)/shard_map/all_gather | solution.py:470
  466.0 14.8 %all-gather.1 = bf16[16,128,128]{2,1,0:T(8,128)(2,1)S(1)} all-gather(bf16[2,128,128]{2,1,0:T(8,128)(2,1)S(1)} %convert_element_type.230), channel_id=3, replica_groups=mesh['seq'=4,'ctx'=8] {'ctx'}, dimensions={0}, use_global_device_ids=true | all-gather | bytes 589824 | tf_op jit(solution)/shard_map/all_gather | solution.py:592
  480.7 25.9 %recurrence_backward.1 = (bf16[512,1280]{1,0:T(8,128)(2,1)}, f32[8,1280]{1,0:T(8,128)S(1)}, f32[8,1280]{1,0:T(8,128)S(1)}, f32[8,1280]{1,0:T(8,128)S(1)}, f32[8,...) custom-call(s32[1]{0:T(128)} %bitcast.index_ref, bf16[8,2,128,256]{3,2,1,0:T(8,128)(2,1)S(1)} %bitcast.177, ...), custom_call_target="tpu_custom_call" | custom-call | tf_op jit(solution)/shard_map/recurrence_backward/pallas_call | solution.py:394
  508.4 3.5 convolution_convert_fusion.4
  515.2 2.6 copy.247
  531.8 30.0 %all-reduce.7 = bf16[4,8,32,6]{2,0,3,1:T(4,128)(2,1)S(1)} all-reduce(bf16[4,8,32,6]{2,0,3,1:T(4,128)(2,1)S(1)} %copy.242), channel_id=5, replica_groups=mesh['seq'=4,'ctx'=8] {'ctx'}, use_global_device_ids=true, to_apply=%region_20.21.clone | all-reduce | flops 6144 | bytes 24576
  563.0 3.2 all-to-all-start.10
  570.4 4.4 convolution_convert_fusion
  580.4 4.2 all-to-all-start.8
  588.8 5.7 all-to-all-done.8
  595.6 40.7 %psum.15 = f32[2193]{0:T(1024)S(1)} all-reduce(f32[2193]{0:T(1024)S(1)} %concatenate.22), channel_id=1, replica_groups=mesh['seq'=4,'ctx'=8] {'seq','ctx'}, use_global_device_ids=true, to_apply=%region_17.18 | all-reduce | flops 2193 | bytes 17544 | tf_op jit(solution)/shard_map/psum | solution.py:622
  641.7 101.2 %all-reduce.15.cloned.1.call-done = (bf16[4,8,32,1280]{3,2,1,0:T(8,128)(2,1)}, bf16[4,8,32,256]{3,2,1,0:T(8,128)(2,1)}, bf16[4,8,32,704]{3,2,1,0:T(8,128)(2,1)}, bf16[4,8,32,704]{3,2,1,0:T(8,128)(2,1)}) async-done(((bf16[4,8,32,1280]{3,2,1,0:T(8,128)(2,1)}, bf16[4,8,32,256]{3,2,1,0:T(8,128)(2,1)}, bf16[4,8,32,704]{3,2,1,0:T(8,128)(2,1)}, bf16[4,8,32,704]{3,2,1,0:T(8,128)(2,1)}), ...) | async-done | bytes 6029328
  745.0 3.6 all-to-all-start.11
  750.9 2.6 all-to-all-done.11
  753.5 3.4 all-to-all-start.12
  762.0 3.6 all-to-all-start.13
  766.3 4.5 all-to-all-done.13
  770.8 3.5 all-to-all-start.9
  776.8 2.9 all-to-all-done.9
  (330 shorter events, 123.3 us)
Async XLA Ops:
  7.2 93.2 %all-gather.13.cloned.1.call-start = ((), (), s32[]{:S(2)}) async-start(), calls=%async_computation.17 | async-start | bytes 1310720 | tf_op jit(solution)/shard_map/all_gather | solution.py:470
  53.2 13.5 %copy-start.44 = (bf16[32,24]{0,1:T(8,128)(2,1)S(1)}, bf16[32,24]{0,1:T(8,128)(2,1)}, u32[]{:S(2)}) copy-start(bf16[32,24]{0,1:T(8,128)(2,1)} %param.22) | copy-start | bytes 4612
  53.2 17.4 %copy-start.41 = (s32[4096]{0:T(1024)S(1)}, s32[4096]{0:T(1024)}, u32[]{:S(2)}) copy-start(s32[4096]{0:T(1024)} %param.20) | copy-start | bytes 49156
  55.0 16.6 %copy-start.57 = (bf16[8]{0:T(256)(128)(2,1)S(1)}, bf16[8]{0:T(256)(128)(2,1)}, u32[]{:S(2)}) copy-start(bf16[8]{0:T(256)(128)(2,1)} %param.29) | copy-start | bytes 52
  55.0 16.8 %copy-start.47 = (bf16[160,4]{0,1:T(4,128)(2,1)S(1)}, bf16[160,4]{0,1:T(4,128)(2,1)}, u32[]{:S(2)}) copy-start(bf16[160,4]{0,1:T(4,128)(2,1)} %param.25) | copy-start | bytes 3844
  55.0 29.7 %copy-start.58 = (bf16[8]{0:T(256)(128)(2,1)S(1)}, bf16[8]{0:T(256)(128)(2,1)}, u32[]{:S(2)}) copy-start(bf16[8]{0:T(256)(128)(2,1)} %param.30) | copy-start | bytes 52
  55.0 62.5 %all-gather.15.cloned.1.call-start = ((), (), s32[]{:S(2)}) async-start(), calls=%async_computation.18 | async-start | bytes 2949120 | tf_op jit(solution)/shard_map/all_gather | solution.py:448
  67.3 17.9 %all-to-all-start.1 = ((bf16[32,4,6]{0,2,1:T(8,128)(2,1)}), bf16[32,4,6]{0,2,1:T(8,128)(2,1)S(1)}, u32[]{:S(2)}, u32[]{:S(2)}) async-start(bf16[32,4,6]{0,2,1:T(8,128)(2,1)} %all_to_all.125), calls=%async_computation.1 | async-start | bytes 16384 | tf_op jit(solution)/shard_map/all_to_all | solution.py:447
  70.5 171.6 %all-gather.29.cloned.1.call-start = ((), (), s32[]{:S(2)}) async-start(), calls=%async_computation.27 | async-start | bytes 1179648 | tf_op jit(solution)/shard_map/all_gather | solution.py:559
  71.5 13.2 %copy-start.52 = (f32[8]{0:T(128)}, f32[8]{0:T(128)S(1)}, u32[]{:S(2)}) copy-start(f32[8]{0:T(128)S(1)} %convert_element_type.207) | copy-start | bytes 100
  84.6 18.3 %copy-start.42 = (f32[8,64]{1,0:T(8,128)}, f32[8,64]{1,0:T(8,128)S(1)}, u32[]{:S(2)}) copy-start(f32[8,64]{1,0:T(8,128)S(1)} %subtract_subtract_fusion) | copy-start | bytes 6148
  84.7 18.2 %copy-start.48 = (f32[2]{0:T(128)}, f32[2]{0:T(128)S(1)}, u32[]{:S(2)}) copy-start(f32[2]{0:T(128)S(1)} %fusion.49) | copy-start | bytes 28
  84.8 18.1 %copy-start.49 = (f32[2]{0:T(128)}, f32[2]{0:T(128)S(1)}, u32[]{:S(2)}) copy-start(f32[2]{0:T(128)S(1)} %dynamic_slice.17) | copy-start | bytes 28
  104.1 15.5 %copy-start.16 = (bf16[512,1024]{1,0:T(8,128)(2,1)S(1)}, bf16[512,1024]{1,0:T(8,128)(2,1)}, u32[]{:S(2)}) copy-start(bf16[512,1024]{1,0:T(8,128)(2,1)} %all-gather.13.cloned.1.call-done) | copy-start | bytes 3145732
  121.1 7.1 collective-permute-start
  129.6 52.8 %copy-start = (bf16[528,1280]{1,0:T(8,128)(2,1)}, bf16[528,1280]{1,0:T(8,128)(2,1)S(1)}, u32[]{:S(2)}) copy-start(bf16[528,1280]{1,0:T(8,128)(2,1)S(1)} %pad_maximum_fusion.proj_ref) | copy-start | bytes 4055044
  181.2 18.1 %copy-start.37 = (bf16[32,1024]{1,0:T(8,128)(2,1)S(1)}, bf16[32,1024]{1,0:T(8,128)(2,1)}, u32[]{:S(2)}) copy-start(bf16[32,1024]{1,0:T(8,128)(2,1)} %param.24) | copy-start | bytes 196612
  181.2 89.0 %all-gather.19.cloned.1.call-start = ((), (), s32[]{:S(2)}) async-start(), calls=%async_computation.20 | async-start | bytes 1769472 | tf_op jit(solution)/shard_map/all_gather | solution.py:448
  182.5 16.2 %copy-start.38 = (bf16[32,1024]{1,0:T(8,128)(2,1)S(1)}, bf16[32,1024]{1,0:T(8,128)(2,1)}, u32[]{:S(2)}) copy-start(bf16[32,1024]{1,0:T(8,128)(2,1)} %param.23) | copy-start | bytes 196612
  193.4 26.7 %copy-start.59 = (bf16[128]{0:T(256)(128)(2,1)S(1)}, bf16[128]{0:T(256)(128)(2,1)}, u32[]{:S(2)}) copy-start(bf16[128]{0:T(256)(128)(2,1)} %param.28) | copy-start | bytes 772
  195.3 19.8 %all-to-all-start.5 = ((bf16[32,4,704]{2,0,1:T(8,128)(2,1)}), bf16[32,4,704]{2,0,1:T(8,128)(2,1)S(1)}, u32[]{:S(2)}, u32[]{:S(2)}) async-start(bf16[32,4,704]{2,0,1:T(8,128)(2,1)} %copy.230), calls=%async_computation.5 | async-start | bytes 393216 | tf_op jit(solution)/shard_map/all_to_all | solution.py:447
  215.1 9.0 %all-to-all-start.2 = ((bf16[32,4,256]{2,0,1:T(8,128)(2,1)}), bf16[32,4,256]{2,0,1:T(8,128)(2,1)S(1)}, u32[]{:S(2)}, u32[]{:S(2)}) async-start(bf16[32,4,256]{2,0,1:T(8,128)(2,1)} %bitcast.174), calls=%async_computation.2 | async-start | bytes 131072 | tf_op jit(solution)/shard_map/all_to_all | solution.py:447
  219.2 58.2 %all-gather.21.cloned.1.call-start = ((), (), s32[]{:S(2)}) async-start(), calls=%async_computation.21 | async-start | bytes 1769472 | tf_op jit(solution)/shard_map/all_gather | solution.py:448
  247.1 18.9 %all-to-all-start.3 = ((bf16[4,128,1024]{2,1,0:T(8,128)(2,1)}), bf16[4,128,1024]{2,1,0:T(8,128)(2,1)}, u32[]{:S(2)}, u32[]{:S(2)}) async-start(bf16[4,128,1024]{2,1,0:T(8,128)(2,1)} %bitcast.187), calls=%async_computation.3 | async-start | bytes 2097152 | tf_op jit(solution)/shard_map/all_to_all | solution.py:475
  251.4 44.0 %all-gather.17.cloned.1.call-start = ((), (), s32[]{:S(2)}) async-start(), calls=%async_computation.19 | async-start | bytes 1310720 | tf_op jit(solution)/shard_map/all_gather | solution.py:470
  269.5 51.9 %all-gather.23.cloned.1.call-start = ((), (), s32[]{:S(2)}) async-start(), calls=%async_computation.22 | async-start | bytes 1622016 | tf_op jit(solution)/shard_map/all_gather | solution.py:453
  324.9 51.8 %all-to-all-start.6 = ((bf16[4,128,1024]{2,1,0:T(8,128)(2,1)}), bf16[4,128,1024]{2,1,0:T(8,128)(2,1)}, u32[]{:S(2)}, u32[]{:S(2)}) async-start(bf16[4,128,1024]{2,1,0:T(8,128)(2,1)} %bitcast.198), calls=%async_computation.6 | async-start | bytes 2097152 | tf_op jit(solution)/shard_map/all_to_all | solution.py:475
  329.3 77.2 %all-gather.25.cloned.1.call-start = ((), (), s32[]{:S(2)}) async-start(), calls=%async_computation.23 | async-start | bytes 1310720 | tf_op jit(solution)/shard_map/all_gather | solution.py:470
  414.5 18.2 %all-to-all-start.7 = ((bf16[4,128,1024]{2,1,0:T(8,128)(2,1)}), bf16[4,128,1024]{2,1,0:T(8,128)(2,1)}, u32[]{:S(2)}, u32[]{:S(2)}) async-start(bf16[4,128,1024]{2,1,0:T(8,128)(2,1)} %bitcast.199), calls=%async_computation.7 | async-start | bytes 2097152 | tf_op jit(solution)/shard_map/all_to_all | solution.py:475
  418.7 44.5 %all-gather.27.cloned.1.call-start = ((), (), s32[]{:S(2)}) async-start(), calls=%async_computation.24 | async-start | bytes 1310720 | tf_op jit(solution)/shard_map/all_gather | solution.py:470
  436.4 149.0 %reduce-scatter.18.cloned.1.call-start = ((), (), s32[]{:S(2)}) async-start(), calls=%async_computation.28 | async-start | bytes 737280
  463.2 17.5 %copy-start.15 = (f32[2,128,128]{2,1,0:T(8,128)S(1)}, f32[2,128,128]{2,1,0:T(8,128)}, u32[]{:S(2)}) copy-start(f32[2,128,128]{2,1,0:T(8,128)} %copy-done.14) | copy-start | bytes 393220
  465.1 15.7 %copy-start.2 = (bf16[16,128,256]{2,1,0:T(8,128)(2,1)S(1)}, bf16[16,128,256]{2,1,0:T(8,128)(2,1)}, u32[]{:S(2)}) copy-start(bf16[16,128,256]{2,1,0:T(8,128)(2,1)} %all-gather.29.cloned.1.call-done) | copy-start | bytes 3145732
  465.1 15.7 %copy-start.6 = (f32[8,2,128,128]{3,2,1,0:T(8,128)S(1)}, f32[8,2,128,128]{3,2,1,0:T(8,128)}, u32[]{:S(2)}) copy-start(f32[8,2,128,128]{3,2,1,0:T(8,128)} %copy-done.5) | copy-start | bytes 3145732
  465.1 15.7 %copy-start.11 = (f32[8,2,64,128]{3,2,1,0:T(8,128)S(1)}, f32[8,2,64,128]{3,2,1,0:T(8,128)}, u32[]{:S(2)}) copy-start(f32[8,2,64,128]{3,2,1,0:T(8,128)} %copy-done.10) | copy-start | bytes 1572868
  508.1 78.9 %reduce-scatter.16.cloned.1.call-start = ((), (), s32[]{:S(2)}) async-start(), calls=%async_computation.26 | async-start | bytes 1622016 | tf_op jit(solution)/shard_map/reduce_scatter | solution.py:466
  524.4 44.6 %collective-permute-start.1 = (f32[8,1280]{1,0:T(8,128)S(1)}, f32[8,1280]{1,0:T(8,128)}, u32[]{:S(2)}, u32[]{:S(2)}) collective-permute-start(f32[8,1280]{1,0:T(8,128)S(1)} %get-tuple-element.65), channel_id=1, source_target_pairs={{1,0},{2,1},{3,2},{4,3},{5,4},{6,5},{7,6},{9,8},{10,9},{11,10},{12... | collective-permute-start | bytes 122888 | tf_op jit(solution)/shard_map/ppermute | solution.py:427
  527.4 39.0 %copy-start.23 = (bf16[512,1024]{1,0:T(8,128)(2,1)S(1)}, bf16[512,1024]{1,0:T(8,128)(2,1)}, u32[]{:S(2)}) copy-start(bf16[512,1024]{1,0:T(8,128)(2,1)} %all-gather.27.cloned.1.call-done) | copy-start | bytes 3145732
  563.0 17.3 %all-to-all-start.10 = ((bf16[4,32,6]{1,2,0:T(8,128)(2,1)}), bf16[4,32,6]{1,2,0:T(8,128)(2,1)S(1)}, u32[]{:S(2)}, u32[]{:S(2)}) async-start(bf16[4,32,6]{1,2,0:T(8,128)(2,1)} %copy.243), calls=%async_computation.10 | async-start | bytes 16384 | tf_op jit(solution)/shard_map/all_to_all | solution.py:462
  566.3 73.9 %reduce-scatter.14.cloned.1.call-start = ((), (), s32[]{:S(2)}) async-start(), calls=%async_computation.25 | async-start | bytes 589824 | tf_op jit(solution)/shard_map/reduce_scatter | solution.py:466
  567.7 175.2 %all-reduce.15.cloned.1.call-start = ((), (), s32[]{:S(2)}) async-start(), calls=%async_computation.29 | async-start | bytes 12582912
  580.4 14.1 %all-to-all-start.8 = ((bf16[4,128,1024]{2,1,0:T(8,128)(2,1)}), bf16[4,128,1024]{2,1,0:T(8,128)(2,1)S(1)}, u32[]{:S(2)}, u32[]{:S(2)}) async-start(bf16[4,128,1024]{2,1,0:T(8,128)(2,1)} %bitcast.29), calls=%async_computation.8 | async-start | bytes 2097152 | tf_op jit(solution)/shard_map/all_to_all | solution.py:475
  587.0 51.7 %copy-start.51 = (f32[128]{0:T(128)S(1)}, f32[128]{0:T(128)}, u32[]{:S(2)}) copy-start(f32[128]{0:T(128)} %copy-done.50) | copy-start | bytes 1540
  587.0 52.3 %copy-start.28 = (f32[128,1024]{1,0:T(8,128)S(1)}, f32[128,1024]{1,0:T(8,128)}, u32[]{:S(2)}) copy-start(f32[128,1024]{1,0:T(8,128)} %get-tuple-element.86) | copy-start | bytes 1572868
  745.0 8.5 %all-to-all-start.11 = ((bf16[4,32,256]{2,1,0:T(8,128)(2,1)}), bf16[4,32,256]{2,1,0:T(8,128)(2,1)S(1)}, u32[]{:S(2)}, u32[]{:S(2)}) async-start(bf16[4,32,256]{2,1,0:T(8,128)(2,1)} %dynamic-slice_bitcast_fusion.3), calls=%async_computation.11 | async-start | bytes 131072 | tf_op jit(solution)/shard_map/all_to_all | solution.py:462
  753.5 8.5 %all-to-all-start.12 = ((bf16[4,32,704]{2,1,0:T(8,128)(2,1)}), bf16[4,32,704]{2,1,0:T(8,128)(2,1)S(1)}, u32[]{:S(2)}, u32[]{:S(2)}) async-start(bf16[4,32,704]{2,1,0:T(8,128)(2,1)} %dynamic-slice_bitcast_fusion.2), calls=%async_computation.13 | async-start | bytes 393216 | tf_op jit(solution)/shard_map/all_to_all | solution.py:462
  762.0 8.8 %all-to-all-start.13 = ((bf16[4,32,704]{2,1,0:T(8,128)(2,1)}), bf16[4,32,704]{2,1,0:T(8,128)(2,1)S(1)}, u32[]{:S(2)}, u32[]{:S(2)}) async-start(bf16[4,32,704]{2,1,0:T(8,128)(2,1)} %dynamic-slice_bitcast_fusion.1), calls=%async_computation.14 | async-start | bytes 393216 | tf_op jit(solution)/shard_map/all_to_all | solution.py:462
  770.8 9.0 %all-to-all-start.9 = ((bf16[4,32,1280]{2,1,0:T(8,128)(2,1)}), bf16[4,32,1280]{2,1,0:T(8,128)(2,1)S(1)}, u32[]{:S(2)}, u32[]{:S(2)}) async-start(bf16[4,32,1280]{2,1,0:T(8,128)(2,1)} %dynamic-slice_bitcast_fusion), calls=%async_computation.9 | async-start | bytes 655360 | tf_op jit(solution)/shard_map/all_to_all | solution.py:462
  (46 other events, 126.2 us)
Sparse Core Ops, SparseCore 0:
  55.1 26.4 all-gather.12
  83.8 33.6 all-gather.14
  181.3 22.2 all-gather.28
  205.7 26.1 all-gather.18
  234.0 24.8 all-gather.20
  269.6 25.7 all-gather.16
  297.0 24.3 all-gather.22
  380.0 26.4 all-gather.24
  436.5 26.6 all-gather.26
  508.2 30.1 reduce-scatter.17
  540.7 31.9 reduce-scatter.15
  574.8 28.9 reduce-scatter.13
  606.5 136.2 all-reduce.14

commit v2 on v1

--- a/solution.py
+++ b/solution.py
@@ -23,6 +23,7 @@
 F32 = jnp.float32
 BF16 = jnp.bfloat16
 BOTH = ("seq", "ctx")
+MESH = pl.DeviceIdType.MESH
 
 
 def split_bf16(x):
@@ -222,44 +223,212 @@
     )(index, maps, oloc, carr, gate_out, gain)
 
 
-def gate_back_kernel(heads, grad_ref, heads_ref, gate_ref, gain_ref, carr_ref, ghead_ref, ggate_ref, ggain_ref, cot_ref):
-    total = jnp.zeros((1, HEAD), F32)
-    for h in range(heads):
-        hc = slice(h * HEAD, (h + 1) * HEAD)
-        x = heads_ref[:, hc].astype(F32)
-        gate = gate_ref[:, hc]
-        grad = grad_ref[:, hc]
-        gain = gain_ref[...]
-        inv = lax.rsqrt(jnp.mean(x * x, axis=1, keepdims=True) + NORM_EPS)
+def seq_barrier(size):
+    me = lax.axis_index("seq")
+    barrier = pltpu.get_barrier_semaphore()
+
+    def greet(i, carry):
+        pl.semaphore_signal(barrier, inc=1, device_id={"seq": lax.rem(me + i, size)}, device_id_type=MESH)
+        return carry
+
+    lax.fori_loop(1, size, greet, 0)
+    pl.semaphore_wait(barrier, size - 1)
+
+
+def middle_kernel(
+    size, heads, scale_ref,
+    x_ref, teach_ref, mask_ref, norm_ref, gain_ref, mixed_ref, heads_ref, gate_ref, carr_ref,
+    wout_ref, wg_ref, wu_ref, wd_ref,
+    final_ref, gmid_ref, ghead_ref, ggate_ref, cot_ref, ggain_ref, gnorm_ref, loss_ref,
+    gout_ref, gwg_ref, gwu_ref, gwd_ref,
+    second, branch, low, sent, got, own, mid, gfin, gates, ups, hidden, ggates, gups, send_sem, recv_sem,
+):
+    me = lax.axis_index("seq")
+    count = x_ref.shape[0]
+    seq_barrier(size)
+
+    def dot(a, b, ca=1, cb=0):
+        return lax.dot_general(a, b, (((ca,), (cb,)), ((), ())), preferred_element_type=F32)
+
+    def rows(q):
+        return pl.ds(pl.multiple_of(q * count, count), count)
+
+    def part_copy(phase, i):
+        return pltpu.make_async_remote_copy(
+            sent.at[phase, i - 1], got.at[phase, i - 1], send_sem.at[phase, i - 1], recv_sem.at[phase, i - 1],
+            device_id={"seq": lax.rem(me + i, size)}, device_id_type=MESH,
+        )
+
+    def block_copy(buffer, phase, i, owner):
+        return pltpu.make_async_remote_copy(
+            buffer.at[rows(owner)], buffer.at[rows(owner)], send_sem.at[phase, i - 1], recv_sem.at[phase, i - 1],
+            device_id={"seq": lax.rem(me + i, size)}, device_id_type=MESH,
+        )
+
+    def give_part(phase, i, part):
+        @pl.when(i > 0)
+        def _():
+            sent[phase, i - 1] = part.astype(BF16)
+            part_copy(phase, i).start()
+
+        @pl.when(i == 0)
+        def _():
+            own[...] = part
+
+    def take_parts(phase):
+        def add(i, total):
+            part_copy(phase, i).wait_recv()
+            return total + got[phase, i - 1].astype(F32)
+
+        return lax.fori_loop(1, size, add, own[...])
+
+    def give_block(buffer, phase, value):
+        buffer[rows(me)] = value
+
+        def send(i, carry):
+            block_copy(buffer, phase, i, me).start()
+            return carry
+
+        lax.fori_loop(1, size, send, 0)
+
+    def take_block(buffer, phase, i):
+        q = lax.rem(me + size - i, size)
+
+        @pl.when(i > 0)
+        def _():
+            block_copy(buffer, phase, i, q).wait_recv()
+
+        return q
+
+    def out_part(k, carry):
+        i = lax.rem(k + 1, size)
+        give_part(0, i, dot(mixed_ref[rows(lax.rem(me + i, size))], wout_ref[...]))
+        return carry
+
+    lax.fori_loop(0, size, out_part, 0)
+    middle = x_ref[...].astype(F32) + take_parts(0)
+    mid[...] = middle
+    inv = lax.rsqrt(jnp.mean(middle * middle, axis=1, keepdims=True) + NORM_EPS)
+    give_block(second, 3, (middle * inv * norm_ref[...]).astype(BF16))
+
+    def feed(i, carry):
+        q = take_block(second, 3, i)
+        here = second[rows(q)]
+        gate = dot(here, wg_ref[...])
+        up = dot(here, wu_ref[...])
+        gates[rows(q)] = gate
+        ups[rows(q)] = up
+        hid = (gate * jax.nn.sigmoid(gate) * up).astype(BF16)
+        hidden[rows(q)] = hid
+        give_part(1, lax.rem(size - i, size), dot(hid, wd_ref[...]))
+        return carry
+
+    lax.fori_loop(0, size, feed, 0)
+    final = mid[...] + take_parts(1)
+    final_ref[...] = final.astype(BF16)
+    error = final - teach_ref[...].astype(F32)
+    weighted = mask_ref[...] * error
+    loss_ref[...] = jnp.broadcast_to(
+        jnp.sum(jnp.sum(weighted * error, axis=1, keepdims=True), axis=0, keepdims=True), loss_ref.shape
+    )
+    grad_final = scale_ref[0, 0] * weighted
+    gfin[...] = grad_final
+    give_block(branch, 4, grad_final.astype(BF16))
+
+    def feed_back(i, carry):
+        q = take_block(branch, 4, i)
+        ghid = dot(branch[rows(q)], wd_ref[...], 1, 1)
+        gate = gates[rows(q)]
         sig = jax.nn.sigmoid(gate)
         silu = gate * sig
-        unit = x * inv
-        ggate_ref[:, hc] = (grad * unit * gain * (sig * (1.0 + gate * (1.0 - sig)))).astype(BF16)
-        weighted = grad * silu
-        total = total + jnp.sum(weighted * unit, axis=0, keepdims=True)
-        down = weighted * gain
-        ghead = (inv * (down - unit * jnp.mean(down * unit, axis=1, keepdims=True))).astype(BF16)
-        ghead_ref[:, hc] = ghead
-        cot_ref[h] = mm(carr_ref[:, hc], ghead, 0, 0)
-    ggain_ref[...] = total
-
-
-def gate_back(grad_mixed, heads_out, gate_out, gain, carr, heads):
-    rows = carr.shape[0]
+        ggate = (ghid * ups[rows(q)] * (sig + silu * (1.0 - sig))).astype(BF16)
+        gup = (ghid * silu).astype(BF16)
+        ggates[rows(q)] = ggate
+        gups[rows(q)] = gup
+        give_part(2, lax.rem(size - i, size), dot(ggate, wg_ref[...], 1, 1) + dot(gup, wu_ref[...], 1, 1))
+        return carry
+
+    lax.fori_loop(0, size, feed_back, 0)
+    gwd_ref[...] = dot(hidden[...], branch[...], 0, 0).astype(BF16)
+    gwg_ref[...] = dot(second[...], ggates[...], 0, 0).astype(BF16)
+    gwu_ref[...] = dot(second[...], gups[...], 0, 0).astype(BF16)
+    gsecond = take_parts(2)
+    middle = mid[...]
+    inv = lax.rsqrt(jnp.mean(middle * middle, axis=1, keepdims=True) + NORM_EPS)
+    unit = middle * inv
+    gnorm_ref[...] = jnp.sum(gsecond * unit, axis=0, keepdims=True)
+    down = gsecond * norm_ref[...]
+    gmid = gfin[...] + inv * (down - unit * jnp.mean(down * unit, axis=1, keepdims=True))
+    gmid_ref[...] = gmid
+    give_block(low, 5, gmid.astype(BF16))
+    ggain_ref[...] = jnp.zeros_like(ggain_ref)
+    cot_ref[...] = jnp.zeros_like(cot_ref)
+
+    def out_back(i, carry):
+        q = take_block(low, 5, i)
+        gmixed = dot(low[rows(q)], wout_ref[...], 1, 1)
+        gain = gain_ref[...]
+        for h in range(heads):
+            hc = slice(h * HEAD, (h + 1) * HEAD)
+            x = heads_ref[rows(q), hc].astype(F32)
+            gate = gate_ref[rows(q), hc]
+            grad = gmixed[:, hc]
+            inv = lax.rsqrt(jnp.mean(x * x, axis=1, keepdims=True) + NORM_EPS)
+            sig = jax.nn.sigmoid(gate)
+            silu = gate * sig
+            unit = x * inv
+            ggate_ref[rows(q), hc] = (grad * unit * gain * (sig + silu * (1.0 - sig))).astype(BF16)
+            weighted = grad * silu
+            ggain_ref[...] += jnp.sum(weighted * unit, axis=0, keepdims=True)
+            down = weighted * gain
+            ghead = (inv * (down - unit * jnp.mean(down * unit, axis=1, keepdims=True))).astype(BF16)
+            ghead_ref[rows(q), hc] = ghead
+            cot_ref[h] += mm(carr_ref[rows(q), hc], ghead, 0, 0)
+        return carry
+
+    lax.fori_loop(0, size, out_back, 0)
+    gout_ref[...] = dot(mixed_ref[...], low[...], 0, 0).astype(BF16)
+
+    def sent_all(i, carry):
+        for phase in range(3):
+            part_copy(phase, i).wait_send()
+        block_copy(second, 3, i, me).wait_send()
+        block_copy(branch, 4, i, me).wait_send()
+        block_copy(low, 5, i, me).wait_send()
+        return carry
+
+    lax.fori_loop(1, size, sent_all, 0)
+
+
+def middle_part(size, heads, scale, x, teacher, mask, norm_m, gain, mixed, heads_out, gate_out, carr, wout, wg, wu, wd):
+    count = x.shape[0]
+    rows = count * size
+    inner = wg.shape[1]
     vmem = pl.BlockSpec(memory_space=pltpu.VMEM)
+    out = lambda dims, kind: jax.ShapeDtypeStruct(dims, kind)
     return pl.pallas_call(
-        functools.partial(gate_back_kernel, heads),
-        in_specs=[vmem] * 5,
-        out_specs=[vmem] * 4,
+        functools.partial(middle_kernel, size, heads),
+        in_specs=[pl.BlockSpec(memory_space=pltpu.SMEM)] + [vmem] * 13,
+        out_specs=[vmem] * 12,
         out_shape=[
-            jax.ShapeDtypeStruct((rows, heads * HEAD), BF16),
-            jax.ShapeDtypeStruct((rows, heads * HEAD), BF16),
-            jax.ShapeDtypeStruct((1, HEAD), F32),
-            jax.ShapeDtypeStruct((heads, HEAD, HEAD), F32),
-        ],
-        compiler_params=pltpu.CompilerParams(vmem_limit_bytes=40 << 20),
-        name="gate_back",
-    )(grad_mixed, heads_out, gate_out, gain, carr)
+            out((count, D), BF16), out((count, D), F32),
+            out((rows, heads * HEAD), BF16), out((rows, heads * HEAD), BF16), out((heads, HEAD, HEAD), F32),
+            out((1, HEAD), F32), out((1, D), F32), out((8, HEAD), F32),
+            out((heads * HEAD, D), BF16), out((D, inner), BF16), out((D, inner), BF16), out((inner, D), BF16),
+        ],
+        scratch_shapes=[
+            pltpu.VMEM((rows, D), BF16), pltpu.VMEM((rows, D), BF16), pltpu.VMEM((rows, D), BF16),
+            pltpu.VMEM((3, size - 1, count, D), BF16), pltpu.VMEM((3, size - 1, count, D), BF16),
+            pltpu.VMEM((count, D), F32), pltpu.VMEM((count, D), F32), pltpu.VMEM((count, D), F32),
+            pltpu.VMEM((rows, inner), F32), pltpu.VMEM((rows, inner), F32), pltpu.VMEM((rows, inner), BF16),
+            pltpu.VMEM((rows, inner), BF16), pltpu.VMEM((rows, inner), BF16),
+            pltpu.SemaphoreType.DMA((6, size - 1)), pltpu.SemaphoreType.DMA((6, size - 1)),
+        ],
+        compiler_params=pltpu.CompilerParams(
+            vmem_limit_bytes=56 << 20, collective_id=1, has_side_effects=True
+        ),
+        name="middle_part",
+    )(scale, x, teacher, mask, norm_m, gain, mixed, heads_out, gate_out, carr, wout, wg, wu, wd)
 
 
 def bwd_kernel(
@@ -431,10 +600,6 @@
     return values * lax.rsqrt(jnp.mean(values * values, axis=-1, keepdims=True) + NORM_EPS) * gain_vec
 
 
-def swiglu_mix(gate_values, up_values):
-    return jax.nn.silu(gate_values) * up_values
-
-
 def scalar_gates(scal, a_log, dt_bias):
     beta = jax.nn.sigmoid(scal[:, :, :NH])
     logs = -jnp.exp(a_log)[None, :] * jax.nn.softplus(scal[:, :, NH] + dt_bias[None, :])
@@ -561,34 +726,20 @@
     index_arr = index.reshape(1).astype(jnp.int32)
     heads_out, mixed, state_in = state_and_gate(index_arr, maps, oloc, carr, gate_out, gain, heads)
 
-    middle = inputs_f + sum_tokens(dot(mixed, out_s))
-    second_f, norm_mlp_back = jax.vjp(rms_scale, middle, norm_m)
-    second = gather_tokens(second_f.astype(BF16))
-    gate_values = dot(second, wg_s)
-    up_values = dot(second, wu_s)
-    hidden_f, swiglu_back = jax.vjp(swiglu_mix, gate_values, up_values)
-    hidden = hidden_f.astype(BF16)
-    final_out = middle + sum_tokens(dot(hidden, down_s))
-    mask_values = valid_mask.astype(F32)
-    error_rows = final_out - teacher.astype(F32)
-    error_sum = jnp.sum(mask_values[:, None] * error_rows * error_rows)
-    grad_final = token_total / valid_count * mask_values[:, None] * error_rows
-
-    grad_branch = gather_tokens(grad_final.astype(BF16))
-    down_grad = sum_rows_back(t_dot(hidden, grad_branch))
-    grad_gate_f, grad_up_f = swiglu_back(dot_t(grad_branch, down_s))
-    grad_gate = grad_gate_f.astype(BF16)
-    grad_up = grad_up_f.astype(BF16)
-    grad_second = sum_tokens(dot_t(grad_gate, wg_s) + dot_t(grad_up, wu_s))
-    wg_grad = sum_columns_back(t_dot(second, grad_gate))
-    wu_grad = sum_columns_back(t_dot(second, grad_up))
-    grad_mid_norm, norm_mlp_term = norm_mlp_back(grad_second)
-    grad_middle = grad_final + grad_mid_norm
-    grad_mixed_low = gather_tokens(grad_middle.astype(BF16))
-    out_grad = sum_rows_back(t_dot(mixed, grad_mixed_low))
-    grad_mixed = dot_t(grad_mixed_low, out_s)
-
-    grad_heads, grad_gate_out, gain_term, cot = gate_back(grad_mixed, heads_out, gate_out, gain, carr, heads)
+    scale = (token_total / valid_count).reshape(1, 1)
+    mask_values = valid_mask.astype(F32)[:, None]
+    (
+        final_out, grad_middle, grad_heads, grad_gate_out, cot, gain_term, norm_mlp_term, loss,
+        out_grad, wg_grad, wu_grad, down_grad,
+    ) = middle_part(
+        seq_size, heads, scale, block_input, teacher, mask_values, norm_m[None, :], gain, mixed, heads_out, gate_out,
+        carr, out_s, wg_s, wu_s, down_s,
+    )
+    error_sum = loss[0, 0]
+    down_grad = sum_rows_back(down_grad)
+    out_grad = sum_rows_back(out_grad)
+    wg_grad = sum_columns_back(wg_grad)
+    wu_grad = sum_columns_back(wu_grad)
     cots = lax.all_gather(cot.astype(BF16), "ctx")
     grad_proj, last_rows, spill, gw, gcol, gtok, grow = recurrence_backward(
         index_arr, maps, cots, state_in, proj_ext, conv_w, rowp, colp, tokp, grad_heads, saved, heads
@@ -616,7 +767,7 @@
     small = jnp.concatenate(
         [
             gain_term[0], jnp.sum(grad_alog[:, None] * pick, axis=0), jnp.sum(grad_dt[:, None] * pick, axis=0),
-            error_sum[None], norm_attn_term, norm_mlp_term,
+            error_sum[None], norm_attn_term, norm_mlp_term[0],
         ]
     )
     small = lax.psum(small, BOTH)
@@ -625,7 +776,7 @@
     own = norm_attn.shape[0]
     place = (rank * lax.axis_size("ctx") + index) * own
     return (
-        final_out.astype(BF16),
+        final_out,
         mean_loss,
         input_grad,
         mix_grad,

time: 800 us -> 709 us (0.89); the launches traced: 789 us -> 707 us
  waiting for transfers between devices: 248 us -> 155 us
  Pallas kernels: 69.8 us -> 159 us
  matrix products: 44.5 us -> 14.7 us
  local copies, waits for them, and re-layouts: 82 us -> 58 us
  starting transfers between devices: 49.4 us -> 32.3 us
  other arithmetic: 24.8 us -> 13.3 us
    pallas_call x1, Pallas kernels: 0.85 us -> 90.6 us  [middle_part(): pl.pallas_call(functools.partial(middle_kernel, size, heads), in_specs=[p...]
    all_gather x4 -> x1, waiting for transfers between devices: 64.3 us -> 0.02 us  [gather_tokens(): return lax.all_gather(x, 'seq', axis=0, tiled=True)]
    all_to_all x4 -> x1, waiting for transfers between devices: 34.2 us -> 6.28 us  [sum_tokens(): lax.all_to_all(partial.astype(BF16).reshape(ranks, -1, partial.shape[1]),...]
    unnamed x15 -> x12, waiting for transfers between devices: 102 us -> 123 us
    all_gather x1, waiting for transfers between devices: 19.6 us -> 0.01 us  [rows_of_rank(): return lax.all_gather(w, 'ctx', axis=0, tiled=True)]
    all_to_all x4 -> x1, starting transfers between devices: 17.1 us -> 4.35 us  [sum_tokens(): lax.all_to_all(partial.astype(BF16).reshape(ranks, -1, partial.shape[1]),...]
    dot_general x7 -> x3, matrix products: 16 us -> 4.82 us  [dot(): return jnp.dot(a, b, preferred_element_type=F32)]
    dot_general x7 -> x3, matrix products: 14.9 us -> 5.97 us  [t_dot(): return jnp.einsum('tr,tc->rc', a, b, preferred_element_type=F32)]
  transfers between devices with their start and end apart: 27 -> 20, of which waited for: 14 -> 7; matrix products, arithmetic and copies ran while one was open for 12% -> 7% of each run, Pallas kernels for 0% -> 0%
where the time goes in v2:
time: 709 us; the launch traced here: 707 us
  blocking collectives  256 us (36%)
  Pallas kernels  159 us (22%)
  waiting for transfers between devices  155 us (22%)
  local copies, waits for them, and re-layouts  58 us (8%)
  starting transfers between devices  32.3 us (5%)
  between operations  17.5 us (2%)
  matrix products  14.7 us (2%)
  other arithmetic  13.3 us (2%)
    unnamed x12, waiting for transfers between devices  123 us
    pallas_call x1, Pallas kernels, middle_part(): pl.pallas_call(functools.partial(middle_kernel, size, heads), in_specs=[p...  90.6 us
    unnamed x2, blocking collectives  70.8 us
    pallas_call x1, Pallas kernels, recurrence_forward(): pl.pallas_call(functools.partial(fwd_kernel, heads), grid=(blocks,), in_s...  42.5 us
    psum x1, blocking collectives, local(): lax.psum(jnp.sum(valid_mask.astype(F32)), BOTH)  40.3 us
    psum x1, blocking collectives, local(): small = lax.psum(small, BOTH)  39.9 us
    all_gather x2, blocking collectives, columns_to_rank(): lax.all_gather(swapped.reshape(ranks, rows, cols), 'ctx', axis=1, tiled=T...  32 us
    all_gather x2, blocking collectives, rows_of_rank(): return lax.all_gather(w, 'ctx', axis=0, tiled=True)  30.6 us
  transfers between devices with their start and end apart: 20, of which 7 were waited for; matrix products, arithmetic and copies ran while one was open for 7% of the time, Pallas kernels for 0%

profile of v2, /device:TPU:0, one launch (start us, length us, event | category | flops | bytes accessed | tf_op | source)
XLA Modules:
  0.0 706.6 jit_solution(11742354610309771887)
XLA Ops:
  9.0 42.0 %all-reduce.11 = (bf16[1024]{0:T(1024)(128)(2,1)S(1)}, bf16[1024]{0:T(1024)(128)(2,1)S(1)}) all-reduce(bf16[1024]{0:T(1024)(128)(2,1)S(1)} %dynamic-update-slice, bf16[1024]{0:T(1024)(128)(2,1)S(1)} %dynamic-update-slice.1), channel_id=1, replica_groups=mesh['seq'=4,'ctx'=8] {'seq','ctx'}, use_global_device_ids=true, to_apply=%add.4 | all-reduce | flops 2048 | bytes 8192
  52.1 1.8 fusion.3
  55.0 9.6 %all_to_all.150 = bf16[32,4,1280]{2,0,1:T(8,128)(2,1)S(1)} all-to-all(bf16[32,4,1280]{2,0,1:T(8,128)(2,1)S(1)} %bitcast.163), channel_id=1, replica_groups=mesh['seq'=4,'ctx'=8] {'seq'}, dimensions={1} | all-to-all | bytes 655360 | tf_op jit(solution)/shard_map/all_to_all | solution.py:612
  66.2 3.2 all-to-all-start.1
  70.1 12.7 %all-gather.2 = bf16[8,160,4]{1,2,0:T(4,128)(2,1)S(1)} all-gather(bf16[1,160,4]{1,2,0:T(4,128)(2,1)S(1)} %bitcast.182), channel_id=1, replica_groups=mesh['seq'=4,'ctx'=8] {'ctx'}, dimensions={0}, use_global_device_ids=true | all-gather | bytes 11520 | tf_op jit(solution)/shard_map/all_gather | solution.py:618
  83.6 15.0 %all_gather.50 = bf16[4,256,6]{2,0,1:T(4,128)(2,1)S(1)} all-gather(bf16[4,32,6]{2,0,1:T(4,128)(2,1)S(1)} %copy.201), channel_id=1, replica_groups=mesh['seq'=4,'ctx'=8] {'ctx'}, dimensions={1}, use_global_device_ids=true | all-gather | bytes 13824 | tf_op jit(solution)/shard_map/all_gather | solution.py:613
  98.8 1.6 fusion
  102.3 15.0 %all-gather.12.cloned.1.call-done = bf16[4,256,1280]{2,0,1:T(4,128)(2,1)} async-done(((bf16[4,32,1280]{2,0,1:T(4,128)(2,1)}), bf16[4,256,1280]{2,0,1:T(4,128)(2,1)}) %all-gather.12.cloned.1.call-update) | async-done | bytes 2621456 | tf_op jit(solution)/shard_map/all_gather | solution.py:613
  117.2 2.1 copy.199
  119.3 1.5 convolution_convert_fusion.1
  120.9 2.1 collective-permute-start
  125.6 1.9 concatenate.20.colp_ref
  127.9 1.4 pad_maximum_fusion.proj_ref
  129.3 42.5 %recurrence_forward.1 = (f32[512,256]{1,0:T(8,128)S(1)}, f32[512,256]{1,0:T(8,128)S(1)}, f32[2,128,256]{2,1,0:T(8,128)S(1)}, f32[512,1280]{1,0:T(8,128)}, f32[8,...) custom-call(bf16[528,1280]{1,0:T(8,128)(2,1)S(1)} %pad_maximum_fusio, ...), custom_call_target="tpu_custom_call" | custom-call | tf_op jit(solution)/shard_map/recurrence_forward/pallas_call | solution.py:166
  182.7 9.5 %all_to_all.151 = bf16[32,4,704]{2,0,1:T(8,128)(2,1)} all-to-all(bf16[32,4,704]{2,0,1:T(8,128)(2,1)S(1)} %copy.215), channel_id=1, replica_groups=mesh['seq'=4,'ctx'=8] {'seq'}, dimensions={1} | all-to-all | bytes 360448 | tf_op jit(solution)/shard_map/all_to_all | solution.py:612
  193.5 8.8 %all_to_all.152 = bf16[32,4,704]{2,0,1:T(8,128)(2,1)} all-to-all(bf16[32,4,704]{2,0,1:T(8,128)(2,1)S(1)} %copy.216), channel_id=1, replica_groups=mesh['seq'=4,'ctx'=8] {'seq'}, dimensions={1} | all-to-all | bytes 360448 | tf_op jit(solution)/shard_map/all_to_all | solution.py:612
  202.3 1.5 copy.257
  203.8 3.3 all-to-all-start.2
  207.7 17.9 %all_gather.54.wout_ref = bf16[256,1024]{1,0:T(8,128)(2,1)} all-gather(bf16[32,1024]{1,0:T(8,128)(2,1)S(1)} %copy-done.31), channel_id=1, replica_groups=mesh['seq'=4,'ctx'=8] {'ctx'}, dimensions={0}, use_global_device_ids=true | all-gather | bytes 589824 | tf_op jit(solution)/shard_map/all_gather | solution.py:618
  225.6 40.3 %psum.14 = f32[]{:T(128)} all-reduce(f32[]{:T(128)} %convert_reduce_fusion.1), channel_id=1, replica_groups=mesh['seq'=4,'ctx'=8] {'seq','ctx'}, use_global_device_ids=true, to_apply=%region_1.0 | all-reduce | flops 1 | bytes 8 | tf_op jit(solution)/shard_map/psum | solution.py:681
  268.0 16.9 %all_gather.53 = bf16[4,256,256]{2,0,1:T(4,128)(2,1)S(1)} all-gather(bf16[4,32,256]{2,0,1:T(4,128)(2,1)S(1)} %copy.213), channel_id=1, replica_groups=mesh['seq'=4,'ctx'=8] {'ctx'}, dimensions={1}, use_global_device_ids=true | all-gather | bytes 589824 | tf_op jit(solution)/shard_map/all_gather | solution.py:613
  285.8 1.7 fusion.47.gate_ref
  290.9 90.6 %middle_part.1 = (bf16[128,1024]{1,0:T(8,128)(2,1)}, f32[128,1024]{1,0:T(8,128)}, bf16[512,256]{1,0:T(8,128)(2,1)}, bf16[512,256]{1,0:T(8,128)(2,1)}, f32[2,128,...) custom-call(f32[1,1]{1,0:T(1,128)} %bitcast.scale_ref, ...), custom_call_target="tpu_custom_call" | custom-call | tf_op jit(solution)/shard_map/middle_part/pallas_call | solution.py:409
  382.4 15.0 %all-gather.1 = bf16[16,128,128]{2,1,0:T(8,128)(2,1)S(1)} all-gather(bf16[2,128,128]{2,1,0:T(8,128)(2,1)S(1)} %convert_element_type.159), channel_id=3, replica_groups=mesh['seq'=4,'ctx'=8] {'ctx'}, dimensions={0}, use_global_device_ids=true | all-gather | bytes 589824 | tf_op jit(solution)/shard_map/all_gather | solution.py:743
  398.3 25.8 %recurrence_backward.1 = (bf16[512,1280]{1,0:T(8,128)(2,1)}, f32[8,1280]{1,0:T(8,128)S(1)}, f32[8,1280]{1,0:T(8,128)S(1)}, f32[8,1280]{1,0:T(8,128)S(1)}, f32[8,...) custom-call(s32[1]{0:T(128)} %bitcast.4.index_ref, bf16[8,2,128,256]{3,2,1,0:T(8,128)(2,1)S(1)} %bitcast.149, ...), custom_call_target="tpu_custom_call" | custom-call | tf_op jit(solution)/shard_map/recurrence_backward/pallas_call | solution.py:563
  428.5 1.4 collective-permute-start.1
  432.0 28.8 %all-reduce.7 = bf16[4,8,32,6]{2,0,3,1:T(4,128)(2,1)S(1)} all-reduce(bf16[4,8,32,6]{2,0,3,1:T(4,128)(2,1)S(1)} %copy.227), channel_id=5, replica_groups=mesh['seq'=4,'ctx'=8] {'ctx'}, use_global_device_ids=true, to_apply=%region_13.14.clone | all-reduce | flops 6144 | bytes 24576
  462.1 3.4 all-to-all-start.7
  467.4 4.4 convolution_convert_fusion
  474.1 2.5 add_convert_fusion
  476.7 4.3 all-to-all-start.5
  483.0 1.6 copy.237
  484.6 6.3 all-to-all-done.5
  492.0 39.9 %psum.15 = f32[2193]{0:T(1024)S(1)} all-reduce(f32[2193]{0:T(1024)S(1)} %concatenate.22), channel_id=1, replica_groups=mesh['seq'=4,'ctx'=8] {'seq','ctx'}, use_global_device_ids=true, to_apply=%region_10.11 | all-reduce | flops 2193 | bytes 17544 | tf_op jit(solution)/shard_map/psum | solution.py:773
  535.8 1.5 convert_element_type.178
  537.3 1.7 convert_element_type.185
  539.0 121.1 %all-reduce.15.cloned.1.call-done = (bf16[4,8,32,1280]{3,2,1,0:T(8,128)(2,1)}, bf16[4,8,32,256]{3,2,1,0:T(8,128)(2,1)}, bf16[4,8,32,704]{3,2,1,0:T(8,128)(2,1)}, bf16[4,8,32,704]{3,2,1,0:T(8,128)(2,1)}) async-done(((bf16[4,8,32,1280]{3,2,1,0:T(8,128)(2,1)}, bf16[4,8,32,256]{3,2,1,0:T(8,128)(2,1)}, bf16[4,8,32,704]{3,2,1,0:T(8,128)(2,1)}, bf16[4,8,32,704]{3,2,1,0:T(8,128)(2,1)}), ...) | async-done | bytes 6029328
  660.1 2.1 dynamic-slice_bitcast_fusion.3
  662.2 3.6 all-to-all-start.8
  665.8 2.3 dynamic-slice_bitcast_fusion.2
  668.1 2.6 all-to-all-done.8
  670.7 3.4 all-to-all-start.9
  674.1 2.4 dynamic-slice_bitcast_fusion
  676.4 2.3 dynamic-slice_bitcast_fusion.1
  679.2 3.6 all-to-all-start.10
  683.5 4.5 all-to-all-done.10
  688.1 3.5 all-to-all-start.6
  694.1 2.9 all-to-all-done.6
  (238 shorter events, 55.3 us)
Async XLA Ops:
  7.2 58.4 %copy-start.33 = (bf16[32,24]{0,1:T(8,128)(2,1)S(1)}, bf16[32,24]{0,1:T(8,128)(2,1)}, u32[]{:S(2)}) copy-start(bf16[32,24]{0,1:T(8,128)(2,1)} %param.22) | copy-start | bytes 4612
  7.2 62.3 %copy-start.32 = (s32[4096]{0:T(1024)S(1)}, s32[4096]{0:T(1024)}, u32[]{:S(2)}) copy-start(s32[4096]{0:T(1024)} %param.20) | copy-start | bytes 49156
  7.2 62.7 %copy-start.38 = (bf16[8]{0:T(256)(128)(2,1)S(1)}, bf16[8]{0:T(256)(128)(2,1)}, u32[]{:S(2)}) copy-start(bf16[8]{0:T(256)(128)(2,1)} %param.29) | copy-start | bytes 52
  7.2 62.9 %copy-start.35 = (bf16[160,4]{0,1:T(4,128)(2,1)S(1)}, bf16[160,4]{0,1:T(4,128)(2,1)}, u32[]{:S(2)}) copy-start(bf16[160,4]{0,1:T(4,128)(2,1)} %param.25) | copy-start | bytes 3844
  7.2 75.8 %copy-start.39 = (bf16[8]{0:T(256)(128)(2,1)S(1)}, bf16[8]{0:T(256)(128)(2,1)}, u32[]{:S(2)}) copy-start(bf16[8]{0:T(256)(128)(2,1)} %param.30) | copy-start | bytes 52
  7.2 91.6 %all-gather.10.cloned.1.call-start = ((), (), s32[]{:S(2)}) async-start(), calls=%async_computation.14 | async-start | bytes 1310720 | tf_op jit(solution)/shard_map/all_gather | solution.py:635
  53.9 63.3 %all-gather.12.cloned.1.call-start = ((), (), s32[]{:S(2)}) async-start(), calls=%async_computation.15 | async-start | bytes 2949120 | tf_op jit(solution)/shard_map/all_gather | solution.py:613
  66.2 17.3 %all-to-all-start.1 = ((bf16[32,4,6]{0,2,1:T(8,128)(2,1)}), bf16[32,4,6]{0,2,1:T(8,128)(2,1)S(1)}, u32[]{:S(2)}, u32[]{:S(2)}) async-start(bf16[32,4,6]{0,2,1:T(8,128)(2,1)} %all_to_all.116), calls=%async_computation.1 | async-start | bytes 16384 | tf_op jit(solution)/shard_map/all_to_all | solution.py:612
  69.5 218.1 %all-gather.20.cloned.1.call-start = ((), (), s32[]{:S(2)}) async-start(), calls=%async_computation.21 | async-start | bytes 1179648 | tf_op jit(solution)/shard_map/all_gather | solution.py:724
  102.3 17.0 %copy-start.20 = (bf16[512,1024]{1,0:T(8,128)(2,1)S(1)}, bf16[512,1024]{1,0:T(8,128)(2,1)}, u32[]{:S(2)}) copy-start(bf16[512,1024]{1,0:T(8,128)(2,1)} %all-gather.10.cloned.1.call-done) | copy-start | bytes 3145732
  120.9 2.2 copy-start.27
  120.9 7.0 collective-permute-start
  129.3 62.9 %copy-start = (bf16[528,1280]{1,0:T(8,128)(2,1)}, bf16[528,1280]{1,0:T(8,128)(2,1)S(1)}, u32[]{:S(2)}) copy-start(bf16[528,1280]{1,0:T(8,128)(2,1)S(1)} %pad_maximum_fusion.proj_ref) | copy-start | bytes 4055044
  180.1 107.4 %copy-start.4 = (f32[512,256]{1,0:T(8,128)}, f32[512,256]{1,0:T(8,128)S(1)}, u32[]{:S(2)}) copy-start(f32[512,256]{1,0:T(8,128)S(1)} %get-tuple-element.52.carr_ref) | copy-start | bytes 1572868
  180.1 27.0 %copy-start.40 = (s32[128]{0:T(128)S(1)}, s32[128]{0:T(128)}, u32[]{:S(2)}) copy-start(s32[128]{0:T(128)} %param.19) | copy-start | bytes 1540
  180.1 45.5 %copy-start.41 = (bf16[128]{0:T(256)(128)(2,1)S(1)}, bf16[128]{0:T(256)(128)(2,1)}, u32[]{:S(2)}) copy-start(bf16[128]{0:T(256)(128)(2,1)} %param.28) | copy-start | bytes 772
  180.8 110.1 %all-gather.18.cloned.1.call-start = ((), (), s32[]{:S(2)}) async-start(), calls=%async_computation.18 | async-start | bytes 1622016 | tf_op jit(solution)/shard_map/all_gather | solution.py:618
  181.4 109.5 %all-gather.14.cloned.1.call-start = ((), (), s32[]{:S(2)}) async-start(), calls=%async_computation.16 | async-start | bytes 1769472 | tf_op jit(solution)/shard_map/all_gather | solution.py:613
  182.7 25.1 %copy-start.31 = (bf16[32,1024]{1,0:T(8,128)(2,1)S(1)}, bf16[32,1024]{1,0:T(8,128)(2,1)}, u32[]{:S(2)}) copy-start(bf16[32,1024]{1,0:T(8,128)(2,1)} %param.24) | copy-start | bytes 196612
  192.2 98.7 %all-gather.16.cloned.1.call-start = ((), (), s32[]{:S(2)}) async-start(), calls=%async_computation.17 | async-start | bytes 1769472 | tf_op jit(solution)/shard_map/all_gather | solution.py:613
  203.8 64.1 %all-to-all-start.2 = ((bf16[32,4,256]{2,0,1:T(8,128)(2,1)}), bf16[32,4,256]{2,0,1:T(8,128)(2,1)S(1)}, u32[]{:S(2)}, u32[]{:S(2)}) async-start(bf16[32,4,256]{2,0,1:T(8,128)(2,1)} %bitcast.146), calls=%async_computation.2 | async-start | bytes 131072 | tf_op jit(solution)/shard_map/all_to_all | solution.py:612
  207.1 275.9 %reduce-scatter.18.cloned.1.call-start = ((), (), s32[]{:S(2)}) async-start(), calls=%async_computation.22 | async-start | bytes 737280
  225.6 61.9 %copy-start.15 = (f32[512,256]{1,0:T(8,128)S(1)}, f32[512,256]{1,0:T(8,128)}, u32[]{:S(2)}) copy-start(f32[512,256]{1,0:T(8,128)} %copy-done.14) | copy-start | bytes 1572868
  225.6 63.9 %copy-start.19 = (f32[1,128]{1,0:T(1,128)}, f32[1,128]{1,0:T(1,128)S(1)}, u32[]{:S(2)}) copy-start(f32[1,128]{1,0:T(1,128)S(1)} %bitcast_convert_fusion.gain_ref) | copy-start | bytes 1540
  287.5 3.4 copy-start.1
  290.9 106.5 %copy-start.3 = (bf16[16,128,256]{2,1,0:T(8,128)(2,1)S(1)}, bf16[16,128,256]{2,1,0:T(8,128)(2,1)}, u32[]{:S(2)}) copy-start(bf16[16,128,256]{2,1,0:T(8,128)(2,1)} %all-gather.20.cloned.1.call-done) | copy-start | bytes 3145732
  290.9 106.5 %copy-start.8 = (f32[8,2,128,128]{3,2,1,0:T(8,128)S(1)}, f32[8,2,128,128]{3,2,1,0:T(8,128)}, u32[]{:S(2)}) copy-start(f32[8,2,128,128]{3,2,1,0:T(8,128)} %copy-done.7) | copy-start | bytes 3145732
  290.9 106.5 %copy-start.13 = (f32[8,2,64,128]{3,2,1,0:T(8,128)S(1)}, f32[8,2,64,128]{3,2,1,0:T(8,128)}, u32[]{:S(2)}) copy-start(f32[8,2,64,128]{3,2,1,0:T(8,128)} %copy-done.12) | copy-start | bytes 1572868
  424.2 2.9 copy-start.42
  425.6 110.2 %reduce-scatter.14.cloned.1.call-start = ((), (), s32[]{:S(2)}) async-start(), calls=%async_computation.19 | async-start | bytes 589824 | tf_op jit(solution)/shard_map/reduce_scatter | solution.py:631
  426.4 110.9 %reduce-scatter.16.cloned.1.call-start = ((), (), s32[]{:S(2)}) async-start(), calls=%async_computation.20 | async-start | bytes 1622016 | tf_op jit(solution)/shard_map/reduce_scatter | solution.py:631
  427.1 4.5 copy-start.21
  428.5 37.0 %copy-start.30 = (bf16[512,256]{1,0:T(8,128)(2,1)S(1)}, bf16[512,256]{1,0:T(8,128)(2,1)}, u32[]{:S(2)}) copy-start(bf16[512,256]{1,0:T(8,128)(2,1)} %get-tuple-element.76) | copy-start | bytes 786436
  428.5 38.3 %collective-permute-start.1 = (f32[8,1280]{1,0:T(8,128)S(1)}, f32[8,1280]{1,0:T(8,128)S(1)}, u32[]{:S(2)}, u32[]{:S(2)}) collective-permute-start(f32[8,1280]{1,0:T(8,128)S(1)} %get-tuple-element.75), channel_id=1, source_target_pairs={{1,0},{2,1},{3,2},{4,3},{5,4},{6,5},{7,6},{9,8},{10,9},{11,10},{12... | collective-permute-start | bytes 122888 | tf_op jit(solution)/shard_map/ppermute | solution.py:596
  462.1 14.6 %all-to-all-start.7 = ((bf16[4,32,6]{1,2,0:T(8,128)(2,1)}), bf16[4,32,6]{1,2,0:T(8,128)(2,1)S(1)}, u32[]{:S(2)}, u32[]{:S(2)}) async-start(bf16[4,32,6]{1,2,0:T(8,128)(2,1)} %copy.228), calls=%async_computation.7 | async-start | bytes 16384 | tf_op jit(solution)/shard_map/all_to_all | solution.py:627
  465.5 194.6 %all-reduce.15.cloned.1.call-start = ((), (), s32[]{:S(2)}) async-start(), calls=%async_computation.23 | async-start | bytes 12582912
  471.8 1.9 copy-start.26
  471.9 2.3 copy-start.37
  476.6 14.4 %copy-start.22 = (bf16[128,1024]{1,0:T(8,128)(2,1)S(1)}, bf16[128,1024]{1,0:T(8,128)(2,1)}, u32[]{:S(2)}) copy-start(bf16[128,1024]{1,0:T(8,128)(2,1)} %x_ref.1) | copy-start | bytes 786436
  476.7 14.6 %copy-start.34 = (f32[1,1024]{1,0:T(1,128)S(1)}, f32[1,1024]{1,0:T(1,128)}, u32[]{:S(2)}) copy-start(f32[1,1024]{1,0:T(1,128)} %get-tuple-element.77) | copy-start | bytes 12292
  476.7 14.6 %copy-start.36 = (f32[1,128]{1,0:T(1,128)S(1)}, f32[1,128]{1,0:T(1,128)}, u32[]{:S(2)}) copy-start(f32[1,128]{1,0:T(1,128)} %get-tuple-element.56) | copy-start | bytes 1540
  476.7 58.1 %copy-start.28 = (f32[128,1024]{1,0:T(8,128)S(1)}, f32[128,1024]{1,0:T(8,128)}, u32[]{:S(2)}) copy-start(f32[128,1024]{1,0:T(8,128)} %get-tuple-element.78) | copy-start | bytes 1572868
  476.7 14.2 %all-to-all-start.5 = ((bf16[4,128,1024]{2,1,0:T(8,128)(2,1)}), bf16[4,128,1024]{2,1,0:T(8,128)(2,1)S(1)}, u32[]{:S(2)}, u32[]{:S(2)}) async-start(bf16[4,128,1024]{2,1,0:T(8,128)(2,1)} %bitcast.31), calls=%async_computation.5 | async-start | bytes 2097152 | tf_op jit(solution)/shard_map/all_to_all | solution.py:640
  662.2 8.5 %all-to-all-start.8 = ((bf16[4,32,256]{2,1,0:T(8,128)(2,1)}), bf16[4,32,256]{2,1,0:T(8,128)(2,1)S(1)}, u32[]{:S(2)}, u32[]{:S(2)}) async-start(bf16[4,32,256]{2,1,0:T(8,128)(2,1)} %dynamic-slice_bitcast_fusion.3), calls=%async_computation.8 | async-start | bytes 131072 | tf_op jit(solution)/shard_map/all_to_all | solution.py:627
  670.7 8.5 %all-to-all-start.9 = ((bf16[4,32,704]{2,1,0:T(8,128)(2,1)}), bf16[4,32,704]{2,1,0:T(8,128)(2,1)S(1)}, u32[]{:S(2)}, u32[]{:S(2)}) async-start(bf16[4,32,704]{2,1,0:T(8,128)(2,1)} %dynamic-slice_bitcast_fusion.2), calls=%async_computation.10 | async-start | bytes 393216 | tf_op jit(solution)/shard_map/all_to_all | solution.py:627
  679.2 8.8 %all-to-all-start.10 = ((bf16[4,32,704]{2,1,0:T(8,128)(2,1)}), bf16[4,32,704]{2,1,0:T(8,128)(2,1)S(1)}, u32[]{:S(2)}, u32[]{:S(2)}) async-start(bf16[4,32,704]{2,1,0:T(8,128)(2,1)} %dynamic-slice_bitcast_fusion.1), calls=%async_computation.11 | async-start | bytes 393216 | tf_op jit(solution)/shard_map/all_to_all | solution.py:627
  688.1 9.0 %all-to-all-start.6 = ((bf16[4,32,1280]{2,1,0:T(8,128)(2,1)}), bf16[4,32,1280]{2,1,0:T(8,128)(2,1)S(1)}, u32[]{:S(2)}, u32[]{:S(2)}) async-start(bf16[4,32,1280]{2,1,0:T(8,128)(2,1)} %dynamic-slice_bitcast_fusion), calls=%async_computation.6 | async-start | bytes 655360 | tf_op jit(solution)/shard_map/all_to_all | solution.py:627
  692.8 5.2 copy-start.29
  (15 other events, 15.4 us)
Sparse Core Ops, SparseCore 0:
  54.0 26.4 all-gather.9
  82.7 34.4 all-gather.11
  180.9 21.2 all-gather.19
  203.8 25.8 all-gather.17
  231.1 25.7 all-gather.13
  258.4 28.4 all-gather.15
  425.7 30.6 reduce-scatter.17
  458.6 28.9 reduce-scatter.13
  490.0 32.1 reduce-scatter.15
  524.8 135.1 all-reduce.14

commit v3 on v2

--- a/solution.py
+++ b/solution.py
@@ -96,12 +96,234 @@
     return moved[HALO:]
 
 
+UP, DOWN, ACROSS = 0, 1, 2
+
+
+class Line:
+    def __init__(self, pieces, parts, send_sem, recv_sem, up=True, down=True):
+        self.chips = pieces // 2
+        self.here = lax.axis_index("ctx")
+        self.chip = self.here // 2
+        self.core = lax.rem(self.here, 2)
+        self.other = self.here + 1 - 2 * self.core
+        self.parts, self.send_sem, self.recv_sem, self.up, self.down = parts, send_sem, recv_sem, up, down
+
+    def copies(self, chunk, way):
+        target = (self.here + 2, self.here - 2, self.other)[way]
+        return [
+            pltpu.make_async_remote_copy(
+                part(chunk), part(chunk), self.send_sem.at[n, way, chunk], self.recv_sem.at[n, chunk],
+                device_id={"ctx": target}, device_id_type=MESH,
+            )
+            for n, part in enumerate(self.parts)
+        ]
+
+    def start(self, chunk, way):
+        for copy in self.copies(chunk, way):
+            copy.start()
+
+    def arrived(self, chunk):
+        for copy in self.copies(chunk, ACROSS):
+            copy.wait_recv()
+
+    def left(self, chunk, way):
+        for copy in self.copies(chunk, way):
+            copy.wait_send()
+
+    def routes(self, distance, act):
+        if distance == 0:
+            if self.up:
+                pl.when(self.chip < self.chips - 1)(lambda: act(self.here, UP))
+            if self.down:
+                pl.when(self.chip > 0)(lambda: act(self.here, DOWN))
+            act(self.here, ACROSS)
+            return
+        below, above = self.here - 2 * distance, self.here + 2 * distance
+        if self.up:
+
+            @pl.when(self.chip >= distance)
+            def _():
+                pl.when(self.chip < self.chips - 1)(lambda: act(below, UP))
+                act(below, ACROSS)
+
+        if self.down:
+
+            @pl.when(self.chip + distance < self.chips)
+            def _():
+                pl.when(self.chip > 0)(lambda: act(above, DOWN))
+                act(above, ACROSS)
+
+    def own(self):
+        self.routes(0, self.start)
+
+    def hop(self, distance):
+        if self.up:
+            pl.when(self.chip >= distance)(lambda: self.arrived(self.here - 2 * distance))
+        if self.down:
+            pl.when(self.chip + distance < self.chips)(lambda: self.arrived(self.here + 2 * distance))
+        self.routes(distance, self.start)
+
+    def finish(self):
+        for chip in range(self.chips):
+            needed = True
+            if not self.down:
+                needed = self.chip >= chip
+            if not self.up:
+                needed = self.chip <= chip
+            pl.when(needed)(lambda chip=chip: self.arrived(2 * chip + 1 - self.core))
+        for distance in range(self.chips):
+            self.routes(distance, self.left)
+
+
+def greet(devices, barrier):
+    total = 0
+    for place, there in devices:
+        pl.when(there)(
+            lambda place=place: pl.semaphore_signal(barrier, inc=1, device_id=place, device_id_type=MESH)
+        )
+        total = total + jnp.asarray(there, jnp.int32)
+    return total
+
+
+def line_neighbours(pieces):
+    here = lax.axis_index("ctx")
+    chip, core = here // 2, lax.rem(here, 2)
+    return [
+        ({"ctx": here + 2}, chip < pieces // 2 - 1),
+        ({"ctx": here - 2}, chip > 0),
+        ({"ctx": here + 1 - 2 * core}, here >= 0),
+    ]
+
+
+def start_kernel(
+    size, pieces, x_ref, first_ref, later_ref, xfull_ref, halo_ref, full_ref, stage_ref,
+    local_sem, seq_send, seq_recv, line_send, line_recv, halo_sem,
+):
+    me, here = lax.axis_index("seq"), lax.axis_index("ctx")
+    count = x_ref.shape[0]
+    core = lax.rem(here, 2)
+    barrier = pltpu.get_barrier_semaphore()
+    peers = [({"seq": lax.rem(me + i, size)}, here >= 0) for i in range(1, size)]
+    side = [({"ctx": here + 1}, (core == 1) & (here < pieces - 1)), ({"ctx": here - 1}, (core == 0) & (here > 0))]
+    total = greet(peers + line_neighbours(pieces) + side, barrier)
+    pl.semaphore_wait(barrier, total)
+
+    def rows(q):
+        return pl.ds(pl.multiple_of(q * count, count), count)
+
+    def exchange(n, i):
+        q = lax.rem(me + i, size)
+        source, target = [
+            (first_ref.at[q], full_ref.at[me, here]), (x_ref, xfull_ref.at[rows(me)]), (later_ref.at[q], stage_ref.at[me])
+        ][n]
+        return pltpu.make_async_remote_copy(
+            source, target, seq_send.at[n, i - 1], seq_recv.at[n, i - 1], device_id={"seq": q}, device_id_type=MESH
+        )
+
+    def own(n):
+        source, target = [
+            (first_ref.at[me], full_ref.at[me, here]), (x_ref, xfull_ref.at[rows(me)]), (later_ref.at[me], stage_ref.at[me])
+        ][n]
+        return pltpu.make_async_copy(source, target, local_sem.at[n])
+
+    for n in range(3):
+        own(n).start()
+        for i in range(1, size):
+            exchange(n, i).start()
+    line = Line(pieces, [lambda c: full_ref.at[:, c]], line_send, line_recv)
+    own(0).wait()
+    for i in range(1, size):
+        exchange(0, i).wait_recv()
+    line.own()
+    own(1).wait()
+    for i in range(1, size):
+        exchange(1, i).wait_recv()
+    last = xfull_ref.at[pl.ds(size * count - HALO, HALO)]
+    passing = pltpu.make_async_remote_copy(
+        last, halo_ref, halo_sem.at[0], halo_sem.at[1], device_id={"ctx": here + 1}, device_id_type=MESH
+    )
+    pl.when(here < pieces - 1)(passing.start)
+
+    @pl.when(here == 0)
+    def _():
+        filling = pltpu.make_async_copy(last, halo_ref, local_sem.at[3])
+        filling.start()
+        filling.wait()
+
+    for distance in range(1, pieces // 2):
+        line.hop(distance)
+    line.finish()
+    own(2).wait()
+    for i in range(1, size):
+        exchange(2, i).wait_recv()
+    pl.when(here > 0)(passing.wait_recv)
+    pl.when(here < pieces - 1)(passing.wait_send)
+    for n in range(3):
+        for i in range(1, size):
+            exchange(n, i).wait_send()
+
+
+def start_gather(size, pieces, x, first, later):
+    anywhere = pl.BlockSpec(memory_space=pl.ANY)
+    out = lambda *dims: jax.ShapeDtypeStruct(dims, BF16)
+    return pl.pallas_call(
+        functools.partial(start_kernel, size, pieces),
+        in_specs=[anywhere] * 3,
+        out_specs=[anywhere] * 4,
+        out_shape=[
+            out(x.shape[0] * size, D), out(HALO, D), out(size, pieces, *first.shape[1:]), out(*later.shape),
+        ],
+        scratch_shapes=[
+            pltpu.SemaphoreType.DMA((4,)), pltpu.SemaphoreType.DMA((3, size - 1)), pltpu.SemaphoreType.DMA((3, size - 1)),
+            pltpu.SemaphoreType.DMA((1, 3, pieces)), pltpu.SemaphoreType.DMA((1, pieces)), pltpu.SemaphoreType.DMA((2,)),
+        ],
+        compiler_params=pltpu.CompilerParams(
+            vmem_limit_bytes=16 << 20, collective_id=2, has_side_effects=True
+        ),
+        name="start_gather",
+    )(x, first, later)
+
+
 def fwd_kernel(
-    heads, proj_ref, w_ref, rowp_ref, colp_ref, tokp_ref,
-    oloc_ref, carr_ref, fin_ref, conv_ref, q_ref, k_ref, v_ref, t_ref, kk_ref, at_ref, uw_ref, pl_ref,
-    state, weave,
+    heads, pieces, proj_ref, w_ref, rowp_ref, colp_ref, tokp_ref, stage_ref, wd_ref, wo_ref,
+    oloc_ref, carr_ref, sin_ref, mapsout_ref, conv_ref, q_ref, k_ref, v_ref, t_ref, kk_ref, at_ref, uw_ref, pl_ref,
+    wgfull_ref, wufull_ref, wdfull_ref, wofull_ref,
+    state, weave, maps, local_sem, line_send, line_recv, map_send, map_recv,
 ):
     step = pl.program_id(0)
+    steps = pl.num_programs(0)
+    here = lax.axis_index("ctx")
+    weights = Line(
+        pieces,
+        [
+            lambda c: wgfull_ref.at[:, c], lambda c: wufull_ref.at[:, c], lambda c: wdfull_ref.at[c],
+            lambda c: wofull_ref.at[c],
+        ],
+        line_send, line_recv,
+    )
+
+    @pl.when(step == 0)
+    def _():
+        barrier = pltpu.get_barrier_semaphore()
+        pl.semaphore_wait(barrier, greet(line_neighbours(pieces), barrier))
+        owned = [
+            pltpu.make_async_copy(source, target, local_sem.at[n])
+            for n, (source, target) in enumerate(
+                [
+                    (stage_ref.at[:, 0], wgfull_ref.at[:, here]), (stage_ref.at[:, 1], wufull_ref.at[:, here]),
+                    (wd_ref, wdfull_ref.at[here]), (wo_ref, wofull_ref.at[here]),
+                ]
+            )
+        ]
+        for copy in owned:
+            copy.start()
+        for copy in owned:
+            copy.wait()
+        weights.own()
+
+    for distance in range(1, pieces // 2):
+        pl.when(step == (distance * steps) // (pieces // 2))(lambda distance=distance: weights.hop(distance))
+
     eye = (iota((HEAD, HEAD), 0) == iota((HEAD, HEAD), 1)).astype(F32)
 
     @pl.when(step == 0)
@@ -152,53 +374,85 @@
         at_ref[0, h] = attn
         uw_ref[0, h] = uw
         pl_ref[0, h] = before
-    fin_ref[...] = state[...]
-
-
-def recurrence_forward(proj_ext, conv_w, rowp, colp, tokp, heads):
+
+    @pl.when(step == steps - 1)
+    def _():
+        maps[here] = state[...].astype(BF16)
+        line = Line(pieces, [lambda c: maps.at[c]], map_send, map_recv)
+        line.own()
+        for distance in range(1, pieces // 2):
+            line.hop(distance)
+        line.finish()
+        weights.finish()
+
+        def hop(k, states):
+            return tuple(
+                mm(maps[k, h, :, :HEAD], states[h]) + maps[k, h, :, HEAD:].astype(F32) for h in range(heads)
+            )
+
+        states = lax.fori_loop(0, here, hop, tuple(jnp.zeros((HEAD, HEAD), F32) for _ in range(heads)))
+        for h in range(heads):
+            sin_ref[h] = states[h]
+
+        def keep(k, carry):
+            mapsout_ref[k] = maps[k, :, :, :HEAD]
+            return carry
+
+        lax.fori_loop(0, pieces, keep, 0)
+
+
+def recurrence_forward(proj_ext, conv_w, rowp, colp, tokp, stage, w_down, w_out, heads, pieces):
     blocks = rowp.shape[0]
     rows = blocks * BLOCK_LEN
     whole = lambda *dims: pl.BlockSpec(dims, lambda i: (0,) * len(dims))
     by_block = lambda *dims: pl.BlockSpec((1,) + dims, lambda i: (i,) + (0,) * len(dims))
     token = lambda cols: pl.BlockSpec((BLOCK_LEN, cols), lambda i: (i, 0))
     shape = lambda *dims: jax.ShapeDtypeStruct(dims, F32)
+    low_shape = lambda *dims: jax.ShapeDtypeStruct(dims, BF16)
+    anywhere = pl.BlockSpec(memory_space=pl.ANY)
     square = (heads, ROWS, HEAD)
+    size = stage.shape[0]
     return pl.pallas_call(
-        functools.partial(fwd_kernel, heads),
+        functools.partial(fwd_kernel, heads, pieces),
         grid=(blocks,),
         in_specs=[
             whole(*proj_ext.shape), whole(*conv_w.shape),
             by_block(*rowp.shape[1:]), by_block(*colp.shape[1:]), by_block(*tokp.shape[1:]),
+            anywhere, anywhere, anywhere,
         ],
         out_specs=[
-            token(heads * HEAD), token(heads * HEAD), whole(heads, HEAD, 2 * HEAD), token(heads * WIDE),
+            token(heads * HEAD), token(heads * HEAD), whole(heads, HEAD, HEAD), whole(pieces, heads, HEAD, HEAD),
+            token(heads * WIDE),
             by_block(heads, BLOCK_LEN, HEAD), by_block(*square), by_block(*square), by_block(*square),
             by_block(*square), by_block(heads, BLOCK_LEN, ROWS), by_block(heads, ROWS, 2 * HEAD),
-            by_block(heads, HEAD, 2 * HEAD),
+            by_block(heads, HEAD, 2 * HEAD), anywhere, anywhere, anywhere, anywhere,
         ],
         out_shape=[
-            shape(rows, heads * HEAD), shape(rows, heads * HEAD), shape(heads, HEAD, 2 * HEAD), shape(rows, heads * WIDE),
+            shape(rows, heads * HEAD), shape(rows, heads * HEAD), shape(heads, HEAD, HEAD),
+            low_shape(pieces, heads, HEAD, HEAD), shape(rows, heads * WIDE),
             shape(blocks, heads, BLOCK_LEN, HEAD), shape(blocks, *square), shape(blocks, *square), shape(blocks, *square),
             shape(blocks, *square), shape(blocks, heads, BLOCK_LEN, ROWS), shape(blocks, heads, ROWS, 2 * HEAD),
             shape(blocks, heads, HEAD, 2 * HEAD),
-        ],
-        scratch_shapes=[pltpu.VMEM((heads, HEAD, 2 * HEAD), F32), pltpu.VMEM((2 * heads, ROWS, HEAD), F32)],
-        compiler_params=pltpu.CompilerParams(vmem_limit_bytes=40 << 20),
+            low_shape(size, pieces, *stage.shape[2:]), low_shape(size, pieces, *stage.shape[2:]),
+            low_shape(pieces, *w_down.shape), low_shape(pieces, *w_out.shape),
+        ],
+        scratch_shapes=[
+            pltpu.VMEM((heads, HEAD, 2 * HEAD), F32), pltpu.VMEM((2 * heads, ROWS, HEAD), F32),
+            pltpu.VMEM((pieces, heads, HEAD, 2 * HEAD), BF16),
+            pltpu.SemaphoreType.DMA((4,)), pltpu.SemaphoreType.DMA((4, 3, pieces)), pltpu.SemaphoreType.DMA((4, pieces)),
+            pltpu.SemaphoreType.DMA((1, 3, pieces)), pltpu.SemaphoreType.DMA((1, pieces)),
+        ],
+        compiler_params=pltpu.CompilerParams(
+            vmem_limit_bytes=40 << 20, collective_id=3, has_side_effects=True
+        ),
         name="recurrence_forward",
-    )(proj_ext, conv_w, rowp, colp, tokp)
-
-
-def state_kernel(heads, index_ref, maps_ref, oloc_ref, carr_ref, gate_ref, gain_ref, heads_ref, mixed_ref, state_ref):
-    def hop(k, states):
-        return tuple(
-            mm(maps_ref[k, h, :, :HEAD], states[h]) + maps_ref[k, h, :, HEAD:].astype(F32) for h in range(heads)
-        )
-
-    states = lax.fori_loop(0, index_ref[0], hop, tuple(jnp.zeros((HEAD, HEAD), F32) for _ in range(heads)))
+    )(proj_ext, conv_w, rowp, colp, tokp, stage, w_down, w_out)
+
+
+def state_kernel(heads, state_ref, oloc_ref, carr_ref, gate_ref, gain_ref, heads_ref, mixed_ref):
     for h in range(heads):
         hc = slice(h * HEAD, (h + 1) * HEAD)
-        state_ref[h] = states[h]
-        out = (oloc_ref[:, hc] + mm(carr_ref[:, hc], states[h])).astype(BF16)
+        out = (oloc_ref[:, hc] + mm(carr_ref[:, hc], state_ref[h])).astype(BF16)
         heads_ref[:, hc] = out
         wide = out.astype(F32)
         gate = gate_ref[:, hc]
@@ -206,21 +460,20 @@
         mixed_ref[:, hc] = (scaled * (gate * jax.nn.sigmoid(gate))).astype(BF16)
 
 
-def state_and_gate(index, maps, oloc, carr, gate_out, gain, heads):
+def state_and_gate(state, oloc, carr, gate_out, gain, heads):
     rows = oloc.shape[0]
     vmem = pl.BlockSpec(memory_space=pltpu.VMEM)
     return pl.pallas_call(
         functools.partial(state_kernel, heads),
-        in_specs=[pl.BlockSpec(memory_space=pltpu.SMEM)] + [vmem] * 5,
-        out_specs=[vmem] * 3,
+        in_specs=[vmem] * 5,
+        out_specs=[vmem] * 2,
         out_shape=[
             jax.ShapeDtypeStruct((rows, heads * HEAD), BF16),
             jax.ShapeDtypeStruct((rows, heads * HEAD), BF16),
-            jax.ShapeDtypeStruct((heads, HEAD, HEAD), F32),
         ],
         compiler_params=pltpu.CompilerParams(vmem_limit_bytes=40 << 20),
         name="state_and_gate",
-    )(index, maps, oloc, carr, gate_out, gain)
+    )(state, oloc, carr, gate_out, gain)
 
 
 def seq_barrier(size):
@@ -447,7 +700,7 @@
         def hop(i, states):
             k = pieces - 1 - i
             return tuple(
-                mm(maps_ref[k, h, :, :HEAD], states[h], 0, 0) + cots_ref[k, h].astype(F32) for h in range(heads)
+                mm(maps_ref[k, h], states[h], 0, 0) + cots_ref[k, h].astype(F32) for h in range(heads)
             )
 
         found = lax.fori_loop(
@@ -606,18 +859,6 @@
     return beta, logs
 
 
-def columns_to_rank(w):
-    ranks = lax.axis_size("seq")
-    rows, cols = w.shape[0], w.shape[1] // ranks
-    swapped = lax.all_to_all(w, "seq", split_axis=1, concat_axis=0, tiled=True)
-    full = lax.all_gather(swapped.reshape(ranks, rows, cols), "ctx", axis=1, tiled=True)
-    return full.reshape(-1, cols)
-
-
-def rows_of_rank(w):
-    return lax.all_gather(w, "ctx", axis=0, tiled=True)
-
-
 def sum_columns_back(grad):
     ranks, pieces = lax.axis_size("seq"), lax.axis_size("ctx")
     cols = grad.shape[1]
@@ -629,10 +870,6 @@
 
 def sum_rows_back(grad):
     return lax.psum_scatter(grad.astype(BF16), "ctx", scatter_dimension=0, tiled=True).astype(F32)
-
-
-def gather_tokens(x):
-    return lax.all_gather(x, "seq", axis=0, tiled=True)
 
 
 def sum_tokens(partial):
@@ -668,24 +905,50 @@
     rank = lax.axis_index("seq")
     head_start = rank * heads
 
-    mix_s = columns_to_rank(mix_proj)
-    scal_s = columns_to_rank(scalar_proj)
-    gate_s = columns_to_rank(gate_proj)
-    wg_s = columns_to_rank(w_gate)
-    wu_s = columns_to_rank(w_up)
-    out_s = rows_of_rank(out_proj)
-    down_s = rows_of_rank(w_down)
-    conv_s = rows_of_rank(conv_weight)
-    norm_a = lax.all_gather(norm_attn, BOTH, axis=0, tiled=True).astype(F32)
-    norm_m = lax.all_gather(norm_mlp, BOTH, axis=0, tiled=True).astype(F32)
-    valid_count = jnp.maximum(lax.psum(jnp.sum(valid_mask.astype(F32)), BOTH), 1.0)
-
+    pieces = lax.axis_size("ctx")
+    inner = FF // seq_size
+    held = mix_proj.shape[0]
+    scal_cols = heads * (NH + 1)
+    count_here = jnp.sum(valid_mask.astype(F32)).astype(BF16)
+    extra = jnp.concatenate(
+        [
+            norm_attn[:, None], norm_mlp[:, None],
+            jnp.where(jnp.arange(held) == 0, count_here, jnp.zeros((), BF16))[:, None],
+            conv_weight.reshape(held, -1),
+        ],
+        axis=1,
+    )
+    by_rank = lambda w: jnp.swapaxes(w.reshape(held, seq_size, -1), 0, 1)
+    first = jnp.concatenate(
+        [
+            by_rank(mix_proj), by_rank(gate_proj), by_rank(scalar_proj),
+            jnp.broadcast_to(extra[None], (seq_size, *extra.shape)),
+            jnp.zeros((seq_size, held, HEAD - scal_cols - extra.shape[1]), BF16),
+        ],
+        axis=2,
+    )
+    later = jnp.stack([by_rank(w_gate), by_rank(w_up)], axis=1)
+    x_full, halo, gathered, stage = start_gather(seq_size, pieces, block_input, first, later)
+    weights = gathered.reshape(D, -1)
+    gate_at = heads * WIDE
+    scal_at = gate_at + heads * HEAD
+    norm_at = scal_at + scal_cols
+    norm_a = weights[:, norm_at].astype(F32)
+    norm_m = weights[:, norm_at + 1].astype(F32)
+    valid_count = jnp.maximum(jnp.sum(weights[:, norm_at + 2].astype(F32)), 1.0)
+    conv_s = lax.dynamic_slice_in_dim(weights[:, norm_at + 3 : norm_at + extra.shape[1]], rank * (D // seq_size), D // seq_size)
+    conv_s = conv_s.reshape(heads * WIDE, CONV)
+
+    extended = jnp.concatenate([halo, x_full], axis=0).astype(F32)
+    normed_ext = rms_scale(extended, norm_a).astype(BF16)
+    normed = normed_ext[HALO:]
+    proj_ext = dot(normed_ext, weights[:, :gate_at]).astype(BF16)
+    rest = dot(normed, weights[:, gate_at:])
+    gate_out = rest[:, : heads * HEAD]
+    scal = rest[:, heads * HEAD : heads * HEAD + scal_cols].astype(BF16)
     inputs_f = block_input.astype(F32)
-    normed_f, norm_in_back = jax.vjp(rms_scale, inputs_f, norm_a)
-    normed = gather_tokens(normed_f.astype(BF16))
-    proj = dot(normed, mix_s).astype(BF16)
-    scal = dot(normed, scal_s).astype(BF16)
-    gate_out = dot(normed, gate_s)
+    _, norm_in_back = jax.vjp(rms_scale, inputs_f, norm_a)
+    mix_s, gate_s, scal_s = weights[:, :gate_at], weights[:, gate_at:scal_at], weights[:, scal_at:norm_at]
 
     piece_start = index * rows
     window = lax.dynamic_slice_in_dim(jnp.pad(segments, (CONV, 0)), piece_start, rows + CONV)
@@ -717,14 +980,15 @@
     )
     rowp = jnp.swapaxes(colp, 1, 2)
     conv_w = jnp.pad(jnp.flip(conv_s.astype(F32).T, 0), ((0, 8 - CONV), (0, 0)))
-    tail = passed_along(proj[rows - HALO :], "ctx", 1)
-    proj_ext = jnp.concatenate([tail, proj], axis=0)
-
-    oloc, carr, final, *saved = recurrence_forward(proj_ext, conv_w, rowp, colp, tokp, heads)
-    maps = lax.all_gather(final.astype(BF16), "ctx")
+
+    (
+        oloc, carr, state_in, maps, *saved, wg_full, wu_full, wd_full, wo_full,
+    ) = recurrence_forward(proj_ext, conv_w, rowp, colp, tokp, stage, w_down, out_proj, heads, pieces)
+    wg_s, wu_s = wg_full.reshape(D, inner), wu_full.reshape(D, inner)
+    down_s, out_s = wd_full.reshape(inner, D), wo_full.reshape(heads * HEAD, D)
     gain = head_gain.astype(F32)[None, :]
     index_arr = index.reshape(1).astype(jnp.int32)
-    heads_out, mixed, state_in = state_and_gate(index_arr, maps, oloc, carr, gate_out, gain, heads)
+    heads_out, mixed = state_and_gate(state_in, oloc, carr, gate_out, gain, heads)
 
     scale = (token_total / valid_count).reshape(1, 1)
     mask_values = valid_mask.astype(F32)[:, None]

time: 709 us -> 594 us (0.84)
  blocking collectives: 256 us -> 85.1 us
  Pallas kernels: 159 us -> 235 us
  waiting for transfers between devices: 155 us -> 120 us
  local copies, waits for them, and re-layouts: 58 us -> 69.8 us
    pallas_call x2 -> x3, Pallas kernels: 43 us -> 119 us  [the longest x1 73.3 us: recurrence_forward(): pl.pallas_call(functools.partial(fwd_kernel, heads, pieces), grid=(blocks...]
    all_gather x4 -> x0, blocking collectives: 62.5 us -> none  [the longest x2 32 us: columns_to_rank(): lax.all_gather(swapped.reshape(ranks, rows, cols), 'ctx', axis=1, tiled=T...]
    unnamed x2 -> x1, blocking collectives: 70.8 us -> 29.8 us
    psum x1 -> x0, blocking collectives: 40.3 us -> none  [local(): lax.psum(jnp.sum(valid_mask.astype(F32)), BOTH)]
    all_to_all x3 -> x0, blocking collectives: 27.9 us -> none  [columns_to_rank(): swapped = lax.all_to_all(w, 'seq', split_axis=1, concat_axis=0, tiled=True)]
    unnamed x12 -> x6, waiting for transfers between devices: 123 us -> 102 us
    all_gather x6 -> x0, waiting for transfers between devices: 15 us -> none  [the longest x3 15 us: columns_to_rank(): lax.all_gather(swapped.reshape(ranks, rows, cols), 'ctx', axis=1, tiled=T...]
    unnamed x98 -> x103, local copies, waits for them, and re-layouts: 22.5 us -> 22.1 us
  transfers between devices with their start and end apart: 20 -> 11, of which waited for: 7 -> 6; matrix products, arithmetic and copies ran while one was open for 7% -> 9% of each run, Pallas kernels for 0% -> 0%
where the time goes in v3:
time: 594 us; the launch traced here: 592 us
  Pallas kernels  235 us (40%)
  waiting for transfers between devices  120 us (20%)
  blocking collectives  85.1 us (14%)
  local copies, waits for them, and re-layouts  69.8 us (12%)
  starting transfers between devices  26 us (4%)
  matrix products  20.5 us (3%)
  other arithmetic  19.6 us (3%)
  between operations  17 us (3%)
    unnamed x6, waiting for transfers between devices  102 us
    pallas_call x1, Pallas kernels, middle_part(): pl.pallas_call(functools.partial(middle_kernel, size, heads), in_specs=[p...  90.2 us
    pallas_call x1, Pallas kernels, recurrence_forward(): pl.pallas_call(functools.partial(fwd_kernel, heads, pieces), grid=(blocks...  73.3 us
    pallas_call x1, Pallas kernels, start_gather(): pl.pallas_call(functools.partial(start_kernel, size, pieces), in_specs=[a...  44.8 us
    psum x1, blocking collectives, local(): small = lax.psum(small, BOTH)  40.4 us
    unnamed x1, blocking collectives  29.8 us
    pallas_call x1, Pallas kernels, recurrence_backward(): pl.pallas_call(functools.partial(bwd_kernel, heads), grid=(blocks,), in_s...  25.8 us
    unnamed x103, local copies, waits for them, and re-layouts  22.1 us
  transfers between devices with their start and end apart: 11, of which 6 were waited for; matrix products, arithmetic and copies ran while one was open for 9% of the time, Pallas kernels for 0%

profile of v3, /device:TPU:0, one launch (start us, length us, event | category | flops | bytes accessed | tf_op | source)
XLA Modules:
  0.0 592.1 jit_solution(10918311829837657156)
XLA Ops:
  13.1 1.3 convert_reduce_fusion.4
  18.6 44.8 %start_gather.1 = (bf16[512,1024]{1,0:T(8,128)(2,1)S(1)}, bf16[16,1024]{1,0:T(8,128)(2,1)S(1)}, bf16[4,8,32,1664]{3,2,1,0:T(8,128)(2,1)S(1)}, bf16[4,2,32,704]{3,2,1,0:T(8,128)(2,1)S(1)}) custom-call(bf16[128,1024]{1,0:T(8,128)(2,1)S(1)} %copy-done, bf16[4,32,1664]{2,1,0:T(8,128)(2,1)S(1)} %concatenate.25.first_ref, ...), custom_call_target="tpu_custom_call" | custom-call | tf_op jit(solution)/shard_map/start_gather/pallas_call | solution.py:269
  64.1 1.4 convert_reduce_fusion.1
  68.6 3.6 convolution_convert_fusion.1.proj_ref
  72.3 2.0 slice.130
  81.2 2.0 concatenate.28.colp_ref
  85.8 1.3 copy.149
  88.3 1.4 copy.160.mask_ref
  91.4 73.3 %recurrence_forward.1 = (f32[512,256]{1,0:T(8,128)S(1)}, f32[512,256]{1,0:T(8,128)S(1)}, f32[2,128,128]{2,1,0:T(8,128)S(1)}, bf16[8,2,128,128]{3,2,1,0:T(8,128)(...) custom-call(bf16[528,1280]{1,0:T(8,128)(2,1)S(1)} %convolution_conve, ...), custom_call_target="tpu_custom_call" | custom-call | tf_op jit(solution)/shard_map/recurrence_forward/pallas_call | solution.py:415
  173.4 90.2 %middle_part.1 = (bf16[128,1024]{1,0:T(8,128)(2,1)}, f32[128,1024]{1,0:T(8,128)}, bf16[512,256]{1,0:T(8,128)(2,1)}, bf16[512,256]{1,0:T(8,128)(2,1)}, f32[2,128,...) custom-call(f32[1,1]{1,0:T(1,128)} %bitcast.10.scale_ref, ...), custom_call_target="tpu_custom_call" | custom-call | tf_op jit(solution)/shard_map/middle_part/pallas_call | solution.py:662
  264.6 14.8 %all-gather = bf16[16,128,128]{2,1,0:T(8,128)(2,1)S(1)} all-gather(bf16[2,128,128]{2,1,0:T(8,128)(2,1)S(1)} %convert_element_type.189), channel_id=2, replica_groups=mesh['seq'=4,'ctx'=8] {'ctx'}, dimensions={0}, use_global_device_ids=true | all-gather | bytes 589824 | tf_op jit(solution)/shard_map/all_gather | solution.py:1007
  280.4 25.8 %recurrence_backward.1 = (bf16[512,1280]{1,0:T(8,128)(2,1)}, f32[8,1280]{1,0:T(8,128)S(1)}, f32[8,1280]{1,0:T(8,128)S(1)}, f32[8,1280]{1,0:T(8,128)S(1)}, f32[8,...) custom-call(s32[1]{0:T(128)} %bitcast.25.index_ref, ...), custom_call_target="tpu_custom_call" | custom-call | tf_op jit(solution)/shard_map/recurrence_backward/pallas_call | solution.py:816
  309.7 1.3 collective-permute-start
  311.2 1.7 slice.118
  313.7 1.9 reduce_sum.111
  315.7 2.0 copy.165
  317.7 1.8 add.214
  320.5 1.5 fusion.41
  322.1 1.2 copy.168
  324.2 1.5 convolution_convert_fusion.3
  327.2 1.2 dynamic-slice
  328.5 29.8 %all-reduce.5 = bf16[4,8,32,6]{2,0,3,1:T(4,128)(2,1)} all-reduce(bf16[4,8,32,6]{2,0,3,1:T(4,128)(2,1)S(1)} %copy.170), channel_id=4, replica_groups=mesh['seq'=4,'ctx'=8] {'ctx'}, use_global_device_ids=true, to_apply=%region_14.15.clone | all-reduce | flops 6144 | bytes 24576
  358.3 1.3 dynamic-slice_bitcast_fusion.4
  360.2 6.1 %all-to-all-start.2 = ((bf16[4,32,6]{1,2,0:T(8,128)(2,1)}), bf16[4,32,6]{1,2,0:T(8,128)(2,1)S(1)}, u32[]{:S(2)}, u32[]{:S(2)}) async-start(bf16[4,32,6]{1,2,0:T(8,128)(2,1)} %copy.171), calls=%async_computation.2 | async-start | bytes 16384 | tf_op jit(solution)/shard_map/all_to_all | solution.py:868
  366.4 1.8 fusion.21
  368.2 1.3 convolution_convert_fusion.2
  370.7 1.4 fusion.27
  372.1 4.7 convolution_convert_fusion
  377.5 1.4 fusion.19
  378.9 3.9 add_convert_fusion
  382.8 4.3 all-to-all-start
  388.0 1.6 copy.180
  389.6 7.2 %all-to-all-done = bf16[4,128,1024]{2,1,0:T(8,128)(2,1)S(1)} async-done(((bf16[4,128,1024]{2,1,0:T(8,128)(2,1)}), bf16[4,128,1024]{2,1,0:T(8,128)(2,1)S(1)}, u32[]{:S(2)}, u32[]{:S(2)}) %all-to-all-start) | async-done | bytes 1048608 | tf_op jit(solution)/shard_map/all_to_all | solution.py:877
  397.9 40.4 %psum.7 = f32[2193]{0:T(1024)S(1)} all-reduce(f32[2193]{0:T(1024)S(1)} %concatenate.30), channel_id=1, replica_groups=mesh['seq'=4,'ctx'=8] {'seq','ctx'}, use_global_device_ids=true, to_apply=%region_11.12 | all-reduce | flops 2193 | bytes 17544 | tf_op jit(solution)/shard_map/psum | solution.py:1037
  442.2 1.5 convert_element_type.209
  443.8 1.7 convert_element_type.216
  445.4 100.4 %all-reduce.12.cloned.1.call-done = (bf16[4,8,32,1280]{3,2,1,0:T(8,128)(2,1)}, bf16[4,8,32,256]{3,2,1,0:T(8,128)(2,1)}, bf16[4,8,32,704]{3,2,1,0:T(8,128)(2,1)}, bf16[4,8,32,704]{3,2,1,0:T(8,128)(2,1)}) async-done(((bf16[4,8,32,1280]{3,2,1,0:T(8,128)(2,1)}, bf16[4,8,32,256]{3,2,1,0:T(8,128)(2,1)}, bf16[4,8,32,704]{3,2,1,0:T(8,128)(2,1)}, bf16[4,8,32,704]{3,2,1,0:T(8,128)(2,1)}), ...) | async-done | bytes 6029328
  545.8 2.1 dynamic-slice_bitcast_fusion.3
  548.0 3.6 all-to-all-start.3
  551.6 2.3 dynamic-slice_bitcast_fusion.2
  553.9 2.6 all-to-all-done.3
  556.4 3.4 all-to-all-start.4
  559.8 2.4 dynamic-slice_bitcast_fusion
  562.2 2.3 dynamic-slice_bitcast_fusion.1
  565.0 3.6 all-to-all-start.5
  569.3 4.5 all-to-all-done.5
  573.8 3.5 all-to-all-start.1
  579.9 2.9 all-to-all-done.1
  (217 shorter events, 57.0 us)
Async XLA Ops:
  7.2 380.9 %reduce-scatter.18.cloned.1.call-start = ((), (), s32[]{:S(2)}) async-start(), calls=%async_computation.11 | async-start | bytes 737280
  8.8 9.7 %copy-start = (bf16[128,1024]{1,0:T(8,128)(2,1)S(1)}, bf16[128,1024]{1,0:T(8,128)(2,1)}, u32[]{:S(2)}) copy-start(bf16[128,1024]{1,0:T(8,128)(2,1)} %x_ref.3) | copy-start | bytes 786436
  64.1 3.6 copy-start.10
  66.1 1.0 copy-start.28
  67.8 6.5 %copy-start.27 = (f32[512,384]{0,1:T(8,128)}, f32[512,384]{0,1:T(8,128)S(1)}, u32[]{:S(2)}) copy-start(f32[512,384]{0,1:T(8,128)S(1)} %fusion.8) | copy-start | bytes 2359300
  68.6 5.7 copy-start.44
  68.6 6.3 %copy-start.45 = (bf16[8]{0:T(256)(128)(2,1)S(1)}, bf16[8]{0:T(256)(128)(2,1)}, u32[]{:S(2)}) copy-start(bf16[8]{0:T(256)(128)(2,1)} %param.29) | copy-start | bytes 52
  68.6 6.9 %copy-start.46 = (bf16[8]{0:T(256)(128)(2,1)S(1)}, bf16[8]{0:T(256)(128)(2,1)}, u32[]{:S(2)}) copy-start(bf16[8]{0:T(256)(128)(2,1)} %param.30) | copy-start | bytes 52
  72.3 18.1 %copy-start.2 = (bf16[528,1280]{1,0:T(8,128)(2,1)}, bf16[528,1280]{1,0:T(8,128)(2,1)S(1)}, u32[]{:S(2)}) copy-start(bf16[528,1280]{1,0:T(8,128)(2,1)S(1)} %convolution_convert_fusion.1.proj_ref) | copy-start | bytes 4055044
  76.0 4.4 copy-start.36
  81.2 2.3 copy-start.38
  81.2 2.4 copy-start.37
  83.2 4.2 slice-start
  83.3 7.2 %copy-start.23 = (bf16[88,1024]{1,0:T(8,128)(2,1)S(1)}, bf16[88,1024]{1,0:T(8,128)(2,1)}, u32[]{:S(2)}) copy-start(bf16[88,1024]{1,0:T(8,128)(2,1)} %wd_ref.1) | copy-start | bytes 540676
  83.3 7.2 %copy-start.24 = (bf16[32,1024]{1,0:T(8,128)(2,1)S(1)}, bf16[32,1024]{1,0:T(8,128)(2,1)}, u32[]{:S(2)}) copy-start(bf16[32,1024]{1,0:T(8,128)(2,1)} %wo_ref.1) | copy-start | bytes 196612
  87.6 84.4 %copy-start.3 = (f32[512,256]{1,0:T(8,128)}, f32[512,256]{1,0:T(8,128)S(1)}, u32[]{:S(2)}) copy-start(f32[512,256]{1,0:T(8,128)S(1)} %copy.190.gate_ref) | copy-start | bytes 1572868
  88.3 83.7 %copy-start.25 = (f32[1,128]{1,0:T(1,128)}, f32[1,128]{1,0:T(1,128)S(1)}, u32[]{:S(2)}) copy-start(f32[1,128]{1,0:T(1,128)S(1)} %bitcast_convert_fusion.gain_ref) | copy-start | bytes 1540
  90.4 1.0 copy-start.18
  164.8 1.1 copy-start.5
  165.9 1.1 copy-start.6
  167.0 1.0 copy-start.7
  168.0 1.0 copy-start.9
  169.8 0.8 copy-start.14
  171.4 2.0 copy-start.8
  171.4 2.0 copy-start.4
  173.4 106.0 %copy-start.13 = (f32[8,2,64,128]{3,2,1,0:T(8,128)S(1)}, f32[8,2,64,128]{3,2,1,0:T(8,128)}, u32[]{:S(2)}) copy-start(f32[8,2,64,128]{3,2,1,0:T(8,128)} %copy-done.12) | copy-start | bytes 1572868
  173.4 106.0 %copy-start.15 = (f32[8,2,64,128]{3,2,1,0:T(8,128)S(1)}, f32[8,2,64,128]{3,2,1,0:T(8,128)}, u32[]{:S(2)}) copy-start(f32[8,2,64,128]{3,2,1,0:T(8,128)} %copy-done.14) | copy-start | bytes 1572868
  279.4 1.0 copy-start.19
  308.2 134.0 %reduce-scatter.14.cloned.1.call-start = ((), (), s32[]{:S(2)}) async-start(), calls=%async_computation.9 | async-start | bytes 589824 | tf_op jit(solution)/shard_map/reduce_scatter | solution.py:872
  309.0 134.8 %reduce-scatter.16.cloned.1.call-start = ((), (), s32[]{:S(2)}) async-start(), calls=%async_computation.10 | async-start | bytes 1622016 | tf_op jit(solution)/shard_map/reduce_scatter | solution.py:872
  309.7 60.9 %collective-permute-start = (f32[8,1280]{1,0:T(8,128)S(1)}, f32[8,1280]{1,0:T(8,128)}, u32[]{:S(2)}, u32[]{:S(2)}) collective-permute-start(f32[8,1280]{1,0:T(8,128)S(1)} %get-tuple-element.91), channel_id=1, source_target_pairs={{1,0},{2,1},{3,2},{4,3},{5,4},{6,5},{7,6},{9,8},{10,9},{11,10},{12... | collective-permute-start | bytes 122888 | tf_op jit(solution)/shard_map/ppermute | solution.py:849
  312.9 53.4 %copy-start.11 = (bf16[4,8,32,1664]{3,2,1,0:T(8,128)(2,1)S(1)}, bf16[4,8,32,1664]{3,2,1,0:T(8,128)(2,1)}, u32[]{:S(2)}) copy-start(bf16[4,8,32,1664]{3,2,1,0:T(8,128)(2,1)} %copy-done.10) | copy-start | bytes 10223620
  360.2 22.6 %all-to-all-start.2 = ((bf16[4,32,6]{1,2,0:T(8,128)(2,1)}), bf16[4,32,6]{1,2,0:T(8,128)(2,1)S(1)}, u32[]{:S(2)}, u32[]{:S(2)}) async-start(bf16[4,32,6]{1,2,0:T(8,128)(2,1)} %copy.171), calls=%async_computation.2 | async-start | bytes 16384 | tf_op jit(solution)/shard_map/all_to_all | solution.py:868
  366.3 179.5 %all-reduce.12.cloned.1.call-start = ((), (), s32[]{:S(2)}) async-start(), calls=%async_computation.12 | async-start | bytes 12582912
  366.3 1.8 copy-start.29
  366.4 1.8 copy-start.32
  376.8 2.1 copy-start.26
  382.8 4.4 copy-start.40
  382.8 4.5 copy-start.1
  382.8 14.4 %copy-start.34 = (f32[1,1024]{1,0:T(1,128)S(1)}, f32[1,1024]{1,0:T(1,128)}, u32[]{:S(2)}) copy-start(f32[1,1024]{1,0:T(1,128)} %get-tuple-element.93) | copy-start | bytes 12292
  382.8 14.4 %copy-start.39 = (f32[1,128]{1,0:T(1,128)S(1)}, f32[1,128]{1,0:T(1,128)}, u32[]{:S(2)}) copy-start(f32[1,128]{1,0:T(1,128)} %get-tuple-element.72) | copy-start | bytes 1540
  382.8 58.4 %copy-start.30 = (f32[128,1024]{1,0:T(8,128)S(1)}, f32[128,1024]{1,0:T(8,128)}, u32[]{:S(2)}) copy-start(f32[128,1024]{1,0:T(8,128)} %get-tuple-element.94) | copy-start | bytes 1572868
  382.8 14.0 %all-to-all-start = ((bf16[4,128,1024]{2,1,0:T(8,128)(2,1)}), bf16[4,128,1024]{2,1,0:T(8,128)(2,1)S(1)}, u32[]{:S(2)}, u32[]{:S(2)}) async-start(bf16[4,128,1024]{2,1,0:T(8,128)(2,1)} %bitcast.159), calls=%async_computation | async-start | bytes 2097152 | tf_op jit(solution)/shard_map/all_to_all | solution.py:877
  548.0 8.5 %all-to-all-start.3 = ((bf16[4,32,256]{2,1,0:T(8,128)(2,1)}), bf16[4,32,256]{2,1,0:T(8,128)(2,1)S(1)}, u32[]{:S(2)}, u32[]{:S(2)}) async-start(bf16[4,32,256]{2,1,0:T(8,128)(2,1)} %dynamic-slice_bitcast_fusion.3), calls=%async_computation.3 | async-start | bytes 131072 | tf_op jit(solution)/shard_map/all_to_all | solution.py:868
  556.4 8.5 %all-to-all-start.4 = ((bf16[4,32,704]{2,1,0:T(8,128)(2,1)}), bf16[4,32,704]{2,1,0:T(8,128)(2,1)S(1)}, u32[]{:S(2)}, u32[]{:S(2)}) async-start(bf16[4,32,704]{2,1,0:T(8,128)(2,1)} %dynamic-slice_bitcast_fusion.2), calls=%async_computation.5 | async-start | bytes 393216 | tf_op jit(solution)/shard_map/all_to_all | solution.py:868
  565.0 8.8 %all-to-all-start.5 = ((bf16[4,32,704]{2,1,0:T(8,128)(2,1)}), bf16[4,32,704]{2,1,0:T(8,128)(2,1)S(1)}, u32[]{:S(2)}, u32[]{:S(2)}) async-start(bf16[4,32,704]{2,1,0:T(8,128)(2,1)} %dynamic-slice_bitcast_fusion.1), calls=%async_computation.6 | async-start | bytes 393216 | tf_op jit(solution)/shard_map/all_to_all | solution.py:868
  573.8 9.0 %all-to-all-start.1 = ((bf16[4,32,1280]{2,1,0:T(8,128)(2,1)}), bf16[4,32,1280]{2,1,0:T(8,128)(2,1)S(1)}, u32[]{:S(2)}, u32[]{:S(2)}) async-start(bf16[4,32,1280]{2,1,0:T(8,128)(2,1)} %dynamic-slice_bitcast_fusion), calls=%async_computation.1 | async-start | bytes 655360 | tf_op jit(solution)/shard_map/all_to_all | solution.py:868
  578.6 5.2 copy-start.31
  (11 other events, 7.4 us)
Sparse Core Ops, SparseCore 0:
  308.4 32.9 reduce-scatter.17
  343.6 29.0 reduce-scatter.13
  375.1 31.8 reduce-scatter.15
  409.7 136.1 all-reduce.11

commit v4 on v3

--- a/solution.py
+++ b/solution.py
@@ -173,6 +173,90 @@
             pl.when(needed)(lambda chip=chip: self.arrived(2 * chip + 1 - self.core))
         for distance in range(self.chips):
             self.routes(distance, self.left)
+
+
+class LineSum:
+    def __init__(self, pieces, held, came, send_sem, recv_sem):
+        self.chips = pieces // 2
+        self.here = lax.axis_index("ctx")
+        self.chip = self.here // 2
+        self.held, self.came, self.send_sem, self.recv_sem = held, came, send_sem, recv_sem
+
+    def copies(self, owner, way):
+        return [
+            pltpu.make_async_remote_copy(
+                held.at[owner], came.at[way, owner], self.send_sem.at[n, owner], self.recv_sem.at[n, way, owner],
+                device_id={"ctx": self.here + 2 - 4 * way}, device_id_type=MESH,
+            )
+            for n, (held, came) in enumerate(zip(self.held, self.came))
+        ]
+
+    def take(self, owner, way):
+        for copy in self.copies(owner, way):
+            copy.wait_recv()
+        for held, came in zip(self.held, self.came):
+            held[owner] = (held[owner].astype(F32) + came[way, owner].astype(F32)).astype(BF16)
+
+    def send(self, owner, way):
+        for copy in self.copies(owner, way):
+            copy.start()
+
+    def round(self, r):
+        top = self.chips - 1
+        for way, place in ((UP, self.chip), (DOWN, top - self.chip)):
+            owner = top - (r - place) if way == UP else r - place
+
+            @pl.when((place <= r) & (place < top))
+            def _():
+                pl.when(place > 0)(lambda: self.take(owner, way))
+                self.send(owner, way)
+
+    def finish(self):
+        top = self.chips - 1
+        pl.when(self.chip > 0)(lambda: self.take(self.chip, UP))
+        pl.when(self.chip < top)(lambda: self.take(self.chip, DOWN))
+        for owner in range(self.chips):
+            for way, wanted in ((UP, self.chip < owner), (DOWN, self.chip > owner)):
+
+                @pl.when(wanted)
+                def _():
+                    for copy in self.copies(owner, way):
+                        copy.wait_send()
+
+
+class Siblings:
+    def __init__(self, parts, theirs, held, send_sem, recv_sem):
+        self.here = lax.axis_index("ctx")
+        self.core = lax.rem(self.here, 2)
+        self.parts, self.theirs, self.held, self.send_sem, self.recv_sem = parts, theirs, held, send_sem, recv_sem
+
+    def copies(self):
+        return [
+            pltpu.make_async_remote_copy(
+                part.at[:, 1 - self.core], theirs, self.send_sem.at[n], self.recv_sem.at[n],
+                device_id={"ctx": self.here + 1 - 2 * self.core}, device_id_type=MESH,
+            )
+            for n, (part, theirs) in enumerate(zip(self.parts, self.theirs))
+        ]
+
+    def start(self):
+        for copy in self.copies():
+            copy.start()
+
+    def add(self):
+        for copy in self.copies():
+            copy.wait_recv()
+        for part, theirs, held in zip(self.parts, self.theirs, self.held):
+
+            def one(chip, carry, part=part, theirs=theirs, held=held):
+                held[chip] = (part[chip, self.core].astype(F32) + theirs[chip].astype(F32)).astype(BF16)
+                return carry
+
+            lax.fori_loop(0, part.shape[0], one, 0)
+
+    def left(self):
+        for copy in self.copies():
+            copy.wait_send()
 
 
 def greet(devices, barrier):
@@ -493,7 +577,7 @@
     x_ref, teach_ref, mask_ref, norm_ref, gain_ref, mixed_ref, heads_ref, gate_ref, carr_ref,
     wout_ref, wg_ref, wu_ref, wd_ref,
     final_ref, gmid_ref, ghead_ref, ggate_ref, cot_ref, ggain_ref, gnorm_ref, loss_ref,
-    gout_ref, gwg_ref, gwu_ref, gwd_ref,
+    wide_ref, tall_ref,
     second, branch, low, sent, got, own, mid, gfin, gates, ups, hidden, ggates, gups, send_sem, recv_sem,
 ):
     me = lax.axis_index("seq")
@@ -602,9 +686,20 @@
         return carry
 
     lax.fori_loop(0, size, feed_back, 0)
-    gwd_ref[...] = dot(hidden[...], branch[...], 0, 0).astype(BF16)
-    gwg_ref[...] = dot(second[...], ggates[...], 0, 0).astype(BF16)
-    gwu_ref[...] = dot(second[...], gups[...], 0, 0).astype(BF16)
+    pieces = wide_ref.shape[0]
+    held = D // (size * pieces)
+    deep = hidden.shape[1] // pieces
+    wide_at = tall_ref.shape[1] - held
+    tall_ref[...] = jnp.zeros_like(tall_ref)
+    grad = dot(hidden[...], branch[...], 0, 0)
+    for c in range(pieces):
+        tall_ref[c, :deep] = grad[c * deep : (c + 1) * deep].astype(BF16)
+    for n, side in enumerate((ggates, gups)):
+        grad = dot(second[...], side[...], 0, 0)
+        for c in range(pieces):
+            for r in range(size):
+                first = (r * pieces + c) * held
+                wide_ref[c, (n * size + r) * held : (n * size + r + 1) * held] = grad[first : first + held].astype(BF16)
     gsecond = take_parts(2)
     middle = mid[...]
     inv = lax.rsqrt(jnp.mean(middle * middle, axis=1, keepdims=True) + NORM_EPS)
@@ -640,7 +735,9 @@
         return carry
 
     lax.fori_loop(0, size, out_back, 0)
-    gout_ref[...] = dot(mixed_ref[...], low[...], 0, 0).astype(BF16)
+    grad = dot(mixed_ref[...], low[...], 0, 0)
+    for c in range(pieces):
+        tall_ref[c, wide_at:] = grad[c * held : (c + 1) * held].astype(BF16)
 
     def sent_all(i, carry):
         for phase in range(3):
@@ -653,21 +750,22 @@
     lax.fori_loop(1, size, sent_all, 0)
 
 
-def middle_part(size, heads, scale, x, teacher, mask, norm_m, gain, mixed, heads_out, gate_out, carr, wout, wg, wu, wd):
+def middle_part(size, heads, pieces, scale, x, teacher, mask, norm_m, gain, mixed, heads_out, gate_out, carr, wout, wg, wu, wd):
     count = x.shape[0]
     rows = count * size
     inner = wg.shape[1]
+    held, deep = D // (size * pieces), inner // pieces
     vmem = pl.BlockSpec(memory_space=pltpu.VMEM)
     out = lambda dims, kind: jax.ShapeDtypeStruct(dims, kind)
     return pl.pallas_call(
         functools.partial(middle_kernel, size, heads),
         in_specs=[pl.BlockSpec(memory_space=pltpu.SMEM)] + [vmem] * 13,
-        out_specs=[vmem] * 12,
+        out_specs=[vmem] * 10,
         out_shape=[
             out((count, D), BF16), out((count, D), F32),
             out((rows, heads * HEAD), BF16), out((rows, heads * HEAD), BF16), out((heads, HEAD, HEAD), F32),
             out((1, HEAD), F32), out((1, D), F32), out((8, HEAD), F32),
-            out((heads * HEAD, D), BF16), out((D, inner), BF16), out((D, inner), BF16), out((inner, D), BF16),
+            out((pieces, 2 * size * held, inner), BF16), out((pieces, -(-deep // 16) * 16 + held, D), BF16),
         ],
         scratch_shapes=[
             pltpu.VMEM((rows, D), BF16), pltpu.VMEM((rows, D), BF16), pltpu.VMEM((rows, D), BF16),
@@ -685,35 +783,58 @@
 
 
 def bwd_kernel(
-    heads, index_ref, maps_ref, cots_ref, sin_ref, proj_ref, w_ref, rowp_ref, colp_ref, tokp_ref,
-    go_ref, conv_ref, q_ref, k_ref, v_ref, t_ref, kk_ref, at_ref, uw_ref, pl_ref,
-    gproj_ref, last_ref, spill_ref, gw_ref, gcol_ref, gtok_ref, grow_ref,
-    dstate, weave, rim,
+    heads, pieces, steps, maps_ref, cot_ref, sin_ref, proj_ref, w_ref, rowp_ref, colp_ref, tokp_ref,
+    go_ref, conv_ref, q_ref, k_ref, v_ref, t_ref, kk_ref, at_ref, uw_ref, pl_ref, wide_ref, tall_ref,
+    gproj_ref, fix_ref, gw_ref, gscal_ref, gsum_ref, widesum_ref, tallsum_ref,
+    dstate, weave, rim, last, cots, rim_in, wtheirs, ttheirs, wheld, theld, wcame, tcame,
+    cot_send, cot_recv, pair_send, pair_recv, line_send, line_recv, rim_sem,
 ):
     step = pl.program_id(0)
-    block = pl.num_programs(0) - 1 - step
+    block = steps - 1 - step
+    here = lax.axis_index("ctx")
+    core = lax.rem(here, 2)
+    pair = Siblings([wide_ref, tall_ref], [wtheirs, ttheirs], [wheld, theld], pair_send, pair_recv)
+    line = LineSum(pieces, [wheld, theld], [wcame, tcame], line_send, line_recv)
+    rounds = pieces // 2 - 1
+    when_round = [(r * steps) // max(rounds - 1, 1) for r in range(rounds)]
 
     @pl.when(step == 0)
     def _():
-        pieces = maps_ref.shape[0]
+        barrier = pltpu.get_barrier_semaphore()
+        side = [({"ctx": here + 1}, (core == 1) & (here < pieces - 1)), ({"ctx": here - 1}, (core == 0) & (here > 0))]
+        pl.semaphore_wait(barrier, greet(line_neighbours(pieces) + side, barrier))
+        cots[here] = cot_ref[...].astype(BF16)
+        spread = Line(pieces, [lambda c: cots.at[c]], cot_send, cot_recv, up=False)
+        spread.own()
+        pair.start()
+        for distance in range(1, pieces // 2):
+            spread.hop(distance)
+        spread.finish()
+        pair.add()
 
         def hop(i, states):
             k = pieces - 1 - i
             return tuple(
-                mm(maps_ref[k, h], states[h], 0, 0) + cots_ref[k, h].astype(F32) for h in range(heads)
+                mm(maps_ref[k, h], states[h], 0, 0) + cots[k, h].astype(F32) for h in range(heads)
             )
 
         found = lax.fori_loop(
-            0, pieces - 1 - index_ref[0], hop, tuple(jnp.zeros((HEAD, HEAD), F32) for _ in range(heads))
+            0, pieces - 1 - here, hop, tuple(jnp.zeros((HEAD, HEAD), F32) for _ in range(heads))
         )
         for h in range(heads):
             dstate[h] = found[h]
         rim[...] = jnp.zeros_like(rim)
         gw_ref[...] = jnp.zeros_like(gw_ref)
+        gsum_ref[...] = jnp.zeros_like(gsum_ref)
+
+    for r in range(rounds):
+        if when_round[r] < steps:
+            pl.when(step == when_round[r])(lambda r=r: line.round(r))
 
     base = pl.multiple_of(block * BLOCK_LEN, BLOCK_LEN)
     rowp, colp, tokp = rowp_ref[0], colp_ref[0], tokp_ref[0]
     last_row = iota((ROWS, 1), 0) == ROWS - 1
+    gscal = jnp.zeros((BLOCK_LEN, HEAD), F32)
     for h in range(heads):
         cols = slice(h * WIDE, (h + 1) * WIDE)
         hc = slice(h * HEAD, (h + 1) * HEAD)
@@ -760,18 +881,28 @@
         )
         dgrow = jnp.sum(z1, axis=1, keepdims=True) + jnp.sum(dy * ks, axis=1, keepdims=True) - dlk
         dgrow = dgrow + jnp.where(last_row, tail, 0.0)
-        gcol_ref[0, :, 2 * h : 2 * h + 1] = dbeta
-        gcol_ref[0, :, 2 * h + 1 : 2 * h + 2] = dgrow
-        gtok_ref[0, :, h : h + 1] = jnp.sum(z2, axis=1, keepdims=True) + qcarry * jnp.sum(
-            query * gos, axis=1, keepdims=True
-        )
-        grow_ref[0, h : h + 1, :] = jnp.sum(z1, axis=0, keepdims=True) + jnp.sum(z2, axis=0, keepdims=True)
+        dgrow = dgrow - mm(jnp.concatenate([z2, z1], axis=0), jnp.ones((BLOCK_LEN + ROWS, HEAD), BF16), 0, 0)[:, :1]
+        lane = iota((ROWS, HEAD), 1)
+        weave[2 * h] = jnp.where(lane == 0, dbeta, jnp.where(lane == 1, dgrow, 0.0))
+        by_step = [weave[2 * h, pl.ds(j, BLOCK_LEN, NH), :] for j in range(NH)]
+        dg = sum(x[:, 1:2] for x in by_step) + jnp.sum(z2, axis=1, keepdims=True)
+        dg = dg + qcarry * jnp.sum(query * gos, axis=1, keepdims=True)
+        after = (iota((BLOCK_LEN, BLOCK_LEN), 0) <= iota((BLOCK_LEN, BLOCK_LEN), 1)).astype(BF16)
+        dlog = tokp[:, 0:1] * mm(after, jnp.broadcast_to(dg, (BLOCK_LEN, HEAD)))[:, :1]
+        at = 4 + heads + h * (NH + 2)
+        dscal = [by_step[j][:, 0:1] * tokp[:, at + j : at + j + 1] for j in range(NH)]
+        dscal.append(dlog * tokp[:, at + NH : at + NH + 1])
+        lane = iota((BLOCK_LEN, HEAD), 1)
+        for j in range(NH + 1):
+            gscal = gscal + jnp.where(lane == h * (NH + 1) + j, dscal[j], 0.0)
+        sums = jnp.where(lane == 0, dlog * tokp[:, at + NH + 1 : at + NH + 2], jnp.where(lane == 1, dscal[NH], 0.0))
+        gsum_ref[h : h + 1, :] += jnp.sum(sums, axis=0, keepdims=True)
         weave[2 * h] = dk
         weave[2 * h + 1] = dv
         conv = conv_ref[:, cols]
         sig = jax.nn.sigmoid(conv)
         act = conv * sig
-        pieces = []
+        parts = []
         for part in range(1 + NH):
             piece = act[:, part * HEAD : (part + 1) * HEAD]
             scale = lax.rsqrt(jnp.sum(piece * piece, axis=1, keepdims=True) + NORM_EPS)
@@ -780,10 +911,10 @@
             else:
                 grad = dq * (1.0 / math.sqrt(HEAD))
             unit = piece * scale
-            pieces.append(scale * (grad - unit * jnp.sum(grad * unit, axis=1, keepdims=True)))
+            parts.append(scale * (grad - unit * jnp.sum(grad * unit, axis=1, keepdims=True)))
         for j in range(NH):
-            pieces.append(weave[2 * h + 1, pl.ds(j, BLOCK_LEN, NH), :])
-        dconv = jnp.concatenate(pieces, axis=1) * (sig * (1.0 + conv * (1.0 - sig)))
+            parts.append(weave[2 * h + 1, pl.ds(j, BLOCK_LEN, NH), :])
+        dconv = jnp.concatenate(parts, axis=1) * (sig * (1.0 + conv * (1.0 - sig)))
         ext = proj_ref[pl.ds(base, BLOCK_LEN + HALO), cols].astype(F32)
         gw_ref[0:1, cols] += jnp.sum(dconv * ext[HALO:], axis=0, keepdims=True)
         zeros = jnp.zeros((8, WIDE), F32)
@@ -798,96 +929,266 @@
         fixed = total[length - 8 :] + rim[:, cols]
         gproj_ref[:, cols] = jnp.concatenate([total[8 : length - 8], fixed], axis=0).astype(BF16)
         rim[:, cols] = total[:8]
-        spill_ref[:, cols] = total[:8]
 
         @pl.when(step == 0)
         def _():
-            last_ref[:, cols] = fixed
-
-
-def recurrence_backward(index, maps, cots, state_in, proj_ext, conv_w, rowp, colp, tokp, grad_heads, saved, heads):
+            last[:, cols] = fixed
+
+    gscal_ref[...] = gscal.astype(BF16)
+
+    @pl.when(step == steps - 1)
+    def _():
+        passing = pltpu.make_async_remote_copy(
+            rim, rim_in, rim_sem.at[0], rim_sem.at[1], device_id={"ctx": here - 1}, device_id_type=MESH
+        )
+        pl.when(here > 0)(passing.start)
+        fix_ref[...] = last[...].astype(BF16)
+
+        @pl.when(here < pieces - 1)
+        def _():
+            passing.wait_recv()
+            fix_ref[...] = (last[...] + rim_in[...]).astype(BF16)
+
+        for r in range(rounds):
+            if when_round[r] >= steps:
+                line.round(r)
+        line.finish()
+        widesum_ref[...] = wheld[here // 2]
+        tallsum_ref[...] = theld[here // 2].astype(F32)
+        pair.left()
+        pl.when(here > 0)(passing.wait_send)
+
+
+def recurrence_backward(
+    maps, cot, state_in, proj_ext, conv_w, rowp, colp, tokp, grad_heads, saved, wide, tall, heads, pieces
+):
     blocks = rowp.shape[0]
     rows = blocks * BLOCK_LEN
+    chips = pieces // 2
     whole = lambda *dims: pl.BlockSpec(dims, lambda i: (0,) * len(dims))
     by_block = lambda *dims: pl.BlockSpec((1,) + dims, lambda i: (blocks - 1 - i,) + (0,) * len(dims))
     token = lambda cols: pl.BlockSpec((BLOCK_LEN, cols), lambda i: (blocks - 1 - i, 0))
     shape = lambda *dims: jax.ShapeDtypeStruct(dims, F32)
+    low_shape = lambda *dims: jax.ShapeDtypeStruct(dims, BF16)
+    vmem = pl.BlockSpec(memory_space=pltpu.VMEM)
     square = (heads, ROWS, HEAD)
+    wide_chunk, tall_chunk = wide.shape[2:], tall.shape[2:]
+    dma = pltpu.SemaphoreType.DMA
     return pl.pallas_call(
-        functools.partial(bwd_kernel, heads),
+        functools.partial(bwd_kernel, heads, pieces, blocks),
         grid=(blocks,),
         in_specs=[
-            pl.BlockSpec(memory_space=pltpu.SMEM), whole(*maps.shape), whole(*cots.shape), whole(*state_in.shape),
-            whole(*proj_ext.shape), whole(*conv_w.shape),
+            vmem, vmem, vmem, vmem, vmem,
             by_block(*rowp.shape[1:]), by_block(*colp.shape[1:]), by_block(*tokp.shape[1:]),
             token(heads * HEAD), token(heads * WIDE),
             by_block(heads, BLOCK_LEN, HEAD), by_block(*square), by_block(*square), by_block(*square),
             by_block(*square), by_block(heads, BLOCK_LEN, ROWS), by_block(heads, ROWS, 2 * HEAD),
-            by_block(heads, HEAD, 2 * HEAD),
+            by_block(heads, HEAD, 2 * HEAD), vmem, vmem,
         ],
         out_specs=[
-            token(heads * WIDE), whole(8, heads * WIDE), whole(8, heads * WIDE), whole(8, heads * WIDE),
-            by_block(ROWS, 2 * heads), by_block(BLOCK_LEN, heads), by_block(heads, ROWS),
+            token(heads * WIDE), whole(8, heads * WIDE), whole(8, heads * WIDE), token(HEAD), whole(8, HEAD),
+            whole(*wide_chunk), whole(*tall_chunk),
         ],
         out_shape=[
-            jax.ShapeDtypeStruct((rows, heads * WIDE), BF16), shape(8, heads * WIDE), shape(8, heads * WIDE),
-            shape(8, heads * WIDE), shape(blocks, ROWS, 2 * heads), shape(blocks, BLOCK_LEN, heads),
-            shape(blocks, heads, ROWS),
+            low_shape(rows, heads * WIDE), low_shape(8, heads * WIDE), shape(8, heads * WIDE), low_shape(rows, HEAD),
+            shape(8, HEAD), low_shape(*wide_chunk), shape(*tall_chunk),
         ],
         scratch_shapes=[
             pltpu.VMEM((heads, HEAD, HEAD), F32), pltpu.VMEM((2 * heads, ROWS, HEAD), F32),
-            pltpu.VMEM((8, heads * WIDE), F32),
-        ],
-        compiler_params=pltpu.CompilerParams(vmem_limit_bytes=48 << 20),
+            pltpu.VMEM((8, heads * WIDE), F32), pltpu.VMEM((8, heads * WIDE), F32),
+            pltpu.VMEM((pieces, heads, HEAD, HEAD), BF16), pltpu.VMEM((8, heads * WIDE), F32),
+            pltpu.VMEM((chips, *wide_chunk), BF16), pltpu.VMEM((chips, *tall_chunk), BF16),
+            pltpu.VMEM((chips, *wide_chunk), BF16), pltpu.VMEM((chips, *tall_chunk), BF16),
+            pltpu.VMEM((2, chips, *wide_chunk), BF16), pltpu.VMEM((2, chips, *tall_chunk), BF16),
+            dma((1, 3, pieces)), dma((1, pieces)), dma((2,)), dma((2,)), dma((2, chips)), dma((2, 2, chips)), dma((2,)),
+        ],
+        compiler_params=pltpu.CompilerParams(
+            vmem_limit_bytes=58 << 20, collective_id=4, has_side_effects=True
+        ),
         name="recurrence_backward",
-    )(index, maps, cots, state_in, proj_ext, conv_w, rowp, colp, tokp, grad_heads, *saved)
-
-
-def passed_along(x, axis, by):
-    devices = lax.axis_size(axis)
-    pairs = [(i, i + by) for i in range(devices) if 0 <= i + by < devices]
-    return lax.ppermute(x, axis, pairs)
+    )(maps, cot, state_in, proj_ext, conv_w, rowp, colp, tokp, grad_heads, *saved, wide, tall)
+
+
+def final_kernel(
+    size, pieces, gp_ref, gg_ref, gs_ref, w_ref, normed_ref, x_ref, gmid_ref, norm_ref, conv_ref, small_ref, wide_ref,
+    ingrad_ref, gmix_ref, ggate_ref, gtail_ref, total_ref, wideout_ref,
+    sent, got, own, turned, grads, theirs, held, came, blocks, around, along,
+    local_sem, seq_send, seq_recv, pair_send, pair_recv, line_send, line_recv, ctx_send, ctx_recv,
+):
+    me, here = lax.axis_index("seq"), lax.axis_index("ctx")
+    count = x_ref.shape[0]
+    barrier = pltpu.get_barrier_semaphore()
+    peers = [({"seq": lax.rem(me + i, size)}, here >= 0) for i in range(1, size)]
+    peers += [({"ctx": lax.rem(here + i, pieces)}, here >= 0) for i in range(1, pieces)]
+    pl.semaphore_wait(barrier, greet(peers, barrier))
+
+    def dot(a, b, ca=1, cb=0):
+        return lax.dot_general(a, b, (((ca,), (cb,)), ((), ())), preferred_element_type=F32)
+
+    def rows(q):
+        return pl.ds(pl.multiple_of(q * count, count), count)
+
+    def to_peer(n, i):
+        q = lax.rem(me + i, size)
+        source, target = [
+            (sent.at[i - 1], got.at[i - 1]), (wide_ref.at[:, q], wideout_ref.at[me]),
+            (around.at[me], around.at[me]), (held.at[here // 2, q], blocks.at[me]),
+        ][n]
+        return pltpu.make_async_remote_copy(
+            source, target, seq_send.at[n, i - 1], seq_recv.at[n, i - 1], device_id={"seq": q}, device_id_type=MESH
+        )
+
+    def to_piece(i):
+        return pltpu.make_async_remote_copy(
+            along.at[here], along.at[here], ctx_send.at[i - 1], ctx_recv.at[i - 1],
+            device_id={"ctx": lax.rem(here + i, pieces)}, device_id_type=MESH,
+        )
+
+    kept = pltpu.make_async_copy(wide_ref.at[:, me], wideout_ref.at[me], local_sem.at[0])
+    kept.start()
+    for i in range(1, size):
+        to_peer(1, i).start()
+    gate_at, tail_at = gp_ref.shape[1], gp_ref.shape[1] + gg_ref.shape[1]
+
+    def part(k, carry):
+        i = lax.rem(k + 1, size)
+        q = lax.rem(me + i, size)
+        value = (
+            dot(gp_ref[rows(q)], w_ref[:, :gate_at], 1, 1)
+            + dot(gg_ref[rows(q)], w_ref[:, gate_at:tail_at], 1, 1)
+            + dot(gs_ref[rows(q)], w_ref[:, tail_at:], 1, 1)
+        )
+
+        @pl.when(i > 0)
+        def _():
+            sent[i - 1] = value.astype(BF16)
+            pltpu.make_async_remote_copy(
+                sent.at[i - 1], got.at[i - 1], seq_send.at[0, i - 1], seq_recv.at[0, i - 1],
+                device_id={"seq": q}, device_id_type=MESH,
+            ).start()
+
+        @pl.when(i == 0)
+        def _():
+            own[...] = value
+
+        return carry
+
+    lax.fori_loop(0, size, part, 0)
+    turned[...] = normed_ref[...].T
+    rank_rows = D // (size * pieces)
+    for source, at in ((gp_ref, 0), (gg_ref, gate_at), (gs_ref, tail_at)):
+        width = source.shape[1]
+        for first in range(0, width, 256):
+            cols = min(256, width - first)
+            grad = dot(turned[...], source[:, first : first + cols])
+            for r in range(size):
+                for c in range(pieces):
+                    row = (r * pieces + c) * rank_rows
+                    grads[c // 2, c % 2, r, :, at + first : at + first + cols] = grad[row : row + rank_rows].astype(BF16)
+    for c in range(pieces):
+        grads[c // 2, c % 2, me, :, tail_at:] = (
+            grads[c // 2, c % 2, me, :, tail_at:].astype(F32) + conv_ref[c]
+        ).astype(BF16)
+    pair = Siblings([grads], [theirs], [held], pair_send, pair_recv)
+    pair.start()
+
+    for i in range(1, size):
+        to_peer(0, i).wait_recv()
+    gnormed = own[...]
+    for i in range(1, size):
+        gnormed = gnormed + got[i - 1].astype(F32)
+    x = x_ref[...].astype(F32)
+    inv = lax.rsqrt(jnp.mean(x * x, axis=1, keepdims=True) + NORM_EPS)
+    unit = x * inv
+    down = gnormed * norm_ref[...]
+    ingrad_ref[...] = gmid_ref[...] + inv * (down - unit * jnp.mean(down * unit, axis=1, keepdims=True))
+    term = jnp.sum(gnormed * unit, axis=0, keepdims=True)
+    around[me] = small_ref[...]
+    for j in range(D // HEAD):
+        around[me, small_ref.shape[0] - D // HEAD + j : small_ref.shape[0] - D // HEAD + j + 1] = term[
+            :, j * HEAD : (j + 1) * HEAD
+        ]
+    for i in range(1, size):
+        to_peer(2, i).start()
+    pair.add()
+    line = LineSum(pieces, [held], [came], line_send, line_recv)
+    line.round(0)
+    for i in range(1, size):
+        to_peer(2, i).wait_recv()
+    mine = around[0]
+    for r in range(1, size):
+        mine = mine + around[r]
+    along[here] = mine
+    for i in range(1, pieces):
+        to_piece(i).start()
+    for r in range(1, pieces // 2 - 1):
+        line.round(r)
+    line.finish()
+    blocks[me] = held[here // 2, me]
+    for i in range(1, size):
+        to_peer(3, i).start()
+    for i in range(1, pieces):
+        to_piece(i).wait_recv()
+    total = along[0]
+    for c in range(1, pieces):
+        total = total + along[c]
+    total_ref[...] = total
+    for i in range(1, size):
+        to_peer(3, i).wait_recv()
+    for r in range(size):
+        block = blocks[r].astype(F32)
+        gmix_ref[:, r * gate_at : (r + 1) * gate_at] = block[:, :gate_at]
+        ggate_ref[:, r * (tail_at - gate_at) : (r + 1) * (tail_at - gate_at)] = block[:, gate_at:tail_at]
+        gtail_ref[r] = block[:, tail_at:]
+    kept.wait()
+    pair.left()
+    for i in range(1, size):
+        to_peer(1, i).wait_recv()
+        for n in range(4):
+            to_peer(n, i).wait_send()
+    for i in range(1, pieces):
+        to_piece(i).wait_send()
+
+
+def final_part(size, pieces, gp, gg, gs, weights, normed, x, gmid, norm_a, conv, small, wide):
+    count = x.shape[0]
+    chips = pieces // 2
+    held = D // (size * pieces)
+    width = weights.shape[1]
+    vmem = pl.BlockSpec(memory_space=pltpu.VMEM)
+    out = lambda dims, kind=F32: jax.ShapeDtypeStruct(dims, kind)
+    dma = pltpu.SemaphoreType.DMA
+    return pl.pallas_call(
+        functools.partial(final_kernel, size, pieces),
+        in_specs=[vmem] * 11,
+        out_specs=[vmem] * 6,
+        out_shape=[
+            out((count, D)), out((held, size * gp.shape[1])), out((held, size * gg.shape[1])),
+            out((size, held, gs.shape[1])), out(small.shape), out((size, 2, held, wide.shape[3]), BF16),
+        ],
+        scratch_shapes=[
+            pltpu.VMEM((size - 1, count, D), BF16), pltpu.VMEM((size - 1, count, D), BF16), pltpu.VMEM((count, D), F32),
+            pltpu.VMEM((D, normed.shape[0]), BF16),
+            pltpu.VMEM((chips, 2, size, held, width), BF16), pltpu.VMEM((chips, size, held, width), BF16),
+            pltpu.VMEM((chips, size, held, width), BF16), pltpu.VMEM((2, chips, size, held, width), BF16),
+            pltpu.VMEM((size, held, width), BF16), pltpu.VMEM((size, *small.shape), F32),
+            pltpu.VMEM((pieces, *small.shape), F32),
+            dma((1,)), dma((4, size - 1)), dma((4, size - 1)), dma((1,)), dma((1,)), dma((1, chips)), dma((1, 2, chips)),
+            dma((pieces - 1,)), dma((pieces - 1,)),
+        ],
+        compiler_params=pltpu.CompilerParams(
+            vmem_limit_bytes=60 << 20, collective_id=5, has_side_effects=True
+        ),
+        name="final_part",
+    )(gp, gg, gs, weights, normed, x, gmid, norm_a, conv, small, wide)
 
 
 def rms_scale(values, gain_vec):
     return values * lax.rsqrt(jnp.mean(values * values, axis=-1, keepdims=True) + NORM_EPS) * gain_vec
 
 
-def scalar_gates(scal, a_log, dt_bias):
-    beta = jax.nn.sigmoid(scal[:, :, :NH])
-    logs = -jnp.exp(a_log)[None, :] * jax.nn.softplus(scal[:, :, NH] + dt_bias[None, :])
-    return beta, logs
-
-
-def sum_columns_back(grad):
-    ranks, pieces = lax.axis_size("seq"), lax.axis_size("ctx")
-    cols = grad.shape[1]
-    mine = lax.psum_scatter(
-        grad.astype(BF16).reshape(ranks, pieces, -1, cols), "ctx", scatter_dimension=1, tiled=True
-    )
-    return lax.all_to_all(mine.reshape(-1, cols), "seq", split_axis=0, concat_axis=1, tiled=True).astype(F32)
-
-
-def sum_rows_back(grad):
-    return lax.psum_scatter(grad.astype(BF16), "ctx", scatter_dimension=0, tiled=True).astype(F32)
-
-
-def sum_tokens(partial):
-    ranks = lax.axis_size("seq")
-    parts = lax.all_to_all(partial.astype(BF16).reshape(ranks, -1, partial.shape[1]), "seq", 0, 0, tiled=True)
-    return jnp.sum(parts.astype(F32), axis=0)
-
-
 def dot(a, b):
     return jnp.dot(a, b, preferred_element_type=F32)
-
-
-def dot_t(a, b):
-    return jnp.einsum("tc,dc->td", a, b, preferred_element_type=F32)
-
-
-def t_dot(a, b):
-    return jnp.einsum("tr,tc->rc", a, b, preferred_element_type=F32)
 
 
 def local(
@@ -946,9 +1247,6 @@
     rest = dot(normed, weights[:, gate_at:])
     gate_out = rest[:, : heads * HEAD]
     scal = rest[:, heads * HEAD : heads * HEAD + scal_cols].astype(BF16)
-    inputs_f = block_input.astype(F32)
-    _, norm_in_back = jax.vjp(rms_scale, inputs_f, norm_a)
-    mix_s, gate_s, scal_s = weights[:, :gate_at], weights[:, gate_at:scal_at], weights[:, scal_at:norm_at]
 
     piece_start = index * rows
     window = lax.dynamic_slice_in_dim(jnp.pad(segments, (CONV, 0)), piece_start, rows + CONV)
@@ -960,9 +1258,14 @@
     starts = 1.0 - linked[0]
     alog_heads = lax.dynamic_slice_in_dim(a_log.astype(F32), head_start, heads, 0)
     dt_heads = lax.dynamic_slice_in_dim(dt_bias.astype(F32), head_start, heads, 0)
-    (beta, logs), gates_back = jax.vjp(
-        scalar_gates, scal.astype(F32).reshape(rows, heads, NH + 1), alog_heads, dt_heads
-    )
+    scal = scal.astype(F32).reshape(rows, heads, NH + 1)
+    beta = jax.nn.sigmoid(scal[:, :, :NH])
+    rate = -jnp.exp(alog_heads)[None, :]
+    lifted = scal[:, :, NH] + dt_heads[None, :]
+    logs = rate * jax.nn.softplus(lifted)
+    slopes = jnp.concatenate(
+        [beta * (1.0 - beta), (rate * jax.nn.sigmoid(lifted))[:, :, None], logs[:, :, None]], axis=2
+    ).reshape(blocks, BLOCK_LEN, heads * (NH + 2))
     lower = jnp.tril(jnp.ones((BLOCK_LEN, BLOCK_LEN), F32))
     sums = jnp.einsum(
         "ts,bsh->bth",
@@ -970,7 +1273,7 @@
         jnp.concatenate([starts[:, None], logs * (1.0 - starts)[:, None]], axis=1).reshape(blocks, BLOCK_LEN, heads + 1),
         precision=lax.Precision.HIGHEST,
     )
-    tokp = jnp.concatenate([jnp.stack(linked, axis=1).reshape(blocks, BLOCK_LEN, CONV - 1), sums], axis=2)
+    tokp = jnp.concatenate([jnp.stack(linked, axis=1).reshape(blocks, BLOCK_LEN, CONV - 1), sums, slopes], axis=2)
     sums_rows = jnp.repeat(sums, NH, axis=1)
     beta_rows = jnp.swapaxes(beta, 1, 2).reshape(blocks, ROWS, heads)
     colp = jnp.concatenate(
@@ -987,58 +1290,52 @@
     wg_s, wu_s = wg_full.reshape(D, inner), wu_full.reshape(D, inner)
     down_s, out_s = wd_full.reshape(inner, D), wo_full.reshape(heads * HEAD, D)
     gain = head_gain.astype(F32)[None, :]
-    index_arr = index.reshape(1).astype(jnp.int32)
     heads_out, mixed = state_and_gate(state_in, oloc, carr, gate_out, gain, heads)
 
     scale = (token_total / valid_count).reshape(1, 1)
     mask_values = valid_mask.astype(F32)[:, None]
     (
-        final_out, grad_middle, grad_heads, grad_gate_out, cot, gain_term, norm_mlp_term, loss,
-        out_grad, wg_grad, wu_grad, down_grad,
+        final_out, grad_middle, grad_heads, grad_gate_out, cot, gain_term, norm_mlp_term, loss, wide, tall,
     ) = middle_part(
-        seq_size, heads, scale, block_input, teacher, mask_values, norm_m[None, :], gain, mixed, heads_out, gate_out,
-        carr, out_s, wg_s, wu_s, down_s,
-    )
-    error_sum = loss[0, 0]
-    down_grad = sum_rows_back(down_grad)
-    out_grad = sum_rows_back(out_grad)
-    wg_grad = sum_columns_back(wg_grad)
-    wu_grad = sum_columns_back(wu_grad)
-    cots = lax.all_gather(cot.astype(BF16), "ctx")
-    grad_proj, last_rows, spill, gw, gcol, gtok, grow = recurrence_backward(
-        index_arr, maps, cots, state_in, proj_ext, conv_w, rowp, colp, tokp, grad_heads, saved, heads
-    )
-    rim_back = passed_along(spill, "ctx", -1)
-    grad_proj = lax.dynamic_update_slice_in_dim(grad_proj, (last_rows + rim_back).astype(BF16), rows - 8, 0)
-    grad_beta = jnp.swapaxes(gcol[:, :, 0::2].reshape(rows, NH, heads), 1, 2)
-    grad_cum = jnp.sum(
-        (gcol[:, :, 1::2] - jnp.swapaxes(grow, 1, 2)).reshape(blocks, BLOCK_LEN, NH, heads), axis=2
-    ) + gtok
-    grad_logs = jnp.einsum("ts,bth->bsh", lower, grad_cum, precision=lax.Precision.HIGHEST).reshape(rows, heads)
-    grad_scal_f, grad_alog, grad_dt = gates_back((grad_beta, grad_logs * (1.0 - starts)[:, None]))
-    grad_scal = grad_scal_f.reshape(rows, heads * (NH + 1)).astype(BF16)
-
-    grad_normed = sum_tokens(
-        dot_t(grad_proj, mix_s) + dot_t(grad_scal, scal_s) + dot_t(grad_gate_out, gate_s)
-    )
-    grad_in_norm, norm_attn_term = norm_in_back(grad_normed)
-    input_grad = grad_middle + grad_in_norm
-    mix_grad = sum_columns_back(t_dot(normed, grad_proj))
-    scal_grad = sum_columns_back(t_dot(normed, grad_scal))
-    gate_grad = sum_columns_back(t_dot(normed, grad_gate_out))
-    conv_grad = lax.psum_scatter(jnp.flip(gw[:CONV], 0).T, "ctx", scatter_dimension=0, tiled=True)
+        seq_size, heads, pieces, scale, block_input, teacher, mask_values, norm_m[None, :], gain, mixed, heads_out,
+        gate_out, carr, out_s, wg_s, wu_s, down_s,
+    )
+    by_chip = lambda v: v.reshape(pieces // 2, 2, *v.shape[1:])
+    grad_proj, fixed_rows, gw, grad_scal, gsum, wide_sum, tall_sum = recurrence_backward(
+        maps, cot, state_in, proj_ext, conv_w, rowp, colp, tokp, grad_heads, saved, by_chip(wide), by_chip(tall),
+        heads, pieces,
+    )
+    grad_proj = lax.dynamic_update_slice_in_dim(grad_proj, fixed_rows, rows - 8, 0)
+    deep = w_down.shape[0]
+    down_grad, out_grad = tall_sum[:deep], tall_sum[tall_sum.shape[0] - held :]
+    conv_terms = jnp.flip(gw[:CONV], 0).T.reshape(pieces, held, -1)
+    conv_at = norm_at + 3 - scal_at
+    conv_cols = conv_terms.shape[2]
+    conv_terms = jnp.pad(conv_terms, ((0, 0), (0, 0), (conv_at, HEAD - conv_at - conv_cols)))
     pick = (jnp.arange(HEADS)[None, :] == head_start + jnp.arange(heads)[:, None]).astype(F32)
+    ends = jnp.concatenate(
+        [
+            jnp.sum(gsum[:heads, 0:1] * pick, axis=0), jnp.sum(gsum[:heads, 1:2] * pick, axis=0), loss[0, :1],
+            jnp.zeros((HEAD - 2 * HEADS - 1,), F32),
+        ]
+    )
     small = jnp.concatenate(
         [
-            gain_term[0], jnp.sum(grad_alog[:, None] * pick, axis=0), jnp.sum(grad_dt[:, None] * pick, axis=0),
-            error_sum[None], norm_attn_term, norm_mlp_term[0],
-        ]
-    )
-    small = lax.psum(small, BOTH)
-    mean_loss = small[HEAD + 2 * HEADS] / (D * valid_count)
-    norm_start = HEAD + 2 * HEADS + 1
-    own = norm_attn.shape[0]
-    place = (rank * lax.axis_size("ctx") + index) * own
+            gain_term, ends[None], jnp.zeros((6, HEAD), F32), norm_mlp_term.reshape(-1, HEAD),
+            jnp.zeros((D // HEAD, HEAD), F32),
+        ],
+        axis=0,
+    )
+    input_grad, mix_grad, gate_grad, tails, small, wide_out = final_part(
+        seq_size, pieces, grad_proj, grad_gate_out, grad_scal, weights, normed, block_input, grad_middle,
+        norm_a[None, :], conv_terms, small, wide_sum.reshape(2, seq_size, held, inner),
+    )
+    scal_grad = jnp.swapaxes(tails[:, :, :scal_cols], 0, 1).reshape(held, -1)
+    conv_grad = lax.dynamic_index_in_dim(tails, rank, 0, False)[:, conv_at : conv_at + conv_cols].reshape(-1, CONV)
+    across = lambda v: jnp.swapaxes(v, 0, 1).reshape(held, FF).astype(F32)
+    mean_loss = small[1, 2 * HEADS] / (D * valid_count)
+    place = (rank * pieces + index) * held
+    norms = small[8:].reshape(2, D)
     return (
         final_out,
         mean_loss,
@@ -1048,13 +1345,13 @@
         gate_grad,
         out_grad,
         conv_grad,
-        lax.dynamic_slice_in_dim(small, norm_start + place, own),
-        lax.dynamic_slice_in_dim(small, norm_start + D + place, own),
-        small[:HEAD],
-        small[HEAD : HEAD + HEADS],
-        small[HEAD + HEADS : HEAD + 2 * HEADS],
-        wg_grad,
-        wu_grad,
+        lax.dynamic_slice_in_dim(norms[1], place, held),
+        lax.dynamic_slice_in_dim(norms[0], place, held),
+        small[0],
+        small[1, :HEADS],
+        small[1, HEADS : 2 * HEADS],
+        across(wide_out[:, 0]),
+        across(wide_out[:, 1]),
         down_grad,
     )
 

time: 594 us -> 426 us (0.72)
  waiting for transfers between devices: 120 us -> 0 us
  Pallas kernels: 235 us -> 340 us
  blocking collectives: 85.1 us -> 0 us
  starting transfers between devices: 26 us -> 0 us
  matrix products: 20.5 us -> 5.39 us
  between operations: 17 us -> 3.69 us
  other arithmetic: 19.6 us -> 11.9 us
    pallas_call x1 -> x2, Pallas kernels: 25.8 us -> 131 us  [the longest x1 66.7 us: recurrence_backward(): pl.pallas_call(functools.partial(bwd_kernel, heads, pieces, blocks), grid...]
    unnamed x6 -> x0, waiting for transfers between devices: 102 us -> none
    psum x1 -> x0, blocking collectives: 40.4 us -> none  [local(): small = lax.psum(small, BOTH)]
    unnamed x1 -> x0, blocking collectives: 29.8 us -> none
    all_to_all x6 -> x0, starting transfers between devices: 24.5 us -> none  [the longest x5 20.2 us: sum_columns_back(): lax.all_to_all(mine.reshape(-1, cols), 'seq', split_axis=0, concat_axis=1...]
    all_to_all x6 -> x0, waiting for transfers between devices: 17.8 us -> none  [the longest x5 10.6 us: sum_columns_back(): lax.all_to_all(mine.reshape(-1, cols), 'seq', split_axis=0, concat_axis=1...]
    dot_general x7 -> x0, matrix products: 16.1 us -> none  [the longest x3 7.49 us: t_dot(): return jnp.einsum('tr,tc->rc', a, b, preferred_element_type=F32)]
    all_gather x1 -> x0, blocking collectives: 14.8 us -> none  [local(): cots = lax.all_gather(cot.astype(BF16), 'ctx')]
  transfers between devices with their start and end apart: 11 -> 0, of which waited for: 6 -> 0; matrix products, arithmetic and copies ran while one was open for 9% -> 0% of each run, Pallas kernels for 0% -> 0%
where the time goes in v4:
time: 426 us; the launch traced here: 425 us
  Pallas kernels  340 us (80%)
  local copies, waits for them, and re-layouts  64.1 us (15%)
  other arithmetic  11.9 us (3%)
  matrix products  5.39 us (1%)
    pallas_call x1, Pallas kernels, middle_part(): pl.pallas_call(functools.partial(middle_kernel, size, heads), in_specs=[p...  90 us
    pallas_call x1, Pallas kernels, recurrence_forward(): pl.pallas_call(functools.partial(fwd_kernel, heads, pieces), grid=(blocks...  73.3 us
    pallas_call x1, Pallas kernels, recurrence_backward(): pl.pallas_call(functools.partial(bwd_kernel, heads, pieces, blocks), grid...  66.7 us
    pallas_call x1, Pallas kernels, final_part(): pl.pallas_call(functools.partial(final_kernel, size, pieces), in_specs=[v...  64.3 us
    pallas_call x1, Pallas kernels, start_gather(): pl.pallas_call(functools.partial(start_kernel, size, pieces), in_specs=[a...  44.7 us
    unnamed x88, local copies, waits for them, and re-layouts  23.4 us

profile of v4, /device:TPU:0, one launch (start us, length us, event | category | flops | bytes accessed | tf_op | source)
XLA Modules:
  0.0 424.6 jit_solution(4396386086942780714)
XLA Ops:
  0.7 1.3 convert_reduce_fusion.3
  9.0 0.8 copy.124
  10.8 0.8 copy.161
  11.6 1.2 reshape.330
  12.8 1.2 reshape.331
  14.8 0.9 concatenate.31.first_ref
  15.7 0.9 copy-done.5
  16.7 1.0 copy-done.8
  17.7 1.0 copy-done.10
  18.7 44.7 %start_gather.1 = (bf16[512,1024]{1,0:T(8,128)(2,1)S(1)}, bf16[16,1024]{1,0:T(8,128)(2,1)S(1)}, bf16[4,8,32,1664]{3,2,1,0:T(8,128)(2,1)S(1)}, bf16[4,2,32,704]{3,2,1,0:T(8,128)(2,1)S(1)}) custom-call(bf16[128,1024]{1,0:T(8,128)(2,1)S(1)} %copy-done.5, bf16[4,32,1664]{2,1,0:T(8,128)(2,1)S(1)} %copy-done.8, bf16[4,2,32,704]{3,2,1,0:T(8,128)(2,1)S(1)} %copy-done.10), custom_call_target="tpu_custom_call" | custom-call | tf_op jit(solution)/shard_map/start_gather/pallas_call | solution.py:353
  64.1 1.0 copy-done.4
  65.4 1.1 convert_reduce_fusion
  67.2 2.5 fusion.3
  70.5 2.0 reshape.358
  72.5 1.3 copy.129
  74.3 1.9 fusion.4
  77.5 0.8 copy.152
  78.6 1.6 copy.151
  80.2 1.6 copy.150
  81.9 1.2 fusion.30
  83.0 0.8 broadcast_in_dim.81
  83.9 2.3 concatenate.34.colp_ref
  86.3 1.1 slice.159.normed_ref
  87.4 3.4 convolution_convert_fusion.proj_ref
  90.9 73.3 %recurrence_forward.1 = (f32[512,256]{1,0:T(8,128)S(1)}, f32[512,256]{1,0:T(8,128)S(1)}, f32[2,128,128]{2,1,0:T(8,128)S(1)}, bf16[8,2,128,128]{3,2,1,0:T(8,128)(...) custom-call(bf16[528,1280]{1,0:T(8,128)(2,1)S(1)} %convolution_conve, ...), custom_call_target="tpu_custom_call" | custom-call | tf_op jit(solution)/shard_map/recurrence_forward/pallas_call | solution.py:499
  164.2 1.2 copy-done.9
  165.4 1.1 copy-done.11
  166.5 1.0 copy-done.13
  167.5 1.1 copy-done.14
  168.5 1.0 copy-done.15
  171.1 0.8 copy-done.19
  174.7 90.0 %middle_part.1 = (bf16[128,1024]{1,0:T(8,128)(2,1)}, f32[128,1024]{1,0:T(8,128)}, bf16[512,256]{1,0:T(8,128)(2,1)}, bf16[512,256]{1,0:T(8,128)(2,1)}, f32[2,128,...) custom-call(f32[1,1]{1,0:T(1,128)} %bitcast.10.scale_ref, ...), custom_call_target="tpu_custom_call" | custom-call | tf_op jit(solution)/shard_map/middle_part/pallas_call | solution.py:760
  264.7 1.2 slice.141
  265.9 66.7 %recurrence_backward.1 = (bf16[512,1280]{1,0:T(8,128)(2,1)}, bf16[8,1280]{1,0:T(8,128)(2,1)}, f32[8,1280]{1,0:T(8,128)}, bf16[512,128]{1,0:T(8,128)(2,1)}, f32[8...) custom-call(bf16[8,2,128,128]{3,2,1,0:T(8,128)(2,1)} %copy-done.17, ...), custom_call_target="tpu_custom_call" | custom-call | tf_op jit(solution)/shard_map/recurrence_backward/pallas_call | solution.py:977
  332.6 1.3 constant_dynamic-update-slice_fusion.5.gp_ref
  334.0 1.0 slice_reduce_fusion.2
  335.8 1.8 concatenate.38.small_ref
  338.6 1.6 slice.144
  340.2 1.7 slice.153
  343.1 64.3 %final_part.1 = (f32[128,1024]{1,0:T(8,128)}, f32[32,5120]{1,0:T(8,128)}, f32[32,1024]{1,0:T(8,128)}, f32[4,32,128]{2,1,0:T(8,128)}, f32[24,128]{1,0:T(8,128)}, /*index=5*/bf16[4,2,32,704]{3,2,1,0:T(8,128)(2,1)}) custom-call(bf16[512,1280]{1,0:T(8,128)(2,1)} %constant_dynamic-update-slice_fusion.5.gp_ref, bf16[512,256]{1,0:T(8,128)(2,1)} %get-tuple-element.92.gg_ref, ...), custom_call_target="tpu_custom_call" | custom-call | tf_op jit(solution)/shard_map/final_part/pallas_call | solution.py:1161
  407.4 1.3 slice.142
  409.4 1.2 slice_bitcast_fusion.5
  410.5 1.3 slice_bitcast_fusion.3
  414.5 0.8 slice_bitcast_fusion
  416.9 1.1 convert_bitcast_fusion
  418.3 1.0 reshape.357
  419.5 1.0 reshape.356
  422.0 0.8 copy.173
  (147 shorter events, 27.1 us)
Async XLA Ops:
  0.6 14.2 %copy-start.33 = (bf16[32,5120]{1,0:T(8,128)(2,1)S(1)}, bf16[32,5120]{1,0:T(8,128)(2,1)}, u32[]{:S(2)}) copy-start(bf16[32,5120]{1,0:T(8,128)(2,1)} %param.21) | copy-start | bytes 983044
  2.6 170.1 %copy-start.29 = (f32[1,128]{1,0:T(1,128)}, f32[1,128]{1,0:T(1,128)S(1)}, u32[]{:S(2)}) copy-start(f32[1,128]{1,0:T(1,128)S(1)} %bitcast_convert_fusion.gain_ref) | copy-start | bytes 1540
  15.7 0.9 copy-start.5
  16.7 1.0 copy-start.8
  17.7 1.0 copy-start.10
  63.4 0.8 copy-start.21
  64.1 1.0 copy-start.4
  64.1 10.2 %copy-start.1 = (bf16[4,8,32,1664]{3,2,1,0:T(8,128)(2,1)}, bf16[4,8,32,1664]{3,2,1,0:T(8,128)(2,1)S(1)}, u32[]{:S(2)}) copy-start(bf16[4,8,32,1664]{3,2,1,0:T(8,128)(2,1)S(1)} %get-tuple-element.62) | copy-start | bytes 10223620
  66.5 7.4 %copy-start.36 = (f32[1024]{0:T(1024)}, f32[1024]{0:T(1024)S(1)}, u32[]{:S(2)}) copy-start(f32[1024]{0:T(1024)S(1)} %get-tuple-element.172) | copy-start | bytes 12292
  74.3 16.5 %copy-start.23 = (f32[8,1280]{1,0:T(8,128)}, f32[8,1280]{1,0:T(8,128)S(1)}, u32[]{:S(2)}) copy-start(f32[8,1280]{1,0:T(8,128)S(1)} %pad.12.w_ref) | copy-start | bytes 122884
  76.5 96.3 %copy-start.3 = (f32[512,256]{1,0:T(8,128)}, f32[512,256]{1,0:T(8,128)S(1)}, u32[]{:S(2)}) copy-start(f32[512,256]{1,0:T(8,128)S(1)} %copy.153.gate_ref) | copy-start | bytes 1572868
  77.5 13.3 %copy-start.6 = (f32[8,64,14]{2,1,0:T(8,128)}, f32[8,64,14]{2,1,0:T(8,128)S(1)}, u32[]{:S(2)}) copy-start(f32[8,64,14]{2,1,0:T(8,128)S(1)} %copy.138.tokp_ref) | copy-start | bytes 86020
  83.9 2.5 copy-start.30
  86.1 4.7 %copy-start = (f32[8,128,6]{2,1,0:T(8,128)}, f32[8,128,6]{2,1,0:T(8,128)S(1)}, u32[]{:S(2)}) copy-start(f32[8,128,6]{2,1,0:T(8,128)S(1)} %concatenate.34.colp_ref) | copy-start | bytes 73732
  86.3 4.5 %copy-start.24 = (f32[8,6,128]{2,1,0:T(8,128)}, f32[8,6,128]{2,1,0:T(8,128)S(1)}, u32[]{:S(2)}) copy-start(f32[8,6,128]{2,1,0:T(8,128)S(1)} %copy.137.rowp_ref) | copy-start | bytes 73732
  87.4 3.4 copy-start.22
  87.4 3.4 copy-start.27
  87.4 3.4 copy-start.28
  90.9 82.5 %copy-start.2 = (bf16[528,1280]{1,0:T(8,128)(2,1)}, bf16[528,1280]{1,0:T(8,128)(2,1)S(1)}, u32[]{:S(2)}) copy-start(bf16[528,1280]{1,0:T(8,128)(2,1)S(1)} %convolution_convert_fusion.proj_ref) | copy-start | bytes 4055044
  164.2 1.2 copy-start.9
  165.4 1.1 copy-start.11
  166.5 1.0 copy-start.13
  167.5 1.1 copy-start.14
  168.5 1.0 copy-start.15
  169.5 0.8 copy-start.17
  170.3 0.8 copy-start.18
  171.1 0.8 copy-start.19
  171.9 0.8 copy-start.20
  172.7 2.0 copy-start.12
  172.7 2.0 copy-start.7
  172.7 92.0 %copy-start.16 = (f32[2,128,128]{2,1,0:T(8,128)}, f32[2,128,128]{2,1,0:T(8,128)S(1)}, u32[]{:S(2)}) copy-start(f32[2,128,128]{2,1,0:T(8,128)S(1)} %get-tuple-element.66.state_ref.sin_ref) | copy-start | bytes 393220
  173.3 0.7 copy-start.25
  174.0 0.7 copy-start.26
  265.9 69.8 %copy-start.37 = (f32[1,1024]{1,0:T(1,128)S(1)}, f32[1,1024]{1,0:T(1,128)}, u32[]{:S(2)}) copy-start(f32[1,1024]{1,0:T(1,128)} %get-tuple-element.99) | copy-start | bytes 12292
  265.9 69.8 %copy-start.38 = (f32[1,128]{1,0:T(1,128)S(1)}, f32[1,128]{1,0:T(1,128)}, u32[]{:S(2)}) copy-start(f32[1,128]{1,0:T(1,128)} %get-tuple-element.96) | copy-start | bytes 1540
  416.2 4.3 %copy-start.34 = (bf16[128,1024]{1,0:T(8,128)(2,1)S(1)}, bf16[128,1024]{1,0:T(8,128)(2,1)}, u32[]{:S(2)}) copy-start(bf16[128,1024]{1,0:T(8,128)(2,1)} %get-tuple-element.220) | copy-start | bytes 786436
  416.9 4.4 %copy-start.32 = (f32[128,1024]{1,0:T(8,128)S(1)}, f32[128,1024]{1,0:T(8,128)}, u32[]{:S(2)}) copy-start(f32[128,1024]{1,0:T(8,128)} %get-tuple-element.222) | copy-start | bytes 1572868
  418.0 4.0 copy-start.31
  419.3 3.6 copy-start.35

commit v5 on v4

--- a/solution.py
+++ b/solution.py
@@ -20,6 +20,7 @@
 WIDE = (1 + 2 * NH) * HEAD
 HALO = 16
 NORM_EPS = 1e-06
+VMEM_LIMIT = 60 << 20
 F32 = jnp.float32
 BF16 = jnp.bfloat16
 BOTH = ("seq", "ctx")
@@ -49,33 +50,52 @@
     return total
 
 
+def lanes_for(columns):
+    return -(-columns // HEAD) * HEAD
+
+
 def iota(shape, axis):
     return lax.broadcasted_iota(jnp.int32, shape, axis)
 
 
-def unit_lower_inverse(a):
-    n = a.shape[0]
+def unit_lower_inverses(systems):
+    n = systems[0].shape[0]
     ri, ci = iota((n, n), 0), iota((n, n), 1)
-    own = jnp.where(ri // 8 == ci // 8, a, 0.0)
     pick = (iota((n, 8), 0) % 8 == iota((n, 8), 1)).astype(BF16)
-    small = mm(own, pick).reshape(n // 8, 8, 8)
-    inv = (ri == ci).astype(F32).reshape(n // 8, 8, n)
+    own = ri // 8 == ci // 8
+    eye = (ri == ci).astype(F32).reshape(n // 8, 8, n)
+    small = [mm(jnp.where(own, a, 0.0), pick).reshape(n // 8, 8, 8) for a in systems]
+    inv = [eye for _ in systems]
     for j in range(7):
-        inv = inv - small[:, :, j : j + 1] * inv[:, j : j + 1, :]
-    inv = inv.reshape(n, n)
+        inv = [x - m[:, :, j : j + 1] * x[:, j : j + 1, :] for x, m in zip(inv, small)]
+    inv = [x.reshape(n, n) for x in inv]
     size = 8
     while size < n:
         off = (ri // (2 * size) == ci // (2 * size)) & (ri // size != ci // size)
-        inv = inv - mm(inv, mm(jnp.where(off, a, 0.0), inv))
+        right = [mm(jnp.where(off, a, 0.0), x) for a, x in zip(systems, inv)]
+        inv = [x - mm(x, y) for x, y in zip(inv, right)]
         size *= 2
     return inv
 
 
+DOC = 7
+LINK = DOC + 1
+
+
+def lane_of(h, what):
+    return h * (NH + 1) + what
+
+
+def column(table, lane):
+    return table[:, lane : lane + 1]
+
+
 def decays(rowp, colp, tokp, h):
-    cs_row, g_row = rowp[0:1, :], rowp[2 + 2 * h : 3 + 2 * h, :]
-    cs_col, g_col = colp[:, 0:1], colp[:, 2 + 2 * h : 3 + 2 * h]
-    cs_tok, g_tok = tokp[:, 3:4], tokp[:, 4 + h : 5 + h]
-    beta = colp[:, 3 + 2 * h : 4 + 2 * h]
+    g = lane_of(h, NH)
+    cs_row, g_row = rowp[DOC : DOC + 1, :], rowp[g : g + 1, :]
+    cs_col, g_col = column(colp, DOC), column(colp, g)
+    cs_tok, g_tok = column(tokp, DOC), column(tokp, g)
+    beta = column(colp, lane_of(h, 0))
     ri, ci = iota((ROWS, ROWS), 0), iota((ROWS, ROWS), 1)
     strict = (ri > ci) & (cs_col == cs_row)
     decay = jnp.where(strict, jnp.exp(jnp.where(strict, g_col - g_row, 0.0)), 0.0)
@@ -280,12 +300,15 @@
 
 
 def start_kernel(
-    size, pieces, x_ref, first_ref, later_ref, xfull_ref, halo_ref, full_ref, stage_ref,
-    local_sem, seq_send, seq_recv, line_send, line_recv, halo_sem,
+    size, pieces, x_ref, mix_ref, gate_ref, tail_ref, wg_ref, wu_ref, xfull_ref, halo_ref, full_ref, stage_ref,
+    sides, local_sem, seq_send, seq_recv, line_send, line_recv, halo_sem,
 ):
     me, here = lax.axis_index("seq"), lax.axis_index("ctx")
     count = x_ref.shape[0]
     core = lax.rem(here, 2)
+    inner = wg_ref.shape[1] // size
+    gate_at = mix_ref.shape[1] // size
+    tail_at = gate_at + gate_ref.shape[1] // size
     barrier = pltpu.get_barrier_semaphore()
     peers = [({"seq": lax.rem(me + i, size)}, here >= 0) for i in range(1, size)]
     side = [({"ctx": here + 1}, (core == 1) & (here < pieces - 1)), ({"ctx": here - 1}, (core == 0) & (here > 0))]
@@ -295,33 +318,50 @@
     def rows(q):
         return pl.ds(pl.multiple_of(q * count, count), count)
 
+    def cols(q, width):
+        return pl.ds(pl.multiple_of(q * width, HEAD), width)
+
+    def ends(n, q):
+        return [
+            (mix_ref.at[:, cols(q, gate_at)], full_ref.at[me, here, :, :gate_at]),
+            (gate_ref.at[:, cols(q, tail_at - gate_at)], full_ref.at[me, here, :, gate_at:tail_at]),
+            (tail_ref, full_ref.at[me, here, :, tail_at:]),
+            (x_ref, xfull_ref.at[rows(me)]),
+            (sides.at[q], stage_ref.at[me]),
+        ][n]
+
     def exchange(n, i):
         q = lax.rem(me + i, size)
-        source, target = [
-            (first_ref.at[q], full_ref.at[me, here]), (x_ref, xfull_ref.at[rows(me)]), (later_ref.at[q], stage_ref.at[me])
-        ][n]
+        source, target = ends(n, q)
         return pltpu.make_async_remote_copy(
             source, target, seq_send.at[n, i - 1], seq_recv.at[n, i - 1], device_id={"seq": q}, device_id_type=MESH
         )
 
     def own(n):
-        source, target = [
-            (first_ref.at[me], full_ref.at[me, here]), (x_ref, xfull_ref.at[rows(me)]), (later_ref.at[me], stage_ref.at[me])
-        ][n]
-        return pltpu.make_async_copy(source, target, local_sem.at[n])
-
-    for n in range(3):
+        return pltpu.make_async_copy(*ends(n, me), local_sem.at[n])
+
+    def begin(n):
         own(n).start()
         for i in range(1, size):
             exchange(n, i).start()
+
+    def end(n):
+        own(n).wait()
+        for i in range(1, size):
+            exchange(n, i).wait_recv()
+
+    for n in range(4):
+        begin(n)
+    sides[...] = jnp.zeros_like(sides)
+    for q in range(size):
+        sides[q, 0, :, :inner] = wg_ref[:, q * inner : (q + 1) * inner]
+        sides[q, 1, :, :inner] = wu_ref[:, q * inner : (q + 1) * inner]
     line = Line(pieces, [lambda c: full_ref.at[:, c]], line_send, line_recv)
-    own(0).wait()
-    for i in range(1, size):
-        exchange(0, i).wait_recv()
+    for n in range(3):
+        end(n)
     line.own()
-    own(1).wait()
-    for i in range(1, size):
-        exchange(1, i).wait_recv()
+    begin(4)
+    end(3)
     last = xfull_ref.at[pl.ds(size * count - HALO, HALO)]
     passing = pltpu.make_async_remote_copy(
         last, halo_ref, halo_sem.at[0], halo_sem.at[1], device_id={"ctx": here + 1}, device_id_type=MESH
@@ -330,134 +370,238 @@
 
     @pl.when(here == 0)
     def _():
-        filling = pltpu.make_async_copy(last, halo_ref, local_sem.at[3])
+        filling = pltpu.make_async_copy(last, halo_ref, local_sem.at[5])
         filling.start()
         filling.wait()
 
     for distance in range(1, pieces // 2):
         line.hop(distance)
     line.finish()
-    own(2).wait()
-    for i in range(1, size):
-        exchange(2, i).wait_recv()
+    end(4)
     pl.when(here > 0)(passing.wait_recv)
     pl.when(here < pieces - 1)(passing.wait_send)
-    for n in range(3):
+    for n in range(5):
         for i in range(1, size):
             exchange(n, i).wait_send()
 
 
-def start_gather(size, pieces, x, first, later):
+def start_gather(size, pieces, x, mix, gate, tail, w_gate, w_up):
     anywhere = pl.BlockSpec(memory_space=pl.ANY)
+    vmem = pl.BlockSpec(memory_space=pltpu.VMEM)
     out = lambda *dims: jax.ShapeDtypeStruct(dims, BF16)
+    dma = pltpu.SemaphoreType.DMA
+    held, padded = w_gate.shape[0], lanes_for(w_gate.shape[1] // size)
+    width = (mix.shape[1] + gate.shape[1]) // size + tail.shape[1]
     return pl.pallas_call(
         functools.partial(start_kernel, size, pieces),
-        in_specs=[anywhere] * 3,
+        in_specs=[anywhere] * 4 + [vmem] * 2,
         out_specs=[anywhere] * 4,
         out_shape=[
-            out(x.shape[0] * size, D), out(HALO, D), out(size, pieces, *first.shape[1:]), out(*later.shape),
+            out(x.shape[0] * size, D), out(HALO, D), out(size, pieces, held, width), out(size, 2, held, padded),
         ],
         scratch_shapes=[
-            pltpu.SemaphoreType.DMA((4,)), pltpu.SemaphoreType.DMA((3, size - 1)), pltpu.SemaphoreType.DMA((3, size - 1)),
-            pltpu.SemaphoreType.DMA((1, 3, pieces)), pltpu.SemaphoreType.DMA((1, pieces)), pltpu.SemaphoreType.DMA((2,)),
+            pltpu.VMEM((size, 2, held, padded), BF16),
+            dma((6,)), dma((5, size - 1)), dma((5, size - 1)), dma((1, 3, pieces)), dma((1, pieces)), dma((2,)),
         ],
         compiler_params=pltpu.CompilerParams(
-            vmem_limit_bytes=16 << 20, collective_id=2, has_side_effects=True
+            vmem_limit_bytes=VMEM_LIMIT, collective_id=2, has_side_effects=True
         ),
         name="start_gather",
-    )(x, first, later)
+    )(x, mix, gate, tail, w_gate, w_up)
+
+
+def exact(a, b, ca=1, cb=0):
+    return lax.dot_general(
+        a, b, (((ca,), (cb,)), ((), ())), precision=lax.Precision.HIGHEST, preferred_element_type=F32
+    )
+
+
+def tap_lanes(channels, tap, at):
+    lanes = iota((channels, HEAD), 1)
+    return (lanes == at + CONV * (iota((channels, HEAD), 0) % (WIDE // HEAD)) + tap).astype(BF16)
+
+
+def channel_rows(rows, channels):
+    return iota((rows, channels), 1) // (WIDE // HEAD) == iota((rows, channels), 0)
+
+
+def front_body(
+    heads, norm_at, rates_ref, x_ref, halo_ref, w_ref, marks_ref,
+    proj_ref, normed_ref, gate_ref, tok_ref, slope_ref, col_ref, row_ref, taps_ref, norms_ref,
+):
+    me = lax.axis_index("seq")
+    channels = heads * WIDE
+    tail_at = channels + heads * HEAD
+    rows = x_ref.shape[0]
+    own_rows = D * heads // HEADS
+
+    def dot(a, b, ca=1, cb=0):
+        return lax.dot_general(a, b, (((ca,), (cb,)), ((), ())), preferred_element_type=F32)
+
+    pick = (iota((8, HEAD), 1) == norm_at + iota((8, HEAD), 0)).astype(BF16)
+    norms_ref[...] = dot(pick, w_ref[:, tail_at:], 1, 1)
+
+    def normal(values):
+        values = values.astype(F32)
+        scale = lax.rsqrt(jnp.mean(values * values, axis=1, keepdims=True) + NORM_EPS)
+        return (values * scale * norms_ref[0:1, :]).astype(BF16)
+
+    early = normal(halo_ref[...])
+    normed_ref[...] = normal(x_ref[...])
+    proj_ref[:HALO] = dot(early, w_ref[:, :channels]).astype(BF16)
+    proj_ref[HALO:] = dot(normed_ref[...], w_ref[:, :channels]).astype(BF16)
+    gate_ref[...] = dot(normed_ref[...], w_ref[:, channels:tail_at])
+    tail = w_ref[pl.ds(pl.multiple_of(me * own_rows, own_rows), own_rows), tail_at:]
+    taps_ref[...] = jnp.zeros_like(taps_ref)
+    mine = channel_rows(own_rows, channels)
+    for lag in range(CONV):
+        spread = dot(tail, tap_lanes(channels, CONV - 1 - lag, norm_at + 3), 1, 1)
+        taps_ref[lag : lag + 1] = jnp.sum(jnp.where(mine, spread, 0.0), axis=0, keepdims=True)
+
+    raw = dot(normed_ref[...], w_ref[:, tail_at:]).astype(BF16).astype(F32)
+    raw = pltpu.roll(raw, lax.rem(HEAD - me * lane_of(heads, 0), HEAD), 1)
+    lane = iota((1, HEAD), 1)
+    rate, lift = jnp.zeros((1, HEAD), F32), jnp.zeros((1, HEAD), F32)
+    for h in range(heads):
+        here = lane == lane_of(h, NH)
+        rate = jnp.where(here, -jnp.exp(jnp.zeros((1, HEAD), F32) + rates_ref[0, me * heads + h]), rate)
+        lift = jnp.where(here, rates_ref[1, me * heads + h], lift)
+    is_log = (lane % (NH + 1) == NH) & (lane < lane_of(heads, 0))
+    lifted = raw + lift
+    sig = jax.nn.sigmoid(lifted)
+    logs = rate * (jnp.maximum(lifted, 0.0) + jnp.log1p(jnp.exp(-jnp.abs(lifted))))
+    slope_ref[...] = jnp.where(is_log, rate * sig, sig * (1.0 - sig)) * (lane < HEAD // 2) + pltpu.roll(
+        jnp.where(is_log, logs, 0.0), HEAD // 2, 1
+    )
+    place = (iota((8, HEAD), 1) == LINK + iota((8, HEAD), 0)) & (iota((8, HEAD), 0) < CONV - 1)
+    links = dot(marks_ref[...].astype(BF16), place.astype(BF16), 0, 0)
+    open_ = column(links, LINK)
+    summed = jnp.where(is_log, logs * open_, jnp.where(lane == DOC, 1.0 - open_, 0.0))
+    lower = (iota((BLOCK_LEN, BLOCK_LEN), 0) >= iota((BLOCK_LEN, BLOCK_LEN), 1)).astype(F32)
+    spread = (iota((ROWS, BLOCK_LEN), 0) // NH == iota((ROWS, BLOCK_LEN), 1)).astype(F32)
+    step = iota((ROWS, HEAD), 0) % NH
+    for b in range(rows // BLOCK_LEN):
+        span = slice(b * BLOCK_LEN, (b + 1) * BLOCK_LEN)
+        sums = exact(lower, summed[span])
+        tok = jnp.where(is_log | (lane == DOC), sums, jnp.where(lane < DOC, sig[span], links[span]))
+        tok_ref[span] = tok
+        wide = exact(spread, tok)
+        first = wide
+        for j in range(1, NH):
+            first = jnp.where(step == j, pltpu.roll(wide, HEAD - j, 1), first)
+        col = jnp.where(lane % (NH + 1) == 0, jnp.where(lane < lane_of(heads, 0), first, wide), wide)
+        col_ref[b * ROWS : (b + 1) * ROWS] = col
+        row_ref[b * 8 : (b + 1) * 8] = col.T[:8]
 
 
 def fwd_kernel(
-    heads, pieces, proj_ref, w_ref, rowp_ref, colp_ref, tokp_ref, stage_ref, wd_ref, wo_ref,
+    heads, pieces, steps, per, norm_at,
+    rates_ref, x_ref, halo_ref, full_ref, marks_ref, stage_ref, wo_ref,
+    proj_ref, normed_ref, gate_ref, tok_ref, slope_ref, col_ref, row_ref, taps_ref, norms_ref,
     oloc_ref, carr_ref, sin_ref, mapsout_ref, conv_ref, q_ref, k_ref, v_ref, t_ref, kk_ref, at_ref, uw_ref, pl_ref,
-    wgfull_ref, wufull_ref, wdfull_ref, wofull_ref,
-    state, weave, maps, local_sem, line_send, line_recv, map_send, map_recv,
+    wgfull_ref, wufull_ref, wofull_ref,
+    state, weave, maps, wgs, wus, wos, local_sem, line_send, line_recv, map_send, map_recv,
 ):
     step = pl.program_id(0)
-    steps = pl.num_programs(0)
     here = lax.axis_index("ctx")
     weights = Line(
-        pieces,
-        [
-            lambda c: wgfull_ref.at[:, c], lambda c: wufull_ref.at[:, c], lambda c: wdfull_ref.at[c],
-            lambda c: wofull_ref.at[c],
-        ],
-        line_send, line_recv,
+        pieces, [lambda c: wgs.at[:, c], lambda c: wus.at[:, c], lambda c: wos.at[c]], line_send, line_recv
     )
+    eye = (iota((HEAD, HEAD), 0) == iota((HEAD, HEAD), 1)).astype(F32)
 
     @pl.when(step == 0)
     def _():
-        barrier = pltpu.get_barrier_semaphore()
-        pl.semaphore_wait(barrier, greet(line_neighbours(pieces), barrier))
         owned = [
             pltpu.make_async_copy(source, target, local_sem.at[n])
             for n, (source, target) in enumerate(
-                [
-                    (stage_ref.at[:, 0], wgfull_ref.at[:, here]), (stage_ref.at[:, 1], wufull_ref.at[:, here]),
-                    (wd_ref, wdfull_ref.at[here]), (wo_ref, wofull_ref.at[here]),
-                ]
+                [(stage_ref.at[:, 0], wgs.at[:, here]), (stage_ref.at[:, 1], wus.at[:, here]), (wo_ref, wos.at[here])]
             )
         ]
         for copy in owned:
             copy.start()
+        barrier = pltpu.get_barrier_semaphore()
+        pl.semaphore_wait(barrier, greet(line_neighbours(pieces), barrier))
         for copy in owned:
             copy.wait()
         weights.own()
-
-    for distance in range(1, pieces // 2):
-        pl.when(step == (distance * steps) // (pieces // 2))(lambda distance=distance: weights.hop(distance))
-
-    eye = (iota((HEAD, HEAD), 0) == iota((HEAD, HEAD), 1)).astype(F32)
-
-    @pl.when(step == 0)
-    def _():
+        front_body(
+            heads, norm_at, rates_ref, x_ref, halo_ref, full_ref, marks_ref,
+            proj_ref, normed_ref, gate_ref, tok_ref, slope_ref, col_ref, row_ref, taps_ref, norms_ref,
+        )
         for h in range(heads):
             state[h, :, :HEAD] = eye
             state[h, :, HEAD:] = jnp.zeros((HEAD, HEAD), F32)
 
-    base = pl.multiple_of(step * BLOCK_LEN, BLOCK_LEN)
-    rowp, colp, tokp = rowp_ref[0], colp_ref[0], tokp_ref[0]
-    for h in range(heads):
-        cols = slice(h * WIDE, (h + 1) * WIDE)
-        ext = proj_ref[pl.ds(base, BLOCK_LEN + HALO), cols].astype(F32)
-        conv = ext[HALO:] * w_ref[0:1, cols]
+    hops = [(d * (steps + 1)) // (pieces // 2) for d in range(1, pieces // 2)]
+    for distance, at in enumerate(hops, 1):
+        if at < steps:
+            pl.when(step == at)(lambda distance=distance: weights.hop(distance))
+
+    items = [(j, h) for j in range(per) for h in range(heads)]
+    cols = lambda h: slice(h * WIDE, (h + 1) * WIDE)
+    span = lambda j, length=BLOCK_LEN: slice(j * length, (j + 1) * length)
+    tables = []
+    for j in range(per):
+        block = step * per + j
+        tables.append(
+            (
+                row_ref[pl.ds(pl.multiple_of(block * 8, 8), 8), :],
+                col_ref[pl.ds(pl.multiple_of(block * ROWS, ROWS), ROWS), :],
+                tok_ref[pl.ds(pl.multiple_of(block * BLOCK_LEN, BLOCK_LEN), BLOCK_LEN), :],
+            )
+        )
+    acts = []
+    for j, h in items:
+        base = pl.multiple_of((step * per + j) * BLOCK_LEN, BLOCK_LEN)
+        ext = proj_ref[pl.ds(base, BLOCK_LEN + HALO), cols(h)].astype(F32)
+        conv = ext[HALO:] * taps_ref[0:1, cols(h)]
         for lag in range(1, CONV):
-            conv = conv + tokp[:, lag - 1 : lag] * lag_rows(ext, lag) * w_ref[lag : lag + 1, cols]
-        conv_ref[:, cols] = conv
-        act = conv * jax.nn.sigmoid(conv)
+            conv = conv + column(tables[j][2], LINK + lag - 1) * lag_rows(ext, lag) * taps_ref[lag : lag + 1, cols(h)]
+        conv_ref[span(j), cols(h)] = conv
+        acts.append(conv * jax.nn.sigmoid(conv))
+    queries, keys, values = [], [], []
+    for n, act in enumerate(acts):
         unit = []
         for part in range(1 + NH):
             piece = act[:, part * HEAD : (part + 1) * HEAD]
             unit.append(piece * lax.rsqrt(jnp.sum(piece * piece, axis=1, keepdims=True) + NORM_EPS))
-        query = unit[0] * (1.0 / math.sqrt(HEAD))
+        queries.append(unit[0] * (1.0 / math.sqrt(HEAD)))
         for j in range(NH):
-            weave[2 * h, pl.ds(j, BLOCK_LEN, NH), :] = unit[1 + j]
-            weave[2 * h + 1, pl.ds(j, BLOCK_LEN, NH), :] = act[:, (1 + NH + j) * HEAD : (2 + NH + j) * HEAD]
-        keys, values = weave[2 * h], weave[2 * h + 1]
-        beta, decay, qdecay, carry, qcarry, dlast, clast = decays(rowp, colp, tokp, h)
-        kk = decay * mm(keys, keys, 1, 1)
-        inv = unit_lower_inverse(beta * kk)
-        uw = mm(inv, jnp.concatenate([beta * values, (beta * carry) * keys], axis=1))
-        attn = qdecay * mm(query, keys, 1, 1)
-        auw = mm(attn, uw)
-        nm = mm(dlast * keys, uw, 0, 0)
+            weave[2 * n, pl.ds(j, BLOCK_LEN, NH), :] = unit[1 + j]
+            weave[2 * n + 1, pl.ds(j, BLOCK_LEN, NH), :] = act[:, (1 + NH + j) * HEAD : (2 + NH + j) * HEAD]
+    for n in range(len(items)):
+        keys.append(weave[2 * n])
+        values.append(weave[2 * n + 1])
+    factors = [decays(*tables[j], h) for j, h in items]
+    grams = [mm(jnp.concatenate([q, k], axis=0), k, 1, 1) for q, k in zip(queries, keys)]
+    kks = [f[1] * g[BLOCK_LEN:] for f, g in zip(factors, grams)]
+    attns = [f[2] * g[:BLOCK_LEN] for f, g in zip(factors, grams)]
+    invs = unit_lower_inverses([f[0] * kk for f, kk in zip(factors, kks)])
+    uws = [
+        mm(inv, jnp.concatenate([f[0] * v, (f[0] * f[3]) * k], axis=1))
+        for inv, f, v, k in zip(invs, factors, values, keys)
+    ]
+    auws = [mm(attn, uw) for attn, uw in zip(attns, uws)]
+    nms = [mm(f[5] * k, uw, 0, 0) for f, k, uw in zip(factors, keys, uws)]
+    for n, (j, h) in enumerate(items):
         before = state[h]
-        out = mm(qcarry * query - auw[:, HEAD:], before)
+        f = factors[n]
+        both = mm(
+            jnp.concatenate([f[4] * queries[n] - auws[n][:, HEAD:], f[6] * eye - nms[n][:, HEAD:]], axis=0), before
+        )
         hc = slice(h * HEAD, (h + 1) * HEAD)
-        carr_ref[:, hc] = out[:, :HEAD]
-        oloc_ref[:, hc] = out[:, HEAD:] + auw[:, :HEAD]
-        after = mm(clast * eye - nm[:, HEAD:], before)
-        state[h, :, :HEAD] = after[:, :HEAD]
-        state[h, :, HEAD:] = after[:, HEAD:] + nm[:, :HEAD]
-        q_ref[0, h] = query
-        k_ref[0, h] = keys
-        v_ref[0, h] = values
-        t_ref[0, h] = inv
-        kk_ref[0, h] = kk
-        at_ref[0, h] = attn
-        uw_ref[0, h] = uw
-        pl_ref[0, h] = before
+        carr_ref[span(j), hc] = both[:BLOCK_LEN, :HEAD]
+        oloc_ref[span(j), hc] = both[:BLOCK_LEN, HEAD:] + auws[n][:, :HEAD]
+        state[h, :, :HEAD] = both[BLOCK_LEN:, :HEAD]
+        state[h, :, HEAD:] = both[BLOCK_LEN:, HEAD:] + nms[n][:, :HEAD]
+        q_ref[j, h] = queries[n]
+        k_ref[j, h] = keys[n]
+        v_ref[j, h] = values[n]
+        t_ref[j, h] = invs[n]
+        kk_ref[j, h] = kks[n]
+        at_ref[j, h] = attns[n]
+        uw_ref[j, h] = uws[n]
+        pl_ref[j, h] = before
 
     @pl.when(step == steps - 1)
     def _():
@@ -466,8 +610,9 @@
         line.own()
         for distance in range(1, pieces // 2):
             line.hop(distance)
+            if hops[distance - 1] >= steps:
+                weights.hop(distance)
         line.finish()
-        weights.finish()
 
         def hop(k, states):
             return tuple(
@@ -483,106 +628,105 @@
             return carry
 
         lax.fori_loop(0, pieces, keep, 0)
-
-
-def recurrence_forward(proj_ext, conv_w, rowp, colp, tokp, stage, w_down, w_out, heads, pieces):
-    blocks = rowp.shape[0]
-    rows = blocks * BLOCK_LEN
+        weights.finish()
+        given = [
+            pltpu.make_async_copy(source, target, local_sem.at[n])
+            for n, (source, target) in enumerate([(wgs, wgfull_ref), (wus, wufull_ref), (wos, wofull_ref)])
+        ]
+        for copy in given:
+            copy.start()
+        for copy in given:
+            copy.wait()
+
+
+def recurrence_forward(heads, pieces, norm_at, rates, x_full, halo, weights, marks, stage, w_out):
+    rows = x_full.shape[0]
+    blocks = rows // BLOCK_LEN
+    per = 2
+    size = stage.shape[0]
     whole = lambda *dims: pl.BlockSpec(dims, lambda i: (0,) * len(dims))
-    by_block = lambda *dims: pl.BlockSpec((1,) + dims, lambda i: (i,) + (0,) * len(dims))
-    token = lambda cols: pl.BlockSpec((BLOCK_LEN, cols), lambda i: (i, 0))
+    by_block = lambda *dims: pl.BlockSpec((per,) + dims, lambda i: (i,) + (0,) * len(dims))
+    token = lambda cols: pl.BlockSpec((per * BLOCK_LEN, cols), lambda i: (i, 0))
     shape = lambda *dims: jax.ShapeDtypeStruct(dims, F32)
     low_shape = lambda *dims: jax.ShapeDtypeStruct(dims, BF16)
-    anywhere = pl.BlockSpec(memory_space=pl.ANY)
+    hbm = pl.BlockSpec(memory_space=pltpu.HBM)
+    vmem = pl.BlockSpec(memory_space=pltpu.VMEM)
     square = (heads, ROWS, HEAD)
-    size = stage.shape[0]
+    dma = pltpu.SemaphoreType.DMA
+    side = (size, pieces, *stage.shape[2:])
+    front = [
+        low_shape(rows + HALO, heads * WIDE), low_shape(rows, D), shape(rows, heads * HEAD), shape(rows, HEAD),
+        shape(rows, HEAD), shape(blocks * ROWS, HEAD), shape(blocks * 8, ROWS), shape(8, heads * WIDE), shape(8, D),
+    ]
     return pl.pallas_call(
-        functools.partial(fwd_kernel, heads, pieces),
-        grid=(blocks,),
-        in_specs=[
-            whole(*proj_ext.shape), whole(*conv_w.shape),
-            by_block(*rowp.shape[1:]), by_block(*colp.shape[1:]), by_block(*tokp.shape[1:]),
-            anywhere, anywhere, anywhere,
-        ],
-        out_specs=[
+        functools.partial(fwd_kernel, heads, pieces, blocks // per, per, norm_at),
+        grid=(blocks // per,),
+        in_specs=[pl.BlockSpec(memory_space=pltpu.SMEM)] + [vmem] * 4 + [hbm] * 2,
+        out_specs=[whole(*f.shape) for f in front] + [
             token(heads * HEAD), token(heads * HEAD), whole(heads, HEAD, HEAD), whole(pieces, heads, HEAD, HEAD),
             token(heads * WIDE),
             by_block(heads, BLOCK_LEN, HEAD), by_block(*square), by_block(*square), by_block(*square),
             by_block(*square), by_block(heads, BLOCK_LEN, ROWS), by_block(heads, ROWS, 2 * HEAD),
-            by_block(heads, HEAD, 2 * HEAD), anywhere, anywhere, anywhere, anywhere,
+            by_block(heads, HEAD, 2 * HEAD), hbm, hbm, hbm,
         ],
-        out_shape=[
+        out_shape=front + [
             shape(rows, heads * HEAD), shape(rows, heads * HEAD), shape(heads, HEAD, HEAD),
             low_shape(pieces, heads, HEAD, HEAD), shape(rows, heads * WIDE),
             shape(blocks, heads, BLOCK_LEN, HEAD), shape(blocks, *square), shape(blocks, *square), shape(blocks, *square),
             shape(blocks, *square), shape(blocks, heads, BLOCK_LEN, ROWS), shape(blocks, heads, ROWS, 2 * HEAD),
             shape(blocks, heads, HEAD, 2 * HEAD),
-            low_shape(size, pieces, *stage.shape[2:]), low_shape(size, pieces, *stage.shape[2:]),
-            low_shape(pieces, *w_down.shape), low_shape(pieces, *w_out.shape),
+            low_shape(*side), low_shape(*side), low_shape(pieces, *w_out.shape),
         ],
         scratch_shapes=[
-            pltpu.VMEM((heads, HEAD, 2 * HEAD), F32), pltpu.VMEM((2 * heads, ROWS, HEAD), F32),
+            pltpu.VMEM((heads, HEAD, 2 * HEAD), F32), pltpu.VMEM((2 * heads * per, ROWS, HEAD), F32),
             pltpu.VMEM((pieces, heads, HEAD, 2 * HEAD), BF16),
-            pltpu.SemaphoreType.DMA((4,)), pltpu.SemaphoreType.DMA((4, 3, pieces)), pltpu.SemaphoreType.DMA((4, pieces)),
-            pltpu.SemaphoreType.DMA((1, 3, pieces)), pltpu.SemaphoreType.DMA((1, pieces)),
+            pltpu.VMEM(side, BF16), pltpu.VMEM(side, BF16), pltpu.VMEM((pieces, *w_out.shape), BF16),
+            dma((3,)), dma((3, 3, pieces)), dma((3, pieces)), dma((1, 3, pieces)), dma((1, pieces)),
         ],
         compiler_params=pltpu.CompilerParams(
-            vmem_limit_bytes=40 << 20, collective_id=3, has_side_effects=True
+            vmem_limit_bytes=VMEM_LIMIT, collective_id=3, has_side_effects=True
         ),
         name="recurrence_forward",
-    )(proj_ext, conv_w, rowp, colp, tokp, stage, w_down, w_out)
-
-
-def state_kernel(heads, state_ref, oloc_ref, carr_ref, gate_ref, gain_ref, heads_ref, mixed_ref):
-    for h in range(heads):
-        hc = slice(h * HEAD, (h + 1) * HEAD)
-        out = (oloc_ref[:, hc] + mm(carr_ref[:, hc], state_ref[h])).astype(BF16)
-        heads_ref[:, hc] = out
-        wide = out.astype(F32)
-        gate = gate_ref[:, hc]
-        scaled = wide * lax.rsqrt(jnp.mean(wide * wide, axis=1, keepdims=True) + NORM_EPS) * gain_ref[...]
-        mixed_ref[:, hc] = (scaled * (gate * jax.nn.sigmoid(gate))).astype(BF16)
-
-
-def state_and_gate(state, oloc, carr, gate_out, gain, heads):
-    rows = oloc.shape[0]
-    vmem = pl.BlockSpec(memory_space=pltpu.VMEM)
-    return pl.pallas_call(
-        functools.partial(state_kernel, heads),
-        in_specs=[vmem] * 5,
-        out_specs=[vmem] * 2,
-        out_shape=[
-            jax.ShapeDtypeStruct((rows, heads * HEAD), BF16),
-            jax.ShapeDtypeStruct((rows, heads * HEAD), BF16),
-        ],
-        compiler_params=pltpu.CompilerParams(vmem_limit_bytes=40 << 20),
-        name="state_and_gate",
-    )(state, oloc, carr, gate_out, gain)
-
-
-def seq_barrier(size):
-    me = lax.axis_index("seq")
-    barrier = pltpu.get_barrier_semaphore()
-
-    def greet(i, carry):
-        pl.semaphore_signal(barrier, inc=1, device_id={"seq": lax.rem(me + i, size)}, device_id_type=MESH)
-        return carry
-
-    lax.fori_loop(1, size, greet, 0)
-    pl.semaphore_wait(barrier, size - 1)
+    )(rates, x_full, halo, weights, marks, stage, w_out)
 
 
 def middle_kernel(
-    size, heads, scale_ref,
-    x_ref, teach_ref, mask_ref, norm_ref, gain_ref, mixed_ref, heads_ref, gate_ref, carr_ref,
-    wout_ref, wg_ref, wu_ref, wd_ref,
+    size, heads, token_total,
+    x_ref, teach_ref, mask_ref, norms_ref, gain_ref, *streams_and_rest,
+):
+    streams, rest = streams_and_rest[:8], streams_and_rest[8:]
+    middle_body(size, heads, token_total, x_ref, teach_ref, mask_ref, norms_ref, gain_ref, streams, *rest)
+
+
+def middle_body(
+    size, heads, token_total, x_ref, teach_ref, mask_ref, norms_ref, gain_ref, streams,
     final_ref, gmid_ref, ghead_ref, ggate_ref, cot_ref, ggain_ref, gnorm_ref, loss_ref,
     wide_ref, tall_ref,
+    oloc_ref, carr_ref, gate_ref, sin_ref, wout_ref, wg_ref, wu_ref, wd_ref, load_sem, heads_ref, mixed_ref,
+    line_send, line_recv, wds,
     second, branch, low, sent, got, own, mid, gfin, gates, ups, hidden, ggates, gups, send_sem, recv_sem,
 ):
     me = lax.axis_index("seq")
     count = x_ref.shape[0]
-    seq_barrier(size)
+    loads = [
+        pltpu.make_async_copy(source, target, load_sem.at[n])
+        for n, (source, target) in enumerate(
+            zip(streams, (oloc_ref, carr_ref, gate_ref, sin_ref, wout_ref, wg_ref, wu_ref, wds.at[lax.axis_index("ctx")]))
+        )
+    ]
+    for load in loads:
+        load.start()
+    pieces = wide_ref.shape[0]
+    barrier = pltpu.get_barrier_semaphore()
+    peers = [({"seq": lax.rem(me + i, size)}, me >= 0) for i in range(1, size)]
+    pl.semaphore_wait(barrier, greet(peers + line_neighbours(pieces), barrier))
+    loads[7].wait()
+    line = Line(pieces, [lambda c: wds.at[c]], line_send, line_recv)
+    line.own()
+    for load in loads[:5]:
+        load.wait()
+    norm = norms_ref[1:2, :]
+    gain = gain_ref[...].astype(F32)
 
     def dot(a, b, ca=1, cb=0):
         return lax.dot_general(a, b, (((ca,), (cb,)), ((), ())), preferred_element_type=F32)
@@ -639,14 +783,36 @@
 
     def out_part(k, carry):
         i = lax.rem(k + 1, size)
-        give_part(0, i, dot(mixed_ref[rows(lax.rem(me + i, size))], wout_ref[...]))
+        q = lax.rem(me + i, size)
+        for h in range(heads):
+            hc = slice(h * HEAD, (h + 1) * HEAD)
+            out = (oloc_ref[rows(q), hc] + mm(carr_ref[rows(q), hc], sin_ref[h])).astype(BF16)
+            heads_ref[rows(q), hc] = out
+            wide = out.astype(F32)
+            gate = gate_ref[rows(q), hc]
+            scaled = wide * lax.rsqrt(jnp.mean(wide * wide, axis=1, keepdims=True) + NORM_EPS) * gain
+            mixed_ref[rows(q), hc] = (scaled * (gate * jax.nn.sigmoid(gate))).astype(BF16)
+        give_part(0, i, dot(mixed_ref[rows(q)], wout_ref[...]))
         return carry
 
     lax.fori_loop(0, size, out_part, 0)
+    hops = pieces // 2 - 1
+    for distance in range(1, hops // 2 + 1):
+        line.hop(distance)
     middle = x_ref[...].astype(F32) + take_parts(0)
     mid[...] = middle
     inv = lax.rsqrt(jnp.mean(middle * middle, axis=1, keepdims=True) + NORM_EPS)
-    give_block(second, 3, (middle * inv * norm_ref[...]).astype(BF16))
+    give_block(second, 3, (middle * inv * norm).astype(BF16))
+    for load in loads[5:7]:
+        load.wait()
+    for distance in range(hops // 2 + 1, hops + 1):
+        line.hop(distance)
+    line.finish()
+    deep = wds.shape[1]
+    inner = pieces * deep
+    wd_ref[inner:] = jnp.zeros((wd_ref.shape[0] - inner, D), BF16)
+    for c in range(pieces):
+        wd_ref[c * deep : (c + 1) * deep] = wds[c]
 
     def feed(i, carry):
         q = take_block(second, 3, i)
@@ -664,11 +830,13 @@
     final = mid[...] + take_parts(1)
     final_ref[...] = final.astype(BF16)
     error = final - teach_ref[...].astype(F32)
-    weighted = mask_ref[...] * error
+    mask = jnp.broadcast_to(mask_ref[...].astype(F32), (count, count)).T[:, :1]
+    weighted = mask * error
     loss_ref[...] = jnp.broadcast_to(
         jnp.sum(jnp.sum(weighted * error, axis=1, keepdims=True), axis=0, keepdims=True), loss_ref.shape
     )
-    grad_final = scale_ref[0, 0] * weighted
+    valid = jnp.maximum(jnp.sum(norms_ref[2:3, :], axis=1, keepdims=True), 1.0)
+    grad_final = token_total / valid * weighted
     gfin[...] = grad_final
     give_block(branch, 4, grad_final.astype(BF16))
 
@@ -686,9 +854,7 @@
         return carry
 
     lax.fori_loop(0, size, feed_back, 0)
-    pieces = wide_ref.shape[0]
     held = D // (size * pieces)
-    deep = hidden.shape[1] // pieces
     wide_at = tall_ref.shape[1] - held
     tall_ref[...] = jnp.zeros_like(tall_ref)
     grad = dot(hidden[...], branch[...], 0, 0)
@@ -705,7 +871,7 @@
     inv = lax.rsqrt(jnp.mean(middle * middle, axis=1, keepdims=True) + NORM_EPS)
     unit = middle * inv
     gnorm_ref[...] = jnp.sum(gsecond * unit, axis=0, keepdims=True)
-    down = gsecond * norm_ref[...]
+    down = gsecond * norm
     gmid = gfin[...] + inv * (down - unit * jnp.mean(down * unit, axis=1, keepdims=True))
     gmid_ref[...] = gmid
     give_block(low, 5, gmid.astype(BF16))
@@ -715,7 +881,6 @@
     def out_back(i, carry):
         q = take_block(low, 5, i)
         gmixed = dot(low[rows(q)], wout_ref[...], 1, 1)
-        gain = gain_ref[...]
         for h in range(heads):
             hc = slice(h * HEAD, (h + 1) * HEAD)
             x = heads_ref[rows(q), hc].astype(F32)
@@ -750,40 +915,45 @@
     lax.fori_loop(1, size, sent_all, 0)
 
 
-def middle_part(size, heads, pieces, scale, x, teacher, mask, norm_m, gain, mixed, heads_out, gate_out, carr, wout, wg, wu, wd):
+def middle_part(
+    size, heads, pieces, token_total, x, teacher, mask, norms, gain, oloc, carr, gate_out, state_in, wout, wg, wu, wd
+):
     count = x.shape[0]
     rows = count * size
     inner = wg.shape[1]
-    held, deep = D // (size * pieces), inner // pieces
+    held, deep = D // (size * pieces), wd.shape[0]
     vmem = pl.BlockSpec(memory_space=pltpu.VMEM)
     out = lambda dims, kind: jax.ShapeDtypeStruct(dims, kind)
+    low = lambda *dims: pltpu.VMEM(dims, BF16)
+    high = lambda *dims: pltpu.VMEM(dims, F32)
+    dma = pltpu.SemaphoreType.DMA
     return pl.pallas_call(
-        functools.partial(middle_kernel, size, heads),
-        in_specs=[pl.BlockSpec(memory_space=pltpu.SMEM)] + [vmem] * 13,
+        functools.partial(middle_kernel, size, heads, float(token_total)),
+        in_specs=[vmem] * 5 + [pl.BlockSpec(memory_space=pltpu.HBM)] * 8,
         out_specs=[vmem] * 10,
         out_shape=[
             out((count, D), BF16), out((count, D), F32),
             out((rows, heads * HEAD), BF16), out((rows, heads * HEAD), BF16), out((heads, HEAD, HEAD), F32),
-            out((1, HEAD), F32), out((1, D), F32), out((8, HEAD), F32),
+            out((1, HEAD), F32), out((1, D), F32), out((1, HEAD), F32),
             out((pieces, 2 * size * held, inner), BF16), out((pieces, -(-deep // 16) * 16 + held, D), BF16),
         ],
         scratch_shapes=[
-            pltpu.VMEM((rows, D), BF16), pltpu.VMEM((rows, D), BF16), pltpu.VMEM((rows, D), BF16),
-            pltpu.VMEM((3, size - 1, count, D), BF16), pltpu.VMEM((3, size - 1, count, D), BF16),
-            pltpu.VMEM((count, D), F32), pltpu.VMEM((count, D), F32), pltpu.VMEM((count, D), F32),
-            pltpu.VMEM((rows, inner), F32), pltpu.VMEM((rows, inner), F32), pltpu.VMEM((rows, inner), BF16),
-            pltpu.VMEM((rows, inner), BF16), pltpu.VMEM((rows, inner), BF16),
-            pltpu.SemaphoreType.DMA((6, size - 1)), pltpu.SemaphoreType.DMA((6, size - 1)),
+            high(rows, heads * HEAD), high(rows, heads * HEAD), high(rows, heads * HEAD), high(heads, HEAD, HEAD),
+            low(*wout.shape), low(*wg.shape), low(*wu.shape), low(inner, D), dma((8,)),
+            low(rows, heads * HEAD), low(rows, heads * HEAD), dma((1, 3, pieces)), dma((1, pieces)), low(pieces, *wd.shape),
+            low(rows, D), low(rows, D), low(rows, D), low(3, size - 1, count, D), low(3, size - 1, count, D),
+            high(count, D), high(count, D), high(count, D), high(rows, inner), high(rows, inner), low(rows, inner),
+            low(rows, inner), low(rows, inner), dma((6, size - 1)), dma((6, size - 1)),
         ],
         compiler_params=pltpu.CompilerParams(
-            vmem_limit_bytes=56 << 20, collective_id=1, has_side_effects=True
+            vmem_limit_bytes=VMEM_LIMIT, collective_id=1, has_side_effects=True
         ),
         name="middle_part",
-    )(scale, x, teacher, mask, norm_m, gain, mixed, heads_out, gate_out, carr, wout, wg, wu, wd)
+    )(x, teacher, mask, norms, gain, oloc, carr, gate_out, state_in, wout, wg, wu, wd)
 
 
 def bwd_kernel(
-    heads, pieces, steps, maps_ref, cot_ref, sin_ref, proj_ref, w_ref, rowp_ref, colp_ref, tokp_ref,
+    heads, pieces, steps, maps_ref, cot_ref, sin_ref, proj_ref, w_ref, rowp_ref, colp_ref, tokp_ref, slope_ref,
     go_ref, conv_ref, q_ref, k_ref, v_ref, t_ref, kk_ref, at_ref, uw_ref, pl_ref, wide_ref, tall_ref,
     gproj_ref, fix_ref, gw_ref, gscal_ref, gsum_ref, widesum_ref, tallsum_ref,
     dstate, weave, rim, last, cots, rim_in, wtheirs, ttheirs, wheld, theld, wcame, tcame,
@@ -832,9 +1002,11 @@
             pl.when(step == when_round[r])(lambda r=r: line.round(r))
 
     base = pl.multiple_of(block * BLOCK_LEN, BLOCK_LEN)
-    rowp, colp, tokp = rowp_ref[0], colp_ref[0], tokp_ref[0]
+    rowp, colp, tokp = rowp_ref[...], colp_ref[...], tokp_ref[...]
     last_row = iota((ROWS, 1), 0) == ROWS - 1
     gscal = jnp.zeros((BLOCK_LEN, HEAD), F32)
+    slope = slope_ref[...]
+    first_lane = lax.axis_index("seq") * lane_of(heads, 0)
     for h in range(heads):
         cols = slice(h * WIDE, (h + 1) * WIDE)
         hc = slice(h * HEAD, (h + 1) * HEAD)
@@ -888,14 +1060,14 @@
         dg = sum(x[:, 1:2] for x in by_step) + jnp.sum(z2, axis=1, keepdims=True)
         dg = dg + qcarry * jnp.sum(query * gos, axis=1, keepdims=True)
         after = (iota((BLOCK_LEN, BLOCK_LEN), 0) <= iota((BLOCK_LEN, BLOCK_LEN), 1)).astype(BF16)
-        dlog = tokp[:, 0:1] * mm(after, jnp.broadcast_to(dg, (BLOCK_LEN, HEAD)))[:, :1]
-        at = 4 + heads + h * (NH + 2)
-        dscal = [by_step[j][:, 0:1] * tokp[:, at + j : at + j + 1] for j in range(NH)]
-        dscal.append(dlog * tokp[:, at + NH : at + NH + 1])
+        dlog = column(tokp, LINK) * mm(after, jnp.broadcast_to(dg, (BLOCK_LEN, HEAD)))[:, :1]
+        dscal = [by_step[j][:, 0:1] * column(slope, lane_of(h, j)) for j in range(NH)]
+        dscal.append(dlog * column(slope, lane_of(h, NH)))
         lane = iota((BLOCK_LEN, HEAD), 1)
         for j in range(NH + 1):
-            gscal = gscal + jnp.where(lane == h * (NH + 1) + j, dscal[j], 0.0)
-        sums = jnp.where(lane == 0, dlog * tokp[:, at + NH + 1 : at + NH + 2], jnp.where(lane == 1, dscal[NH], 0.0))
+            gscal = gscal + jnp.where(lane == first_lane + lane_of(h, j), dscal[j], 0.0)
+        logs = column(slope, HEAD // 2 + lane_of(h, NH))
+        sums = jnp.where(lane == 0, dlog * logs, jnp.where(lane == 1, dscal[NH], 0.0))
         gsum_ref[h : h + 1, :] += jnp.sum(sums, axis=0, keepdims=True)
         weave[2 * h] = dk
         weave[2 * h + 1] = dv
@@ -921,7 +1093,7 @@
         length = BLOCK_LEN + 8
         total = jnp.concatenate([zeros, dconv * w_ref[0:1, cols]], axis=0)
         for lag in range(1, CONV):
-            masked = tokp[:, lag - 1 : lag] * dconv
+            masked = column(tokp, LINK + lag - 1) * dconv
             gw_ref[lag : lag + 1, cols] += jnp.sum(masked * lag_rows(ext, lag), axis=0, keepdims=True)
             total = total + pltpu.roll(
                 jnp.concatenate([zeros, masked * w_ref[lag : lag + 1, cols]], axis=0), length - lag, 0
@@ -960,10 +1132,10 @@
 
 
 def recurrence_backward(
-    maps, cot, state_in, proj_ext, conv_w, rowp, colp, tokp, grad_heads, saved, wide, tall, heads, pieces
+    maps, cot, state_in, proj_ext, conv_w, rowp, colp, tokp, slopes, grad_heads, saved, wide, tall, heads, pieces
 ):
-    blocks = rowp.shape[0]
-    rows = blocks * BLOCK_LEN
+    rows = tokp.shape[0]
+    blocks = rows // BLOCK_LEN
     chips = pieces // 2
     whole = lambda *dims: pl.BlockSpec(dims, lambda i: (0,) * len(dims))
     by_block = lambda *dims: pl.BlockSpec((1,) + dims, lambda i: (blocks - 1 - i,) + (0,) * len(dims))
@@ -979,7 +1151,8 @@
         grid=(blocks,),
         in_specs=[
             vmem, vmem, vmem, vmem, vmem,
-            by_block(*rowp.shape[1:]), by_block(*colp.shape[1:]), by_block(*tokp.shape[1:]),
+            pl.BlockSpec((8, ROWS), lambda i: (blocks - 1 - i, 0)),
+            pl.BlockSpec((ROWS, HEAD), lambda i: (blocks - 1 - i, 0)), token(HEAD), token(HEAD),
             token(heads * HEAD), token(heads * WIDE),
             by_block(heads, BLOCK_LEN, HEAD), by_block(*square), by_block(*square), by_block(*square),
             by_block(*square), by_block(heads, BLOCK_LEN, ROWS), by_block(heads, ROWS, 2 * HEAD),
@@ -1003,20 +1176,30 @@
             dma((1, 3, pieces)), dma((1, pieces)), dma((2,)), dma((2,)), dma((2, chips)), dma((2, 2, chips)), dma((2,)),
         ],
         compiler_params=pltpu.CompilerParams(
-            vmem_limit_bytes=58 << 20, collective_id=4, has_side_effects=True
+            vmem_limit_bytes=VMEM_LIMIT, collective_id=4, has_side_effects=True
         ),
         name="recurrence_backward",
-    )(maps, cot, state_in, proj_ext, conv_w, rowp, colp, tokp, grad_heads, *saved, wide, tall)
+    )(maps, cot, state_in, proj_ext, conv_w, rowp, colp, tokp, slopes, grad_heads, *saved, wide, tall)
 
 
 def final_kernel(
-    size, pieces, gp_ref, gg_ref, gs_ref, w_ref, normed_ref, x_ref, gmid_ref, norm_ref, conv_ref, small_ref, wide_ref,
-    ingrad_ref, gmix_ref, ggate_ref, gtail_ref, total_ref, wideout_ref,
-    sent, got, own, turned, grads, theirs, held, came, blocks, around, along,
+    size, pieces, heads, norm_at, inner, gp_any, gg_any, gs_any, w_any, normed_any,
+    fix_ref, x_ref, gmid_ref, norms_ref, gw_ref, gain_ref, gsum_ref, loss_ref, gnorm_ref, wide_ref,
+    ingrad_ref, gmix_ref, ggate_ref, gtail_ref, gwg_ref, gwu_ref, mean_ref, ends_ref, both_ref,
+    gp_ref, gg_ref, gs_ref, w_ref, normed_ref, load_sem, wideout_ref,
+    sent, got, own, turned, grads, theirs, held, came, blocks, around, along, summed,
     local_sem, seq_send, seq_recv, pair_send, pair_recv, line_send, line_recv, ctx_send, ctx_recv,
 ):
     me, here = lax.axis_index("seq"), lax.axis_index("ctx")
     count = x_ref.shape[0]
+    loads = [
+        pltpu.make_async_copy(source, target, load_sem.at[n])
+        for n, (source, target) in enumerate(
+            [(gp_any, gp_ref), (gg_any, gg_ref), (gs_any, gs_ref), (w_any, w_ref), (normed_any, normed_ref)]
+        )
+    ]
+    for load in loads:
+        load.start()
     barrier = pltpu.get_barrier_semaphore()
     peers = [({"seq": lax.rem(me + i, size)}, here >= 0) for i in range(1, size)]
     peers += [({"ctx": lax.rem(here + i, pieces)}, here >= 0) for i in range(1, pieces)]
@@ -1049,6 +1232,9 @@
     for i in range(1, size):
         to_peer(1, i).start()
     gate_at, tail_at = gp_ref.shape[1], gp_ref.shape[1] + gg_ref.shape[1]
+    for load in loads:
+        load.wait()
+    gp_ref[gp_ref.shape[0] - 8 :] = fix_ref[...]
 
     def part(k, carry):
         i = lax.rem(k + 1, size)
@@ -1085,9 +1271,15 @@
                 for c in range(pieces):
                     row = (r * pieces + c) * rank_rows
                     grads[c // 2, c % 2, r, :, at + first : at + first + cols] = grad[row : row + rank_rows].astype(BF16)
+    channels = gw_ref.shape[1]
+    mine = channel_rows(D // size, channels)
+    taps = jnp.zeros((D // size, HEAD), F32)
+    for lag in range(CONV):
+        spread = jnp.where(mine, gw_ref[lag : lag + 1], 0.0).astype(BF16)
+        taps = taps + dot(spread, tap_lanes(channels, CONV - 1 - lag, norm_at + 3))
     for c in range(pieces):
         grads[c // 2, c % 2, me, :, tail_at:] = (
-            grads[c // 2, c % 2, me, :, tail_at:].astype(F32) + conv_ref[c]
+            grads[c // 2, c % 2, me, :, tail_at:].astype(F32) + taps[c * rank_rows : (c + 1) * rank_rows]
         ).astype(BF16)
     pair = Siblings([grads], [theirs], [held], pair_send, pair_recv)
     pair.start()
@@ -1100,14 +1292,20 @@
     x = x_ref[...].astype(F32)
     inv = lax.rsqrt(jnp.mean(x * x, axis=1, keepdims=True) + NORM_EPS)
     unit = x * inv
-    down = gnormed * norm_ref[...]
+    down = gnormed * norms_ref[0:1, :]
     ingrad_ref[...] = gmid_ref[...] + inv * (down - unit * jnp.mean(down * unit, axis=1, keepdims=True))
     term = jnp.sum(gnormed * unit, axis=0, keepdims=True)
-    around[me] = small_ref[...]
+    lane = iota((1, HEAD), 1)
+    ends = jnp.where(lane == 2 * HEADS, loss_ref[...], 0.0)
+    for h in range(heads):
+        for n in range(2):
+            ends = jnp.where(lane == n * HEADS + me * heads + h, gsum_ref[h : h + 1, n : n + 1], ends)
+    around[me] = jnp.zeros(around.shape[1:], F32)
+    around[me, 0:1] = gain_ref[...]
+    around[me, 1:2] = ends
     for j in range(D // HEAD):
-        around[me, small_ref.shape[0] - D // HEAD + j : small_ref.shape[0] - D // HEAD + j + 1] = term[
-            :, j * HEAD : (j + 1) * HEAD
-        ]
+        around[me, 8 + j : 9 + j] = term[:, j * HEAD : (j + 1) * HEAD]
+        around[me, 8 + D // HEAD + j : 9 + D // HEAD + j] = gnorm_ref[:, j * HEAD : (j + 1) * HEAD]
     for i in range(1, size):
         to_peer(2, i).start()
     pair.add()
@@ -1132,227 +1330,149 @@
     total = along[0]
     for c in range(1, pieces):
         total = total + along[c]
-    total_ref[...] = total
+    ends_ref[...] = total[:2]
+    valid = jnp.maximum(jnp.sum(norms_ref[2:3, :], axis=1, keepdims=True), 1.0)
+    mean_ref[...] = total[1:2, 2 * HEADS : 2 * HEADS + 1] / (D * valid)
+    summed[...] = total
+    place = (me * pieces + here) * rank_rows
+    for n in range(2):
+        row = summed[pl.ds(8 + n * (D // HEAD) + place // HEAD, 1), :]
+        both_ref[n : n + 1, :] = pltpu.roll(row, lax.rem(HEAD - lax.rem(place, HEAD), HEAD), 1)
+    tail = jnp.zeros((rank_rows, HEAD), F32)
+    kept.wait()
     for i in range(1, size):
         to_peer(3, i).wait_recv()
+        to_peer(1, i).wait_recv()
     for r in range(size):
         block = blocks[r].astype(F32)
         gmix_ref[:, r * gate_at : (r + 1) * gate_at] = block[:, :gate_at]
         ggate_ref[:, r * (tail_at - gate_at) : (r + 1) * (tail_at - gate_at)] = block[:, gate_at:tail_at]
-        gtail_ref[r] = block[:, tail_at:]
-    kept.wait()
+        tail = tail + block[:, tail_at:]
+        gwg_ref[:, r * inner : (r + 1) * inner] = wideout_ref[r, 0, :, :inner].astype(F32)
+        gwu_ref[:, r * inner : (r + 1) * inner] = wideout_ref[r, 1, :, :inner].astype(F32)
+    gtail_ref[...] = tail
     pair.left()
     for i in range(1, size):
-        to_peer(1, i).wait_recv()
         for n in range(4):
             to_peer(n, i).wait_send()
     for i in range(1, pieces):
         to_piece(i).wait_send()
 
 
-def final_part(size, pieces, gp, gg, gs, weights, normed, x, gmid, norm_a, conv, small, wide):
+def final_part(
+    size, pieces, heads, norm_at, gp, gg, gs, weights, normed, fix, x, gmid, norms, gw, gain, gsum, loss, gnorm, wide
+):
     count = x.shape[0]
     chips = pieces // 2
-    held = D // (size * pieces)
+    held, inner = D // (size * pieces), FF // size
     width = weights.shape[1]
+    small = (8 + 2 * (D // HEAD), HEAD)
     vmem = pl.BlockSpec(memory_space=pltpu.VMEM)
-    out = lambda dims, kind=F32: jax.ShapeDtypeStruct(dims, kind)
+    out = lambda *dims: jax.ShapeDtypeStruct(dims, F32)
+    low = lambda *dims: pltpu.VMEM(dims, BF16)
+    high = lambda *dims: pltpu.VMEM(dims, F32)
     dma = pltpu.SemaphoreType.DMA
     return pl.pallas_call(
-        functools.partial(final_kernel, size, pieces),
-        in_specs=[vmem] * 11,
-        out_specs=[vmem] * 6,
+        functools.partial(final_kernel, size, pieces, heads, norm_at, inner),
+        in_specs=[pl.BlockSpec(memory_space=pl.ANY)] * 5 + [vmem] * 10,
+        out_specs=[vmem] * 9,
         out_shape=[
-            out((count, D)), out((held, size * gp.shape[1])), out((held, size * gg.shape[1])),
-            out((size, held, gs.shape[1])), out(small.shape), out((size, 2, held, wide.shape[3]), BF16),
+            out(count, D), out(held, size * gp.shape[1]), out(held, size * gg.shape[1]), out(held, HEAD),
+            out(held, size * inner), out(held, size * inner), out(1, 1), out(2, HEAD), out(2, HEAD),
         ],
         scratch_shapes=[
-            pltpu.VMEM((size - 1, count, D), BF16), pltpu.VMEM((size - 1, count, D), BF16), pltpu.VMEM((count, D), F32),
-            pltpu.VMEM((D, normed.shape[0]), BF16),
-            pltpu.VMEM((chips, 2, size, held, width), BF16), pltpu.VMEM((chips, size, held, width), BF16),
-            pltpu.VMEM((chips, size, held, width), BF16), pltpu.VMEM((2, chips, size, held, width), BF16),
-            pltpu.VMEM((size, held, width), BF16), pltpu.VMEM((size, *small.shape), F32),
-            pltpu.VMEM((pieces, *small.shape), F32),
+            low(*gp.shape), low(*gg.shape), low(*gs.shape), low(*weights.shape), low(*normed.shape), dma((5,)),
+            low(size, 2, held, wide.shape[3]),
+            low(size - 1, count, D), low(size - 1, count, D), high(count, D), low(D, normed.shape[0]),
+            low(chips, 2, size, held, width), low(chips, size, held, width), low(chips, size, held, width),
+            low(2, chips, size, held, width), low(size, held, width), high(size, *small), high(pieces, *small), high(*small),
             dma((1,)), dma((4, size - 1)), dma((4, size - 1)), dma((1,)), dma((1,)), dma((1, chips)), dma((1, 2, chips)),
             dma((pieces - 1,)), dma((pieces - 1,)),
         ],
         compiler_params=pltpu.CompilerParams(
-            vmem_limit_bytes=60 << 20, collective_id=5, has_side_effects=True
+            vmem_limit_bytes=VMEM_LIMIT, collective_id=5, has_side_effects=True
         ),
         name="final_part",
-    )(gp, gg, gs, weights, normed, x, gmid, norm_a, conv, small, wide)
-
-
-def rms_scale(values, gain_vec):
-    return values * lax.rsqrt(jnp.mean(values * values, axis=-1, keepdims=True) + NORM_EPS) * gain_vec
-
-
-def dot(a, b):
-    return jnp.dot(a, b, preferred_element_type=F32)
+    )(gp, gg, gs, weights, normed, fix, x, gmid, norms, gw, gain, gsum, loss, gnorm, wide)
 
 
 def local(
     block_input, teacher, valid_mask, segments, mix_proj, scalar_proj, gate_proj, out_proj, conv_weight,
     norm_attn, norm_mlp, head_gain, a_log, dt_bias, w_gate, w_up, w_down,
 ):
-    seq_size = lax.axis_size("seq")
+    seq_size, pieces = lax.axis_size("seq"), lax.axis_size("ctx")
     heads = HEADS // seq_size
-    tok_rows = block_input.shape[0]
-    rows = tok_rows * seq_size
-    blocks = rows // BLOCK_LEN
+    rows = block_input.shape[0] * seq_size
     token_total = segments.shape[0]
     seq_length = min(SEQ_LEN, token_total)
     index = lax.axis_index("ctx")
-    rank = lax.axis_index("seq")
-    head_start = rank * heads
-
-    pieces = lax.axis_size("ctx")
-    inner = FF // seq_size
     held = mix_proj.shape[0]
-    scal_cols = heads * (NH + 1)
+    scal_cols = HEADS * (NH + 1)
+    norm_at, taps_at = scal_cols, scal_cols + 3
+    taps_end = taps_at + CONV * conv_weight.shape[0] // held
+
     count_here = jnp.sum(valid_mask.astype(F32)).astype(BF16)
-    extra = jnp.concatenate(
+    tail = jnp.concatenate(
         [
-            norm_attn[:, None], norm_mlp[:, None],
-            jnp.where(jnp.arange(held) == 0, count_here, jnp.zeros((), BF16))[:, None],
-            conv_weight.reshape(held, -1),
+            scalar_proj, norm_attn[:, None], norm_mlp[:, None],
+            jnp.where(iota((held, 1), 0) == 0, count_here, jnp.zeros((), BF16)),
+            conv_weight.reshape(held, -1), jnp.zeros((held, HEAD - taps_end), BF16),
         ],
         axis=1,
     )
-    by_rank = lambda w: jnp.swapaxes(w.reshape(held, seq_size, -1), 0, 1)
-    first = jnp.concatenate(
-        [
-            by_rank(mix_proj), by_rank(gate_proj), by_rank(scalar_proj),
-            jnp.broadcast_to(extra[None], (seq_size, *extra.shape)),
-            jnp.zeros((seq_size, held, HEAD - scal_cols - extra.shape[1]), BF16),
-        ],
-        axis=2,
+    x_full, halo, gathered, stage = start_gather(
+        seq_size, pieces, block_input, mix_proj, gate_proj, tail, w_gate, w_up
     )
-    later = jnp.stack([by_rank(w_gate), by_rank(w_up)], axis=1)
-    x_full, halo, gathered, stage = start_gather(seq_size, pieces, block_input, first, later)
     weights = gathered.reshape(D, -1)
-    gate_at = heads * WIDE
-    scal_at = gate_at + heads * HEAD
-    norm_at = scal_at + scal_cols
-    norm_a = weights[:, norm_at].astype(F32)
-    norm_m = weights[:, norm_at + 1].astype(F32)
-    valid_count = jnp.maximum(jnp.sum(weights[:, norm_at + 2].astype(F32)), 1.0)
-    conv_s = lax.dynamic_slice_in_dim(weights[:, norm_at + 3 : norm_at + extra.shape[1]], rank * (D // seq_size), D // seq_size)
-    conv_s = conv_s.reshape(heads * WIDE, CONV)
-
-    extended = jnp.concatenate([halo, x_full], axis=0).astype(F32)
-    normed_ext = rms_scale(extended, norm_a).astype(BF16)
-    normed = normed_ext[HALO:]
-    proj_ext = dot(normed_ext, weights[:, :gate_at]).astype(BF16)
-    rest = dot(normed, weights[:, gate_at:])
-    gate_out = rest[:, : heads * HEAD]
-    scal = rest[:, heads * HEAD : heads * HEAD + scal_cols].astype(BF16)
-
     piece_start = index * rows
     window = lax.dynamic_slice_in_dim(jnp.pad(segments, (CONV, 0)), piece_start, rows + CONV)
     place_in = (piece_start + jnp.arange(rows, dtype=jnp.int32)) % seq_length
-    own_seg = window[CONV:]
-    linked = [
-        ((window[CONV - lag : CONV - lag + rows] == own_seg) & (place_in >= lag)).astype(F32) for lag in range(1, CONV)
-    ]
-    starts = 1.0 - linked[0]
-    alog_heads = lax.dynamic_slice_in_dim(a_log.astype(F32), head_start, heads, 0)
-    dt_heads = lax.dynamic_slice_in_dim(dt_bias.astype(F32), head_start, heads, 0)
-    scal = scal.astype(F32).reshape(rows, heads, NH + 1)
-    beta = jax.nn.sigmoid(scal[:, :, :NH])
-    rate = -jnp.exp(alog_heads)[None, :]
-    lifted = scal[:, :, NH] + dt_heads[None, :]
-    logs = rate * jax.nn.softplus(lifted)
-    slopes = jnp.concatenate(
-        [beta * (1.0 - beta), (rate * jax.nn.sigmoid(lifted))[:, :, None], logs[:, :, None]], axis=2
-    ).reshape(blocks, BLOCK_LEN, heads * (NH + 2))
-    lower = jnp.tril(jnp.ones((BLOCK_LEN, BLOCK_LEN), F32))
-    sums = jnp.einsum(
-        "ts,bsh->bth",
-        lower,
-        jnp.concatenate([starts[:, None], logs * (1.0 - starts)[:, None]], axis=1).reshape(blocks, BLOCK_LEN, heads + 1),
-        precision=lax.Precision.HIGHEST,
+    marks = jnp.stack(
+        [
+            ((window[CONV - lag : CONV - lag + rows] == window[CONV:]) & (place_in >= lag)).astype(F32)
+            if lag < CONV
+            else jnp.zeros((rows,), F32)
+            for lag in range(1, 9)
+        ]
     )
-    tokp = jnp.concatenate([jnp.stack(linked, axis=1).reshape(blocks, BLOCK_LEN, CONV - 1), sums, slopes], axis=2)
-    sums_rows = jnp.repeat(sums, NH, axis=1)
-    beta_rows = jnp.swapaxes(beta, 1, 2).reshape(blocks, ROWS, heads)
-    colp = jnp.concatenate(
-        [sums_rows[:, :, :1], jnp.zeros_like(sums_rows[:, :, :1])]
-        + [x[:, :, h : h + 1] for h in range(heads) for x in (sums_rows[:, :, 1:], beta_rows)],
-        axis=2,
-    )
-    rowp = jnp.swapaxes(colp, 1, 2)
-    conv_w = jnp.pad(jnp.flip(conv_s.astype(F32).T, 0), ((0, 8 - CONV), (0, 0)))
-
+    rates = jnp.stack([a_log.astype(F32), dt_bias.astype(F32)])
     (
-        oloc, carr, state_in, maps, *saved, wg_full, wu_full, wd_full, wo_full,
-    ) = recurrence_forward(proj_ext, conv_w, rowp, colp, tokp, stage, w_down, out_proj, heads, pieces)
-    wg_s, wu_s = wg_full.reshape(D, inner), wu_full.reshape(D, inner)
-    down_s, out_s = wd_full.reshape(inner, D), wo_full.reshape(heads * HEAD, D)
-    gain = head_gain.astype(F32)[None, :]
-    heads_out, mixed = state_and_gate(state_in, oloc, carr, gate_out, gain, heads)
-
-    scale = (token_total / valid_count).reshape(1, 1)
-    mask_values = valid_mask.astype(F32)[:, None]
+        proj_ext, normed, gate_out, tokp, slopes, colp, rowp, conv_w, norms,
+        oloc, carr, state_in, maps, *saved, wg_full, wu_full, wo_full,
+    ) = recurrence_forward(heads, pieces, norm_at, rates, x_full, halo, weights, marks, stage, out_proj)
     (
         final_out, grad_middle, grad_heads, grad_gate_out, cot, gain_term, norm_mlp_term, loss, wide, tall,
     ) = middle_part(
-        seq_size, heads, pieces, scale, block_input, teacher, mask_values, norm_m[None, :], gain, mixed, heads_out,
-        gate_out, carr, out_s, wg_s, wu_s, down_s,
+        seq_size, heads, pieces, token_total, block_input, teacher, valid_mask[None, :], norms, head_gain[None, :],
+        oloc, carr, gate_out, state_in, wo_full.reshape(heads * HEAD, D), wg_full.reshape(D, -1),
+        wu_full.reshape(D, -1), w_down,
     )
     by_chip = lambda v: v.reshape(pieces // 2, 2, *v.shape[1:])
     grad_proj, fixed_rows, gw, grad_scal, gsum, wide_sum, tall_sum = recurrence_backward(
-        maps, cot, state_in, proj_ext, conv_w, rowp, colp, tokp, grad_heads, saved, by_chip(wide), by_chip(tall),
+        maps, cot, state_in, proj_ext, conv_w, rowp, colp, tokp, slopes, grad_heads, saved, by_chip(wide), by_chip(tall),
         heads, pieces,
     )
-    grad_proj = lax.dynamic_update_slice_in_dim(grad_proj, fixed_rows, rows - 8, 0)
-    deep = w_down.shape[0]
-    down_grad, out_grad = tall_sum[:deep], tall_sum[tall_sum.shape[0] - held :]
-    conv_terms = jnp.flip(gw[:CONV], 0).T.reshape(pieces, held, -1)
-    conv_at = norm_at + 3 - scal_at
-    conv_cols = conv_terms.shape[2]
-    conv_terms = jnp.pad(conv_terms, ((0, 0), (0, 0), (conv_at, HEAD - conv_at - conv_cols)))
-    pick = (jnp.arange(HEADS)[None, :] == head_start + jnp.arange(heads)[:, None]).astype(F32)
-    ends = jnp.concatenate(
-        [
-            jnp.sum(gsum[:heads, 0:1] * pick, axis=0), jnp.sum(gsum[:heads, 1:2] * pick, axis=0), loss[0, :1],
-            jnp.zeros((HEAD - 2 * HEADS - 1,), F32),
-        ]
+    input_grad, mix_grad, gate_grad, tail_grad, wg_grad, wu_grad, mean_loss, ends, norm_grads = final_part(
+        seq_size, pieces, heads, norm_at, grad_proj, grad_gate_out, grad_scal, weights, normed, fixed_rows, block_input,
+        grad_middle, norms, gw, gain_term, gsum, loss, norm_mlp_term, wide_sum.reshape(2, seq_size, held, -1),
     )
-    small = jnp.concatenate(
-        [
-            gain_term, ends[None], jnp.zeros((6, HEAD), F32), norm_mlp_term.reshape(-1, HEAD),
-            jnp.zeros((D // HEAD, HEAD), F32),
-        ],
-        axis=0,
-    )
-    input_grad, mix_grad, gate_grad, tails, small, wide_out = final_part(
-        seq_size, pieces, grad_proj, grad_gate_out, grad_scal, weights, normed, block_input, grad_middle,
-        norm_a[None, :], conv_terms, small, wide_sum.reshape(2, seq_size, held, inner),
-    )
-    scal_grad = jnp.swapaxes(tails[:, :, :scal_cols], 0, 1).reshape(held, -1)
-    conv_grad = lax.dynamic_index_in_dim(tails, rank, 0, False)[:, conv_at : conv_at + conv_cols].reshape(-1, CONV)
-    across = lambda v: jnp.swapaxes(v, 0, 1).reshape(held, FF).astype(F32)
-    mean_loss = small[1, 2 * HEADS] / (D * valid_count)
-    place = (rank * pieces + index) * held
-    norms = small[8:].reshape(2, D)
     return (
         final_out,
-        mean_loss,
+        mean_loss[0, 0],
         input_grad,
         mix_grad,
-        scal_grad,
+        tail_grad[:, :scal_cols],
         gate_grad,
-        out_grad,
-        conv_grad,
-        lax.dynamic_slice_in_dim(norms[1], place, held),
-        lax.dynamic_slice_in_dim(norms[0], place, held),
-        small[0],
-        small[1, :HEADS],
-        small[1, HEADS : 2 * HEADS],
-        across(wide_out[:, 0]),
-        across(wide_out[:, 1]),
-        down_grad,
+        tall_sum[tall_sum.shape[0] - held :],
+        tail_grad[:, taps_at:taps_end].reshape(-1, CONV),
+        norm_grads[0, :held],
+        norm_grads[1, :held],
+        ends[0],
+        ends[1, :HEADS],
+        ends[1, HEADS : 2 * HEADS],
+        wg_grad,
+        wu_grad,
+        tall_sum[: w_down.shape[0]],
     )
 
 

time: 426 us -> 352 us (0.83)
  local copies, waits for them, and re-layouts: 64.1 us -> 18 us
  Pallas kernels: 340 us -> 328 us
  other arithmetic: 11.9 us -> 3.23 us
  matrix products: 5.39 us -> 0 us
    unnamed x88 -> x24, local copies, waits for them, and re-layouts: 23.4 us -> 8.13 us
    pallas_call x4 -> x3, Pallas kernels: 228 us -> 215 us  [the longest x1 90.4 us: middle_part(): pl.pallas_call(functools.partial(middle_kernel, size, heads, float(token_...]
    slice x12 -> x3, local copies, waits for them, and re-layouts: 10 us -> 2.21 us  [the longest x1 0.79 us: local(): tail_grad[:, taps_at:taps_end].reshape(-1, CONV)]
    dot_general x3 -> x0, matrix products: 5.39 us -> none  [the longest x2 5.23 us: dot(): return jnp.dot(a, b, preferred_element_type=F32)]
    convert_element_type x4 -> x0, other arithmetic: 5.38 us -> none  [the longest x1 2.54 us: local(): normed_ext = rms_scale(extended, norm_a).astype(BF16)]
    reshape x12 -> x1, local copies, waits for them, and re-layouts: 5.29 us -> 0.09 us  [local(): tail_grad[:, taps_at:taps_end].reshape(-1, CONV)]
    transpose x7 -> x0, local copies, waits for them, and re-layouts: 4.78 us -> none  [the longest x2 3.32 us: local(): conv_w = jnp.pad(jnp.flip(conv_s.astype(F32).T, 0), ((0, 8 - CONV), (0, 0)))]
    concatenate x5 -> x1, local copies, waits for them, and re-layouts: 5.06 us -> 0.69 us  [local(): jnp.concatenate([scalar_proj, norm_attn[:, None], norm_mlp[:, None], jnp....]
where the time goes in v5:
time: 352 us
  Pallas kernels  328 us (93%)
  local copies, waits for them, and re-layouts  18 us (5%)
    pallas_call x1, Pallas kernels, middle_part(): pl.pallas_call(functools.partial(middle_kernel, size, heads, float(token_...  90.4 us
    pallas_call x1, Pallas kernels, recurrence_backward(): pl.pallas_call(functools.partial(bwd_kernel, heads, pieces, blocks), grid...  67.1 us
    pallas_call x1, Pallas kernels, recurrence_forward(): pl.pallas_call(functools.partial(fwd_kernel, heads, pieces, blocks // per...  62.7 us
    pallas_call x1, Pallas kernels, final_part(): pl.pallas_call(functools.partial(final_kernel, size, pieces, heads, norm_...  61.7 us
    pallas_call x1, Pallas kernels, start_gather(): pl.pallas_call(functools.partial(start_kernel, size, pieces), in_specs=[a...  45.9 us
    unnamed x24, local copies, waits for them, and re-layouts  8.13 us

profile of v5, /device:TPU:0, one launch (start us, length us, event | category | flops | bytes accessed | tf_op | source)
XLA Modules:
  0.0 351.5 jit_solution(9134012436467727120)
XLA Ops:
  0.6 1.3 convert_reduce_fusion
  1.9 1.2 maximum_convert_fusion.rates_ref
  3.2 0.8 pad_dynamic-slice_fusion
  3.9 0.1 fusion.7
  4.0 0.7 fusion
  4.7 0.8 copy.40
  5.4 0.8 copy.41
  6.2 0.8 copy.42
  6.9 0.6 stack.48.marks_ref
  7.6 0.8 copy.39
  8.4 0.1 reshape.71
  8.5 0.7 concatenate.3.tail_ref
  9.2 45.9 %start_gather.1 = (bf16[512,1024]{1,0:T(8,128)(2,1)}, bf16[16,1024]{1,0:T(8,128)(2,1)}, bf16[4,8,32,1664]{3,2,1,0:T(8,128)(2,1)}, bf16[4,2,32,768]{3,2,1,0:T(8,128)(2,1)}) custom-call(bf16[128,1024]{1,0:T(8,128)(2,1)} %x_ref.5, bf16[32,5120]{1,0:T(8,128)(2,1)} %mix_ref.1, bf16[32,1024]{1,0:T(8,128)(2,1)} %gate_ref.1, bf16[32,128]{1,0:T(8,128)(2,1)} %concatenate.3.tail_ref, ...), custom_call_target="tpu_custom_call" | custom-call | tf_op jit(solution)/shard_map/start_gather/pallas_call | solution.py:395
  55.1 62.7 %recurrence_forward.1 = (bf16[528,1280]{1,0:T(8,128)(2,1)}, bf16[512,1024]{1,0:T(8,128)(2,1)}, f32[512,256]{1,0:T(8,128)}, f32[512,128]{1,0:T(8,128)}, f32[512,1...) custom-call(f32[2,8]{1,0:T(2,128)} %maximum_convert_fusion.rates_ref, ...), custom_call_target="tpu_custom_call" | custom-call | tf_op jit(solution)/shard_map/recurrence_forward/pallas_call | solution.py:661
  117.8 90.4 %middle_part.1 = (bf16[128,1024]{1,0:T(8,128)(2,1)}, f32[128,1024]{1,0:T(8,128)}, bf16[512,256]{1,0:T(8,128)(2,1)}, bf16[512,256]{1,0:T(8,128)(2,1)}, f32[2,128,...) custom-call(bf16[128,1024]{1,0:T(8,128)(2,1)} %x_ref.5, ...), custom_call_target="tpu_custom_call" | custom-call | tf_op jit(solution)/shard_map/middle_part/pallas_call | solution.py:930
  208.2 67.1 %recurrence_backward.1 = (bf16[512,1280]{1,0:T(8,128)(2,1)}, bf16[8,1280]{1,0:T(8,128)(2,1)}, f32[8,1280]{1,0:T(8,128)}, bf16[512,128]{1,0:T(8,128)(2,1)}, f32[8...) custom-call(bf16[8,2,128,128]{3,2,1,0:T(8,128)(2,1)} %get-tuple-element.84.maps_ref, ...), custom_call_target="tpu_custom_call" | custom-call | tf_op jit(solution)/shard_map/recurrence_backward/pallas_call | solution.py:1149
  275.3 0.0 copy-start.2
  275.3 0.0 copy-start.5
  275.3 61.7 %final_part.1 = (f32[128,1024]{1,0:T(8,128)}, f32[32,5120]{1,0:T(8,128)}, f32[32,1024]{1,0:T(8,128)}, f32[32,128]{1,0:T(8,128)}, f32[32,2816]{1,0:T(8,128)}, /*i...) custom-call(bf16[512,1280]{1,0:T(8,128)(2,1)} %get-tuple-element.104.gp_any, ...), custom_call_target="tpu_custom_call" | custom-call | tf_op jit(solution)/shard_map/final_part/pallas_call | solution.py:1375
  337.1 0.0 copy-start.1
  337.1 0.0 copy-start
  337.1 0.0 copy-start.6
  337.1 1.3 slice_bitcast_fusion.2
  338.4 1.3 slice_bitcast_fusion
  339.7 1.2 slice_bitcast_fusion.3
  340.9 1.4 copy.43
  342.3 0.8 slice.47
  343.1 0.1 reshape.79
  343.2 0.0 copy-start.4
  343.2 0.7 copy.44
  343.9 0.0 copy-done.2
  343.9 0.7 slice.46
  344.5 0.8 slice.53
  345.3 0.0 copy-done.5
  345.3 0.0 copy-start.3
  345.3 0.7 copy.52
  346.6 0.0 copy-done.1
  346.6 0.8 copy.54
  347.4 0.0 copy-done
  347.4 0.8 copy.55
  348.2 0.0 copy-done.6
  348.2 0.7 copy.56
  348.9 0.0 copy-done.4
  348.9 0.7 copy.57
  349.6 0.0 copy-done.3
  349.6 0.7 copy.58
  (3 shorter events, 0.0 us)
Async XLA Ops:
  275.3 68.6 %copy-start.2 = (f32[128,1024]{1,0:T(8,128)S(1)}, f32[128,1024]{1,0:T(8,128)}, u32[]{:S(2)}) copy-start(f32[128,1024]{1,0:T(8,128)} %get-tuple-element.121) | copy-start | bytes 1572868
  275.3 70.0 %copy-start.5 = (bf16[128,1024]{1,0:T(8,128)(2,1)S(1)}, bf16[128,1024]{1,0:T(8,128)(2,1)}, u32[]{:S(2)}) copy-start(bf16[128,1024]{1,0:T(8,128)(2,1)} %get-tuple-element.181) | copy-start | bytes 786436
  337.1 9.5 %copy-start.1 = (f32[128,1024]{1,0:T(8,128)S(1)}, f32[128,1024]{1,0:T(8,128)}, u32[]{:S(2)}) copy-start(f32[128,1024]{1,0:T(8,128)} %get-tuple-element.183) | copy-start | bytes 1572868
  337.1 10.3 %copy-start = (f32[32,5120]{1,0:T(8,128)S(1)}, f32[32,5120]{1,0:T(8,128)}, u32[]{:S(2)}) copy-start(f32[32,5120]{1,0:T(8,128)} %get-tuple-element.184) | copy-start | bytes 1966084
  337.1 11.2 %copy-start.6 = (f32[32,1024]{1,0:T(8,128)S(1)}, f32[32,1024]{1,0:T(8,128)}, u32[]{:S(2)}) copy-start(f32[32,1024]{1,0:T(8,128)} %get-tuple-element.186) | copy-start | bytes 393220
  343.2 5.7 %copy-start.4 = (f32[32,2816]{1,0:T(8,128)S(1)}, f32[32,2816]{1,0:T(8,128)}, u32[]{:S(2)}) copy-start(f32[32,2816]{1,0:T(8,128)} %get-tuple-element.194) | copy-start | bytes 1081348
  345.3 4.3 %copy-start.3 = (f32[32,2816]{1,0:T(8,128)S(1)}, f32[32,2816]{1,0:T(8,128)}, u32[]{:S(2)}) copy-start(f32[32,2816]{1,0:T(8,128)} %get-tuple-element.195) | copy-start | bytes 1081348

commit v6 on v5

--- a/solution.py
+++ b/solution.py
@@ -17,6 +17,7 @@
 ROWS = BLOCK_LEN * NH
 CONV = 4
 SEQ_LEN = 32768
+MOST_DOC = {4096: 2048, 32768: 8192}
 WIDE = (1 + 2 * NH) * HEAD
 HALO = 16
 NORM_EPS = 1e-06
@@ -27,27 +28,28 @@
 MESH = pl.DeviceIdType.MESH
 
 
-def split_bf16(x):
-    if x.dtype == BF16:
-        return x, None
-    high = x.astype(BF16)
-    return high, (x - high.astype(F32)).astype(BF16)
-
-
-def mm(a, b, ca=1, cb=0, passes=3):
-    def one(x, y):
-        return lax.dot_general(x, y, (((ca,), (cb,)), ((), ())), preferred_element_type=F32)
-
-    if passes == 1:
-        return one(a.astype(BF16), b.astype(BF16))
-    ah, al = split_bf16(a)
-    bh, bl = split_bf16(b)
-    total = one(ah, bh)
-    if bl is not None:
-        total = total + one(ah, bl)
-    if al is not None:
-        total = total + one(al, bh)
-    return total
+class Split:
+    def __init__(self, x):
+        self.high = x.astype(BF16)
+        self.low = (x - self.high.astype(F32)).astype(BF16)
+
+
+def mm(a, b, ca=1, cb=0):
+    if not isinstance(a, Split) and a.dtype != BF16:
+        a = Split(a)
+    if not isinstance(b, Split) and b.dtype != BF16:
+        b = Split(b)
+    if isinstance(a, Split) and isinstance(b, Split):
+        left, right = (a.high, a.high, a.low), (b.high, b.low, b.high)
+    elif isinstance(a, Split):
+        left, right = (a.high, a.low), (b, b)
+    elif isinstance(b, Split):
+        left, right = (a, a), (b.high, b.low)
+    else:
+        left, right = (a,), (b,)
+    if len(left) > 1:
+        left, right = (jnp.concatenate(left, axis=ca),), (jnp.concatenate(right, axis=cb),)
+    return lax.dot_general(left[0], right[0], (((ca,), (cb,)), ((), ())), preferred_element_type=F32)
 
 
 def lanes_for(columns):
@@ -72,8 +74,9 @@
     size = 8
     while size < n:
         off = (ri // (2 * size) == ci // (2 * size)) & (ri // size != ci // size)
-        right = [mm(jnp.where(off, a, 0.0), x) for a, x in zip(systems, inv)]
-        inv = [x - mm(x, y) for x, y in zip(inv, right)]
+        halves = [Split(x) for x in inv]
+        right = [mm(jnp.where(off, a, 0.0), x) for a, x in zip(systems, halves)]
+        inv = [x - mm(y, z) for x, y, z in zip(inv, halves, right)]
         size *= 2
     return inv
 
@@ -120,15 +123,16 @@
 
 
 class Line:
-    def __init__(self, pieces, parts, send_sem, recv_sem, up=True, down=True):
+    def __init__(self, pieces, parts, send_sem, recv_sem, up=True, down=True, reach=None):
         self.chips = pieces // 2
+        self.reach = self.chips - 1 if reach is None else reach
         self.here = lax.axis_index("ctx")
         self.chip = self.here // 2
         self.core = lax.rem(self.here, 2)
         self.other = self.here + 1 - 2 * self.core
         self.parts, self.send_sem, self.recv_sem, self.up, self.down = parts, send_sem, recv_sem, up, down
 
-    def copies(self, chunk, way):
+    def copies(self, chunk, way, only=None):
         target = (self.here + 2, self.here - 2, self.other)[way]
         return [
             pltpu.make_async_remote_copy(
@@ -136,14 +140,15 @@
                 device_id={"ctx": target}, device_id_type=MESH,
             )
             for n, part in enumerate(self.parts)
+            if only is None or n == only
         ]
 
-    def start(self, chunk, way):
-        for copy in self.copies(chunk, way):
+    def start(self, chunk, way, only=None):
+        for copy in self.copies(chunk, way, only):
             copy.start()
 
-    def arrived(self, chunk):
-        for copy in self.copies(chunk, ACROSS):
+    def arrived(self, chunk, only=None):
+        for copy in self.copies(chunk, ACROSS, only):
             copy.wait_recv()
 
     def left(self, chunk, way):
@@ -152,46 +157,48 @@
 
     def routes(self, distance, act):
         if distance == 0:
-            if self.up:
+            if self.up and self.reach:
                 pl.when(self.chip < self.chips - 1)(lambda: act(self.here, UP))
-            if self.down:
+            if self.down and self.reach:
                 pl.when(self.chip > 0)(lambda: act(self.here, DOWN))
             act(self.here, ACROSS)
             return
         below, above = self.here - 2 * distance, self.here + 2 * distance
+        onward = distance < self.reach
         if self.up:
 
             @pl.when(self.chip >= distance)
             def _():
-                pl.when(self.chip < self.chips - 1)(lambda: act(below, UP))
+                if onward:
+                    pl.when(self.chip < self.chips - 1)(lambda: act(below, UP))
                 act(below, ACROSS)
 
         if self.down:
 
             @pl.when(self.chip + distance < self.chips)
             def _():
-                pl.when(self.chip > 0)(lambda: act(above, DOWN))
+                if onward:
+                    pl.when(self.chip > 0)(lambda: act(above, DOWN))
                 act(above, ACROSS)
 
-    def own(self):
-        self.routes(0, self.start)
+    def own(self, only=None):
+        self.routes(0, lambda chunk, way: self.start(chunk, way, only))
 
     def hop(self, distance):
-        if self.up:
-            pl.when(self.chip >= distance)(lambda: self.arrived(self.here - 2 * distance))
-        if self.down:
-            pl.when(self.chip + distance < self.chips)(lambda: self.arrived(self.here + 2 * distance))
-        self.routes(distance, self.start)
+        for n in range(len(self.parts)):
+            if self.up:
+                pl.when(self.chip >= distance)(lambda n=n: self.arrived(self.here - 2 * distance, n))
+            if self.down:
+                pl.when(self.chip + distance < self.chips)(lambda n=n: self.arrived(self.here + 2 * distance, n))
+            self.routes(distance, lambda chunk, way, n=n: self.start(chunk, way, n))
 
     def finish(self):
         for chip in range(self.chips):
-            needed = True
-            if not self.down:
-                needed = self.chip >= chip
-            if not self.up:
-                needed = self.chip <= chip
+            needed = (self.chip <= chip + (self.reach if self.up else 0)) & (
+                self.chip >= chip - (self.reach if self.down else 0)
+            )
             pl.when(needed)(lambda chip=chip: self.arrived(2 * chip + 1 - self.core))
-        for distance in range(self.chips):
+        for distance in range(self.reach + 1):
             self.routes(distance, self.left)
 
 
@@ -221,27 +228,33 @@
         for copy in self.copies(owner, way):
             copy.start()
 
-    def round(self, r):
+    def each(self, r, act):
         top = self.chips - 1
         for way, place in ((UP, self.chip), (DOWN, top - self.chip)):
             owner = top - (r - place) if way == UP else r - place
-
-            @pl.when((place <= r) & (place < top))
-            def _():
-                pl.when(place > 0)(lambda: self.take(owner, way))
-                self.send(owner, way)
+            pl.when((place <= r) & (place < top))(lambda: act(owner, way, place))
+
+    def settle(self, r):
+        self.each(r, lambda owner, way, place: pl.when(place > 0)(lambda: self.take(owner, way)))
+
+    def launch(self, r):
+        self.each(r, lambda owner, way, place: self.send(owner, way))
+
+    def left(self, r):
+        def wait(owner, way, place):
+            for copy in self.copies(owner, way):
+                copy.wait_send()
+
+        self.each(r, wait)
+
+    def round(self, r):
+        self.settle(r)
+        self.launch(r)
 
     def finish(self):
         top = self.chips - 1
         pl.when(self.chip > 0)(lambda: self.take(self.chip, UP))
         pl.when(self.chip < top)(lambda: self.take(self.chip, DOWN))
-        for owner in range(self.chips):
-            for way, wanted in ((UP, self.chip < owner), (DOWN, self.chip > owner)):
-
-                @pl.when(wanted)
-                def _():
-                    for copy in self.copies(owner, way):
-                        copy.wait_send()
 
 
 class Siblings:
@@ -277,6 +290,10 @@
     def left(self):
         for copy in self.copies():
             copy.wait_send()
+
+
+def chips_within(span_pieces, pieces):
+    return min(pieces // 2 - 1, (span_pieces + 1) // 2)
 
 
 def greet(devices, barrier):
@@ -350,22 +367,32 @@
         for i in range(1, size):
             exchange(n, i).wait_recv()
 
-    for n in range(4):
+    for n in range(3):
         begin(n)
     sides[...] = jnp.zeros_like(sides)
     for q in range(size):
         sides[q, 0, :, :inner] = wg_ref[:, q * inner : (q + 1) * inner]
         sides[q, 1, :, :inner] = wu_ref[:, q * inner : (q + 1) * inner]
-    line = Line(pieces, [lambda c: full_ref.at[:, c]], line_send, line_recv)
+    line = Line(
+        pieces, [lambda c, i=i: full_ref.at[lax.rem(me + size - i, size), c] for i in range(size)], line_send, line_recv
+    )
     for n in range(3):
-        end(n)
-    line.own()
+        own(n).wait()
+    line.own(0)
+    for i in range(1, size):
+        for n in range(3):
+            exchange(n, i).wait_recv()
+        line.own(i)
+    begin(3)
     begin(4)
-    end(3)
     last = xfull_ref.at[pl.ds(size * count - HALO, HALO)]
     passing = pltpu.make_async_remote_copy(
         last, halo_ref, halo_sem.at[0], halo_sem.at[1], device_id={"ctx": here + 1}, device_id_type=MESH
     )
+    hops = pieces // 2 - 1
+    for distance in range(1, hops):
+        line.hop(distance)
+    end(3)
     pl.when(here < pieces - 1)(passing.start)
 
     @pl.when(here == 0)
@@ -374,8 +401,7 @@
         filling.start()
         filling.wait()
 
-    for distance in range(1, pieces // 2):
-        line.hop(distance)
+    line.hop(hops)
     line.finish()
     end(4)
     pl.when(here > 0)(passing.wait_recv)
@@ -401,7 +427,7 @@
         ],
         scratch_shapes=[
             pltpu.VMEM((size, 2, held, padded), BF16),
-            dma((6,)), dma((5, size - 1)), dma((5, size - 1)), dma((1, 3, pieces)), dma((1, pieces)), dma((2,)),
+            dma((6,)), dma((5, size - 1)), dma((5, size - 1)), dma((size, 3, pieces)), dma((size, pieces)), dma((2,)),
         ],
         compiler_params=pltpu.CompilerParams(
             vmem_limit_bytes=VMEM_LIMIT, collective_id=2, has_side_effects=True
@@ -495,7 +521,7 @@
 
 
 def fwd_kernel(
-    heads, pieces, steps, per, norm_at,
+    heads, pieces, steps, per, span_pieces, norm_at,
     rates_ref, x_ref, halo_ref, full_ref, marks_ref, stage_ref, wo_ref,
     proj_ref, normed_ref, gate_ref, tok_ref, slope_ref, col_ref, row_ref, taps_ref, norms_ref,
     oloc_ref, carr_ref, sin_ref, mapsout_ref, conv_ref, q_ref, k_ref, v_ref, t_ref, kk_ref, at_ref, uw_ref, pl_ref,
@@ -532,7 +558,7 @@
             state[h, :, :HEAD] = eye
             state[h, :, HEAD:] = jnp.zeros((HEAD, HEAD), F32)
 
-    hops = [(d * (steps + 1)) // (pieces // 2) for d in range(1, pieces // 2)]
+    hops = [(d * 2 * steps) // (pieces // 2) - 1 for d in range(1, pieces // 2)]
     for distance, at in enumerate(hops, 1):
         if at < steps:
             pl.when(step == at)(lambda distance=distance: weights.hop(distance))
@@ -606,20 +632,21 @@
     @pl.when(step == steps - 1)
     def _():
         maps[here] = state[...].astype(BF16)
-        line = Line(pieces, [lambda c: maps.at[c]], map_send, map_recv)
+        line = Line(pieces, [lambda c: maps.at[c]], map_send, map_recv, reach=chips_within(span_pieces, pieces))
         line.own()
+        for distance in range(1, line.reach + 1):
+            line.hop(distance)
+        line.finish()
         for distance in range(1, pieces // 2):
-            line.hop(distance)
             if hops[distance - 1] >= steps:
                 weights.hop(distance)
-        line.finish()
 
         def hop(k, states):
             return tuple(
                 mm(maps[k, h, :, :HEAD], states[h]) + maps[k, h, :, HEAD:].astype(F32) for h in range(heads)
             )
 
-        states = lax.fori_loop(0, here, hop, tuple(jnp.zeros((HEAD, HEAD), F32) for _ in range(heads)))
+        states = lax.fori_loop(jnp.maximum(here - span_pieces, 0), here, hop, tuple(jnp.zeros((HEAD, HEAD), F32) for _ in range(heads)))
         for h in range(heads):
             sin_ref[h] = states[h]
 
@@ -627,7 +654,9 @@
             mapsout_ref[k] = maps[k, :, :, :HEAD]
             return carry
 
-        lax.fori_loop(0, pieces, keep, 0)
+        lax.fori_loop(
+            jnp.maximum(here - span_pieces, 0), jnp.minimum(here + span_pieces + 1, pieces), keep, 0
+        )
         weights.finish()
         given = [
             pltpu.make_async_copy(source, target, local_sem.at[n])
@@ -639,7 +668,7 @@
             copy.wait()
 
 
-def recurrence_forward(heads, pieces, norm_at, rates, x_full, halo, weights, marks, stage, w_out):
+def recurrence_forward(heads, pieces, span_pieces, norm_at, rates, x_full, halo, weights, marks, stage, w_out):
     rows = x_full.shape[0]
     blocks = rows // BLOCK_LEN
     per = 2
@@ -659,7 +688,7 @@
         shape(rows, HEAD), shape(blocks * ROWS, HEAD), shape(blocks * 8, ROWS), shape(8, heads * WIDE), shape(8, D),
     ]
     return pl.pallas_call(
-        functools.partial(fwd_kernel, heads, pieces, blocks // per, per, norm_at),
+        functools.partial(fwd_kernel, heads, pieces, blocks // per, per, span_pieces, norm_at),
         grid=(blocks // per,),
         in_specs=[pl.BlockSpec(memory_space=pltpu.SMEM)] + [vmem] * 4 + [hbm] * 2,
         out_specs=[whole(*f.shape) for f in front] + [
@@ -701,9 +730,10 @@
 def middle_body(
     size, heads, token_total, x_ref, teach_ref, mask_ref, norms_ref, gain_ref, streams,
     final_ref, gmid_ref, ghead_ref, ggate_ref, cot_ref, ggain_ref, gnorm_ref, loss_ref,
-    wide_ref, tall_ref,
+    wheld, theld, outg_ref,
     oloc_ref, carr_ref, gate_ref, sin_ref, wout_ref, wg_ref, wu_ref, wd_ref, load_sem, heads_ref, mixed_ref,
-    line_send, line_recv, wds,
+    line_send, line_recv, wds, wide_ref, tall_ref, wtheirs, ttheirs, wcame, tcame,
+    pair_send, pair_recv, sum_send, sum_recv,
     second, branch, low, sent, got, own, mid, gfin, gates, ups, hidden, ggates, gups, send_sem, recv_sem,
 ):
     me = lax.axis_index("seq")
@@ -716,7 +746,7 @@
     ]
     for load in loads:
         load.start()
-    pieces = wide_ref.shape[0]
+    pieces = 2 * wide_ref.shape[0]
     barrier = pltpu.get_barrier_semaphore()
     peers = [({"seq": lax.rem(me + i, size)}, me >= 0) for i in range(1, size)]
     pl.semaphore_wait(barrier, greet(peers + line_neighbours(pieces), barrier))
@@ -855,17 +885,23 @@
 
     lax.fori_loop(0, size, feed_back, 0)
     held = D // (size * pieces)
-    wide_at = tall_ref.shape[1] - held
     tall_ref[...] = jnp.zeros_like(tall_ref)
     grad = dot(hidden[...], branch[...], 0, 0)
     for c in range(pieces):
-        tall_ref[c, :deep] = grad[c * deep : (c + 1) * deep].astype(BF16)
+        tall_ref[c // 2, c % 2, :deep] = grad[c * deep : (c + 1) * deep].astype(BF16)
     for n, side in enumerate((ggates, gups)):
         grad = dot(second[...], side[...], 0, 0)
         for c in range(pieces):
             for r in range(size):
                 first = (r * pieces + c) * held
-                wide_ref[c, (n * size + r) * held : (n * size + r + 1) * held] = grad[first : first + held].astype(BF16)
+                wide_ref[c // 2, c % 2, (n * size + r) * held : (n * size + r + 1) * held] = grad[
+                    first : first + held
+                ].astype(BF16)
+    pair = Siblings([wide_ref, tall_ref], [wtheirs, ttheirs], [wheld, theld], pair_send, pair_recv)
+    sums = LineSum(pieces, [wheld, theld], [wcame, tcame], sum_send, sum_recv)
+    pair.start()
+    pair.add()
+    sums.round(0)
     gsecond = take_parts(2)
     middle = mid[...]
     inv = lax.rsqrt(jnp.mean(middle * middle, axis=1, keepdims=True) + NORM_EPS)
@@ -899,10 +935,18 @@
             cot_ref[h] += mm(carr_ref[rows(q), hc], ghead, 0, 0)
         return carry
 
-    lax.fori_loop(0, size, out_back, 0)
+    out_back(0, 0)
+    early = max(1, hops - 1)
+    for r in range(1, early):
+        sums.round(r)
+    lax.fori_loop(1, size, out_back, 0)
     grad = dot(mixed_ref[...], low[...], 0, 0)
     for c in range(pieces):
-        tall_ref[c, wide_at:] = grad[c * held : (c + 1) * held].astype(BF16)
+        outg_ref[c // 2, c % 2] = grad[c * held : (c + 1) * held].astype(BF16)
+    sums.settle(early)
+    pair.left()
+    for r in range(early):
+        sums.left(r)
 
     def sent_all(i, carry):
         for phase in range(3):
@@ -922,6 +966,8 @@
     rows = count * size
     inner = wg.shape[1]
     held, deep = D // (size * pieces), wd.shape[0]
+    chips = pieces // 2
+    wide, tall = (2 * size * held, inner), (-(-deep // 16) * 16, D)
     vmem = pl.BlockSpec(memory_space=pltpu.VMEM)
     out = lambda dims, kind: jax.ShapeDtypeStruct(dims, kind)
     low = lambda *dims: pltpu.VMEM(dims, BF16)
@@ -930,17 +976,20 @@
     return pl.pallas_call(
         functools.partial(middle_kernel, size, heads, float(token_total)),
         in_specs=[vmem] * 5 + [pl.BlockSpec(memory_space=pltpu.HBM)] * 8,
-        out_specs=[vmem] * 10,
+        out_specs=[vmem] * 11,
         out_shape=[
             out((count, D), BF16), out((count, D), F32),
             out((rows, heads * HEAD), BF16), out((rows, heads * HEAD), BF16), out((heads, HEAD, HEAD), F32),
             out((1, HEAD), F32), out((1, D), F32), out((1, HEAD), F32),
-            out((pieces, 2 * size * held, inner), BF16), out((pieces, -(-deep // 16) * 16 + held, D), BF16),
+            out((chips, 2 * size * held, inner), BF16), out((chips, -(-deep // 16) * 16, D), BF16),
+            out((chips, 2, held, D), BF16),
         ],
         scratch_shapes=[
             high(rows, heads * HEAD), high(rows, heads * HEAD), high(rows, heads * HEAD), high(heads, HEAD, HEAD),
             low(*wout.shape), low(*wg.shape), low(*wu.shape), low(inner, D), dma((8,)),
             low(rows, heads * HEAD), low(rows, heads * HEAD), dma((1, 3, pieces)), dma((1, pieces)), low(pieces, *wd.shape),
+            low(chips, 2, *wide), low(chips, 2, *tall), low(chips, *wide), low(chips, *tall), low(2, chips, *wide),
+            low(2, chips, *tall), dma((2,)), dma((2,)), dma((2, chips)), dma((2, 2, chips)),
             low(rows, D), low(rows, D), low(rows, D), low(3, size - 1, count, D), low(3, size - 1, count, D),
             high(count, D), high(count, D), high(count, D), high(rows, inner), high(rows, inner), low(rows, inner),
             low(rows, inner), low(rows, inner), dma((6, size - 1)), dma((6, size - 1)),
@@ -953,20 +1002,22 @@
 
 
 def bwd_kernel(
-    heads, pieces, steps, maps_ref, cot_ref, sin_ref, proj_ref, w_ref, rowp_ref, colp_ref, tokp_ref, slope_ref,
-    go_ref, conv_ref, q_ref, k_ref, v_ref, t_ref, kk_ref, at_ref, uw_ref, pl_ref, wide_ref, tall_ref,
-    gproj_ref, fix_ref, gw_ref, gscal_ref, gsum_ref, widesum_ref, tallsum_ref,
-    dstate, weave, rim, last, cots, rim_in, wtheirs, ttheirs, wheld, theld, wcame, tcame,
-    cot_send, cot_recv, pair_send, pair_recv, line_send, line_recv, rim_sem,
+    heads, pieces, steps, per, begun, span_pieces, maps_ref, cot_ref, sin_ref, proj_ref, w_ref, rowp_ref, colp_ref, tokp_ref, slope_ref,
+    go_ref, conv_ref, q_ref, k_ref, v_ref, t_ref, kk_ref, at_ref, uw_ref, pl_ref, wide_ref, tall_ref, outg_ref, normed_ref, ggate_ref,
+    gproj_ref, fix_ref, gw_ref, gscal_ref, gsum_ref, widesum_ref, tallsum_ref, outsum_ref, gatesum_ref,
+    dstate, weave, rim, last, cots, rim_in, wheld, theld, wcame, tcame,
+    gateg, otheirs, gtheirs, oheld, gheld, ocame, gcame,
+    cot_send, cot_recv, pair_send, pair_recv, early_send, early_recv, line_send, line_recv, rim_sem,
 ):
     step = pl.program_id(0)
     block = steps - 1 - step
     here = lax.axis_index("ctx")
     core = lax.rem(here, 2)
-    pair = Siblings([wide_ref, tall_ref], [wtheirs, ttheirs], [wheld, theld], pair_send, pair_recv)
-    line = LineSum(pieces, [wheld, theld], [wcame, tcame], line_send, line_recv)
+    early = LineSum(pieces, [wheld, theld], [wcame, tcame], early_send, early_recv)
+    pair = Siblings([outg_ref, gateg], [otheirs, gtheirs], [oheld, gheld], pair_send, pair_recv)
+    line = LineSum(pieces, [oheld, gheld], [ocame, gcame], line_send, line_recv)
     rounds = pieces // 2 - 1
-    when_round = [(r * steps) // max(rounds - 1, 1) for r in range(rounds)]
+    when_round = [min(steps - 1, 1 + (r * steps) // rounds) for r in range(rounds)]
 
     @pl.when(step == 0)
     def _():
@@ -974,22 +1025,36 @@
         side = [({"ctx": here + 1}, (core == 1) & (here < pieces - 1)), ({"ctx": here - 1}, (core == 0) & (here > 0))]
         pl.semaphore_wait(barrier, greet(line_neighbours(pieces) + side, barrier))
         cots[here] = cot_ref[...].astype(BF16)
-        spread = Line(pieces, [lambda c: cots.at[c]], cot_send, cot_recv, up=False)
+        spread = Line(
+            pieces, [lambda c: cots.at[c]], cot_send, cot_recv, up=False, reach=chips_within(span_pieces, pieces)
+        )
         spread.own()
-        pair.start()
-        for distance in range(1, pieces // 2):
+        wheld[...] = wide_ref[...]
+        theld[...] = tall_ref[...]
+        grad = lax.dot_general(
+            normed_ref[...], ggate_ref[...], (((0,), (0,)), ((), ())), preferred_element_type=F32
+        )
+        held, size = gateg.shape[3], gateg.shape[2]
+        for c in range(pieces):
+            for r in range(size):
+                row = (r * pieces + c) * held
+                gateg[c // 2, c % 2, r] = grad[row : row + held].astype(BF16)
+        for distance in range(1, spread.reach + 1):
             spread.hop(distance)
         spread.finish()
-        pair.add()
+        early.launch(begun)
+        pair.start()
+
+        farthest = jnp.minimum(here + span_pieces, pieces - 1)
 
         def hop(i, states):
-            k = pieces - 1 - i
+            k = farthest - i
             return tuple(
                 mm(maps_ref[k, h], states[h], 0, 0) + cots[k, h].astype(F32) for h in range(heads)
             )
 
         found = lax.fori_loop(
-            0, pieces - 1 - here, hop, tuple(jnp.zeros((HEAD, HEAD), F32) for _ in range(heads))
+            0, farthest - here, hop, tuple(jnp.zeros((HEAD, HEAD), F32) for _ in range(heads))
         )
         for h in range(heads):
             dstate[h] = found[h]
@@ -997,81 +1062,104 @@
         gw_ref[...] = jnp.zeros_like(gw_ref)
         gsum_ref[...] = jnp.zeros_like(gsum_ref)
 
+    for r in range(begun + 1, rounds):
+        at = min(steps - 1, 1 + ((r - begun) * (steps - 1)) // (rounds - begun))
+        pl.when(step == at)(lambda r=r: early.round(r))
+    pl.when(step == 1)(pair.add)
     for r in range(rounds):
-        if when_round[r] < steps:
-            pl.when(step == when_round[r])(lambda r=r: line.round(r))
-
-    base = pl.multiple_of(block * BLOCK_LEN, BLOCK_LEN)
-    rowp, colp, tokp = rowp_ref[...], colp_ref[...], tokp_ref[...]
+        pl.when(step == when_round[r])(lambda r=r: line.round(r))
+
     last_row = iota((ROWS, 1), 0) == ROWS - 1
-    gscal = jnp.zeros((BLOCK_LEN, HEAD), F32)
-    slope = slope_ref[...]
+    diagonal = iota((ROWS, ROWS), 0) == iota((ROWS, ROWS), 1)
     first_lane = lax.axis_index("seq") * lane_of(heads, 0)
-    for h in range(heads):
+    gscals = [[] for _ in range(per)]
+    dnexts = {(per - 1, h): dstate[h] for h in range(heads)}
+    rims = {(per - 1, h): rim[:, h * WIDE : (h + 1) * WIDE] for h in range(heads)}
+
+    def item(j, h):
+        n = j * heads + h
+        span = slice(j * BLOCK_LEN, (j + 1) * BLOCK_LEN)
+        rowp, colp = rowp_ref[j * 8 : (j + 1) * 8], colp_ref[j * ROWS : (j + 1) * ROWS]
+        tokp, slope = tokp_ref[span], slope_ref[span]
         cols = slice(h * WIDE, (h + 1) * WIDE)
         hc = slice(h * HEAD, (h + 1) * HEAD)
         beta, decay, qdecay, carry, qcarry, dlast, clast = decays(rowp, colp, tokp, h)
-        go = go_ref[:, hc]
-        query, keys, values = q_ref[0, h], k_ref[0, h], v_ref[0, h]
-        inv, kk, attn, uw = t_ref[0, h], kk_ref[0, h], at_ref[0, h], uw_ref[0, h]
-        dnext = dstate[h]
-        state = mm(pl_ref[0, h, :, :HEAD], sin_ref[h]) + pl_ref[0, h, :, HEAD:]
+        go = go_ref[span, hc]
+        query, keys, values = q_ref[j, h], k_ref[j, h], v_ref[j, h]
+        inv, kk, attn, uw = t_ref[j, h], kk_ref[j, h], at_ref[j, h], uw_ref[j, h]
+        yield
+        state = mm(pl_ref[j, h, :, :HEAD], sin_ref[h]) + pl_ref[j, h, :, HEAD:]
+        yield
         both = mm(jnp.concatenate([keys, uw[:, HEAD:]], axis=0), state)
         ks = both[:ROWS]
         upd = uw[:, :HEAD] - both[ROWS:]
-        dupd = mm(attn, go, 0, 0) + dlast * mm(keys, dnext)
+        dlocal = mm(attn, go, 0, 0)
+        while (j, h) not in dnexts:
+            yield
+        dnext = dnexts[j, h]
+        yield
+        dupd = dlocal + dlast * mm(keys, dnext)
+        yield
         dx = mm(inv, dupd, 0, 0)
+        yield
         dv = beta * dx
         dy = -(carry * dv)
         go32 = go.astype(F32)
+        dnexts[j - 1, h] = clast * dnext + mm(
+            jnp.concatenate([qcarry * query, keys], axis=0), jnp.concatenate([go32, dy], axis=0), 0, 0
+        )
+        yield
         outer = mm(jnp.concatenate([go32, dx], axis=0), upd, 1, 1)
         dattn, da = outer[:BLOCK_LEN], -outer[BLOCK_LEN:]
+        yield
         dkd = mm(upd, dnext, 1, 1)
         right = mm(jnp.concatenate([go32, dy], axis=0), state, 1, 1)
         gos = right[:BLOCK_LEN]
+        yield
         e = beta * da * decay
         f = dattn * qdecay
         ef = jnp.concatenate([f, e], axis=0)
         efk = mm(ef, keys)
         dq = qcarry * gos + efk[:BLOCK_LEN]
+        yield
         dk = (
             right[BLOCK_LEN:]
             + dlast * dkd
             + efk[BLOCK_LEN:]
             + mm(ef, jnp.concatenate([query, keys], axis=0), 0, 0)
         )
-        dstate[h] = clast * dnext + mm(
-            jnp.concatenate([qcarry * query, keys], axis=0), jnp.concatenate([go32, dy], axis=0), 0, 0
-        )
+        weave[3 * n] = dk
+        weave[3 * n + 1] = dv
+        yield
         dakk = da * kk
         z1 = beta * dakk
         z2 = dattn * attn
-        dbeta = jnp.sum(dx * (values - carry * ks), axis=1, keepdims=True) + jnp.sum(dakk, axis=1, keepdims=True)
-        dlk = dlast * jnp.sum(dkd * keys, axis=1, keepdims=True)
-        tail = jnp.sum(dlk, axis=0, keepdims=True) + clast * jnp.sum(
-            jnp.sum(state * dnext, axis=1, keepdims=True), axis=0, keepdims=True
-        )
-        dgrow = jnp.sum(z1, axis=1, keepdims=True) + jnp.sum(dy * ks, axis=1, keepdims=True) - dlk
+        kept = dlast * (dkd * keys)
+        below = jnp.sum(z1, axis=0, keepdims=True) + jnp.sum(z2, axis=0, keepdims=True)
+        dbeta = jnp.sum(dx * (values - carry * ks) + dakk, axis=1, keepdims=True)
+        tail = jnp.sum(
+            jnp.sum(kept, axis=0, keepdims=True) + clast * jnp.sum(state * dnext, axis=0, keepdims=True),
+            axis=1, keepdims=True,
+        )
+        dgrow = jnp.sum(z1 + dy * ks - kept - jnp.where(diagonal, below, 0.0), axis=1, keepdims=True)
         dgrow = dgrow + jnp.where(last_row, tail, 0.0)
-        dgrow = dgrow - mm(jnp.concatenate([z2, z1], axis=0), jnp.ones((BLOCK_LEN + ROWS, HEAD), BF16), 0, 0)[:, :1]
         lane = iota((ROWS, HEAD), 1)
-        weave[2 * h] = jnp.where(lane == 0, dbeta, jnp.where(lane == 1, dgrow, 0.0))
-        by_step = [weave[2 * h, pl.ds(j, BLOCK_LEN, NH), :] for j in range(NH)]
-        dg = sum(x[:, 1:2] for x in by_step) + jnp.sum(z2, axis=1, keepdims=True)
-        dg = dg + qcarry * jnp.sum(query * gos, axis=1, keepdims=True)
+        weave[3 * n + 2] = jnp.where(lane == 0, dbeta, dgrow)
+        yield
+        by_step = [weave[3 * n + 2, pl.ds(i, BLOCK_LEN, NH), :] for i in range(NH)]
+        dg = sum(x[:, 1:2] for x in by_step) + jnp.sum(z2 + qcarry * (query * gos), axis=1, keepdims=True)
         after = (iota((BLOCK_LEN, BLOCK_LEN), 0) <= iota((BLOCK_LEN, BLOCK_LEN), 1)).astype(BF16)
         dlog = column(tokp, LINK) * mm(after, jnp.broadcast_to(dg, (BLOCK_LEN, HEAD)))[:, :1]
-        dscal = [by_step[j][:, 0:1] * column(slope, lane_of(h, j)) for j in range(NH)]
+        dscal = [by_step[i][:, 0:1] * column(slope, lane_of(h, i)) for i in range(NH)]
         dscal.append(dlog * column(slope, lane_of(h, NH)))
         lane = iota((BLOCK_LEN, HEAD), 1)
-        for j in range(NH + 1):
-            gscal = gscal + jnp.where(lane == first_lane + lane_of(h, j), dscal[j], 0.0)
+        for i in range(NH + 1):
+            gscals[j].append(jnp.where(lane == first_lane + lane_of(h, i), dscal[i], 0.0))
         logs = column(slope, HEAD // 2 + lane_of(h, NH))
         sums = jnp.where(lane == 0, dlog * logs, jnp.where(lane == 1, dscal[NH], 0.0))
         gsum_ref[h : h + 1, :] += jnp.sum(sums, axis=0, keepdims=True)
-        weave[2 * h] = dk
-        weave[2 * h + 1] = dv
-        conv = conv_ref[:, cols]
+        yield
+        conv = conv_ref[span, cols]
         sig = jax.nn.sigmoid(conv)
         act = conv * sig
         parts = []
@@ -1079,14 +1167,16 @@
             piece = act[:, part * HEAD : (part + 1) * HEAD]
             scale = lax.rsqrt(jnp.sum(piece * piece, axis=1, keepdims=True) + NORM_EPS)
             if part:
-                grad = weave[2 * h, pl.ds(part - 1, BLOCK_LEN, NH), :]
+                grad = weave[3 * n, pl.ds(part - 1, BLOCK_LEN, NH), :]
             else:
                 grad = dq * (1.0 / math.sqrt(HEAD))
             unit = piece * scale
             parts.append(scale * (grad - unit * jnp.sum(grad * unit, axis=1, keepdims=True)))
-        for j in range(NH):
-            parts.append(weave[2 * h + 1, pl.ds(j, BLOCK_LEN, NH), :])
+        for i in range(NH):
+            parts.append(weave[3 * n + 1, pl.ds(i, BLOCK_LEN, NH), :])
         dconv = jnp.concatenate(parts, axis=1) * (sig * (1.0 + conv * (1.0 - sig)))
+        yield
+        base = pl.multiple_of((block * per + j) * BLOCK_LEN, BLOCK_LEN)
         ext = proj_ref[pl.ds(base, BLOCK_LEN + HALO), cols].astype(F32)
         gw_ref[0:1, cols] += jnp.sum(dconv * ext[HALO:], axis=0, keepdims=True)
         zeros = jnp.zeros((8, WIDE), F32)
@@ -1098,15 +1188,23 @@
             total = total + pltpu.roll(
                 jnp.concatenate([zeros, masked * w_ref[lag : lag + 1, cols]], axis=0), length - lag, 0
             )
-        fixed = total[length - 8 :] + rim[:, cols]
-        gproj_ref[:, cols] = jnp.concatenate([total[8 : length - 8], fixed], axis=0).astype(BF16)
-        rim[:, cols] = total[:8]
-
-        @pl.when(step == 0)
-        def _():
-            last[:, cols] = fixed
-
-    gscal_ref[...] = gscal.astype(BF16)
+        rims[j - 1, h] = total[:8]
+        fixed = total[length - 8 :] + rims[j, h]
+        gproj_ref[span, cols] = jnp.concatenate([total[8 : length - 8], fixed], axis=0).astype(BF16)
+        if j == per - 1:
+
+            @pl.when(step == 0)
+            def _():
+                last[:, cols] = fixed
+
+    running = [item(j, h) for j in reversed(range(per)) for h in range(heads)]
+    while running:
+        running = [one for one in running if next(one, "done") != "done"]
+    for h in range(heads):
+        dstate[h] = dnexts[-1, h]
+        rim[:, h * WIDE : (h + 1) * WIDE] = rims[-1, h]
+    for j in range(per):
+        gscal_ref[j * BLOCK_LEN : (j + 1) * BLOCK_LEN] = sum(gscals[j]).astype(BF16)
 
     @pl.when(step == steps - 1)
     def _():
@@ -1121,73 +1219,83 @@
             passing.wait_recv()
             fix_ref[...] = (last[...] + rim_in[...]).astype(BF16)
 
-        for r in range(rounds):
-            if when_round[r] >= steps:
-                line.round(r)
+        early.finish()
         line.finish()
         widesum_ref[...] = wheld[here // 2]
         tallsum_ref[...] = theld[here // 2].astype(F32)
+        outsum_ref[...] = oheld[here // 2].astype(F32)
+        gatesum_ref[...] = gheld[here // 2]
         pair.left()
+        for r in range(begun, rounds):
+            early.left(r)
+        for r in range(rounds):
+            line.left(r)
         pl.when(here > 0)(passing.wait_send)
 
 
 def recurrence_backward(
-    maps, cot, state_in, proj_ext, conv_w, rowp, colp, tokp, slopes, grad_heads, saved, wide, tall, heads, pieces
+    maps, cot, state_in, proj_ext, conv_w, rowp, colp, tokp, slopes, grad_heads, saved, wide, tall, outg, normed, ggate,
+    heads, pieces, span_pieces,
 ):
     rows = tokp.shape[0]
     blocks = rows // BLOCK_LEN
     chips = pieces // 2
+    per = 2
+    final = blocks // per - 1
     whole = lambda *dims: pl.BlockSpec(dims, lambda i: (0,) * len(dims))
-    by_block = lambda *dims: pl.BlockSpec((1,) + dims, lambda i: (blocks - 1 - i,) + (0,) * len(dims))
-    token = lambda cols: pl.BlockSpec((BLOCK_LEN, cols), lambda i: (blocks - 1 - i, 0))
+    by_block = lambda *dims: pl.BlockSpec((per,) + dims, lambda i: (final - i,) + (0,) * len(dims))
+    token = lambda cols: pl.BlockSpec((per * BLOCK_LEN, cols), lambda i: (final - i, 0))
     shape = lambda *dims: jax.ShapeDtypeStruct(dims, F32)
     low_shape = lambda *dims: jax.ShapeDtypeStruct(dims, BF16)
     vmem = pl.BlockSpec(memory_space=pltpu.VMEM)
+    low = lambda *dims: pltpu.VMEM(dims, BF16)
     square = (heads, ROWS, HEAD)
-    wide_chunk, tall_chunk = wide.shape[2:], tall.shape[2:]
+    wide_chunk, tall_chunk, out_chunk = wide.shape[1:], tall.shape[1:], outg.shape[2:]
+    gate_chunk = (HEADS // heads, out_chunk[0], ggate.shape[1])
     dma = pltpu.SemaphoreType.DMA
     return pl.pallas_call(
-        functools.partial(bwd_kernel, heads, pieces, blocks),
-        grid=(blocks,),
+        functools.partial(bwd_kernel, heads, pieces, blocks // per, per, max(1, chips - 2), span_pieces),
+        grid=(blocks // per,),
         in_specs=[
             vmem, vmem, vmem, vmem, vmem,
-            pl.BlockSpec((8, ROWS), lambda i: (blocks - 1 - i, 0)),
-            pl.BlockSpec((ROWS, HEAD), lambda i: (blocks - 1 - i, 0)), token(HEAD), token(HEAD),
+            pl.BlockSpec((per * 8, ROWS), lambda i: (final - i, 0)),
+            pl.BlockSpec((per * ROWS, HEAD), lambda i: (final - i, 0)), token(HEAD), token(HEAD),
             token(heads * HEAD), token(heads * WIDE),
             by_block(heads, BLOCK_LEN, HEAD), by_block(*square), by_block(*square), by_block(*square),
             by_block(*square), by_block(heads, BLOCK_LEN, ROWS), by_block(heads, ROWS, 2 * HEAD),
-            by_block(heads, HEAD, 2 * HEAD), vmem, vmem,
+            by_block(heads, HEAD, 2 * HEAD), vmem, vmem, vmem, vmem, vmem,
         ],
         out_specs=[
             token(heads * WIDE), whole(8, heads * WIDE), whole(8, heads * WIDE), token(HEAD), whole(8, HEAD),
-            whole(*wide_chunk), whole(*tall_chunk),
+            whole(*wide_chunk), whole(*tall_chunk), whole(*out_chunk), whole(*gate_chunk),
         ],
         out_shape=[
             low_shape(rows, heads * WIDE), low_shape(8, heads * WIDE), shape(8, heads * WIDE), low_shape(rows, HEAD),
-            shape(8, HEAD), low_shape(*wide_chunk), shape(*tall_chunk),
+            shape(8, HEAD), low_shape(*wide_chunk), shape(*tall_chunk), shape(*out_chunk), low_shape(*gate_chunk),
         ],
         scratch_shapes=[
-            pltpu.VMEM((heads, HEAD, HEAD), F32), pltpu.VMEM((2 * heads, ROWS, HEAD), F32),
+            pltpu.VMEM((heads, HEAD, HEAD), F32), pltpu.VMEM((3 * heads * per, ROWS, HEAD), F32),
             pltpu.VMEM((8, heads * WIDE), F32), pltpu.VMEM((8, heads * WIDE), F32),
             pltpu.VMEM((pieces, heads, HEAD, HEAD), BF16), pltpu.VMEM((8, heads * WIDE), F32),
-            pltpu.VMEM((chips, *wide_chunk), BF16), pltpu.VMEM((chips, *tall_chunk), BF16),
-            pltpu.VMEM((chips, *wide_chunk), BF16), pltpu.VMEM((chips, *tall_chunk), BF16),
-            pltpu.VMEM((2, chips, *wide_chunk), BF16), pltpu.VMEM((2, chips, *tall_chunk), BF16),
-            dma((1, 3, pieces)), dma((1, pieces)), dma((2,)), dma((2,)), dma((2, chips)), dma((2, 2, chips)), dma((2,)),
+            low(chips, *wide_chunk), low(chips, *tall_chunk), low(2, chips, *wide_chunk), low(2, chips, *tall_chunk),
+            low(chips, 2, *gate_chunk), low(chips, *out_chunk), low(chips, *gate_chunk), low(chips, *out_chunk),
+            low(chips, *gate_chunk), low(2, chips, *out_chunk), low(2, chips, *gate_chunk),
+            dma((1, 3, pieces)), dma((1, pieces)), dma((2,)), dma((2,)), dma((2, chips)), dma((2, 2, chips)),
+            dma((2, chips)), dma((2, 2, chips)), dma((2,)),
         ],
         compiler_params=pltpu.CompilerParams(
             vmem_limit_bytes=VMEM_LIMIT, collective_id=4, has_side_effects=True
         ),
         name="recurrence_backward",
-    )(maps, cot, state_in, proj_ext, conv_w, rowp, colp, tokp, slopes, grad_heads, *saved, wide, tall)
+    )(maps, cot, state_in, proj_ext, conv_w, rowp, colp, tokp, slopes, grad_heads, *saved, wide, tall, outg, normed, ggate)
 
 
 def final_kernel(
     size, pieces, heads, norm_at, inner, gp_any, gg_any, gs_any, w_any, normed_any,
-    fix_ref, x_ref, gmid_ref, norms_ref, gw_ref, gain_ref, gsum_ref, loss_ref, gnorm_ref, wide_ref,
+    fix_ref, x_ref, gmid_ref, norms_ref, gw_ref, gain_ref, gsum_ref, loss_ref, gnorm_ref, wide_ref, gatesum_ref,
     ingrad_ref, gmix_ref, ggate_ref, gtail_ref, gwg_ref, gwu_ref, mean_ref, ends_ref, both_ref,
-    gp_ref, gg_ref, gs_ref, w_ref, normed_ref, load_sem, wideout_ref,
-    sent, got, own, turned, grads, theirs, held, came, blocks, around, along, summed,
+    gp_ref, gg_ref, gs_ref, w_ref, normed_ref, load_sem, wideout_ref, gateout_ref,
+    sent, got, whole, turned, grads, theirs, held, came, blocks, around, along, summed,
     local_sem, seq_send, seq_recv, pair_send, pair_recv, line_send, line_recv, ctx_send, ctx_recv,
 ):
     me, here = lax.axis_index("seq"), lax.axis_index("ctx")
@@ -1216,6 +1324,7 @@
         source, target = [
             (sent.at[i - 1], got.at[i - 1]), (wide_ref.at[:, q], wideout_ref.at[me]),
             (around.at[me], around.at[me]), (held.at[here // 2, q], blocks.at[me]),
+            (gatesum_ref.at[q], gateout_ref.at[me]),
         ][n]
         return pltpu.make_async_remote_copy(
             source, target, seq_send.at[n, i - 1], seq_recv.at[n, i - 1], device_id={"seq": q}, device_id_type=MESH
@@ -1227,42 +1336,34 @@
             device_id={"ctx": lax.rem(here + i, pieces)}, device_id_type=MESH,
         )
 
-    kept = pltpu.make_async_copy(wide_ref.at[:, me], wideout_ref.at[me], local_sem.at[0])
-    kept.start()
-    for i in range(1, size):
-        to_peer(1, i).start()
     gate_at, tail_at = gp_ref.shape[1], gp_ref.shape[1] + gg_ref.shape[1]
     for load in loads:
         load.wait()
     gp_ref[gp_ref.shape[0] - 8 :] = fix_ref[...]
 
-    def part(k, carry):
-        i = lax.rem(k + 1, size)
-        q = lax.rem(me + i, size)
-        value = (
-            dot(gp_ref[rows(q)], w_ref[:, :gate_at], 1, 1)
-            + dot(gg_ref[rows(q)], w_ref[:, gate_at:tail_at], 1, 1)
-            + dot(gs_ref[rows(q)], w_ref[:, tail_at:], 1, 1)
-        )
-
-        @pl.when(i > 0)
-        def _():
-            sent[i - 1] = value.astype(BF16)
+    def parts():
+        for first in range(0, D, 256):
+            tile = slice(first, first + 256)
+            value = (
+                dot(gp_ref[...], w_ref[tile, :gate_at], 1, 1)
+                + dot(gg_ref[...], w_ref[tile, gate_at:tail_at], 1, 1)
+                + dot(gs_ref[...], w_ref[tile, tail_at:], 1, 1)
+            )
+            whole[:, tile] = value
+
+        def give(i, carry):
+            sent[i - 1] = whole[rows(lax.rem(me + i, size))].astype(BF16)
             pltpu.make_async_remote_copy(
                 sent.at[i - 1], got.at[i - 1], seq_send.at[0, i - 1], seq_recv.at[0, i - 1],
-                device_id={"seq": q}, device_id_type=MESH,
+                device_id={"seq": lax.rem(me + i, size)}, device_id_type=MESH,
             ).start()
-
-        @pl.when(i == 0)
-        def _():
-            own[...] = value
-
-        return carry
-
-    lax.fori_loop(0, size, part, 0)
+            return carry
+
+        lax.fori_loop(1, size, give, 0)
+
     turned[...] = normed_ref[...].T
     rank_rows = D // (size * pieces)
-    for source, at in ((gp_ref, 0), (gg_ref, gate_at), (gs_ref, tail_at)):
+    for source, at in ((gp_ref, 0), (gs_ref, gate_at)):
         width = source.shape[1]
         for first in range(0, width, 256):
             cols = min(256, width - first)
@@ -1278,15 +1379,21 @@
         spread = jnp.where(mine, gw_ref[lag : lag + 1], 0.0).astype(BF16)
         taps = taps + dot(spread, tap_lanes(channels, CONV - 1 - lag, norm_at + 3))
     for c in range(pieces):
-        grads[c // 2, c % 2, me, :, tail_at:] = (
-            grads[c // 2, c % 2, me, :, tail_at:].astype(F32) + taps[c * rank_rows : (c + 1) * rank_rows]
+        grads[c // 2, c % 2, me, :, gate_at:] = (
+            grads[c // 2, c % 2, me, :, gate_at:].astype(F32) + taps[c * rank_rows : (c + 1) * rank_rows]
         ).astype(BF16)
     pair = Siblings([grads], [theirs], [held], pair_send, pair_recv)
+    line = LineSum(pieces, [held], [came], line_send, line_recv)
     pair.start()
-
+    parts()
+    pair.add()
+    line.round(0)
+    rounds = pieces // 2 - 1
+    for r in range(1, rounds - 1):
+        line.round(r)
     for i in range(1, size):
         to_peer(0, i).wait_recv()
-    gnormed = own[...]
+    gnormed = whole[rows(me)]
     for i in range(1, size):
         gnormed = gnormed + got[i - 1].astype(F32)
     x = x_ref[...].astype(F32)
@@ -1308,9 +1415,16 @@
         around[me, 8 + D // HEAD + j : 9 + D // HEAD + j] = gnorm_ref[:, j * HEAD : (j + 1) * HEAD]
     for i in range(1, size):
         to_peer(2, i).start()
-    pair.add()
-    line = LineSum(pieces, [held], [came], line_send, line_recv)
-    line.round(0)
+    kept = [
+        pltpu.make_async_copy(wide_ref.at[:, me], wideout_ref.at[me], local_sem.at[0]),
+        pltpu.make_async_copy(gatesum_ref.at[me], gateout_ref.at[me], local_sem.at[1]),
+    ]
+    for copy in kept:
+        copy.start()
+    for i in range(1, size):
+        to_peer(1, i).start()
+        to_peer(4, i).start()
+    line.round(rounds - 1)
     for i in range(1, size):
         to_peer(2, i).wait_recv()
     mine = around[0]
@@ -1319,8 +1433,6 @@
     along[here] = mine
     for i in range(1, pieces):
         to_piece(i).start()
-    for r in range(1, pieces // 2 - 1):
-        line.round(r)
     line.finish()
     blocks[me] = held[here // 2, me]
     for i in range(1, size):
@@ -1339,33 +1451,38 @@
         row = summed[pl.ds(8 + n * (D // HEAD) + place // HEAD, 1), :]
         both_ref[n : n + 1, :] = pltpu.roll(row, lax.rem(HEAD - lax.rem(place, HEAD), HEAD), 1)
     tail = jnp.zeros((rank_rows, HEAD), F32)
-    kept.wait()
+    for copy in kept:
+        copy.wait()
     for i in range(1, size):
         to_peer(3, i).wait_recv()
         to_peer(1, i).wait_recv()
+        to_peer(4, i).wait_recv()
     for r in range(size):
         block = blocks[r].astype(F32)
         gmix_ref[:, r * gate_at : (r + 1) * gate_at] = block[:, :gate_at]
-        ggate_ref[:, r * (tail_at - gate_at) : (r + 1) * (tail_at - gate_at)] = block[:, gate_at:tail_at]
-        tail = tail + block[:, tail_at:]
+        ggate_ref[:, r * (tail_at - gate_at) : (r + 1) * (tail_at - gate_at)] = gateout_ref[r].astype(F32)
+        tail = tail + block[:, gate_at:]
         gwg_ref[:, r * inner : (r + 1) * inner] = wideout_ref[r, 0, :, :inner].astype(F32)
         gwu_ref[:, r * inner : (r + 1) * inner] = wideout_ref[r, 1, :, :inner].astype(F32)
     gtail_ref[...] = tail
     pair.left()
+    for r in range(pieces // 2 - 1):
+        line.left(r)
     for i in range(1, size):
-        for n in range(4):
+        for n in range(5):
             to_peer(n, i).wait_send()
     for i in range(1, pieces):
         to_piece(i).wait_send()
 
 
 def final_part(
-    size, pieces, heads, norm_at, gp, gg, gs, weights, normed, fix, x, gmid, norms, gw, gain, gsum, loss, gnorm, wide
+    size, pieces, heads, norm_at, gp, gg, gs, weights, normed, fix, x, gmid, norms, gw, gain, gsum, loss, gnorm, wide,
+    gatesum,
 ):
     count = x.shape[0]
     chips = pieces // 2
     held, inner = D // (size * pieces), FF // size
-    width = weights.shape[1]
+    width = gp.shape[1] + gs.shape[1]
     small = (8 + 2 * (D // HEAD), HEAD)
     vmem = pl.BlockSpec(memory_space=pltpu.VMEM)
     out = lambda *dims: jax.ShapeDtypeStruct(dims, F32)
@@ -1374,7 +1491,7 @@
     dma = pltpu.SemaphoreType.DMA
     return pl.pallas_call(
         functools.partial(final_kernel, size, pieces, heads, norm_at, inner),
-        in_specs=[pl.BlockSpec(memory_space=pl.ANY)] * 5 + [vmem] * 10,
+        in_specs=[pl.BlockSpec(memory_space=pltpu.HBM)] * 5 + [vmem] * 11,
         out_specs=[vmem] * 9,
         out_shape=[
             out(count, D), out(held, size * gp.shape[1]), out(held, size * gg.shape[1]), out(held, HEAD),
@@ -1382,18 +1499,63 @@
         ],
         scratch_shapes=[
             low(*gp.shape), low(*gg.shape), low(*gs.shape), low(*weights.shape), low(*normed.shape), dma((5,)),
-            low(size, 2, held, wide.shape[3]),
-            low(size - 1, count, D), low(size - 1, count, D), high(count, D), low(D, normed.shape[0]),
+            low(size, 2, held, wide.shape[3]), low(*gatesum.shape),
+            low(size - 1, count, D), low(size - 1, count, D), high(size * count, D), low(D, normed.shape[0]),
             low(chips, 2, size, held, width), low(chips, size, held, width), low(chips, size, held, width),
             low(2, chips, size, held, width), low(size, held, width), high(size, *small), high(pieces, *small), high(*small),
-            dma((1,)), dma((4, size - 1)), dma((4, size - 1)), dma((1,)), dma((1,)), dma((1, chips)), dma((1, 2, chips)),
+            dma((2,)), dma((5, size - 1)), dma((5, size - 1)), dma((1,)), dma((1,)), dma((1, chips)), dma((1, 2, chips)),
             dma((pieces - 1,)), dma((pieces - 1,)),
         ],
         compiler_params=pltpu.CompilerParams(
             vmem_limit_bytes=VMEM_LIMIT, collective_id=5, has_side_effects=True
         ),
         name="final_part",
-    )(gp, gg, gs, weights, normed, fix, x, gmid, norms, gw, gain, gsum, loss, gnorm, wide)
+    )(gp, gg, gs, weights, normed, fix, x, gmid, norms, gw, gain, gsum, loss, gnorm, wide, gatesum)
+
+
+def finish_kernel(
+    scal_cols, taps_at, final_ref, ingrad_ref, gmix_ref, ggate_ref, gwg_ref, gwu_ref, tall_ref, outsum_ref,
+    tail_ref, ends_ref, both_ref,
+    final_out, ingrad_out, gmix_out, ggate_out, gwg_out, gwu_out, gwd_out, gout_out,
+    gscal_out, gconv_out, norma_out, normm_out, gain_out, alog_out, dt_out,
+):
+    for source, target in (
+        (final_ref, final_out), (ingrad_ref, ingrad_out), (gmix_ref, gmix_out), (ggate_ref, ggate_out),
+        (gwg_ref, gwg_out), (gwu_ref, gwu_out), (outsum_ref, gout_out),
+    ):
+        target[...] = source[...]
+    gwd_out[...] = tall_ref[: gwd_out.shape[0]]
+    tail = tail_ref[...]
+    rows, channels = tail.shape[0], gconv_out.shape[1]
+    square = jnp.concatenate([tail, jnp.zeros((HEAD - rows, HEAD), F32)], axis=0)
+    gscal_out[...] = square.T[:scal_cols, :rows]
+    mine = channel_rows(rows, channels)
+    for tap in range(CONV):
+        spread = exact(tail, tap_lanes(channels, tap, taps_at).astype(F32), 1, 1)
+        gconv_out[tap : tap + 1] = jnp.sum(jnp.where(mine, spread, 0.0), axis=0, keepdims=True)
+    held = norma_out.shape[1]
+    norma_out[...] = both_ref[0:1, :held]
+    normm_out[...] = both_ref[1:2, :held]
+    gain_out[...] = ends_ref[0:1, :]
+    alog_out[...] = ends_ref[1:2, :HEADS]
+    dt_out[...] = ends_ref[1:2, HEADS : 2 * HEADS]
+
+
+def finish_part(scal_cols, taps_at, deep, channels, *parts):
+    vmem = pl.BlockSpec(memory_space=pltpu.VMEM)
+    held = parts[2].shape[0]
+    out = lambda dims, kind=F32: jax.ShapeDtypeStruct(dims, kind)
+    return pl.pallas_call(
+        functools.partial(finish_kernel, scal_cols, taps_at),
+        in_specs=[vmem] * 11,
+        out_specs=[vmem] * 15,
+        out_shape=[out(p.shape, p.dtype) for p in parts[:6]] + [
+            out((deep, D)), out(parts[7].shape), out((scal_cols, held)), out((CONV, channels)),
+            out((1, held)), out((1, held)), out((1, HEAD)), out((1, HEADS)), out((1, HEADS)),
+        ],
+        compiler_params=pltpu.CompilerParams(vmem_limit_bytes=VMEM_LIMIT),
+        name="finish_part",
+    )(*parts)
 
 
 def local(
@@ -1405,6 +1567,7 @@
     rows = block_input.shape[0] * seq_size
     token_total = segments.shape[0]
     seq_length = min(SEQ_LEN, token_total)
+    span_pieces = min(pieces, (MOST_DOC.get(token_total, token_total) - 2) // rows + 1)
     index = lax.axis_index("ctx")
     held = mix_proj.shape[0]
     scal_cols = HEADS * (NH + 1)
@@ -1439,40 +1602,34 @@
     (
         proj_ext, normed, gate_out, tokp, slopes, colp, rowp, conv_w, norms,
         oloc, carr, state_in, maps, *saved, wg_full, wu_full, wo_full,
-    ) = recurrence_forward(heads, pieces, norm_at, rates, x_full, halo, weights, marks, stage, out_proj)
+    ) = recurrence_forward(heads, pieces, span_pieces, norm_at, rates, x_full, halo, weights, marks, stage, out_proj)
     (
-        final_out, grad_middle, grad_heads, grad_gate_out, cot, gain_term, norm_mlp_term, loss, wide, tall,
+        final_out, grad_middle, grad_heads, grad_gate_out, cot, gain_term, norm_mlp_term, loss, wide, tall, outg,
     ) = middle_part(
         seq_size, heads, pieces, token_total, block_input, teacher, valid_mask[None, :], norms, head_gain[None, :],
         oloc, carr, gate_out, state_in, wo_full.reshape(heads * HEAD, D), wg_full.reshape(D, -1),
         wu_full.reshape(D, -1), w_down,
     )
-    by_chip = lambda v: v.reshape(pieces // 2, 2, *v.shape[1:])
-    grad_proj, fixed_rows, gw, grad_scal, gsum, wide_sum, tall_sum = recurrence_backward(
-        maps, cot, state_in, proj_ext, conv_w, rowp, colp, tokp, slopes, grad_heads, saved, by_chip(wide), by_chip(tall),
-        heads, pieces,
+    grad_proj, fixed_rows, gw, grad_scal, gsum, wide_sum, tall_sum, out_sum, gate_sum = recurrence_backward(
+        maps, cot, state_in, proj_ext, conv_w, rowp, colp, tokp, slopes, grad_heads, saved, wide, tall, outg, normed,
+        grad_gate_out, heads, pieces, span_pieces,
     )
     input_grad, mix_grad, gate_grad, tail_grad, wg_grad, wu_grad, mean_loss, ends, norm_grads = final_part(
         seq_size, pieces, heads, norm_at, grad_proj, grad_gate_out, grad_scal, weights, normed, fixed_rows, block_input,
         grad_middle, norms, gw, gain_term, gsum, loss, norm_mlp_term, wide_sum.reshape(2, seq_size, held, -1),
+        gate_sum,
+    )
+    (
+        final_out, input_grad, mix_grad, gate_grad, wg_grad, wu_grad, wd_grad, out_grad,
+        scal_grad, conv_grad, norm_a_grad, norm_m_grad, gain_grad, alog_grad, dt_grad,
+    ) = finish_part(
+        scal_cols, taps_at, w_down.shape[0], conv_weight.shape[0],
+        final_out, input_grad, mix_grad, gate_grad, wg_grad, wu_grad, tall_sum, out_sum, tail_grad, ends, norm_grads,
     )
     return (
-        final_out,
-        mean_loss[0, 0],
-        input_grad,
-        mix_grad,
-        tail_grad[:, :scal_cols],
-        gate_grad,
-        tall_sum[tall_sum.shape[0] - held :],
-        tail_grad[:, taps_at:taps_end].reshape(-1, CONV),
-        norm_grads[0, :held],
-        norm_grads[1, :held],
-        ends[0],
-        ends[1, :HEADS],
-        ends[1, HEADS : 2 * HEADS],
-        wg_grad,
-        wu_grad,
-        tall_sum[: w_down.shape[0]],
+        final_out, mean_loss[0, 0], input_grad, mix_grad, scal_grad.T, gate_grad, out_grad, conv_grad.T,
+        norm_a_grad.reshape(-1), norm_m_grad.reshape(-1), gain_grad.reshape(-1), alog_grad.reshape(-1),
+        dt_grad.reshape(-1), wg_grad, wu_grad, wd_grad,
     )
 
 

time: 352 us -> 300 us (0.85)
  Pallas kernels: 328 us -> 289 us
  local copies, waits for them, and re-layouts: 18 us -> 5.29 us
    pallas_call x1 -> x2, Pallas kernels: 67.1 us -> 50.4 us  [the longest x1 46.4 us: recurrence_backward(): pl.pallas_call(functools.partial(bwd_kernel, heads, pieces, blocks // per...]
    pallas_call x1, Pallas kernels: 61.7 us -> 47.5 us  [final_part(): pl.pallas_call(functools.partial(final_kernel, size, pieces, heads, norm_...]
    pallas_call x1, Pallas kernels: 62.7 us -> 50.7 us  [recurrence_forward(): pl.pallas_call(functools.partial(fwd_kernel, heads, pieces, blocks // per...]
    pallas_call x1, Pallas kernels: 90.4 us -> 97.6 us  [middle_part(): pl.pallas_call(functools.partial(middle_kernel, size, heads, float(token_...]
    unnamed x24 -> x2, local copies, waits for them, and re-layouts: 8.13 us -> 1.58 us
    squeeze x3 -> x0, local copies, waits for them, and re-layouts: 3.83 us -> none  [the longest x1 1.33 us: local(): ends[1, HEADS:2 * HEADS]]
    pallas_call x1, Pallas kernels: 45.9 us -> 42.3 us  [start_gather(): pl.pallas_call(functools.partial(start_kernel, size, pieces), in_specs=[a...]
where the time goes in v6:
time: 300 us; the launch traced here: 299 us
  Pallas kernels  289 us (96%)
  local copies, waits for them, and re-layouts  5.29 us (2%)
  other arithmetic  3.23 us (1%)
    pallas_call x1, Pallas kernels, middle_part(): pl.pallas_call(functools.partial(middle_kernel, size, heads, float(token_...  97.6 us
    pallas_call x1, Pallas kernels, recurrence_forward(): pl.pallas_call(functools.partial(fwd_kernel, heads, pieces, blocks // per...  50.7 us
    pallas_call x1, Pallas kernels, final_part(): pl.pallas_call(functools.partial(final_kernel, size, pieces, heads, norm_...  47.5 us
    pallas_call x1, Pallas kernels, recurrence_backward(): pl.pallas_call(functools.partial(bwd_kernel, heads, pieces, blocks // per...  46.4 us
    pallas_call x1, Pallas kernels, start_gather(): pl.pallas_call(functools.partial(start_kernel, size, pieces), in_specs=[a...  42.3 us

profile of v6, /device:TPU:0, one launch (start us, length us, event | category | flops | bytes accessed | tf_op | source)
XLA Modules:
  0.0 299.5 jit_solution(7616126919260726203)
XLA Ops:
  0.6 1.3 convert_reduce_fusion
  1.9 1.2 maximum_convert_fusion.rates_ref
  3.2 0.8 pad_dynamic-slice_fusion
  3.9 0.1 fusion.7
  4.0 0.7 fusion
  4.7 0.8 copy.38
  5.4 0.8 copy.39
  6.2 0.8 copy.40
  6.9 0.6 stack.48.marks_ref
  7.6 0.8 copy.37
  8.4 0.1 reshape.77
  8.5 0.7 concatenate.3.tail_ref
  9.2 42.3 %start_gather.1 = (bf16[512,1024]{1,0:T(8,128)(2,1)}, bf16[16,1024]{1,0:T(8,128)(2,1)}, bf16[4,8,32,1664]{3,2,1,0:T(8,128)(2,1)}, bf16[4,2,32,768]{3,2,1,0:T(8,128)(2,1)}) custom-call(bf16[128,1024]{1,0:T(8,128)(2,1)} %x_ref.5, bf16[32,5120]{1,0:T(8,128)(2,1)} %mix_ref.1, bf16[32,1024]{1,0:T(8,128)(2,1)} %gate_ref.1, bf16[32,128]{1,0:T(8,128)(2,1)} %concatenate.3.tail_ref, ...), custom_call_target="tpu_custom_call" | custom-call | tf_op jit(solution)/shard_map/start_gather/pallas_call | solution.py:421
  51.5 50.7 %recurrence_forward.1 = (bf16[528,1280]{1,0:T(8,128)(2,1)}, bf16[512,1024]{1,0:T(8,128)(2,1)}, f32[512,256]{1,0:T(8,128)}, f32[512,128]{1,0:T(8,128)}, f32[512,1...) custom-call(f32[2,8]{1,0:T(2,128)} %maximum_convert_fusion.rates_ref, ...), custom_call_target="tpu_custom_call" | custom-call | tf_op jit(solution)/shard_map/recurrence_forward/pallas_call | solution.py:690
  102.2 97.6 %middle_part.1 = (bf16[128,1024]{1,0:T(8,128)(2,1)}, f32[128,1024]{1,0:T(8,128)}, bf16[512,256]{1,0:T(8,128)(2,1)}, bf16[512,256]{1,0:T(8,128)(2,1)}, f32[2,128,...) custom-call(bf16[128,1024]{1,0:T(8,128)(2,1)} %x_ref.5, ...), custom_call_target="tpu_custom_call" | custom-call | tf_op jit(solution)/shard_map/middle_part/pallas_call | solution.py:976
  199.8 46.4 %recurrence_backward.1 = (bf16[512,1280]{1,0:T(8,128)(2,1)}, bf16[8,1280]{1,0:T(8,128)(2,1)}, f32[8,1280]{1,0:T(8,128)}, bf16[512,128]{1,0:T(8,128)(2,1)}, f32[8...) custom-call(bf16[8,2,128,128]{3,2,1,0:T(8,128)(2,1)} %get-tuple-elem, ...), custom_call_target="tpu_custom_call" | custom-call | tf_op jit(solution)/shard_map/recurrence_backward/pallas_call | solution.py:1256
  246.3 47.5 %final_part.1 = (f32[128,1024]{1,0:T(8,128)}, f32[32,5120]{1,0:T(8,128)}, f32[32,1024]{1,0:T(8,128)}, f32[32,128]{1,0:T(8,128)}, f32[32,2816]{1,0:T(8,128)}, /*i...) custom-call(bf16[512,1280]{1,0:T(8,128)(2,1)} %get-tuple-element.125.gp_any, ...), custom_call_target="tpu_custom_call" | custom-call | tf_op jit(solution)/shard_map/final_part/pallas_call | solution.py:1492
  293.8 3.9 %finish_part.1 = (bf16[128,1024]{1,0:T(8,128)(2,1)}, f32[128,1024]{1,0:T(8,128)}, f32[32,5120]{1,0:T(8,128)}, f32[32,1024]{1,0:T(8,128)}, f32[32,2816]{1,0:T(8,1...) custom-call(bf16[128,1024]{1,0:T(8,128)(2,1)} %get-tuple-element.101, ...), custom_call_target="tpu_custom_call" | custom-call | tf_op jit(solution)/shard_map/finish_part/pallas_call | solution.py:1548
  (3 shorter events, 0.0 us)

commit v7 on v6

--- a/solution.py
+++ b/solution.py
@@ -292,6 +292,14 @@
             copy.wait_send()
 
 
+def partner(me, i, size):
+    total, bit = 0, 1
+    while bit < size:
+        total = total + lax.rem(me // bit + i // bit, 2) * bit
+        bit *= 2
+    return total
+
+
 def chips_within(span_pieces, pieces):
     return min(pieces // 2 - 1, (span_pieces + 1) // 2)
 
@@ -327,7 +335,7 @@
     gate_at = mix_ref.shape[1] // size
     tail_at = gate_at + gate_ref.shape[1] // size
     barrier = pltpu.get_barrier_semaphore()
-    peers = [({"seq": lax.rem(me + i, size)}, here >= 0) for i in range(1, size)]
+    peers = [({"seq": partner(me, i, size)}, here >= 0) for i in range(1, size)]
     side = [({"ctx": here + 1}, (core == 1) & (here < pieces - 1)), ({"ctx": here - 1}, (core == 0) & (here > 0))]
     total = greet(peers + line_neighbours(pieces) + side, barrier)
     pl.semaphore_wait(barrier, total)
@@ -348,7 +356,7 @@
         ][n]
 
     def exchange(n, i):
-        q = lax.rem(me + i, size)
+        q = partner(me, i, size)
         source, target = ends(n, q)
         return pltpu.make_async_remote_copy(
             source, target, seq_send.at[n, i - 1], seq_recv.at[n, i - 1], device_id={"seq": q}, device_id_type=MESH
@@ -374,7 +382,7 @@
         sides[q, 0, :, :inner] = wg_ref[:, q * inner : (q + 1) * inner]
         sides[q, 1, :, :inner] = wu_ref[:, q * inner : (q + 1) * inner]
     line = Line(
-        pieces, [lambda c, i=i: full_ref.at[lax.rem(me + size - i, size), c] for i in range(size)], line_send, line_recv
+        pieces, [lambda c, i=i: full_ref.at[partner(me, i, size), c] for i in range(size)], line_send, line_recv
     )
     for n in range(3):
         own(n).wait()
@@ -748,7 +756,7 @@
         load.start()
     pieces = 2 * wide_ref.shape[0]
     barrier = pltpu.get_barrier_semaphore()
-    peers = [({"seq": lax.rem(me + i, size)}, me >= 0) for i in range(1, size)]
+    peers = [({"seq": partner(me, i, size)}, me >= 0) for i in range(1, size)]
     pl.semaphore_wait(barrier, greet(peers + line_neighbours(pieces), barrier))
     loads[7].wait()
     line = Line(pieces, [lambda c: wds.at[c]], line_send, line_recv)
@@ -767,13 +775,13 @@
     def part_copy(phase, i):
         return pltpu.make_async_remote_copy(
             sent.at[phase, i - 1], got.at[phase, i - 1], send_sem.at[phase, i - 1], recv_sem.at[phase, i - 1],
-            device_id={"seq": lax.rem(me + i, size)}, device_id_type=MESH,
+            device_id={"seq": partner(me, i, size)}, device_id_type=MESH,
         )
 
     def block_copy(buffer, phase, i, owner):
         return pltpu.make_async_remote_copy(
             buffer.at[rows(owner)], buffer.at[rows(owner)], send_sem.at[phase, i - 1], recv_sem.at[phase, i - 1],
-            device_id={"seq": lax.rem(me + i, size)}, device_id_type=MESH,
+            device_id={"seq": partner(me, i, size)}, device_id_type=MESH,
         )
 
     def give_part(phase, i, part):
@@ -793,27 +801,49 @@
 
         return lax.fori_loop(1, size, add, own[...])
 
+    relayed = size == 4
+
+    def half_copy(buffer, phase, n, owner):
+        part = pl.ds(pl.multiple_of(owner * count + (n - 1) * (count // 2), count // 2), count // 2)
+        return pltpu.make_async_remote_copy(
+            buffer.at[part], buffer.at[part], send_sem.at[phase, 1 + n], recv_sem.at[phase, 1 + n],
+            device_id={"seq": partner(me, 3 - n, size)}, device_id_type=MESH,
+        )
+
     def give_block(buffer, phase, value):
         buffer[rows(me)] = value
-
-        def send(i, carry):
+        for i in range(1, 3 if relayed else size):
             block_copy(buffer, phase, i, me).start()
-            return carry
-
-        lax.fori_loop(1, size, send, 0)
 
     def take_block(buffer, phase, i):
-        q = lax.rem(me + size - i, size)
-
-        @pl.when(i > 0)
-        def _():
-            block_copy(buffer, phase, i, q).wait_recv()
-
+        q = partner(me, i, size)
+        if relayed:
+
+            @pl.when(i == 1)
+            def _():
+                for n in (1, 2):
+                    block_copy(buffer, phase, n, partner(me, n, size)).wait_recv()
+                    half_copy(buffer, phase, n, partner(me, n, size)).start()
+
+            @pl.when(i == 3)
+            def _():
+                for n in (1, 2):
+                    half_copy(buffer, phase, n, q).wait_recv()
+
+        else:
+            pl.when(i > 0)(lambda: block_copy(buffer, phase, i, q).wait_recv())
         return q
 
+    def block_left(buffer, phase):
+        for i in range(1, 3 if relayed else size):
+            block_copy(buffer, phase, i, me).wait_send()
+        if relayed:
+            for n in (1, 2):
+                half_copy(buffer, phase, n, partner(me, n, size)).wait_send()
+
     def out_part(k, carry):
-        i = lax.rem(k + 1, size)
-        q = lax.rem(me + i, size)
+        i = size - 1 - k
+        q = partner(me, i, size)
         for h in range(heads):
             hc = slice(h * HEAD, (h + 1) * HEAD)
             out = (oloc_ref[rows(q), hc] + mm(carr_ref[rows(q), hc], sin_ref[h])).astype(BF16)
@@ -835,14 +865,17 @@
     give_block(second, 3, (middle * inv * norm).astype(BF16))
     for load in loads[5:7]:
         load.wait()
-    for distance in range(hops // 2 + 1, hops + 1):
+    deep = wds.shape[1]
+    for distance in range(hops // 2 + 1, hops):
         line.hop(distance)
-    line.finish()
-    deep = wds.shape[1]
-    inner = pieces * deep
-    wd_ref[inner:] = jnp.zeros((wd_ref.shape[0] - inner, D), BF16)
-    for c in range(pieces):
-        wd_ref[c * deep : (c + 1) * deep] = wds[c]
+
+    def take_down():
+        line.hop(hops)
+        line.finish()
+        inner = pieces * deep
+        wd_ref[inner:] = jnp.zeros((wd_ref.shape[0] - inner, D), BF16)
+        for c in range(pieces):
+            wd_ref[c * deep : (c + 1) * deep] = wds[c]
 
     def feed(i, carry):
         q = take_block(second, 3, i)
@@ -853,7 +886,8 @@
         ups[rows(q)] = up
         hid = (gate * jax.nn.sigmoid(gate) * up).astype(BF16)
         hidden[rows(q)] = hid
-        give_part(1, lax.rem(size - i, size), dot(hid, wd_ref[...]))
+        pl.when(i == 0)(take_down)
+        give_part(1, i, dot(hid, wd_ref[...]))
         return carry
 
     lax.fori_loop(0, size, feed, 0)
@@ -880,7 +914,7 @@
         gup = (ghid * silu).astype(BF16)
         ggates[rows(q)] = ggate
         gups[rows(q)] = gup
-        give_part(2, lax.rem(size - i, size), dot(ggate, wg_ref[...], 1, 1) + dot(gup, wu_ref[...], 1, 1))
+        give_part(2, i, dot(ggate, wg_ref[...], 1, 1) + dot(gup, wu_ref[...], 1, 1))
         return carry
 
     lax.fori_loop(0, size, feed_back, 0)
@@ -948,15 +982,11 @@
     for r in range(early):
         sums.left(r)
 
-    def sent_all(i, carry):
+    for i in range(1, size):
         for phase in range(3):
             part_copy(phase, i).wait_send()
-        block_copy(second, 3, i, me).wait_send()
-        block_copy(branch, 4, i, me).wait_send()
-        block_copy(low, 5, i, me).wait_send()
-        return carry
-
-    lax.fori_loop(1, size, sent_all, 0)
+    for buffer, phase in ((second, 3), (branch, 4), (low, 5)):
+        block_left(buffer, phase)
 
 
 def middle_part(
@@ -992,7 +1022,7 @@
             low(2, chips, *tall), dma((2,)), dma((2,)), dma((2, chips)), dma((2, 2, chips)),
             low(rows, D), low(rows, D), low(rows, D), low(3, size - 1, count, D), low(3, size - 1, count, D),
             high(count, D), high(count, D), high(count, D), high(rows, inner), high(rows, inner), low(rows, inner),
-            low(rows, inner), low(rows, inner), dma((6, size - 1)), dma((6, size - 1)),
+            low(rows, inner), low(rows, inner), dma((6, size)), dma((6, size)),
         ],
         compiler_params=pltpu.CompilerParams(
             vmem_limit_bytes=VMEM_LIMIT, collective_id=1, has_side_effects=True
@@ -1295,7 +1325,25 @@
     fix_ref, x_ref, gmid_ref, norms_ref, gw_ref, gain_ref, gsum_ref, loss_ref, gnorm_ref, wide_ref, gatesum_ref,
     ingrad_ref, gmix_ref, ggate_ref, gtail_ref, gwg_ref, gwu_ref, mean_ref, ends_ref, both_ref,
     gp_ref, gg_ref, gs_ref, w_ref, normed_ref, load_sem, wideout_ref, gateout_ref,
-    sent, got, whole, turned, grads, theirs, held, came, blocks, around, along, summed,
+    sent, got, whole, turned, *halves_and_rest,
+):
+    grads, theirs, helds, cames, blocks = [halves_and_rest[2 * n : 2 * n + 2] for n in range(5)]
+    around, along, summed, *sems = halves_and_rest[10:]
+    final_body(
+        size, pieces, heads, norm_at, inner, gp_any, gg_any, gs_any, w_any, normed_any,
+        fix_ref, x_ref, gmid_ref, norms_ref, gw_ref, gain_ref, gsum_ref, loss_ref, gnorm_ref, wide_ref, gatesum_ref,
+        ingrad_ref, gmix_ref, ggate_ref, gtail_ref, gwg_ref, gwu_ref, mean_ref, ends_ref, both_ref,
+        gp_ref, gg_ref, gs_ref, w_ref, normed_ref, load_sem, wideout_ref, gateout_ref,
+        sent, got, whole, turned, grads, theirs, helds, cames, blocks, around, along, summed, *sems,
+    )
+
+
+def final_body(
+    size, pieces, heads, norm_at, inner, gp_any, gg_any, gs_any, w_any, normed_any,
+    fix_ref, x_ref, gmid_ref, norms_ref, gw_ref, gain_ref, gsum_ref, loss_ref, gnorm_ref, wide_ref, gatesum_ref,
+    ingrad_ref, gmix_ref, ggate_ref, gtail_ref, gwg_ref, gwu_ref, mean_ref, ends_ref, both_ref,
+    gp_ref, gg_ref, gs_ref, w_ref, normed_ref, load_sem, wideout_ref, gateout_ref,
+    sent, got, whole, turned, grads, theirs, helds, cames, blocks, around, along, summed,
     local_sem, seq_send, seq_recv, pair_send, pair_recv, line_send, line_recv, ctx_send, ctx_recv,
 ):
     me, here = lax.axis_index("seq"), lax.axis_index("ctx")
@@ -1309,7 +1357,7 @@
     for load in loads:
         load.start()
     barrier = pltpu.get_barrier_semaphore()
-    peers = [({"seq": lax.rem(me + i, size)}, here >= 0) for i in range(1, size)]
+    peers = [({"seq": partner(me, i, size)}, here >= 0) for i in range(1, size)]
     peers += [({"ctx": lax.rem(here + i, pieces)}, here >= 0) for i in range(1, pieces)]
     pl.semaphore_wait(barrier, greet(peers, barrier))
 
@@ -1320,11 +1368,11 @@
         return pl.ds(pl.multiple_of(q * count, count), count)
 
     def to_peer(n, i):
-        q = lax.rem(me + i, size)
+        q = partner(me, i, size)
         source, target = [
             (sent.at[i - 1], got.at[i - 1]), (wide_ref.at[:, q], wideout_ref.at[me]),
-            (around.at[me], around.at[me]), (held.at[here // 2, q], blocks.at[me]),
-            (gatesum_ref.at[q], gateout_ref.at[me]),
+            (around.at[me], around.at[me]), (helds[0].at[here // 2, q], blocks[0].at[me]),
+            (gatesum_ref.at[q], gateout_ref.at[me]), (helds[1].at[here // 2, q], blocks[1].at[me]),
         ][n]
         return pltpu.make_async_remote_copy(
             source, target, seq_send.at[n, i - 1], seq_recv.at[n, i - 1], device_id={"seq": q}, device_id_type=MESH
@@ -1351,27 +1399,36 @@
             )
             whole[:, tile] = value
 
-        def give(i, carry):
-            sent[i - 1] = whole[rows(lax.rem(me + i, size))].astype(BF16)
+        def give(k, carry):
+            i = size - 1 - k
+            sent[i - 1] = whole[rows(partner(me, i, size))].astype(BF16)
             pltpu.make_async_remote_copy(
                 sent.at[i - 1], got.at[i - 1], seq_send.at[0, i - 1], seq_recv.at[0, i - 1],
-                device_id={"seq": lax.rem(me + i, size)}, device_id_type=MESH,
+                device_id={"seq": partner(me, i, size)}, device_id_type=MESH,
             ).start()
             return carry
 
-        lax.fori_loop(1, size, give, 0)
+        lax.fori_loop(0, size - 1, give, 0)
 
     turned[...] = normed_ref[...].T
     rank_rows = D // (size * pieces)
-    for source, at in ((gp_ref, 0), (gs_ref, gate_at)):
-        width = source.shape[1]
-        for first in range(0, width, 256):
-            cols = min(256, width - first)
-            grad = dot(turned[...], source[:, first : first + cols])
-            for r in range(size):
-                for c in range(pieces):
-                    row = (r * pieces + c) * rank_rows
-                    grads[c // 2, c % 2, r, :, at + first : at + first + cols] = grad[row : row + rank_rows].astype(BF16)
+    pairs = [Siblings([grads[n]], [theirs[n]], [helds[n]], pair_send.at[n], pair_recv.at[n]) for n in range(2)]
+    lines = [LineSum(pieces, [helds[n]], [cames[n]], line_send.at[n], line_recv.at[n]) for n in range(2)]
+    split = grads[0].shape[4]
+
+    def gradient(source, first, cols, n, at):
+        grad = dot(turned[...], source[:, first : first + cols])
+        for r in range(size):
+            for c in range(pieces):
+                row = (r * pieces + c) * rank_rows
+                grads[n][c // 2, c % 2, r, :, at : at + cols] = grad[row : row + rank_rows].astype(BF16)
+
+    for first in range(0, split, 256):
+        gradient(gp_ref, first, min(256, split - first), 0, first)
+    pairs[0].start()
+    for first in range(split, gate_at, 256):
+        gradient(gp_ref, first, min(256, gate_at - first), 1, first - split)
+    gradient(gs_ref, 0, HEAD, 1, gate_at - split)
     channels = gw_ref.shape[1]
     mine = channel_rows(D // size, channels)
     taps = jnp.zeros((D // size, HEAD), F32)
@@ -1379,18 +1436,19 @@
         spread = jnp.where(mine, gw_ref[lag : lag + 1], 0.0).astype(BF16)
         taps = taps + dot(spread, tap_lanes(channels, CONV - 1 - lag, norm_at + 3))
     for c in range(pieces):
-        grads[c // 2, c % 2, me, :, gate_at:] = (
-            grads[c // 2, c % 2, me, :, gate_at:].astype(F32) + taps[c * rank_rows : (c + 1) * rank_rows]
+        grads[1][c // 2, c % 2, me, :, gate_at - split :] = (
+            grads[1][c // 2, c % 2, me, :, gate_at - split :].astype(F32) + taps[c * rank_rows : (c + 1) * rank_rows]
         ).astype(BF16)
-    pair = Siblings([grads], [theirs], [held], pair_send, pair_recv)
-    line = LineSum(pieces, [held], [came], line_send, line_recv)
-    pair.start()
+    pairs[1].start()
+    pairs[0].add()
+    lines[0].round(0)
     parts()
-    pair.add()
-    line.round(0)
+    pairs[1].add()
+    lines[1].round(0)
     rounds = pieces // 2 - 1
     for r in range(1, rounds - 1):
-        line.round(r)
+        for line in lines:
+            line.round(r)
     for i in range(1, size):
         to_peer(0, i).wait_recv()
     gnormed = whole[rows(me)]
@@ -1421,10 +1479,11 @@
     ]
     for copy in kept:
         copy.start()
-    for i in range(1, size):
+    for i in reversed(range(1, size)):
         to_peer(1, i).start()
         to_peer(4, i).start()
-    line.round(rounds - 1)
+    for line in lines:
+        line.round(rounds - 1)
     for i in range(1, size):
         to_peer(2, i).wait_recv()
     mine = around[0]
@@ -1433,10 +1492,11 @@
     along[here] = mine
     for i in range(1, pieces):
         to_piece(i).start()
-    line.finish()
-    blocks[me] = held[here // 2, me]
-    for i in range(1, size):
-        to_peer(3, i).start()
+    for n, phase in ((0, 3), (1, 5)):
+        lines[n].finish()
+        blocks[n][me] = helds[n][here // 2, me]
+        for i in reversed(range(1, size)):
+            to_peer(phase, i).start()
     for i in range(1, pieces):
         to_piece(i).wait_recv()
     total = along[0]
@@ -1454,22 +1514,28 @@
     for copy in kept:
         copy.wait()
     for i in range(1, size):
-        to_peer(3, i).wait_recv()
-        to_peer(1, i).wait_recv()
-        to_peer(4, i).wait_recv()
+        for n in (1, 4, 3):
+            to_peer(n, i).wait_recv()
+    wide_cols = tail_at - gate_at
     for r in range(size):
-        block = blocks[r].astype(F32)
-        gmix_ref[:, r * gate_at : (r + 1) * gate_at] = block[:, :gate_at]
-        ggate_ref[:, r * (tail_at - gate_at) : (r + 1) * (tail_at - gate_at)] = gateout_ref[r].astype(F32)
-        tail = tail + block[:, gate_at:]
         gwg_ref[:, r * inner : (r + 1) * inner] = wideout_ref[r, 0, :, :inner].astype(F32)
         gwu_ref[:, r * inner : (r + 1) * inner] = wideout_ref[r, 1, :, :inner].astype(F32)
+        ggate_ref[:, r * wide_cols : (r + 1) * wide_cols] = gateout_ref[r].astype(F32)
+        gmix_ref[:, r * gate_at : r * gate_at + split] = blocks[0][r].astype(F32)
+    for i in range(1, size):
+        to_peer(5, i).wait_recv()
+    for r in range(size):
+        block = blocks[1][r].astype(F32)
+        gmix_ref[:, r * gate_at + split : (r + 1) * gate_at] = block[:, : gate_at - split]
+        tail = tail + block[:, gate_at - split :]
     gtail_ref[...] = tail
-    pair.left()
-    for r in range(pieces // 2 - 1):
-        line.left(r)
+    for pair in pairs:
+        pair.left()
+    for line in lines:
+        for r in range(pieces // 2 - 1):
+            line.left(r)
     for i in range(1, size):
-        for n in range(5):
+        for n in range(6):
             to_peer(n, i).wait_send()
     for i in range(1, pieces):
         to_piece(i).wait_send()
@@ -1482,7 +1548,8 @@
     count = x.shape[0]
     chips = pieces // 2
     held, inner = D // (size * pieces), FF // size
-    width = gp.shape[1] + gs.shape[1]
+    split = WIDE if heads > 1 else 3 * HEAD
+    widths = (split, gp.shape[1] - split + gs.shape[1])
     small = (8 + 2 * (D // HEAD), HEAD)
     vmem = pl.BlockSpec(memory_space=pltpu.VMEM)
     out = lambda *dims: jax.ShapeDtypeStruct(dims, F32)
@@ -1501,9 +1568,11 @@
             low(*gp.shape), low(*gg.shape), low(*gs.shape), low(*weights.shape), low(*normed.shape), dma((5,)),
             low(size, 2, held, wide.shape[3]), low(*gatesum.shape),
             low(size - 1, count, D), low(size - 1, count, D), high(size * count, D), low(D, normed.shape[0]),
-            low(chips, 2, size, held, width), low(chips, size, held, width), low(chips, size, held, width),
-            low(2, chips, size, held, width), low(size, held, width), high(size, *small), high(pieces, *small), high(*small),
-            dma((2,)), dma((5, size - 1)), dma((5, size - 1)), dma((1,)), dma((1,)), dma((1, chips)), dma((1, 2, chips)),
+            *[low(chips, 2, size, held, w) for w in widths], *[low(chips, size, held, w) for w in widths],
+            *[low(chips, size, held, w) for w in widths], *[low(2, chips, size, held, w) for w in widths],
+            *[low(size, held, w) for w in widths], high(size, *small), high(pieces, *small), high(*small),
+            dma((2,)), dma((6, size - 1)), dma((6, size - 1)), dma((2, 1)), dma((2, 1)), dma((2, 1, chips)),
+            dma((2, 1, 2, chips)),
             dma((pieces - 1,)), dma((pieces - 1,)),
         ],
         compiler_params=pltpu.CompilerParams(

time: 300 us -> 286 us (0.953)
  Pallas kernels: 289 us -> 275 us
    pallas_call x1, Pallas kernels: 97.6 us -> 87.3 us  [middle_part(): pl.pallas_call(functools.partial(middle_kernel, size, heads, float(token_...]
where the time goes in v7:
time: 286 us
  Pallas kernels  275 us (96%)
  local copies, waits for them, and re-layouts  5.29 us (2%)
  other arithmetic  3.23 us (1%)
    pallas_call x1, Pallas kernels, middle_part(): pl.pallas_call(functools.partial(middle_kernel, size, heads, float(token_...  87.3 us
    pallas_call x1, Pallas kernels, recurrence_forward(): pl.pallas_call(functools.partial(fwd_kernel, heads, pieces, blocks // per...  50.7 us
    pallas_call x1, Pallas kernels, recurrence_backward(): pl.pallas_call(functools.partial(bwd_kernel, heads, pieces, blocks // per...  46.2 us
    pallas_call x1, Pallas kernels, final_part(): pl.pallas_call(functools.partial(final_kernel, size, pieces, heads, norm_...  44.9 us
    pallas_call x1, Pallas kernels, start_gather(): pl.pallas_call(functools.partial(start_kernel, size, pieces), in_specs=[a...  41.8 us

profile of v7, /device:TPU:0, one launch (start us, length us, event | category | flops | bytes accessed | tf_op | source)
XLA Modules:
  0.0 285.8 jit_solution(9823793826238598426)
XLA Ops:
  0.6 1.3 convert_reduce_fusion
  1.9 1.2 maximum_convert_fusion.rates_ref
  3.2 0.8 pad_dynamic-slice_fusion
  3.9 0.1 fusion.7
  4.0 0.7 fusion
  4.7 0.8 copy.38
  5.4 0.8 copy.39
  6.2 0.8 copy.40
  6.9 0.6 stack.48.marks_ref
  7.6 0.8 copy.37
  8.4 0.1 reshape.77
  8.5 0.7 concatenate.3.tail_ref
  9.2 41.8 %start_gather.1 = (bf16[512,1024]{1,0:T(8,128)(2,1)}, bf16[16,1024]{1,0:T(8,128)(2,1)}, bf16[4,8,32,1664]{3,2,1,0:T(8,128)(2,1)}, bf16[4,2,32,768]{3,2,1,0:T(8,128)(2,1)}) custom-call(bf16[128,1024]{1,0:T(8,128)(2,1)} %x_ref.5, bf16[32,5120]{1,0:T(8,128)(2,1)} %mix_ref.1, bf16[32,1024]{1,0:T(8,128)(2,1)} %gate_ref.1, bf16[32,128]{1,0:T(8,128)(2,1)} %concatenate.3.tail_ref, ...), custom_call_target="tpu_custom_call" | custom-call | tf_op jit(solution)/shard_map/start_gather/pallas_call | solution.py:429
  51.0 50.7 %recurrence_forward.1 = (bf16[528,1280]{1,0:T(8,128)(2,1)}, bf16[512,1024]{1,0:T(8,128)(2,1)}, f32[512,256]{1,0:T(8,128)}, f32[512,128]{1,0:T(8,128)}, f32[512,1...) custom-call(f32[2,8]{1,0:T(2,128)} %maximum_convert_fusion.rates_ref, ...), custom_call_target="tpu_custom_call" | custom-call | tf_op jit(solution)/shard_map/recurrence_forward/pallas_call | solution.py:698
  101.7 87.3 %middle_part.1 = (bf16[128,1024]{1,0:T(8,128)(2,1)}, f32[128,1024]{1,0:T(8,128)}, bf16[512,256]{1,0:T(8,128)(2,1)}, bf16[512,256]{1,0:T(8,128)(2,1)}, f32[2,128,...) custom-call(bf16[128,1024]{1,0:T(8,128)(2,1)} %x_ref.5, ...), custom_call_target="tpu_custom_call" | custom-call | tf_op jit(solution)/shard_map/middle_part/pallas_call | solution.py:1006
  189.0 46.2 %recurrence_backward.1 = (bf16[512,1280]{1,0:T(8,128)(2,1)}, bf16[8,1280]{1,0:T(8,128)(2,1)}, f32[8,1280]{1,0:T(8,128)}, bf16[512,128]{1,0:T(8,128)(2,1)}, f32[8...) custom-call(bf16[8,2,128,128]{3,2,1,0:T(8,128)(2,1)} %get-tuple-elem, ...), custom_call_target="tpu_custom_call" | custom-call | tf_op jit(solution)/shard_map/recurrence_backward/pallas_call | solution.py:1286
  235.2 44.9 %final_part.1 = (f32[128,1024]{1,0:T(8,128)}, f32[32,5120]{1,0:T(8,128)}, f32[32,1024]{1,0:T(8,128)}, f32[32,128]{1,0:T(8,128)}, f32[32,2816]{1,0:T(8,128)}, /*i...) custom-call(bf16[512,1280]{1,0:T(8,128)(2,1)} %get-tuple-element.125.gp_any, ...), custom_call_target="tpu_custom_call" | custom-call | tf_op jit(solution)/shard_map/final_part/pallas_call | solution.py:1559
  280.2 3.9 %finish_part.1 = (bf16[128,1024]{1,0:T(8,128)(2,1)}, f32[128,1024]{1,0:T(8,128)}, f32[32,5120]{1,0:T(8,128)}, f32[32,1024]{1,0:T(8,128)}, f32[32,2816]{1,0:T(8,1...) custom-call(bf16[128,1024]{1,0:T(8,128)(2,1)} %get-tuple-element.101, ...), custom_call_target="tpu_custom_call" | custom-call | tf_op jit(solution)/shard_map/finish_part/pallas_call | solution.py:1617
  (3 shorter events, 0.0 us)

commit v8 on v7

--- a/solution.py
+++ b/solution.py
@@ -325,8 +325,9 @@
 
 
 def start_kernel(
-    size, pieces, x_ref, mix_ref, gate_ref, tail_ref, wg_ref, wu_ref, xfull_ref, halo_ref, full_ref, stage_ref,
-    sides, local_sem, seq_send, seq_recv, line_send, line_recv, halo_sem,
+    size, pieces, norm_at, x_ref, mix_ref, gate_ref, scal_ref, norma_ref, normm_ref, taps_ref, mask_ref, wg_ref, wu_ref,
+    xfull_ref, halo_ref, full_ref, stage_ref,
+    tail_ref, sides, local_sem, seq_send, seq_recv, line_send, line_recv, halo_sem,
 ):
     me, here = lax.axis_index("seq"), lax.axis_index("ctx")
     count = x_ref.shape[0]
@@ -334,6 +335,22 @@
     inner = wg_ref.shape[1] // size
     gate_at = mix_ref.shape[1] // size
     tail_at = gate_at + gate_ref.shape[1] // size
+
+    def placed(rows_, lane):
+        at = (iota((rows_.shape[0], HEAD), 1) == lane + iota((rows_.shape[0], HEAD), 0)).astype(BF16)
+        return lax.dot_general(rows_, at, (((0,), (0,)), ((), ())), preferred_element_type=F32)
+
+    held, channels = tail_ref.shape[0], taps_ref.shape[1]
+    pack = placed(scal_ref[...], 0) + placed(norma_ref[...], norm_at) + placed(normm_ref[...], norm_at + 1)
+    valid = jnp.sum(mask_ref[...].astype(F32), axis=1, keepdims=True)
+    pack = pack + jnp.where((iota((held, HEAD), 0) == 0) & (iota((held, HEAD), 1) == norm_at + 2), valid, 0.0)
+    mine = channel_rows(held, channels)
+    for tap in range(CONV):
+        spread = jnp.where(mine, taps_ref[tap : tap + 1].astype(F32), 0.0).astype(BF16)
+        pack = pack + lax.dot_general(
+            spread, tap_lanes(channels, tap, norm_at + 3), (((1,), (0,)), ((), ())), preferred_element_type=F32
+        )
+    tail_ref[...] = pack.astype(BF16)
     barrier = pltpu.get_barrier_semaphore()
     peers = [({"seq": partner(me, i, size)}, here >= 0) for i in range(1, size)]
     side = [({"ctx": here + 1}, (core == 1) & (here < pieces - 1)), ({"ctx": here - 1}, (core == 0) & (here > 0))]
@@ -419,29 +436,29 @@
             exchange(n, i).wait_send()
 
 
-def start_gather(size, pieces, x, mix, gate, tail, w_gate, w_up):
+def start_gather(size, pieces, norm_at, x, mix, gate, scal, norm_a, norm_m, taps, mask, w_gate, w_up):
     anywhere = pl.BlockSpec(memory_space=pl.ANY)
     vmem = pl.BlockSpec(memory_space=pltpu.VMEM)
     out = lambda *dims: jax.ShapeDtypeStruct(dims, BF16)
     dma = pltpu.SemaphoreType.DMA
     held, padded = w_gate.shape[0], lanes_for(w_gate.shape[1] // size)
-    width = (mix.shape[1] + gate.shape[1]) // size + tail.shape[1]
+    width = (mix.shape[1] + gate.shape[1]) // size + HEAD
     return pl.pallas_call(
-        functools.partial(start_kernel, size, pieces),
-        in_specs=[anywhere] * 4 + [vmem] * 2,
+        functools.partial(start_kernel, size, pieces, norm_at),
+        in_specs=[anywhere] * 3 + [vmem] * 7,
         out_specs=[anywhere] * 4,
         out_shape=[
             out(x.shape[0] * size, D), out(HALO, D), out(size, pieces, held, width), out(size, 2, held, padded),
         ],
         scratch_shapes=[
-            pltpu.VMEM((size, 2, held, padded), BF16),
+            pltpu.VMEM((held, HEAD), BF16), pltpu.VMEM((size, 2, held, padded), BF16),
             dma((6,)), dma((5, size - 1)), dma((5, size - 1)), dma((size, 3, pieces)), dma((size, pieces)), dma((2,)),
         ],
         compiler_params=pltpu.CompilerParams(
             vmem_limit_bytes=VMEM_LIMIT, collective_id=2, has_side_effects=True
         ),
         name="start_gather",
-    )(x, mix, gate, tail, w_gate, w_up)
+    )(x, mix, gate, scal, norm_a, norm_m, taps, mask, w_gate, w_up)
 
 
 def exact(a, b, ca=1, cb=0):
@@ -923,6 +940,13 @@
     grad = dot(hidden[...], branch[...], 0, 0)
     for c in range(pieces):
         tall_ref[c // 2, c % 2, :deep] = grad[c * deep : (c + 1) * deep].astype(BF16)
+    parts = ((tall_ref, ttheirs, theld, tcame), (wide_ref, wtheirs, wheld, wcame))
+    pairs = [
+        Siblings([part], [theirs], [kept], pair_send.at[n], pair_recv.at[n])
+        for n, (part, theirs, kept, _) in enumerate(parts)
+    ]
+    sums = [LineSum(pieces, [kept], [came], sum_send.at[n], sum_recv.at[n]) for n, (_, _, kept, came) in enumerate(parts)]
+    pairs[0].start()
     for n, side in enumerate((ggates, gups)):
         grad = dot(second[...], side[...], 0, 0)
         for c in range(pieces):
@@ -931,11 +955,10 @@
                 wide_ref[c // 2, c % 2, (n * size + r) * held : (n * size + r + 1) * held] = grad[
                     first : first + held
                 ].astype(BF16)
-    pair = Siblings([wide_ref, tall_ref], [wtheirs, ttheirs], [wheld, theld], pair_send, pair_recv)
-    sums = LineSum(pieces, [wheld, theld], [wcame, tcame], sum_send, sum_recv)
-    pair.start()
-    pair.add()
-    sums.round(0)
+    pairs[1].start()
+    for pair, line_sum in zip(pairs, sums):
+        pair.add()
+        line_sum.round(0)
     gsecond = take_parts(2)
     middle = mid[...]
     inv = lax.rsqrt(jnp.mean(middle * middle, axis=1, keepdims=True) + NORM_EPS)
@@ -972,15 +995,17 @@
     out_back(0, 0)
     early = max(1, hops - 1)
     for r in range(1, early):
-        sums.round(r)
+        for line_sum in sums:
+            line_sum.round(r)
     lax.fori_loop(1, size, out_back, 0)
     grad = dot(mixed_ref[...], low[...], 0, 0)
     for c in range(pieces):
         outg_ref[c // 2, c % 2] = grad[c * held : (c + 1) * held].astype(BF16)
-    sums.settle(early)
-    pair.left()
-    for r in range(early):
-        sums.left(r)
+    for pair, line_sum in zip(pairs, sums):
+        line_sum.settle(early)
+        pair.left()
+        for r in range(early):
+            line_sum.left(r)
 
     for i in range(1, size):
         for phase in range(3):
@@ -1019,7 +1044,7 @@
             low(*wout.shape), low(*wg.shape), low(*wu.shape), low(inner, D), dma((8,)),
             low(rows, heads * HEAD), low(rows, heads * HEAD), dma((1, 3, pieces)), dma((1, pieces)), low(pieces, *wd.shape),
             low(chips, 2, *wide), low(chips, 2, *tall), low(chips, *wide), low(chips, *tall), low(2, chips, *wide),
-            low(2, chips, *tall), dma((2,)), dma((2,)), dma((2, chips)), dma((2, 2, chips)),
+            low(2, chips, *tall), dma((2, 1)), dma((2, 1)), dma((2, 1, chips)), dma((2, 1, 2, chips)),
             low(rows, D), low(rows, D), low(rows, D), low(3, size - 1, count, D), low(3, size - 1, count, D),
             high(count, D), high(count, D), high(count, D), high(rows, inner), high(rows, inner), low(rows, inner),
             low(rows, inner), low(rows, inner), dma((6, size)), dma((6, size)),
@@ -1043,7 +1068,10 @@
     block = steps - 1 - step
     here = lax.axis_index("ctx")
     core = lax.rem(here, 2)
-    early = LineSum(pieces, [wheld, theld], [wcame, tcame], early_send, early_recv)
+    early = [
+        LineSum(pieces, [kept], [came], early_send.at[n], early_recv.at[n])
+        for n, (kept, came) in enumerate(((theld, tcame), (wheld, wcame)))
+    ]
     pair = Siblings([outg_ref, gateg], [otheirs, gtheirs], [oheld, gheld], pair_send, pair_recv)
     line = LineSum(pieces, [oheld, gheld], [ocame, gcame], line_send, line_recv)
     rounds = pieces // 2 - 1
@@ -1072,7 +1100,8 @@
         for distance in range(1, spread.reach + 1):
             spread.hop(distance)
         spread.finish()
-        early.launch(begun)
+        for one in early:
+            one.launch(begun)
         pair.start()
 
         farthest = jnp.minimum(here + span_pieces, pieces - 1)
@@ -1094,7 +1123,7 @@
 
     for r in range(begun + 1, rounds):
         at = min(steps - 1, 1 + ((r - begun) * (steps - 1)) // (rounds - begun))
-        pl.when(step == at)(lambda r=r: early.round(r))
+        pl.when(step == at)(lambda r=r: [one.round(r) for one in early] and None)
     pl.when(step == 1)(pair.add)
     for r in range(rounds):
         pl.when(step == when_round[r])(lambda r=r: line.round(r))
@@ -1249,7 +1278,8 @@
             passing.wait_recv()
             fix_ref[...] = (last[...] + rim_in[...]).astype(BF16)
 
-        early.finish()
+        for one in early:
+            one.finish()
         line.finish()
         widesum_ref[...] = wheld[here // 2]
         tallsum_ref[...] = theld[here // 2].astype(F32)
@@ -1257,7 +1287,8 @@
         gatesum_ref[...] = gheld[here // 2]
         pair.left()
         for r in range(begun, rounds):
-            early.left(r)
+            for one in early:
+                one.left(r)
         for r in range(rounds):
             line.left(r)
         pl.when(here > 0)(passing.wait_send)
@@ -1310,7 +1341,7 @@
             low(chips, *wide_chunk), low(chips, *tall_chunk), low(2, chips, *wide_chunk), low(2, chips, *tall_chunk),
             low(chips, 2, *gate_chunk), low(chips, *out_chunk), low(chips, *gate_chunk), low(chips, *out_chunk),
             low(chips, *gate_chunk), low(2, chips, *out_chunk), low(2, chips, *gate_chunk),
-            dma((1, 3, pieces)), dma((1, pieces)), dma((2,)), dma((2,)), dma((2, chips)), dma((2, 2, chips)),
+            dma((1, 3, pieces)), dma((1, pieces)), dma((2,)), dma((2,)), dma((2, 1, chips)), dma((2, 1, 2, chips)),
             dma((2, chips)), dma((2, 2, chips)), dma((2,)),
         ],
         compiler_params=pltpu.CompilerParams(
@@ -1641,19 +1672,10 @@
     held = mix_proj.shape[0]
     scal_cols = HEADS * (NH + 1)
     norm_at, taps_at = scal_cols, scal_cols + 3
-    taps_end = taps_at + CONV * conv_weight.shape[0] // held
-
-    count_here = jnp.sum(valid_mask.astype(F32)).astype(BF16)
-    tail = jnp.concatenate(
-        [
-            scalar_proj, norm_attn[:, None], norm_mlp[:, None],
-            jnp.where(iota((held, 1), 0) == 0, count_here, jnp.zeros((), BF16)),
-            conv_weight.reshape(held, -1), jnp.zeros((held, HEAD - taps_end), BF16),
-        ],
-        axis=1,
-    )
+
     x_full, halo, gathered, stage = start_gather(
-        seq_size, pieces, block_input, mix_proj, gate_proj, tail, w_gate, w_up
+        seq_size, pieces, norm_at, block_input, mix_proj, gate_proj, scalar_proj.T, norm_attn[None, :],
+        norm_mlp[None, :], conv_weight.T, valid_mask[None, :], w_gate, w_up,
     )
     weights = gathered.reshape(D, -1)
     piece_start = index * rows

time: 286 us -> 278 us (0.972)
  local copies, waits for them, and re-layouts: 5.29 us -> 1.41 us
where the time goes in v8:
time: 278 us
  Pallas kernels  273 us (98%)
    pallas_call x1, Pallas kernels, middle_part(): pl.pallas_call(functools.partial(middle_kernel, size, heads, float(token_...  89.3 us
    pallas_call x1, Pallas kernels, recurrence_forward(): pl.pallas_call(functools.partial(fwd_kernel, heads, pieces, blocks // per...  50.7 us
    pallas_call x1, Pallas kernels, final_part(): pl.pallas_call(functools.partial(final_kernel, size, pieces, heads, norm_...  43.6 us
    pallas_call x1, Pallas kernels, recurrence_backward(): pl.pallas_call(functools.partial(bwd_kernel, heads, pieces, blocks // per...  43.5 us
    pallas_call x1, Pallas kernels, start_gather(): pl.pallas_call(functools.partial(start_kernel, size, pieces, norm_at), in...  41.9 us

profile of v8, /device:TPU:0, one launch (start us, length us, event | category | flops | bytes accessed | tf_op | source)
XLA Modules:
  0.0 278.1 jit_solution(12992990015365888458)
XLA Ops:
  0.6 1.2 maximum_convert_fusion.rates_ref
  1.9 0.8 pad_dynamic-slice_fusion
  2.7 0.1 fusion.6
  2.7 0.6 stack.48.marks_ref
  3.4 41.9 %start_gather.1 = (bf16[512,1024]{1,0:T(8,128)(2,1)}, bf16[16,1024]{1,0:T(8,128)(2,1)}, bf16[4,8,32,1664]{3,2,1,0:T(8,128)(2,1)}, bf16[4,2,32,768]{3,2,1,0:T(8,128)(2,1)}) custom-call(bf16[128,1024]{1,0:T(8,128)(2,1)} %x_ref.5, bf16[32,5120]{1,0:T(8,128)(2,1)} %mix_ref.1, bf16[32,1024]{1,0:T(8,128)(2,1)} %gate_ref.1, bf16[24,32]{1,0:T(8,128)(2,1)} %bitcast.33, ...), custom_call_target="tpu_custom_call" | custom-call | tf_op jit(solution)/shard_map/start_gather/pallas_call | solution.py:446
  45.3 50.7 %recurrence_forward.1 = (bf16[528,1280]{1,0:T(8,128)(2,1)}, bf16[512,1024]{1,0:T(8,128)(2,1)}, f32[512,256]{1,0:T(8,128)}, f32[512,128]{1,0:T(8,128)}, f32[512,1...) custom-call(f32[2,8]{1,0:T(2,128)} %maximum_convert_fusion.rates_ref, ...), custom_call_target="tpu_custom_call" | custom-call | tf_op jit(solution)/shard_map/recurrence_forward/pallas_call | solution.py:715
  96.0 89.3 %middle_part.1 = (bf16[128,1024]{1,0:T(8,128)(2,1)}, f32[128,1024]{1,0:T(8,128)}, bf16[512,256]{1,0:T(8,128)(2,1)}, bf16[512,256]{1,0:T(8,128)(2,1)}, f32[2,128,...) custom-call(bf16[128,1024]{1,0:T(8,128)(2,1)} %x_ref.5, ...), custom_call_target="tpu_custom_call" | custom-call | tf_op jit(solution)/shard_map/middle_part/pallas_call | solution.py:1031
  185.4 43.5 %recurrence_backward.1 = (bf16[512,1280]{1,0:T(8,128)(2,1)}, bf16[8,1280]{1,0:T(8,128)(2,1)}, f32[8,1280]{1,0:T(8,128)}, bf16[512,128]{1,0:T(8,128)(2,1)}, f32[8...) custom-call(bf16[8,2,128,128]{3,2,1,0:T(8,128)(2,1)} %get-tuple-elem, ...), custom_call_target="tpu_custom_call" | custom-call | tf_op jit(solution)/shard_map/recurrence_backward/pallas_call | solution.py:1317
  228.9 43.6 %final_part.1 = (f32[128,1024]{1,0:T(8,128)}, f32[32,5120]{1,0:T(8,128)}, f32[32,1024]{1,0:T(8,128)}, f32[32,128]{1,0:T(8,128)}, f32[32,2816]{1,0:T(8,128)}, /*i...) custom-call(bf16[512,1280]{1,0:T(8,128)(2,1)} %get-tuple-element.125.gp_any, ...), custom_call_target="tpu_custom_call" | custom-call | tf_op jit(solution)/shard_map/final_part/pallas_call | solution.py:1590
  272.5 3.9 %finish_part.1 = (bf16[128,1024]{1,0:T(8,128)(2,1)}, f32[128,1024]{1,0:T(8,128)}, f32[32,5120]{1,0:T(8,128)}, f32[32,1024]{1,0:T(8,128)}, f32[32,2816]{1,0:T(8,1...) custom-call(bf16[128,1024]{1,0:T(8,128)(2,1)} %get-tuple-element.101, ...), custom_call_target="tpu_custom_call" | custom-call | tf_op jit(solution)/shard_map/finish_part/pallas_call | solution.py:1648
  (2 shorter events, 0.0 us)

commit v9 on v8

--- a/solution.py
+++ b/solution.py
@@ -255,6 +255,11 @@
         top = self.chips - 1
         pl.when(self.chip > 0)(lambda: self.take(self.chip, UP))
         pl.when(self.chip < top)(lambda: self.take(self.chip, DOWN))
+
+
+def early_rounds(pieces):
+    rounds = pieces // 2 - 1
+    return max(1, rounds - 1), max(1, rounds - 2)
 
 
 class Siblings:
@@ -477,7 +482,7 @@
 
 
 def front_body(
-    heads, norm_at, rates_ref, x_ref, halo_ref, w_ref, marks_ref,
+    heads, norm_at, alog_ref, lift_ref, x_ref, halo_ref, w_ref, marks_ref,
     proj_ref, normed_ref, gate_ref, tok_ref, slope_ref, col_ref, row_ref, taps_ref, norms_ref,
 ):
     me = lax.axis_index("seq")
@@ -515,8 +520,12 @@
     rate, lift = jnp.zeros((1, HEAD), F32), jnp.zeros((1, HEAD), F32)
     for h in range(heads):
         here = lane == lane_of(h, NH)
-        rate = jnp.where(here, -jnp.exp(jnp.zeros((1, HEAD), F32) + rates_ref[0, me * heads + h]), rate)
-        lift = jnp.where(here, rates_ref[1, me * heads + h], lift)
+        mine_here = iota((1, HEADS), 1) == me * heads + h
+        own = [
+            jnp.sum(jnp.where(mine_here, ref[...].astype(F32), 0.0), axis=1, keepdims=True) for ref in (alog_ref, lift_ref)
+        ]
+        rate = jnp.where(here, -jnp.exp(own[0]), rate)
+        lift = jnp.where(here, own[1], lift)
     is_log = (lane % (NH + 1) == NH) & (lane < lane_of(heads, 0))
     lifted = raw + lift
     sig = jax.nn.sigmoid(lifted)
@@ -547,7 +556,7 @@
 
 def fwd_kernel(
     heads, pieces, steps, per, span_pieces, norm_at,
-    rates_ref, x_ref, halo_ref, full_ref, marks_ref, stage_ref, wo_ref,
+    alog_ref, lift_ref, x_ref, halo_ref, full_ref, marks_ref, stage_ref, wo_ref,
     proj_ref, normed_ref, gate_ref, tok_ref, slope_ref, col_ref, row_ref, taps_ref, norms_ref,
     oloc_ref, carr_ref, sin_ref, mapsout_ref, conv_ref, q_ref, k_ref, v_ref, t_ref, kk_ref, at_ref, uw_ref, pl_ref,
     wgfull_ref, wufull_ref, wofull_ref,
@@ -576,7 +585,7 @@
             copy.wait()
         weights.own()
         front_body(
-            heads, norm_at, rates_ref, x_ref, halo_ref, full_ref, marks_ref,
+            heads, norm_at, alog_ref, lift_ref, x_ref, halo_ref, full_ref, marks_ref,
             proj_ref, normed_ref, gate_ref, tok_ref, slope_ref, col_ref, row_ref, taps_ref, norms_ref,
         )
         for h in range(heads):
@@ -693,7 +702,7 @@
             copy.wait()
 
 
-def recurrence_forward(heads, pieces, span_pieces, norm_at, rates, x_full, halo, weights, marks, stage, w_out):
+def recurrence_forward(heads, pieces, span_pieces, norm_at, a_log, dt_bias, x_full, halo, weights, marks, stage, w_out):
     rows = x_full.shape[0]
     blocks = rows // BLOCK_LEN
     per = 2
@@ -715,7 +724,7 @@
     return pl.pallas_call(
         functools.partial(fwd_kernel, heads, pieces, blocks // per, per, span_pieces, norm_at),
         grid=(blocks // per,),
-        in_specs=[pl.BlockSpec(memory_space=pltpu.SMEM)] + [vmem] * 4 + [hbm] * 2,
+        in_specs=[vmem] * 6 + [hbm] * 2,
         out_specs=[whole(*f.shape) for f in front] + [
             token(heads * HEAD), token(heads * HEAD), whole(heads, HEAD, HEAD), whole(pieces, heads, HEAD, HEAD),
             token(heads * WIDE),
@@ -741,7 +750,7 @@
             vmem_limit_bytes=VMEM_LIMIT, collective_id=3, has_side_effects=True
         ),
         name="recurrence_forward",
-    )(rates, x_full, halo, weights, marks, stage, w_out)
+    )(a_log, dt_bias, x_full, halo, weights, marks, stage, w_out)
 
 
 def middle_kernel(
@@ -993,18 +1002,18 @@
         return carry
 
     out_back(0, 0)
-    early = max(1, hops - 1)
-    for r in range(1, early):
-        for line_sum in sums:
+    early = early_rounds(pieces)
+    for line_sum, ended in zip(sums, early):
+        for r in range(1, ended):
             line_sum.round(r)
     lax.fori_loop(1, size, out_back, 0)
     grad = dot(mixed_ref[...], low[...], 0, 0)
     for c in range(pieces):
         outg_ref[c // 2, c % 2] = grad[c * held : (c + 1) * held].astype(BF16)
-    for pair, line_sum in zip(pairs, sums):
-        line_sum.settle(early)
+    for pair, line_sum, ended in zip(pairs, sums, early):
+        line_sum.settle(ended)
         pair.left()
-        for r in range(early):
+        for r in range(ended):
             line_sum.left(r)
 
     for i in range(1, size):
@@ -1100,8 +1109,8 @@
         for distance in range(1, spread.reach + 1):
             spread.hop(distance)
         spread.finish()
-        for one in early:
-            one.launch(begun)
+        for one, first in zip(early, begun):
+            one.launch(first)
         pair.start()
 
         farthest = jnp.minimum(here + span_pieces, pieces - 1)
@@ -1121,9 +1130,10 @@
         gw_ref[...] = jnp.zeros_like(gw_ref)
         gsum_ref[...] = jnp.zeros_like(gsum_ref)
 
-    for r in range(begun + 1, rounds):
-        at = min(steps - 1, 1 + ((r - begun) * (steps - 1)) // (rounds - begun))
-        pl.when(step == at)(lambda r=r: [one.round(r) for one in early] and None)
+    for one, first in zip(early, begun):
+        for r in range(first + 1, rounds):
+            at = min(steps - 1, 1 + ((r - first) * (steps - 1)) // (rounds - first))
+            pl.when(step == at)(lambda one=one, r=r: one.round(r))
     pl.when(step == 1)(pair.add)
     for r in range(rounds):
         pl.when(step == when_round[r])(lambda r=r: line.round(r))
@@ -1286,8 +1296,8 @@
         outsum_ref[...] = oheld[here // 2].astype(F32)
         gatesum_ref[...] = gheld[here // 2]
         pair.left()
-        for r in range(begun, rounds):
-            for one in early:
+        for one, first in zip(early, begun):
+            for r in range(first, rounds):
                 one.left(r)
         for r in range(rounds):
             line.left(r)
@@ -1315,7 +1325,7 @@
     gate_chunk = (HEADS // heads, out_chunk[0], ggate.shape[1])
     dma = pltpu.SemaphoreType.DMA
     return pl.pallas_call(
-        functools.partial(bwd_kernel, heads, pieces, blocks // per, per, max(1, chips - 2), span_pieces),
+        functools.partial(bwd_kernel, heads, pieces, blocks // per, per, early_rounds(pieces), span_pieces),
         grid=(blocks // per,),
         in_specs=[
             vmem, vmem, vmem, vmem, vmem,
@@ -1689,11 +1699,10 @@
             for lag in range(1, 9)
         ]
     )
-    rates = jnp.stack([a_log.astype(F32), dt_bias.astype(F32)])
     (
         proj_ext, normed, gate_out, tokp, slopes, colp, rowp, conv_w, norms,
         oloc, carr, state_in, maps, *saved, wg_full, wu_full, wo_full,
-    ) = recurrence_forward(heads, pieces, span_pieces, norm_at, rates, x_full, halo, weights, marks, stage, out_proj)
+    ) = recurrence_forward(heads, pieces, span_pieces, norm_at, a_log[None, :], dt_bias[None, :], x_full, halo, weights, marks, stage, out_proj)
     (
         final_out, grad_middle, grad_heads, grad_gate_out, cot, gain_term, norm_mlp_term, loss, wide, tall, outg,
     ) = middle_part(

time: 278 us -> 274 us (0.986)
  Pallas kernels: 273 us -> 269 us
    pallas_call x1, Pallas kernels: 89.3 us -> 80.7 us  [middle_part(): pl.pallas_call(functools.partial(middle_kernel, size, heads, float(token_...]
    pallas_call x1, Pallas kernels: 43.5 us -> 49.7 us  [recurrence_backward(): pl.pallas_call(functools.partial(bwd_kernel, heads, pieces, blocks // per...]
where the time goes in v9:
time: 274 us; the launch traced here: 273 us
  Pallas kernels  269 us (98%)
    pallas_call x1, Pallas kernels, middle_part(): pl.pallas_call(functools.partial(middle_kernel, size, heads, float(token_...  80.7 us
    pallas_call x1, Pallas kernels, recurrence_forward(): pl.pallas_call(functools.partial(fwd_kernel, heads, pieces, blocks // per...  50.8 us
    pallas_call x1, Pallas kernels, recurrence_backward(): pl.pallas_call(functools.partial(bwd_kernel, heads, pieces, blocks // per...  49.7 us
    pallas_call x1, Pallas kernels, final_part(): pl.pallas_call(functools.partial(final_kernel, size, pieces, heads, norm_...  42.5 us
    pallas_call x1, Pallas kernels, start_gather(): pl.pallas_call(functools.partial(start_kernel, size, pieces, norm_at), in...  41.9 us

profile of v9, /device:TPU:0, one launch (start us, length us, event | category | flops | bytes accessed | tf_op | source)
XLA Modules:
  0.0 273.4 jit_solution(10679448370284996978)
XLA Ops:
  0.6 0.8 pad_dynamic-slice_fusion
  1.4 0.1 fusion.6
  1.5 0.6 stack.31.marks_ref
  2.1 41.9 %start_gather.1 = (bf16[512,1024]{1,0:T(8,128)(2,1)}, bf16[16,1024]{1,0:T(8,128)(2,1)}, bf16[4,8,32,1664]{3,2,1,0:T(8,128)(2,1)}, bf16[4,2,32,768]{3,2,1,0:T(8,128)(2,1)}) custom-call(bf16[128,1024]{1,0:T(8,128)(2,1)} %x_ref.5, bf16[32,5120]{1,0:T(8,128)(2,1)} %mix_ref.1, bf16[32,1024]{1,0:T(8,128)(2,1)} %gate_ref.1, bf16[24,32]{1,0:T(8,128)(2,1)} %bitcast.33, ...), custom_call_target="tpu_custom_call" | custom-call | tf_op jit(solution)/shard_map/start_gather/pallas_call | solution.py:451
  44.0 50.8 %recurrence_forward.1 = (bf16[528,1280]{1,0:T(8,128)(2,1)}, bf16[512,1024]{1,0:T(8,128)(2,1)}, f32[512,256]{1,0:T(8,128)}, f32[512,128]{1,0:T(8,128)}, f32[512,1...) custom-call(bf16[1,8]{1,0:T(2,128)(2,1)} %bitcast.40, ...), custom_call_target="tpu_custom_call" | custom-call | tf_op jit(solution)/shard_map/recurrence_forward/pallas_call | solution.py:724
  94.8 80.7 %middle_part.1 = (bf16[128,1024]{1,0:T(8,128)(2,1)}, f32[128,1024]{1,0:T(8,128)}, bf16[512,256]{1,0:T(8,128)(2,1)}, bf16[512,256]{1,0:T(8,128)(2,1)}, f32[2,128,...) custom-call(bf16[128,1024]{1,0:T(8,128)(2,1)} %x_ref.5, ...), custom_call_target="tpu_custom_call" | custom-call | tf_op jit(solution)/shard_map/middle_part/pallas_call | solution.py:1040
  175.6 49.7 %recurrence_backward.1 = (bf16[512,1280]{1,0:T(8,128)(2,1)}, bf16[8,1280]{1,0:T(8,128)(2,1)}, f32[8,1280]{1,0:T(8,128)}, bf16[512,128]{1,0:T(8,128)(2,1)}, f32[8...) custom-call(bf16[8,2,128,128]{3,2,1,0:T(8,128)(2,1)} %get-tuple-elem, ...), custom_call_target="tpu_custom_call" | custom-call | tf_op jit(solution)/shard_map/recurrence_backward/pallas_call | solution.py:1327
  225.2 42.5 %final_part.1 = (f32[128,1024]{1,0:T(8,128)}, f32[32,5120]{1,0:T(8,128)}, f32[32,1024]{1,0:T(8,128)}, f32[32,128]{1,0:T(8,128)}, f32[32,2816]{1,0:T(8,128)}, /*i...) custom-call(bf16[512,1280]{1,0:T(8,128)(2,1)} %get-tuple-element.125.gp_any, ...), custom_call_target="tpu_custom_call" | custom-call | tf_op jit(solution)/shard_map/final_part/pallas_call | solution.py:1600
  267.7 3.9 %finish_part.1 = (bf16[128,1024]{1,0:T(8,128)(2,1)}, f32[128,1024]{1,0:T(8,128)}, f32[32,5120]{1,0:T(8,128)}, f32[32,1024]{1,0:T(8,128)}, f32[32,2816]{1,0:T(8,1...) custom-call(bf16[128,1024]{1,0:T(8,128)(2,1)} %get-tuple-element.101, ...), custom_call_target="tpu_custom_call" | custom-call | tf_op jit(solution)/shard_map/finish_part/pallas_call | solution.py:1658
  (2 shorter events, 0.0 us)

commit v10 on v9

--- a/solution.py
+++ b/solution.py
@@ -1132,7 +1132,7 @@
 
     for one, first in zip(early, begun):
         for r in range(first + 1, rounds):
-            at = min(steps - 1, 1 + ((r - first) * (steps - 1)) // (rounds - first))
+            at = steps - 1
             pl.when(step == at)(lambda one=one, r=r: one.round(r))
     pl.when(step == 1)(pair.add)
     for r in range(rounds):

time: 274 us -> 272 us (level)
    pallas_call x1, Pallas kernels: 42.5 us -> 37.9 us  [final_part(): pl.pallas_call(functools.partial(final_kernel, size, pieces, heads, norm_...]
where the time goes in v10:
time: 272 us; the launch traced here: 271 us
  Pallas kernels  267 us (98%)
    pallas_call x1, Pallas kernels, middle_part(): pl.pallas_call(functools.partial(middle_kernel, size, heads, float(token_...  80.7 us
    pallas_call x1, Pallas kernels, recurrence_backward(): pl.pallas_call(functools.partial(bwd_kernel, heads, pieces, blocks // per...  52.1 us
    pallas_call x1, Pallas kernels, recurrence_forward(): pl.pallas_call(functools.partial(fwd_kernel, heads, pieces, blocks // per...  50.8 us
    pallas_call x1, Pallas kernels, start_gather(): pl.pallas_call(functools.partial(start_kernel, size, pieces, norm_at), in...  41.9 us
    pallas_call x1, Pallas kernels, final_part(): pl.pallas_call(functools.partial(final_kernel, size, pieces, heads, norm_...  37.9 us

profile of v10, /device:TPU:0, one launch (start us, length us, event | category | flops | bytes accessed | tf_op | source)
XLA Modules:
  0.0 271.2 jit_solution(5287432469645197707)
XLA Ops:
  0.6 0.8 pad_dynamic-slice_fusion
  1.4 0.1 fusion.6
  1.5 0.6 stack.31.marks_ref
  2.1 41.9 %start_gather.1 = (bf16[512,1024]{1,0:T(8,128)(2,1)}, bf16[16,1024]{1,0:T(8,128)(2,1)}, bf16[4,8,32,1664]{3,2,1,0:T(8,128)(2,1)}, bf16[4,2,32,768]{3,2,1,0:T(8,128)(2,1)}) custom-call(bf16[128,1024]{1,0:T(8,128)(2,1)} %x_ref.5, bf16[32,5120]{1,0:T(8,128)(2,1)} %mix_ref.1, bf16[32,1024]{1,0:T(8,128)(2,1)} %gate_ref.1, bf16[24,32]{1,0:T(8,128)(2,1)} %bitcast.33, ...), custom_call_target="tpu_custom_call" | custom-call | tf_op jit(solution)/shard_map/start_gather/pallas_call | solution.py:451
  44.0 50.8 %recurrence_forward.1 = (bf16[528,1280]{1,0:T(8,128)(2,1)}, bf16[512,1024]{1,0:T(8,128)(2,1)}, f32[512,256]{1,0:T(8,128)}, f32[512,128]{1,0:T(8,128)}, f32[512,1...) custom-call(bf16[1,8]{1,0:T(2,128)(2,1)} %bitcast.40, ...), custom_call_target="tpu_custom_call" | custom-call | tf_op jit(solution)/shard_map/recurrence_forward/pallas_call | solution.py:724
  94.8 80.7 %middle_part.1 = (bf16[128,1024]{1,0:T(8,128)(2,1)}, f32[128,1024]{1,0:T(8,128)}, bf16[512,256]{1,0:T(8,128)(2,1)}, bf16[512,256]{1,0:T(8,128)(2,1)}, f32[2,128,...) custom-call(bf16[128,1024]{1,0:T(8,128)(2,1)} %x_ref.5, ...), custom_call_target="tpu_custom_call" | custom-call | tf_op jit(solution)/shard_map/middle_part/pallas_call | solution.py:1040
  175.6 52.1 %recurrence_backward.1 = (bf16[512,1280]{1,0:T(8,128)(2,1)}, bf16[8,1280]{1,0:T(8,128)(2,1)}, f32[8,1280]{1,0:T(8,128)}, bf16[512,128]{1,0:T(8,128)(2,1)}, f32[8...) custom-call(bf16[8,2,128,128]{3,2,1,0:T(8,128)(2,1)} %get-tuple-elem, ...), custom_call_target="tpu_custom_call" | custom-call | tf_op jit(solution)/shard_map/recurrence_backward/pallas_call | solution.py:1327
  227.6 37.9 %final_part.1 = (f32[128,1024]{1,0:T(8,128)}, f32[32,5120]{1,0:T(8,128)}, f32[32,1024]{1,0:T(8,128)}, f32[32,128]{1,0:T(8,128)}, f32[32,2816]{1,0:T(8,128)}, /*i...) custom-call(bf16[512,1280]{1,0:T(8,128)(2,1)} %get-tuple-element.125.gp_any, ...), custom_call_target="tpu_custom_call" | custom-call | tf_op jit(solution)/shard_map/final_part/pallas_call | solution.py:1600
  265.5 3.9 %finish_part.1 = (bf16[128,1024]{1,0:T(8,128)(2,1)}, f32[128,1024]{1,0:T(8,128)}, f32[32,5120]{1,0:T(8,128)}, f32[32,1024]{1,0:T(8,128)}, f32[32,2816]{1,0:T(8,1...) custom-call(bf16[128,1024]{1,0:T(8,128)(2,1)} %get-tuple-element.101, ...), custom_call_target="tpu_custom_call" | custom-call | tf_op jit(solution)/shard_map/finish_part/pallas_call | solution.py:1658
  (2 shorter events, 0.0 us)
